TPU v7x, 256 devices: a whole 4x4x8 slice. The times are simulated.
256 devices in a mesh: seq: 16 (over z, core), tp: 16 (over y, x).
Axes of the slice: x: 4, y: 4, z: 8, core: 2. Of those that a mesh axis runs over, the one named last changes fastest.
Arguments:
- tokens: bfloat16 [8192, 4096], P('seq', 'tp'), may hold values from -60 to 60
- w_qkv: bfloat16 [4096, 3, 4096], P(None, None, 'tp'), may hold values from -0.09375 to 0.09375
- w_out: bfloat16 [4096, 4096], P('tp'), may hold values from -0.09375 to 0.09375
- rand_blocks: int32 [128, 32, 3], P('seq', 'tp'), may hold values from 0 to 127, as said below
- glob_blocks: int32 [2], replicated, may hold values from 0 to 127, as said below
- window_radius: int32 [32], P('tp'), may hold values from 0 to 1, as said below
Outputs:
- mixed: bfloat16 [8192, 4096], P('seq', 'tp')
Inputs may be any that keep to these rules, and one draw needn't show every extreme that they name: `rand_blocks`: split the blocks into aligned runs of 8 blocks. For one head and the query blocks of one run, the 24 entries lie at most C = ceil(8 * 3 / 16) times in any one run, and exactly C times in some run. `glob_blocks`: the 2 ids are distinct; the last block, 127, is always one of them. `window_radius`: some head has radius 1.
All inputs are finite; a program needn't handle non-finite values.
Results may differ from a plain program's by a relative error of at most 0.033.
Values may be sent and summed in bfloat16 or wider, within the bound.
No kernel may reach another device: no remote copies, remote signals or barrier semaphores. Data moves between devices by JAX's collectives and lax.ppermute only.
A program may use at most 128 MiB of HBM per device.

v0:
```python
import math

import jax
import jax.numpy as jnp
from jax import lax
from jax.experimental import pallas as pl
from jax.experimental.pallas import tpu as pltpu
from jax.sharding import Mesh, PartitionSpec as P

DH = 128
BLK = 64
NZ = 8
NXY = 4
NEG = -1e30
OFFS = (0, -1, 1, 2)


def shift(a, axis, step):
    n = lax.axis_size(axis)
    return lax.ppermute(a, axis, [(i, (i + step) % n) for i in range(n)])


def around4(a, axis):
    return [shift(a, axis, 1), shift(a, axis, -1), shift(a, axis, 2)]


def plane_matmul(a, w, finish, out_shape, name, extra=()):
    n = a.shape[0] // 2
    near, far = [], []
    for part, first, second in ((a[:n], "x", "y"), (a[n:], "y", "x")):
        stack = jnp.concatenate([part, *around4(part, first)], axis=0)
        near.append(stack)
        far.append((shift(stack, second, 1), shift(stack, second, -1)))

    def blocks(v):
        return v.reshape(-1, n, 256)

    sums = partial_matmul((0,), [[blocks(v)] for v in near], w, None, name)
    far, sums, extra = lax.optimization_barrier((far, sums, extra))
    last = []
    for (low, high), second in zip(far, "yx"):
        last.append((shift(low[: 2 * n], second, 1), shift(high[2 * n :], second, -1)))
    sums = partial_matmul((1, 2), [[blocks(v) for v in f] for f in far], w, sums, name)
    out = partial_matmul((3,), [[blocks(v) for v in f] for f in last], w, sums, name, finish, out_shape)
    return out, extra


def partial_kernel(steps, counts, n, groups, has_sums, finish, *refs):
    n_x = sum(len(c) for c in counts)
    x_refs, w_ref = refs[:n_x], refs[n_x]
    sums_ref = refs[n_x + 1] if has_sums else None
    x_buf, w_buf, acc, x_sem, w_sem, s_sem = refs[-6:]
    outs = refs[n_x + 1 + has_sums : -6]
    y = lax.axis_index("y")
    x = lax.axis_index("x")
    copies = []
    i = 0
    for half in range(2):
        at = 0
        for count in counts[half]:
            copies.append(
                pltpu.make_async_copy(x_refs[i], x_buf.at[half, pl.ds(at, count)], x_sem.at[i])
            )
            at += count
            i += 1
    for k, step in enumerate(steps):
        for half in range(2):
            for j in range(NXY):
                iy, ix = (step, j) if half == 0 else (j, step)
                owner = lax.rem(y + OFFS[iy] + NXY, NXY) * NXY + lax.rem(x + OFFS[ix] + NXY, NXY)
                row = pl.multiple_of(owner * 256, 256)
                copies.append(
                    pltpu.make_async_copy(
                        w_ref.at[:, pl.ds(row, 256)],
                        w_buf.at[2 * k + half, :, pl.ds(j * 256, 256)],
                        w_sem.at[2 * k + half, j],
                    )
                )
    if has_sums:
        copies.append(pltpu.make_async_copy(sums_ref, acc, s_sem))
    for copy in copies:
        copy.start()
    for copy in copies:
        copy.wait()
    for half in range(2):
        span = slice(half * n, (half + 1) * n)
        for k in range(len(steps)):
            rows = jnp.concatenate([x_buf[half, NXY * k + j] for j in range(NXY)], axis=1)
            for g in range(groups):
                cols = slice(g * 256, (g + 1) * 256)
                part = jnp.dot(rows, w_buf[2 * k + half, g], preferred_element_type=jnp.float32)
                if has_sums or k:
                    part = acc[span, cols] + part
                acc[span, cols] = part
    if finish is None:
        copy = pltpu.make_async_copy(acc, outs[0], s_sem)
        copy.start()
        copy.wait()
    else:
        finish(acc, *outs)


ANY = pl.BlockSpec(memory_space=pl.ANY)
VMEM = pl.BlockSpec(memory_space=pltpu.VMEM)
SMEM = pl.BlockSpec(memory_space=pltpu.SMEM)
PARAMS = pltpu.CompilerParams(vmem_limit_bytes=56 * 1024 * 1024)


def partial_matmul(steps, halves, w, sums, name, finish=None, out_shape=None):
    counts = [[v.shape[0] for v in half] for half in halves]
    xs = [v for half in halves for v in half]
    n, groups = xs[0].shape[1], w.shape[0]
    total = jax.ShapeDtypeStruct((2 * n, 256 * groups), jnp.float32)
    has_sums = sums is not None
    operands = [*xs, w] + ([sums] if has_sums else [])
    bf16 = jnp.bfloat16
    return pl.pallas_call(
        lambda *refs: partial_kernel(steps, counts, n, groups, has_sums, finish, *refs),
        out_shape=total if finish is None else out_shape,
        in_specs=[ANY] * len(operands),
        out_specs=ANY if finish is None else jax.tree.map(lambda _: VMEM, out_shape),
        scratch_shapes=[
            pltpu.VMEM((2, NXY * len(steps), n, 256), bf16),
            pltpu.VMEM((2 * len(steps), groups, 1024, 256), bf16),
            pltpu.VMEM((2 * n, 256 * groups), jnp.float32),
            pltpu.SemaphoreType.DMA((len(xs),)),
            pltpu.SemaphoreType.DMA((2 * len(steps), NXY)),
            pltpu.SemaphoreType.DMA(()),
        ],
        compiler_params=PARAMS,
        name=name + str(steps[0]),
    )(*operands)


def split_heads(acc, mine_ref, send_ref):
    first = lax.axis_index("core") == 0
    for g in range(3):
        h0 = acc[:, g * 256 : g * 256 + DH].astype(jnp.bfloat16)
        h1 = acc[:, g * 256 + DH : (g + 1) * 256].astype(jnp.bfloat16)
        mine_ref[g] = jnp.where(first, h0, h1)
        send_ref[g] = jnp.where(first, h1, h0)


def round_out(acc, o_ref):
    o_ref[...] = acc[...].astype(jnp.bfloat16)


def order_kernel(w_ref, o_ref):
    first = lax.axis_index("core") == 0
    h0, h1 = w_ref[:DH], w_ref[DH:]
    o_ref[:DH] = jnp.where(first, h0, h1)
    o_ref[DH:] = jnp.where(first, h1, h0)


def order(w_out):
    return pl.pallas_call(
        order_kernel,
        out_shape=jax.ShapeDtypeStruct((4096, 256), jnp.bfloat16),
        grid=(16,),
        in_specs=[pl.BlockSpec((256, 256), lambda t: (0, t))],
        out_specs=pl.BlockSpec((256, 256), lambda t: (t, 0)),
        name="order",
    )(w_out)


def z_ring(kv):
    f1, b1 = shift(kv, "z", 1), shift(kv, "z", -1)
    f2, b2 = shift(f1, "z", 1), shift(b1, "z", -1)
    f3, b3 = shift(f2, "z", 1), shift(b2, "z", -1)
    return [kv, f1, b1, f2, b2, f3, b3, shift(f3[0], "z", 1), shift(b3[1], "z", -1)]


SLOTS = (0, 7, 1, 6, 2, 5, 3)


def attend_kernel(*refs):
    rand_ref, glob_ref, radius_ref, mine_ref, theirs_ref = refs[:5]
    kv_refs = refs[5:14]
    o_ref, kv_buf, q_buf, sem = refs[14:]
    k_buf, v_buf = kv_buf.at[0], kv_buf.at[1]
    copies = [(mine_ref.at[0], q_buf.at[0]), (theirs_ref.at[0], q_buf.at[1])]
    copies += [(array, kv_buf.at[:, slot]) for array, slot in zip(kv_refs, SLOTS)]
    copies += [(kv_refs[7], k_buf.at[4]), (kv_refs[8], v_buf.at[4])]
    copies = [pltpu.make_async_copy(src, dst, sem.at[i]) for i, (src, dst) in enumerate(copies)]
    for copy in copies:
        copy.start()
    for copy in copies:
        copy.wait()

    z = lax.axis_index("z")
    core = lax.axis_index("core")
    radius = radius_ref[core]
    scale = 1.0 / math.sqrt(DH)

    def place(block):
        slot = lax.rem(block // 16 - z + NZ, NZ)
        side = lax.rem(block // 8 + core, 2)
        return slot, pl.multiple_of(side * 512 + lax.rem(block, 8) * BLK, BLK)

    column = lax.broadcasted_iota(jnp.int32, (BLK, 8 * BLK), 1) // BLK
    nt = (((1,), (1,)), ((), ()))

    def one_block(side, j):
        block = z * 16 + lax.rem(core + side, 2) * 8 + j
        base = lax.rem(core + side, 2) * 48 + (j * 2 + core) * 3
        ids = [jnp.maximum(block - 1, 0), block, jnp.minimum(block + 1, 127)]
        ids += [rand_ref[base + r] for r in range(3)] + [glob_ref[g] for g in range(2)]
        places = [place(i) for i in ids]
        keys = jnp.concatenate([k_buf[slot, pl.ds(row, BLK)] for slot, row in places], axis=0)
        values = jnp.concatenate([v_buf[slot, pl.ds(row, BLK)] for slot, row in places], axis=0)
        mine = pl.ds(pl.multiple_of(j * BLK, BLK), BLK)
        scores = lax.dot_general(q_buf[side, mine], keys, nt, preferred_element_type=jnp.float32) * scale
        low_off = jnp.where((radius >= 1) & (block > 0), -1, 0)
        high_off = jnp.where((radius >= 1) & (block < 127), -1, 2)
        scores = jnp.where((column == low_off) | (column == high_off), NEG, scores)
        top = jnp.max(scores, axis=1, keepdims=True)
        probs = jnp.exp(scores - top)
        total = jnp.sum(probs, axis=1, keepdims=True)
        acc = jnp.dot(probs.astype(jnp.bfloat16), values, preferred_element_type=jnp.float32)
        o_ref[side, mine] = (acc / total).astype(jnp.bfloat16)

    def four_blocks(i, carry):
        for u in range(4):
            one_block(i // 2, lax.rem(i, 2) * 4 + u)
        return carry

    lax.fori_loop(0, 4, four_blocks, 0)

    glob = [glob_ref[g] for g in range(2)]
    owned = [g // 16 == z for g in glob]

    @pl.when(owned[0] | owned[1])
    def _():
        queries = []
        for g in glob:
            row = pl.multiple_of(lax.rem(g, 8) * BLK, BLK)
            queries.append(q_buf[lax.rem(g // 8 + core, 2), pl.ds(row, BLK)])
        query = jnp.concatenate(queries, axis=0)

        def step(i, carry):
            top, total, acc = carry
            scores = lax.dot_general(query, k_buf[i], nt, preferred_element_type=jnp.float32) * scale
            new = jnp.maximum(top, jnp.max(scores, axis=1, keepdims=True))
            factor = jnp.exp(top - new)
            probs = jnp.exp(scores - new)
            total = total * factor + jnp.sum(probs, axis=1, keepdims=True)
            acc = acc * factor + jnp.dot(probs.astype(jnp.bfloat16), v_buf[i], preferred_element_type=jnp.float32)
            return new, total, acc

        init = (
            jnp.full((2 * BLK, 1), NEG, jnp.float32),
            jnp.zeros((2 * BLK, 1), jnp.float32),
            jnp.zeros((2 * BLK, DH), jnp.float32),
        )
        _, total, acc = lax.fori_loop(0, NZ, step, init)
        result = (acc / total).astype(jnp.bfloat16)
        for k, g in enumerate(glob):

            @pl.when(owned[k])
            def _(k=k, g=g):
                row = pl.multiple_of(lax.rem(g, 8) * BLK, BLK)
                o_ref[lax.rem(g // 8 + core, 2), pl.ds(row, BLK)] = result[k * BLK : (k + 1) * BLK]


def attend(rand, glob, radius, mine, theirs, ring):
    bf16 = jnp.bfloat16
    return pl.pallas_call(
        attend_kernel,
        out_shape=jax.ShapeDtypeStruct((2, 512, DH), bf16),
        in_specs=[SMEM] * 3 + [ANY] * 11,
        out_specs=VMEM,
        scratch_shapes=[
            pltpu.VMEM((2, NZ, 1024, DH), bf16),
            pltpu.VMEM((2, 512, DH), bf16),
            pltpu.SemaphoreType.DMA((11,)),
        ],
        compiler_params=PARAMS,
        name="attend",
    )(rand, glob, radius, mine, theirs, *ring)


def swap(a):
    return lax.ppermute(a, "core", [(0, 1), (1, 0)])


def body(tokens, w_qkv, w_out, rand_blocks, glob_blocks, window_radius):
    bf16 = jnp.bfloat16
    rand = lax.all_gather(rand_blocks.reshape(-1), "core", axis=0, tiled=True)
    part = jax.ShapeDtypeStruct((3, 512, DH), bf16)
    (mine, send), (ordered, rand) = plane_matmul(
        tokens, w_qkv.transpose(1, 0, 2), split_heads, (part, part), "project", (order(w_out), rand)
    )
    theirs = swap(send)
    ring = z_ring(jnp.concatenate([mine[1:], theirs[1:]], axis=1))
    ordered, _ = lax.optimization_barrier((ordered, ring[1]))
    w_cols = lax.all_to_all(ordered, ("y", "x"), 0, 0, tiled=True)
    mine, w_cols = lax.optimization_barrier((mine, w_cols))
    att = attend(rand, glob_blocks, window_radius, mine, theirs, ring)
    attended = jnp.concatenate([att[0], swap(att[1])], axis=1)
    out = jax.ShapeDtypeStruct((512, 256), bf16)
    return plane_matmul(attended, w_cols[None], round_out, out, "output")[0]


def solution(mesh):
    grid = Mesh(mesh.devices.reshape(NZ, 2, NXY, NXY), ("z", "core", "y", "x"))
    seq, tp = ("z", "core"), ("y", "x")
    return jax.shard_map(
        body,
        mesh=grid,
        in_specs=(P(seq, tp), P(None, None, tp), P(tp, None), P(seq, tp, None), P(), P(tp)),
        out_specs=P(seq, tp),
        check_vma=False,
    )
```

profile of v0, /device:TPU:24, one launch (start us, length us, event | category | flops | bytes accessed | tf_op | source)
XLA Modules:
  0.0 176.1 jit_solution(13076060774393632977)
XLA Ops:
  1.0 3.1 %collective-permute-start.2 = (bf16[256,256]{1,0:T(8,128)(2,1)S(1)}, bf16[256,256]{1,0:T(8,128)(2,1)S(1)}, u32[]{:S(2)}, u32[]{:S(2)}) collective-permute-start(bf16[256,256]{1,0:T(8,128)(2,1)S(1)} %get-tuple-element.44), channel_id=1, source_target_pairs={{0,2},{1,3},{2,0},{3,1},{4,6},{5,7},{6,4},{7,5},{8,10},{9,11},{10,... | collective-permute-start | bytes 393224 | tf_op jit(solution)/shard_map/ppermute | solution.py:20
  8.8 1.8 %collective-permute-start.5 = (bf16[256,256]{1,0:T(8,128)(2,1)S(1)}, bf16[256,256]{1,0:T(8,128)(2,1)S(1)}, u32[]{:S(2)}, u32[]{:S(2)}) collective-permute-start(bf16[256,256]{1,0:T(8,128)(2,1)S(1)} %get-tuple-element.43), channel_id=1, source_target_pairs={{0,4},{4,8},{8,12},{12,0},{1,5},{5,9},{9,13},{13,1},{2,6},{6,10},{... | collective-permute-start | bytes 393224 | tf_op jit(solution)/shard_map/ppermute | solution.py:20
  12.3 2.5 %collective-permute-start.3 = (bf16[1024,256]{1,0:T(8,128)(2,1)S(1)}, bf16[1024,256]{1,0:T(8,128)(2,1)S(1)}, u32[]{:S(2)}, u32[]{:S(2)}) collective-permute-start(bf16[1024,256]{1,0:T(8,128)(2,1)S(1)} %pad_maximum_fusion), channel_id=1, source_target_pairs={{0,4},{4,8},{8,12},{12,0},{1,5},{5,9},{9,13},{13,1},{2,6},{6,10},{... | collective-permute-start | bytes 1572872 | tf_op jit(solution)/shard_map/ppermute | solution.py:20
  18.3 9.5 %order.1 = bf16[4096,256]{1,0:T(8,128)(2,1)} custom-call(bf16[256,4096]{1,0:T(8,128)(2,1)} %w_ref.1), custom_call_target="tpu_custom_call" | custom-call | tf_op jit(solution)/shard_map/order/pallas_call | solution.py:156
  29.3 2.3 %all-reduce.refs_0_ = s32[96]{0:T(128)} all-reduce(s32[96]{0:T(128)S(1)} %dynamic-update-slice), channel_id=1, replica_groups=mesh['z'=8,'core'=2,'y'=4,'x'=4] {'core'}, use_global_device_ids=true, to_apply=%add | all-reduce | flops 96 | bytes 768 | tf_op jit(solution)/shard_map/optimization_barrier | solution.py:39
  31.7 4.4 %project0.1.refs_5_ = f32[512,768]{1,0:T(8,128)} custom-call(bf16[4,256,256]{2,1,0:T(8,128)(2,1)} %bitcast.40, bf16[4,256,256]{2,1,0:T(8,128)(2,1)} %bitcast.41, bf16[3,4096,256]{2,1,0:T(8,128)(2,1)} %bitcast.33), custom_call_target="tpu_custom_call" | custom-call | tf_op jit(solution)/shard_map/project0/pallas_call | solution.py:117
  36.3 2.5 %collective-permute-start.13 = (bf16[512,256]{1,0:T(8,128)(2,1)S(1)}, bf16[512,256]{1,0:T(8,128)(2,1)S(1)}, u32[]{:S(2)}, u32[]{:S(2)}) collective-permute-start(bf16[512,256]{1,0:T(8,128)(2,1)S(1)} %slice.59), channel_id=1, source_target_pairs={{0,3},{1,0},{2,1},{3,2},{4,7},{5,4},{6,5},{7,6},{8,11},{9,8},{10,9... | collective-permute-start | bytes 786440 | tf_op jit(solution)/shard_map/ppermute | solution.py:20
  38.8 1.8 %collective-permute-start.11 = (bf16[512,256]{1,0:T(8,128)(2,1)S(1)}, bf16[512,256]{1,0:T(8,128)(2,1)S(1)}, u32[]{:S(2)}, u32[]{:S(2)}) collective-permute-start(bf16[512,256]{1,0:T(8,128)(2,1)S(1)} %slice.57), channel_id=1, source_target_pairs={{0,12},{4,0},{8,4},{12,8},{1,13},{5,1},{9,5},{13,9},{2,14},{6,2},{... | collective-permute-start | bytes 786440 | tf_op jit(solution)/shard_map/ppermute | solution.py:20
  42.0 7.1 %project1.1.refs_5_ = f32[512,768]{1,0:T(8,128)} custom-call(bf16[4,256,256]{2,1,0:T(8,128)(2,1)} %bitcast.45, bf16[4,256,256]{2,1,0:T(8,128)(2,1)} %bitcast.44, bf16[4,256,256]{2,1,0:T(8,128)(2,1)} %bitcast.47, bf16[4,256,256]{2,1,0:T(8,128)(2,1)} %bitcast.46, bf16[3,4096,256]{2,1,0:T(8,128)(2,1)} %bitcast.34, f32[512,768]{1,0:T(8,128)} %project0.1.refs_5_), custom_call_target="tpu_custom_call" | custom-call | tf_op jit(solution)/shard_map/project1/pallas_call | solution.py:117
  50.1 4.7 %project3.1 = (bf16[3,512,128]{2,1,0:T(8,128)(2,1)}, bf16[3,512,128]{2,1,0:T(8,128)(2,1)}) custom-call(bf16[2,256,256]{2,1,0:T(8,128)(2,1)} %bitcast.55, bf16[2,256,256]{2,1,0:T(8,128)(2,1)} %bitcast.54, bf16[2,256,256]{2,1,0:T(8,128)(2,1)} %bitcast.53, bf16[2,256,256]{2,1,0:T(8,128)(2,1)} %bitcast.52, bf16[3,4096,256]{2,1,0:T(8,128)(2,1)} %bitcast.35, ...), custom_call_target="tpu_custom_call" | custom-call | tf_op jit(solution)/shard_map/project3/pallas_call | solution.py:117
  56.9 2.0 %collective-permute-start.15 = (bf16[2,1024,128]{2,1,0:T(8,128)(2,1)S(1)}, bf16[2,1024,128]{2,1,0:T(8,128)(2,1)S(1)}, u32[]{:S(2)}, u32[]{:S(2)}) collective-permute-start(bf16[2,1024,128]{2,1,0:T(8,128)(2,1)S(1)} %pad_maximum_fusion.2.refs_5_), channel_id=1, source_target_pairs={{0,32},{32,64},{64,96},{96,128},{128,160},{160,192},{192,224},{224... | collective-permute-start | bytes 1572872 | tf_op jit(solution)/shard_map/ppermute | solution.py:20
  58.9 4.0 %collective-permute-start.16 = (bf16[2,1024,128]{2,1,0:T(8,128)(2,1)S(1)}, bf16[2,1024,128]{2,1,0:T(8,128)(2,1)}, u32[]{:S(2)}, u32[]{:S(2)}) collective-permute-start(bf16[2,1024,128]{2,1,0:T(8,128)(2,1)S(1)} %pad_maximum_fusion.2.refs_5_), channel_id=1, source_target_pairs={{0,224},{32,0},{64,32},{96,64},{128,96},{160,128},{192,160},{224,1... | collective-permute-start | bytes 1572872 | tf_op jit(solution)/shard_map/ppermute | solution.py:20
  62.9 12.1 %collective-permute-done.15.refs_6_ = bf16[2,1024,128]{2,1,0:T(8,128)(2,1)S(1)} collective-permute-done((bf16[2,1024,128]{2,1,0:T(8,128)(2,1)S(1)}, bf16[2,1024,128]{2,1,0:T(8,128)(2,1)S(1)}, u32[]{:S(2)}, u32[]{:S(2)}) %collective-permute-start.15) | collective-permute-done | bytes 524320 | tf_op jit(solution)/shard_map/ppermute | solution.py:20
  75.0 7.3 %all-to-all-start = ((bf16[16,256,256]{2,1,0:T(8,128)(2,1)}), bf16[16,256,256]{2,1,0:T(8,128)(2,1)S(1)}, u32[]{:S(2)}, u32[]{:S(2)}) async-start(bf16[16,256,256]{2,1,0:T(8,128)(2,1)} %bitcast.39), calls=%async_computation | async-start | bytes 4194304 | tf_op jit(solution)/shard_map/all_to_all | solution.py:296
  82.3 1.8 %collective-permute-start.18 = (bf16[2,1024,128]{2,1,0:T(8,128)(2,1)}, bf16[2,1024,128]{2,1,0:T(8,128)(2,1)S(1)}, u32[]{:S(2)}, u32[]{:S(2)}) collective-permute-start(bf16[2,1024,128]{2,1,0:T(8,128)(2,1)} %collective-permute-done.16.refs_7_), channel_id=1, source_target_pairs={{0,224},{32,0},{64,32},{96,64},{128,96},{160,128},{192,160},{224,1... | collective-permute-start | bytes 1572872 | tf_op jit(solution)/shard_map/ppermute | solution.py:20
  84.4 11.1 %collective-permute-done.18.refs_9_ = bf16[2,1024,128]{2,1,0:T(8,128)(2,1)S(1)} collective-permute-done((bf16[2,1024,128]{2,1,0:T(8,128)(2,1)}, bf16[2,1024,128]{2,1,0:T(8,128)(2,1)S(1)}, u32[]{:S(2)}, u32[]{:S(2)}) %collective-permute-start.18) | collective-permute-done | bytes 524320 | tf_op jit(solution)/shard_map/ppermute | solution.py:20
  95.5 2.7 %collective-permute-start.20 = (bf16[2,1024,128]{2,1,0:T(8,128)(2,1)S(1)}, bf16[2,1024,128]{2,1,0:T(8,128)(2,1)S(1)}, u32[]{:S(2)}, u32[]{:S(2)}) collective-permute-start(bf16[2,1024,128]{2,1,0:T(8,128)(2,1)S(1)} %collective-permute-done.18.refs_9_), channel_id=1, source_target_pairs={{0,224},{32,0},{64,32},{96,64},{128,96},{160,128},{192,160},{224,1... | collective-permute-start | bytes 1572872 | tf_op jit(solution)/shard_map/ppermute | solution.py:20
  98.3 9.2 %collective-permute-done.20.refs_11_ = bf16[2,1024,128]{2,1,0:T(8,128)(2,1)S(1)} collective-permute-done((bf16[2,1024,128]{2,1,0:T(8,128)(2,1)S(1)}, bf16[2,1024,128]{2,1,0:T(8,128)(2,1)S(1)}, u32[]{:S(2)}, u32[]{:S(2)}) %collective-permute-start.20) | collective-permute-done | bytes 524320 | tf_op jit(solution)/shard_map/ppermute | solution.py:20
  108.3 3.7 %collective-permute-start.22 = (bf16[1024,128]{1,0:T(8,128)(2,1)}, bf16[1024,128]{1,0:T(8,128)(2,1)S(1)}, u32[]{:S(2)}, u32[]{:S(2)}) collective-permute-start(bf16[1024,128]{1,0:T(8,128)(2,1)} %slice_bitcast_fusion), channel_id=1, source_target_pairs={{0,224},{32,0},{64,32},{96,64},{128,96},{160,128},{192,160},{224,1... | collective-permute-start | bytes 786440 | tf_op jit(solution)/shard_map/ppermute | solution.py:20
  112.8 3.4 %collective-permute-done.22.refs_13_ = bf16[1024,128]{1,0:T(8,128)(2,1)S(1)} collective-permute-done((bf16[1024,128]{1,0:T(8,128)(2,1)}, bf16[1024,128]{1,0:T(8,128)(2,1)S(1)}, u32[]{:S(2)}, u32[]{:S(2)}) %collective-permute-start.22) | collective-permute-done | bytes 262176 | tf_op jit(solution)/shard_map/ppermute | solution.py:20
  116.2 4.5 %collective-permute-done.21.refs_12_ = bf16[1024,128]{1,0:T(8,128)(2,1)} collective-permute-done((bf16[1024,128]{1,0:T(8,128)(2,1)}, bf16[1024,128]{1,0:T(8,128)(2,1)}, u32[]{:S(2)}, u32[]{:S(2)}) %collective-permute-start.21) | collective-permute-done | bytes 262176 | tf_op jit(solution)/shard_map/ppermute | solution.py:20
  120.6 8.7 %attend.1 = bf16[2,512,128]{2,1,0:T(8,128)(2,1)} custom-call(s32[96]{0:T(128)} %all-reduce.refs_0_, s32[2]{0:T(128)} %refs_1_.1, s32[2]{0:T(128)} %refs_2_.1, bf16[3,512,128]{2,1,0:T(8,128)(2,1)} %get-tuple-element.32.refs_3_, bf16[3,512,128]{2,1,0:T(8,128)(2,1)} %copy-done.16, bf16[2,1024,128]{2,1,0:T(8,128)(2,1)} %copy-done.1, ...), custom_call_target="tpu_custom_call" | custom-call | tf_op jit(solution)/shard_map/attend/pallas_call | solution.py:267
  131.8 3.1 %collective-permute-start.26 = (bf16[256,256]{1,0:T(8,128)(2,1)S(1)}, bf16[256,256]{1,0:T(8,128)(2,1)S(1)}, u32[]{:S(2)}, u32[]{:S(2)}) collective-permute-start(bf16[256,256]{1,0:T(8,128)(2,1)S(1)} %get-tuple-element.40), channel_id=1, source_target_pairs={{0,2},{1,3},{2,0},{3,1},{4,6},{5,7},{6,4},{7,5},{8,10},{9,11},{10,... | collective-permute-start | bytes 393224 | tf_op jit(solution)/shard_map/ppermute | solution.py:20
  139.7 1.8 %collective-permute-start.29 = (bf16[256,256]{1,0:T(8,128)(2,1)S(1)}, bf16[256,256]{1,0:T(8,128)(2,1)S(1)}, u32[]{:S(2)}, u32[]{:S(2)}) collective-permute-start(bf16[256,256]{1,0:T(8,128)(2,1)S(1)} %get-tuple-element.39), channel_id=1, source_target_pairs={{0,4},{4,8},{8,12},{12,0},{1,5},{5,9},{9,13},{13,1},{2,6},{6,10},{... | collective-permute-start | bytes 393224 | tf_op jit(solution)/shard_map/ppermute | solution.py:20
  143.4 2.4 %collective-permute-start.27 = (bf16[1024,256]{1,0:T(8,128)(2,1)S(1)}, bf16[1024,256]{1,0:T(8,128)(2,1)S(1)}, u32[]{:S(2)}, u32[]{:S(2)}) collective-permute-start(bf16[1024,256]{1,0:T(8,128)(2,1)S(1)} %pad_maximum_fusion.3), channel_id=1, source_target_pairs={{0,4},{4,8},{8,12},{12,0},{1,5},{5,9},{9,13},{13,1},{2,6},{6,10},{... | collective-permute-start | bytes 1572872 | tf_op jit(solution)/shard_map/ppermute | solution.py:20
  148.8 2.9 %output0.1.refs_5_ = f32[512,256]{1,0:T(8,128)} custom-call(bf16[4,256,256]{2,1,0:T(8,128)(2,1)} %bitcast.42, bf16[4,256,256]{2,1,0:T(8,128)(2,1)} %bitcast.43, bf16[1,4096,256]{2,1,0:T(8,128)(2,1)} %bitcast.36), custom_call_target="tpu_custom_call" | custom-call | tf_op jit(solution)/shard_map/output0/pallas_call | solution.py:117
  151.7 5.5 %collective-permute-done.28 = bf16[1024,256]{1,0:T(8,128)(2,1)S(1)} collective-permute-done((bf16[1024,256]{1,0:T(8,128)(2,1)S(1)}, bf16[1024,256]{1,0:T(8,128)(2,1)S(1)}, u32[]{:S(2)}, u32[]{:S(2)}) %collective-permute-start.28) | collective-permute-done | bytes 524320 | tf_op jit(solution)/shard_map/ppermute | solution.py:20
  157.2 1.9 %collective-permute-done.33 = bf16[1024,256]{1,0:T(8,128)(2,1)S(1)} collective-permute-done((bf16[1024,256]{1,0:T(8,128)(2,1)S(1)}, bf16[1024,256]{1,0:T(8,128)(2,1)S(1)}, u32[]{:S(2)}, u32[]{:S(2)}) %collective-permute-start.33) | collective-permute-done | bytes 524320 | tf_op jit(solution)/shard_map/ppermute | solution.py:20
  159.1 3.3 %collective-permute-done.32 = bf16[1024,256]{1,0:T(8,128)(2,1)S(1)} collective-permute-done((bf16[1024,256]{1,0:T(8,128)(2,1)S(1)}, bf16[1024,256]{1,0:T(8,128)(2,1)S(1)}, u32[]{:S(2)}, u32[]{:S(2)}) %collective-permute-start.32) | collective-permute-done | bytes 524320 | tf_op jit(solution)/shard_map/ppermute | solution.py:20
  165.2 2.6 %collective-permute-start.34 = (bf16[512,256]{1,0:T(8,128)(2,1)S(1)}, bf16[512,256]{1,0:T(8,128)(2,1)S(1)}, u32[]{:S(2)}, u32[]{:S(2)}) collective-permute-start(bf16[512,256]{1,0:T(8,128)(2,1)S(1)} %slice.68), channel_id=1, source_target_pairs={{0,4},{4,8},{8,12},{12,0},{1,5},{5,9},{9,13},{13,1},{2,6},{6,10},{... | collective-permute-start | bytes 786440 | tf_op jit(solution)/shard_map/ppermute | solution.py:20
  167.8 4.1 %output1.1.refs_5_ = f32[512,256]{1,0:T(8,128)} custom-call(bf16[4,256,256]{2,1,0:T(8,128)(2,1)} %bitcast.49, bf16[4,256,256]{2,1,0:T(8,128)(2,1)} %bitcast.48, bf16[4,256,256]{2,1,0:T(8,128)(2,1)} %bitcast.51, bf16[4,256,256]{2,1,0:T(8,128)(2,1)} %bitcast.50, bf16[1,4096,256]{2,1,0:T(8,128)(2,1)} %bitcast.37, f32[512,256]{1,0:T(8,128)} %output0.1.refs_5_), custom_call_target="tpu_custom_call" | custom-call | tf_op jit(solution)/shard_map/output1/pallas_call | solution.py:117
  173.0 3.0 %output3.1 = bf16[512,256]{1,0:T(8,128)(2,1)} custom-call(bf16[2,256,256]{2,1,0:T(8,128)(2,1)} %bitcast.59, bf16[2,256,256]{2,1,0:T(8,128)(2,1)} %bitcast.58, bf16[2,256,256]{2,1,0:T(8,128)(2,1)} %bitcast.57, bf16[2,256,256]{2,1,0:T(8,128)(2,1)} %bitcast.56, bf16[1,4096,256]{2,1,0:T(8,128)(2,1)} %bitcast.38, f32[512,256]{1,0:T(8,128)} %output1.1.refs_5_), custom_call_target="tpu_custom_call" | custom-call | tf_op jit(solution)/shard_map/output3/pallas_call | solution.py:117
  (142 shorter events, 34.0 us)
Async XLA Ops:
  1.0 7.8 %collective-permute-start.2 = (bf16[256,256]{1,0:T(8,128)(2,1)S(1)}, bf16[256,256]{1,0:T(8,128)(2,1)S(1)}, u32[]{:S(2)}, u32[]{:S(2)}) collective-permute-start(bf16[256,256]{1,0:T(8,128)(2,1)S(1)} %get-tuple-element.44), channel_id=1, source_target_pairs={{0,2},{1,3},{2,0},{3,1},{4,6},{5,7},{6,4},{7,5},{8,10},{9,11},{10,... | collective-permute-start | bytes 393224 | tf_op jit(solution)/shard_map/ppermute | solution.py:20
  6.1 8.7 %collective-permute-start.7 = (bf16[256,256]{1,0:T(8,128)(2,1)S(1)}, bf16[256,256]{1,0:T(8,128)(2,1)S(1)}, u32[]{:S(2)}, u32[]{:S(2)}) collective-permute-start(bf16[256,256]{1,0:T(8,128)(2,1)S(1)} %get-tuple-element.43), channel_id=1, source_target_pairs={{0,8},{4,12},{8,0},{12,4},{1,9},{5,13},{9,1},{13,5},{2,10},{6,14},... | collective-permute-start | bytes 393224 | tf_op jit(solution)/shard_map/ppermute | solution.py:20
  7.4 8.6 %collective-permute-start.6 = (bf16[256,256]{1,0:T(8,128)(2,1)S(1)}, bf16[256,256]{1,0:T(8,128)(2,1)S(1)}, u32[]{:S(2)}, u32[]{:S(2)}) collective-permute-start(bf16[256,256]{1,0:T(8,128)(2,1)S(1)} %get-tuple-element.43), channel_id=1, source_target_pairs={{0,12},{4,0},{8,4},{12,8},{1,13},{5,1},{9,5},{13,9},{2,14},{6,2},{... | collective-permute-start | bytes 393224 | tf_op jit(solution)/shard_map/ppermute | solution.py:20
  8.8 7.2 %collective-permute-start.5 = (bf16[256,256]{1,0:T(8,128)(2,1)S(1)}, bf16[256,256]{1,0:T(8,128)(2,1)S(1)}, u32[]{:S(2)}, u32[]{:S(2)}) collective-permute-start(bf16[256,256]{1,0:T(8,128)(2,1)S(1)} %get-tuple-element.43), channel_id=1, source_target_pairs={{0,4},{4,8},{8,12},{12,0},{1,5},{5,9},{9,13},{13,1},{2,6},{6,10},{... | collective-permute-start | bytes 393224 | tf_op jit(solution)/shard_map/ppermute | solution.py:20
  11.5 24.6 %collective-permute-start.4 = (bf16[1024,256]{1,0:T(8,128)(2,1)S(1)}, bf16[1024,256]{1,0:T(8,128)(2,1)S(1)}, u32[]{:S(2)}, u32[]{:S(2)}) collective-permute-start(bf16[1024,256]{1,0:T(8,128)(2,1)S(1)} %pad_maximum_fusion), channel_id=1, source_target_pairs={{0,12},{4,0},{8,4},{12,8},{1,13},{5,1},{9,5},{13,9},{2,14},{6,2},{... | collective-permute-start | bytes 1572872 | tf_op jit(solution)/shard_map/ppermute | solution.py:20
  12.3 23.8 %collective-permute-start.3 = (bf16[1024,256]{1,0:T(8,128)(2,1)S(1)}, bf16[1024,256]{1,0:T(8,128)(2,1)S(1)}, u32[]{:S(2)}, u32[]{:S(2)}) collective-permute-start(bf16[1024,256]{1,0:T(8,128)(2,1)S(1)} %pad_maximum_fusion), channel_id=1, source_target_pairs={{0,4},{4,8},{8,12},{12,0},{1,5},{5,9},{9,13},{13,1},{2,6},{6,10},{... | collective-permute-start | bytes 1572872 | tf_op jit(solution)/shard_map/ppermute | solution.py:20
  16.0 20.1 %collective-permute-start.9 = (bf16[1024,256]{1,0:T(8,128)(2,1)S(1)}, bf16[1024,256]{1,0:T(8,128)(2,1)S(1)}, u32[]{:S(2)}, u32[]{:S(2)}) collective-permute-start(bf16[1024,256]{1,0:T(8,128)(2,1)S(1)} %pad_maximum_fusion.1), channel_id=1, source_target_pairs={{0,3},{1,0},{2,1},{3,2},{4,7},{5,4},{6,5},{7,6},{8,11},{9,8},{10,9... | collective-permute-start | bytes 1572872 | tf_op jit(solution)/shard_map/ppermute | solution.py:20
  17.3 18.8 %collective-permute-start.8 = (bf16[1024,256]{1,0:T(8,128)(2,1)S(1)}, bf16[1024,256]{1,0:T(8,128)(2,1)S(1)}, u32[]{:S(2)}, u32[]{:S(2)}) collective-permute-start(bf16[1024,256]{1,0:T(8,128)(2,1)S(1)} %pad_maximum_fusion.1), channel_id=1, source_target_pairs={{0,1},{1,2},{2,3},{3,0},{4,5},{5,6},{6,7},{7,4},{8,9},{9,10},{10,1... | collective-permute-start | bytes 1572872 | tf_op jit(solution)/shard_map/ppermute | solution.py:20
  36.3 12.8 %collective-permute-start.13 = (bf16[512,256]{1,0:T(8,128)(2,1)S(1)}, bf16[512,256]{1,0:T(8,128)(2,1)S(1)}, u32[]{:S(2)}, u32[]{:S(2)}) collective-permute-start(bf16[512,256]{1,0:T(8,128)(2,1)S(1)} %slice.59), channel_id=1, source_target_pairs={{0,3},{1,0},{2,1},{3,2},{4,7},{5,4},{6,5},{7,6},{8,11},{9,8},{10,9... | collective-permute-start | bytes 786440 | tf_op jit(solution)/shard_map/ppermute | solution.py:20
  38.8 10.4 %collective-permute-start.12 = (bf16[512,256]{1,0:T(8,128)(2,1)S(1)}, bf16[512,256]{1,0:T(8,128)(2,1)S(1)}, u32[]{:S(2)}, u32[]{:S(2)}) collective-permute-start(bf16[512,256]{1,0:T(8,128)(2,1)S(1)} %slice.58), channel_id=1, source_target_pairs={{0,1},{1,2},{2,3},{3,0},{4,5},{5,6},{6,7},{7,4},{8,9},{9,10},{10,1... | collective-permute-start | bytes 786440 | tf_op jit(solution)/shard_map/ppermute | solution.py:20
  38.8 10.4 %collective-permute-start.11 = (bf16[512,256]{1,0:T(8,128)(2,1)S(1)}, bf16[512,256]{1,0:T(8,128)(2,1)S(1)}, u32[]{:S(2)}, u32[]{:S(2)}) collective-permute-start(bf16[512,256]{1,0:T(8,128)(2,1)S(1)} %slice.57), channel_id=1, source_target_pairs={{0,12},{4,0},{8,4},{12,8},{1,13},{5,1},{9,5},{13,9},{2,14},{6,2},{... | collective-permute-start | bytes 786440 | tf_op jit(solution)/shard_map/ppermute | solution.py:20
  40.6 8.6 %collective-permute-start.10 = (bf16[512,256]{1,0:T(8,128)(2,1)S(1)}, bf16[512,256]{1,0:T(8,128)(2,1)S(1)}, u32[]{:S(2)}, u32[]{:S(2)}) collective-permute-start(bf16[512,256]{1,0:T(8,128)(2,1)S(1)} %slice.56), channel_id=1, source_target_pairs={{0,4},{4,8},{8,12},{12,0},{1,5},{5,9},{9,13},{13,1},{2,6},{6,10},{... | collective-permute-start | bytes 786440 | tf_op jit(solution)/shard_map/ppermute | solution.py:20
  56.9 18.2 %collective-permute-start.15 = (bf16[2,1024,128]{2,1,0:T(8,128)(2,1)S(1)}, bf16[2,1024,128]{2,1,0:T(8,128)(2,1)S(1)}, u32[]{:S(2)}, u32[]{:S(2)}) collective-permute-start(bf16[2,1024,128]{2,1,0:T(8,128)(2,1)S(1)} %pad_maximum_fusion.2.refs_5_), channel_id=1, source_target_pairs={{0,32},{32,64},{64,96},{96,128},{128,160},{160,192},{192,224},{224... | collective-permute-start | bytes 1572872 | tf_op jit(solution)/shard_map/ppermute | solution.py:20
  58.9 23.4 %collective-permute-start.16 = (bf16[2,1024,128]{2,1,0:T(8,128)(2,1)S(1)}, bf16[2,1024,128]{2,1,0:T(8,128)(2,1)}, u32[]{:S(2)}, u32[]{:S(2)}) collective-permute-start(bf16[2,1024,128]{2,1,0:T(8,128)(2,1)S(1)} %pad_maximum_fusion.2.refs_5_), channel_id=1, source_target_pairs={{0,224},{32,0},{64,32},{96,64},{128,96},{160,128},{192,160},{224,1... | collective-permute-start | bytes 1572872 | tf_op jit(solution)/shard_map/ppermute | solution.py:20
  75.0 37.7 %all-to-all-start = ((bf16[16,256,256]{2,1,0:T(8,128)(2,1)}), bf16[16,256,256]{2,1,0:T(8,128)(2,1)S(1)}, u32[]{:S(2)}, u32[]{:S(2)}) async-start(bf16[16,256,256]{2,1,0:T(8,128)(2,1)} %bitcast.39), calls=%async_computation | async-start | bytes 4194304 | tf_op jit(solution)/shard_map/all_to_all | solution.py:296
  82.3 13.2 %collective-permute-start.18 = (bf16[2,1024,128]{2,1,0:T(8,128)(2,1)}, bf16[2,1024,128]{2,1,0:T(8,128)(2,1)S(1)}, u32[]{:S(2)}, u32[]{:S(2)}) collective-permute-start(bf16[2,1024,128]{2,1,0:T(8,128)(2,1)} %collective-permute-done.16.refs_7_), channel_id=1, source_target_pairs={{0,224},{32,0},{64,32},{96,64},{128,96},{160,128},{192,160},{224,1... | collective-permute-start | bytes 1572872 | tf_op jit(solution)/shard_map/ppermute | solution.py:20
  84.1 14.1 %collective-permute-start.17 = (bf16[2,1024,128]{2,1,0:T(8,128)(2,1)S(1)}, bf16[2,1024,128]{2,1,0:T(8,128)(2,1)S(1)}, u32[]{:S(2)}, u32[]{:S(2)}) collective-permute-start(bf16[2,1024,128]{2,1,0:T(8,128)(2,1)S(1)} %collective-permute-done.15.refs_6_), channel_id=1, source_target_pairs={{0,32},{32,64},{64,96},{96,128},{128,160},{160,192},{192,224},{224... | collective-permute-start | bytes 1572872 | tf_op jit(solution)/shard_map/ppermute | solution.py:20
  95.5 12.0 %collective-permute-start.20 = (bf16[2,1024,128]{2,1,0:T(8,128)(2,1)S(1)}, bf16[2,1024,128]{2,1,0:T(8,128)(2,1)S(1)}, u32[]{:S(2)}, u32[]{:S(2)}) collective-permute-start(bf16[2,1024,128]{2,1,0:T(8,128)(2,1)S(1)} %collective-permute-done.18.refs_9_), channel_id=1, source_target_pairs={{0,224},{32,0},{64,32},{96,64},{128,96},{160,128},{192,160},{224,1... | collective-permute-start | bytes 1572872 | tf_op jit(solution)/shard_map/ppermute | solution.py:20
  98.2 13.7 %collective-permute-start.19 = (bf16[2,1024,128]{2,1,0:T(8,128)(2,1)S(1)}, bf16[2,1024,128]{2,1,0:T(8,128)(2,1)S(1)}, u32[]{:S(2)}, u32[]{:S(2)}) collective-permute-start(bf16[2,1024,128]{2,1,0:T(8,128)(2,1)S(1)} %collective-permute-done.17.refs_8_), channel_id=1, source_target_pairs={{0,32},{32,64},{64,96},{96,128},{128,160},{160,192},{192,224},{224... | collective-permute-start | bytes 1572872 | tf_op jit(solution)/shard_map/ppermute | solution.py:20
  108.3 7.9 %collective-permute-start.22 = (bf16[1024,128]{1,0:T(8,128)(2,1)}, bf16[1024,128]{1,0:T(8,128)(2,1)S(1)}, u32[]{:S(2)}, u32[]{:S(2)}) collective-permute-start(bf16[1024,128]{1,0:T(8,128)(2,1)} %slice_bitcast_fusion), channel_id=1, source_target_pairs={{0,224},{32,0},{64,32},{96,64},{128,96},{160,128},{192,160},{224,1... | collective-permute-start | bytes 786440 | tf_op jit(solution)/shard_map/ppermute | solution.py:20
  112.7 7.9 %collective-permute-start.21 = (bf16[1024,128]{1,0:T(8,128)(2,1)}, bf16[1024,128]{1,0:T(8,128)(2,1)}, u32[]{:S(2)}, u32[]{:S(2)}) collective-permute-start(bf16[1024,128]{1,0:T(8,128)(2,1)} %slice_bitcast_fusion.1), channel_id=1, source_target_pairs={{0,32},{32,64},{64,96},{96,128},{128,160},{160,192},{192,224},{224... | collective-permute-start | bytes 786440 | tf_op jit(solution)/shard_map/ppermute | solution.py:20
  131.8 7.9 %collective-permute-start.26 = (bf16[256,256]{1,0:T(8,128)(2,1)S(1)}, bf16[256,256]{1,0:T(8,128)(2,1)S(1)}, u32[]{:S(2)}, u32[]{:S(2)}) collective-permute-start(bf16[256,256]{1,0:T(8,128)(2,1)S(1)} %get-tuple-element.40), channel_id=1, source_target_pairs={{0,2},{1,3},{2,0},{3,1},{4,6},{5,7},{6,4},{7,5},{8,10},{9,11},{10,... | collective-permute-start | bytes 393224 | tf_op jit(solution)/shard_map/ppermute | solution.py:20
  136.9 8.9 %collective-permute-start.31 = (bf16[256,256]{1,0:T(8,128)(2,1)S(1)}, bf16[256,256]{1,0:T(8,128)(2,1)S(1)}, u32[]{:S(2)}, u32[]{:S(2)}) collective-permute-start(bf16[256,256]{1,0:T(8,128)(2,1)S(1)} %get-tuple-element.39), channel_id=1, source_target_pairs={{0,8},{4,12},{8,0},{12,4},{1,9},{5,13},{9,1},{13,5},{2,10},{6,14},... | collective-permute-start | bytes 393224 | tf_op jit(solution)/shard_map/ppermute | solution.py:20
  138.4 8.2 %collective-permute-start.30 = (bf16[256,256]{1,0:T(8,128)(2,1)S(1)}, bf16[256,256]{1,0:T(8,128)(2,1)S(1)}, u32[]{:S(2)}, u32[]{:S(2)}) collective-permute-start(bf16[256,256]{1,0:T(8,128)(2,1)S(1)} %get-tuple-element.39), channel_id=1, source_target_pairs={{0,12},{4,0},{8,4},{12,8},{1,13},{5,1},{9,5},{13,9},{2,14},{6,2},{... | collective-permute-start | bytes 393224 | tf_op jit(solution)/shard_map/ppermute | solution.py:20
  142.4 14.7 %collective-permute-start.28 = (bf16[1024,256]{1,0:T(8,128)(2,1)S(1)}, bf16[1024,256]{1,0:T(8,128)(2,1)S(1)}, u32[]{:S(2)}, u32[]{:S(2)}) collective-permute-start(bf16[1024,256]{1,0:T(8,128)(2,1)S(1)} %pad_maximum_fusion.3), channel_id=1, source_target_pairs={{0,12},{4,0},{8,4},{12,8},{1,13},{5,1},{9,5},{13,9},{2,14},{6,2},{... | collective-permute-start | bytes 1572872 | tf_op jit(solution)/shard_map/ppermute | solution.py:20
  143.4 13.8 %collective-permute-start.27 = (bf16[1024,256]{1,0:T(8,128)(2,1)S(1)}, bf16[1024,256]{1,0:T(8,128)(2,1)S(1)}, u32[]{:S(2)}, u32[]{:S(2)}) collective-permute-start(bf16[1024,256]{1,0:T(8,128)(2,1)S(1)} %pad_maximum_fusion.3), channel_id=1, source_target_pairs={{0,4},{4,8},{8,12},{12,0},{1,5},{5,9},{9,13},{13,1},{2,6},{6,10},{... | collective-permute-start | bytes 1572872 | tf_op jit(solution)/shard_map/ppermute | solution.py:20
  146.6 12.4 %collective-permute-start.33 = (bf16[1024,256]{1,0:T(8,128)(2,1)S(1)}, bf16[1024,256]{1,0:T(8,128)(2,1)S(1)}, u32[]{:S(2)}, u32[]{:S(2)}) collective-permute-start(bf16[1024,256]{1,0:T(8,128)(2,1)S(1)} %pad_maximum_fusion.4), channel_id=1, source_target_pairs={{0,3},{1,0},{2,1},{3,2},{4,7},{5,4},{6,5},{7,6},{8,11},{9,8},{10,9... | collective-permute-start | bytes 1572872 | tf_op jit(solution)/shard_map/ppermute | solution.py:20
  148.4 13.9 %collective-permute-start.32 = (bf16[1024,256]{1,0:T(8,128)(2,1)S(1)}, bf16[1024,256]{1,0:T(8,128)(2,1)S(1)}, u32[]{:S(2)}, u32[]{:S(2)}) collective-permute-start(bf16[1024,256]{1,0:T(8,128)(2,1)S(1)} %pad_maximum_fusion.4), channel_id=1, source_target_pairs={{0,1},{1,2},{2,3},{3,0},{4,5},{5,6},{6,7},{7,4},{8,9},{9,10},{10,1... | collective-permute-start | bytes 1572872 | tf_op jit(solution)/shard_map/ppermute | solution.py:20
  162.5 9.5 %collective-permute-start.37 = (bf16[512,256]{1,0:T(8,128)(2,1)S(1)}, bf16[512,256]{1,0:T(8,128)(2,1)S(1)}, u32[]{:S(2)}, u32[]{:S(2)}) collective-permute-start(bf16[512,256]{1,0:T(8,128)(2,1)S(1)} %slice.71), channel_id=1, source_target_pairs={{0,3},{1,0},{2,1},{3,2},{4,7},{5,4},{6,5},{7,6},{8,11},{9,8},{10,9... | collective-permute-start | bytes 786440 | tf_op jit(solution)/shard_map/ppermute | solution.py:20
  162.8 9.1 %collective-permute-start.36 = (bf16[512,256]{1,0:T(8,128)(2,1)S(1)}, bf16[512,256]{1,0:T(8,128)(2,1)S(1)}, u32[]{:S(2)}, u32[]{:S(2)}) collective-permute-start(bf16[512,256]{1,0:T(8,128)(2,1)S(1)} %slice.70), channel_id=1, source_target_pairs={{0,1},{1,2},{2,3},{3,0},{4,5},{5,6},{6,7},{7,4},{8,9},{9,10},{10,1... | collective-permute-start | bytes 786440 | tf_op jit(solution)/shard_map/ppermute | solution.py:20
  164.6 7.6 %collective-permute-start.35 = (bf16[512,256]{1,0:T(8,128)(2,1)S(1)}, bf16[512,256]{1,0:T(8,128)(2,1)S(1)}, u32[]{:S(2)}, u32[]{:S(2)}) collective-permute-start(bf16[512,256]{1,0:T(8,128)(2,1)S(1)} %slice.69), channel_id=1, source_target_pairs={{0,12},{4,0},{8,4},{12,8},{1,13},{5,1},{9,5},{13,9},{2,14},{6,2},{... | collective-permute-start | bytes 786440 | tf_op jit(solution)/shard_map/ppermute | solution.py:20
  165.2 6.9 %collective-permute-start.34 = (bf16[512,256]{1,0:T(8,128)(2,1)S(1)}, bf16[512,256]{1,0:T(8,128)(2,1)S(1)}, u32[]{:S(2)}, u32[]{:S(2)}) collective-permute-start(bf16[512,256]{1,0:T(8,128)(2,1)S(1)} %slice.68), channel_id=1, source_target_pairs={{0,4},{4,8},{8,12},{12,0},{1,5},{5,9},{9,13},{13,1},{2,6},{6,10},{... | collective-permute-start | bytes 786440 | tf_op jit(solution)/shard_map/ppermute | solution.py:20
  (38 other events, 271.8 us)
where the time goes:
time: 179 us; the launch traced here: 176 us
  starting transfers between devices  60.6 us (34%)
  waiting for transfers between devices  59.9 us (33%)
  Pallas kernels  44.4 us (25%)
  local copies, waits for them, and re-layouts  7.45 us (4%)
  blocking collectives  2.35 us (1%)
    ppermute x36, waiting for transfers between devices, shift(): return lax.ppermute(a, axis, [(i, (i + step) % n) for i in range(n)])  57.6 us
    ppermute x36, starting transfers between devices, shift(): return lax.ppermute(a, axis, [(i, (i + step) % n) for i in range(n)])  53.1 us
    pallas_call x6, Pallas kernels, partial_matmul(): pl.pallas_call(lambda *refs: partial_kernel(steps, counts, n, groups, has...  26.2 us
    pallas_call x1, Pallas kernels, order(): pl.pallas_call(order_kernel, out_shape=jax.ShapeDtypeStruct((4096, 256),...  9.5 us
    pallas_call x1, Pallas kernels, attend(): pl.pallas_call(attend_kernel, out_shape=jax.ShapeDtypeStruct((2, 512, DH)...  8.68 us
    all_to_all x1, starting transfers between devices, body(): w_cols = lax.all_to_all(ordered, ('y', 'x'), 0, 0, tiled=True)  7.27 us
  transfers between devices with their start and end apart: 39, of which 19 were waited for; matrix products, arithmetic and copies ran while one was open for 2% of the time, Pallas kernels for 16%

commit v1 on v0

--- a/solution.py
+++ b/solution.py
@@ -26,22 +26,24 @@
 
 def plane_matmul(a, w, finish, out_shape, name, extra=()):
     n = a.shape[0] // 2
-    near, far = [], []
-    for part, first, second in ((a[:n], "x", "y"), (a[n:], "y", "x")):
-        stack = jnp.concatenate([part, *around4(part, first)], axis=0)
+    parts = ((a[:n], "x", "y"), (a[n:], "y", "x"))
+    around = lax.optimization_barrier([around4(part, first) for part, first, _ in parts])
+    near, next_to, across = [], [], []
+    for (part, _, second), others in zip(parts, around):
+        stack = jnp.concatenate([part, *others], axis=0)
+        low, high, far = around4(stack, second)
         near.append(stack)
-        far.append((shift(stack, second, 1), shift(stack, second, -1)))
+        next_to.append((low, high))
+        across.append(far)
 
     def blocks(v):
         return v.reshape(-1, n, 256)
 
     sums = partial_matmul((0,), [[blocks(v)] for v in near], w, None, name)
-    far, sums, extra = lax.optimization_barrier((far, sums, extra))
-    last = []
-    for (low, high), second in zip(far, "yx"):
-        last.append((shift(low[: 2 * n], second, 1), shift(high[2 * n :], second, -1)))
-    sums = partial_matmul((1, 2), [[blocks(v) for v in f] for f in far], w, sums, name)
-    out = partial_matmul((3,), [[blocks(v) for v in f] for f in last], w, sums, name, finish, out_shape)
+    next_to, sums, extra = lax.optimization_barrier((next_to, sums, extra))
+    sums = partial_matmul((1, 2), [[blocks(v) for v in f] for f in next_to], w, sums, name)
+    across, sums = lax.optimization_barrier((across, sums))
+    out = partial_matmul((3,), [[blocks(v)] for v in across], w, sums, name, finish, out_shape)
     return out, extra
 
 
@@ -53,45 +55,54 @@
     outs = refs[n_x + 1 + has_sums : -6]
     y = lax.axis_index("y")
     x = lax.axis_index("x")
-    copies = []
+    x_copies = []
     i = 0
     for half in range(2):
         at = 0
         for count in counts[half]:
-            copies.append(
-                pltpu.make_async_copy(x_refs[i], x_buf.at[half, pl.ds(at, count)], x_sem.at[i])
-            )
+            x_copies.append(pltpu.make_async_copy(x_refs[i], x_buf.at[half, pl.ds(at, count)], x_sem.at[i]))
             at += count
             i += 1
-    for k, step in enumerate(steps):
-        for half in range(2):
+    n_steps = len(steps)
+
+    def w_copy(part, j, owner):
+        row = pl.multiple_of(owner * 256, 256)
+        return pltpu.make_async_copy(
+            w_ref.at[:, pl.ds(row, 256)], w_buf.at[part, :, pl.ds(j * 256, 256)], w_sem.at[part, j]
+        )
+
+    if has_sums:
+        sums_copy = pltpu.make_async_copy(sums_ref, acc, s_sem)
+        sums_copy.start()
+    for half in range(2):
+        for k, step in enumerate(steps):
             for j in range(NXY):
                 iy, ix = (step, j) if half == 0 else (j, step)
                 owner = lax.rem(y + OFFS[iy] + NXY, NXY) * NXY + lax.rem(x + OFFS[ix] + NXY, NXY)
-                row = pl.multiple_of(owner * 256, 256)
-                copies.append(
-                    pltpu.make_async_copy(
-                        w_ref.at[:, pl.ds(row, 256)],
-                        w_buf.at[2 * k + half, :, pl.ds(j * 256, 256)],
-                        w_sem.at[2 * k + half, j],
-                    )
-                )
+                w_copy(half * n_steps + k, j, owner).start()
+        for copy, owner_half in zip(x_copies, [h for h in range(2) for _ in counts[h]]):
+            if owner_half == half:
+                copy.start()
     if has_sums:
-        copies.append(pltpu.make_async_copy(sums_ref, acc, s_sem))
-    for copy in copies:
-        copy.start()
-    for copy in copies:
+        sums_copy.wait()
+    for copy in x_copies:
         copy.wait()
-    for half in range(2):
-        span = slice(half * n, (half + 1) * n)
-        for k in range(len(steps)):
-            rows = jnp.concatenate([x_buf[half, NXY * k + j] for j in range(NXY)], axis=1)
-            for g in range(groups):
-                cols = slice(g * 256, (g + 1) * 256)
-                part = jnp.dot(rows, w_buf[2 * k + half, g], preferred_element_type=jnp.float32)
-                if has_sums or k:
-                    part = acc[span, cols] + part
-                acc[span, cols] = part
+
+    def multiply(part, carry):
+        half, k = part // n_steps, lax.rem(part, n_steps)
+        for j in range(NXY):
+            w_copy(part, j, 0).wait()
+        rows = jnp.concatenate([x_buf[half, NXY * k + j] for j in range(NXY)], axis=1)
+        span = pl.ds(pl.multiple_of(half * n, n), n)
+        for g in range(groups):
+            cols = slice(g * 256, (g + 1) * 256)
+            value = jnp.dot(rows, w_buf[part, g], preferred_element_type=jnp.float32)
+            if has_sums:
+                value = acc[span, cols] + value
+            acc[span, cols] = value
+        return carry
+
+    lax.fori_loop(0, 2 * n_steps, multiply, 0)
     if finish is None:
         copy = pltpu.make_async_copy(acc, outs[0], s_sem)
         copy.start()
@@ -145,42 +156,48 @@
     o_ref[...] = acc[...].astype(jnp.bfloat16)
 
 
-def order_kernel(w_ref, o_ref):
-    first = lax.axis_index("core") == 0
-    h0, h1 = w_ref[:DH], w_ref[DH:]
-    o_ref[:DH] = jnp.where(first, h0, h1)
-    o_ref[DH:] = jnp.where(first, h1, h0)
+def order_kernel(w_ref, o_ref, sem):
+    core = lax.axis_index("core")
+    copies = []
+    for h in range(2):
+        row = pl.multiple_of(lax.rem(core + h, 2) * DH, DH)
+        for t in range(16):
+            src = w_ref.at[pl.ds(row, DH), pl.ds(t * 256, 256)]
+            copies.append(pltpu.make_async_copy(src, o_ref.at[t, pl.ds(h * DH, DH)], sem.at[h, t]))
+    for copy in copies:
+        copy.start()
+    for copy in copies:
+        copy.wait()
 
 
 def order(w_out):
     return pl.pallas_call(
         order_kernel,
-        out_shape=jax.ShapeDtypeStruct((4096, 256), jnp.bfloat16),
-        grid=(16,),
-        in_specs=[pl.BlockSpec((256, 256), lambda t: (0, t))],
-        out_specs=pl.BlockSpec((256, 256), lambda t: (t, 0)),
+        out_shape=jax.ShapeDtypeStruct((16, 256, 256), jnp.bfloat16),
+        in_specs=[ANY],
+        out_specs=ANY,
+        scratch_shapes=[pltpu.SemaphoreType.DMA((2, 16))],
         name="order",
-    )(w_out)
-
-
-def z_ring(kv):
-    f1, b1 = shift(kv, "z", 1), shift(kv, "z", -1)
+    )(w_out).reshape(4096, 256)
+
+
+def z_ring(a, last):
+    f1, b1 = shift(a, "z", 1), shift(a, "z", -1)
     f2, b2 = shift(f1, "z", 1), shift(b1, "z", -1)
     f3, b3 = shift(f2, "z", 1), shift(b2, "z", -1)
-    return [kv, f1, b1, f2, b2, f3, b3, shift(f3[0], "z", 1), shift(b3[1], "z", -1)]
-
-
-SLOTS = (0, 7, 1, 6, 2, 5, 3)
+    return [a, f1, b1, f2, b2, f3, b3, shift(f3 if last > 0 else b3, "z", last)]
+
+
+SLOTS = (0, 7, 1, 6, 2, 5, 3, 4)
 
 
 def attend_kernel(*refs):
     rand_ref, glob_ref, radius_ref, mine_ref, theirs_ref = refs[:5]
-    kv_refs = refs[5:14]
-    o_ref, kv_buf, q_buf, sem = refs[14:]
-    k_buf, v_buf = kv_buf.at[0], kv_buf.at[1]
+    k_refs, v_refs, dense_ref = refs[5:13], refs[13:21], refs[21]
+    o_ref, k_buf, v_buf, q_buf, sem = refs[22:]
     copies = [(mine_ref.at[0], q_buf.at[0]), (theirs_ref.at[0], q_buf.at[1])]
-    copies += [(array, kv_buf.at[:, slot]) for array, slot in zip(kv_refs, SLOTS)]
-    copies += [(kv_refs[7], k_buf.at[4]), (kv_refs[8], v_buf.at[4])]
+    for arrays, buf in ((k_refs, k_buf), (v_refs, v_buf)):
+        copies += [(array, buf.at[slot]) for array, slot in zip(arrays, SLOTS)]
     copies = [pltpu.make_async_copy(src, dst, sem.at[i]) for i, (src, dst) in enumerate(copies)]
     for copy in copies:
         copy.start()
@@ -226,57 +243,99 @@
 
     lax.fori_loop(0, 4, four_blocks, 0)
 
-    glob = [glob_ref[g] for g in range(2)]
-    owned = [g // 16 == z for g in glob]
+    glob, owned, rows_of = owned_globals(glob_ref)
 
     @pl.when(owned[0] | owned[1])
     def _():
-        queries = []
-        for g in glob:
-            row = pl.multiple_of(lax.rem(g, 8) * BLK, BLK)
-            queries.append(q_buf[lax.rem(g // 8 + core, 2), pl.ds(row, BLK)])
-        query = jnp.concatenate(queries, axis=0)
-
-        def step(i, carry):
-            top, total, acc = carry
-            scores = lax.dot_general(query, k_buf[i], nt, preferred_element_type=jnp.float32) * scale
-            new = jnp.maximum(top, jnp.max(scores, axis=1, keepdims=True))
-            factor = jnp.exp(top - new)
-            probs = jnp.exp(scores - new)
-            total = total * factor + jnp.sum(probs, axis=1, keepdims=True)
-            acc = acc * factor + jnp.dot(probs.astype(jnp.bfloat16), v_buf[i], preferred_element_type=jnp.float32)
-            return new, total, acc
-
-        init = (
-            jnp.full((2 * BLK, 1), NEG, jnp.float32),
-            jnp.zeros((2 * BLK, 1), jnp.float32),
-            jnp.zeros((2 * BLK, DH), jnp.float32),
-        )
-        _, total, acc = lax.fori_loop(0, NZ, step, init)
+        query = jnp.concatenate([q_buf[side, pl.ds(row, BLK)] for side, row in rows_of], axis=0)
+        state = (dense_ref[0], dense_ref[1], dense_ref[2])
+        _, total, acc = dense_step(query, k_buf[4], v_buf[4], state)
         result = (acc / total).astype(jnp.bfloat16)
-        for k, g in enumerate(glob):
+        for k, (side, row) in enumerate(rows_of):
 
             @pl.when(owned[k])
-            def _(k=k, g=g):
-                row = pl.multiple_of(lax.rem(g, 8) * BLK, BLK)
-                o_ref[lax.rem(g // 8 + core, 2), pl.ds(row, BLK)] = result[k * BLK : (k + 1) * BLK]
-
-
-def attend(rand, glob, radius, mine, theirs, ring):
+            def _(k=k, side=side, row=row):
+                o_ref[side, pl.ds(row, BLK)] = result[k * BLK : (k + 1) * BLK]
+
+
+def owned_globals(glob_ref):
+    z = lax.axis_index("z")
+    core = lax.axis_index("core")
+    glob = [glob_ref[g] for g in range(2)]
+    rows_of = [(lax.rem(g // 8 + core, 2), pl.multiple_of(lax.rem(g, 8) * BLK, BLK)) for g in glob]
+    return glob, [g // 16 == z for g in glob], rows_of
+
+
+def dense_step(query, keys, values, state):
+    top, total, acc = state
+    scores = lax.dot_general(query, keys, (((1,), (1,)), ((), ())), preferred_element_type=jnp.float32)
+    scores = scores * (1.0 / math.sqrt(DH))
+    new = jnp.maximum(top, jnp.max(scores, axis=1, keepdims=True))
+    factor = jnp.exp(top - new)
+    probs = jnp.exp(scores - new[:, :1])
+    total = total * factor + jnp.sum(probs, axis=1, keepdims=True)
+    acc = acc * factor + jnp.dot(probs.astype(jnp.bfloat16), values, preferred_element_type=jnp.float32)
+    return new, total, acc
+
+
+def dense_kernel(*refs):
+    glob_ref, mine_ref, theirs_ref = refs[:3]
+    k_refs, v_refs = refs[3:10], refs[10:17]
+    o_ref, k_buf, v_buf, q_buf, sem = refs[17:]
+    _, owned, rows_of = owned_globals(glob_ref)
+
+    @pl.when(owned[0] | owned[1])
+    def _():
+        copies = [(mine_ref.at[0], q_buf.at[0]), (theirs_ref.at[0], q_buf.at[1])]
+        for arrays, buf in ((k_refs, k_buf), (v_refs, v_buf)):
+            copies += [(array, buf.at[i]) for i, array in enumerate(arrays)]
+        copies = [pltpu.make_async_copy(src, dst, sem.at[i]) for i, (src, dst) in enumerate(copies)]
+        for copy in copies:
+            copy.start()
+        for copy in copies:
+            copy.wait()
+        query = jnp.concatenate([q_buf[side, pl.ds(row, BLK)] for side, row in rows_of], axis=0)
+        shape = (2 * BLK, DH)
+        init = (jnp.full(shape, NEG, jnp.float32), jnp.zeros(shape, jnp.float32), jnp.zeros(shape, jnp.float32))
+        state = lax.fori_loop(0, 7, lambda i, state: dense_step(query, k_buf[i], v_buf[i], state), init)
+        for i, value in enumerate(state):
+            o_ref[i] = value
+
+
+def dense(glob, mine, theirs, keys, values):
+    bf16 = jnp.bfloat16
+    return pl.pallas_call(
+        dense_kernel,
+        out_shape=jax.ShapeDtypeStruct((3, 2 * BLK, DH), jnp.float32),
+        in_specs=[SMEM] + [ANY] * 16,
+        out_specs=VMEM,
+        scratch_shapes=[
+            pltpu.VMEM((7, 1024, DH), bf16),
+            pltpu.VMEM((7, 1024, DH), bf16),
+            pltpu.VMEM((2, 512, DH), bf16),
+            pltpu.SemaphoreType.DMA((16,)),
+        ],
+        compiler_params=PARAMS,
+        name="dense",
+    )(glob, mine, theirs, *keys[:7], *values[:7])
+
+
+def attend(rand, glob, radius, mine, theirs, keys, values, started):
     bf16 = jnp.bfloat16
     return pl.pallas_call(
         attend_kernel,
         out_shape=jax.ShapeDtypeStruct((2, 512, DH), bf16),
-        in_specs=[SMEM] * 3 + [ANY] * 11,
+        in_specs=[SMEM] * 3 + [ANY] * 18 + [VMEM],
         out_specs=VMEM,
         scratch_shapes=[
-            pltpu.VMEM((2, NZ, 1024, DH), bf16),
+            pltpu.VMEM((NZ, 1024, DH), bf16),
+            pltpu.VMEM((NZ, 1024, DH), bf16),
             pltpu.VMEM((2, 512, DH), bf16),
-            pltpu.SemaphoreType.DMA((11,)),
+            pltpu.SemaphoreType.DMA((18,)),
         ],
         compiler_params=PARAMS,
         name="attend",
-    )(rand, glob, radius, mine, theirs, *ring)
+    )(rand, glob, radius, mine, theirs, *keys, *values, started)
 
 
 def swap(a):
@@ -291,11 +350,13 @@
         tokens, w_qkv.transpose(1, 0, 2), split_heads, (part, part), "project", (order(w_out), rand)
     )
     theirs = swap(send)
-    ring = z_ring(jnp.concatenate([mine[1:], theirs[1:]], axis=1))
-    ordered, _ = lax.optimization_barrier((ordered, ring[1]))
+    keys = z_ring(jnp.concatenate([mine[1], theirs[1]], axis=0), 1)
+    values = z_ring(jnp.concatenate([mine[2], theirs[2]], axis=0), -1)
+    ordered, _ = lax.optimization_barrier((ordered, (keys[1:3], values[1:3])))
     w_cols = lax.all_to_all(ordered, ("y", "x"), 0, 0, tiled=True)
-    mine, w_cols = lax.optimization_barrier((mine, w_cols))
-    att = attend(rand, glob_blocks, window_radius, mine, theirs, ring)
+    started = dense(glob_blocks, mine, theirs, keys, values)
+    started, w_cols = lax.optimization_barrier((started, w_cols))
+    att = attend(rand, glob_blocks, window_radius, mine, theirs, keys, values, started)
     attended = jnp.concatenate([att[0], swap(att[1])], axis=1)
     out = jax.ShapeDtypeStruct((512, 256), bf16)
     return plane_matmul(attended, w_cols[None], round_out, out, "output")[0]

time: 179 us -> 262 us (1.46); the launches traced: 176 us -> 263 us
  Pallas kernels: 44.4 us -> 110 us
  waiting for transfers between devices: 59.9 us -> 68.7 us
  starting transfers between devices: 60.6 us -> 67.9 us
  local copies, waits for them, and re-layouts: 7.45 us -> 12.1 us
    pallas_call x1 -> x2, Pallas kernels: 9.5 us -> 72.3 us  [the longest x1 64.9 us: order(): pl.pallas_call(order_kernel, out_shape=jax.ShapeDtypeStruct((16, 256, 256...]
    ppermute x36 -> x38, waiting for transfers between devices: 57.6 us -> 66.6 us  [shift(): return lax.ppermute(a, axis, [(i, (i + step) % n) for i in range(n)])]
    ppermute x36 -> x38, starting transfers between devices: 53.1 us -> 62 us  [shift(): return lax.ppermute(a, axis, [(i, (i + step) % n) for i in range(n)])]
    unnamed x66 -> x70, local copies, waits for them, and re-layouts: 2.71 us -> 8.99 us
  transfers between devices with their start and end apart: 39 -> 41, of which waited for: 19 -> 21; matrix products, arithmetic and copies ran while one was open for 2% -> 1% of each run, Pallas kernels for 16% -> 35%
where the time goes in v1:
time: 262 us; the launch traced here: 263 us
  Pallas kernels  110 us (42%)
  waiting for transfers between devices  68.7 us (26%)
  starting transfers between devices  67.9 us (26%)
  local copies, waits for them, and re-layouts  12.1 us (5%)
    ppermute x38, waiting for transfers between devices, shift(): return lax.ppermute(a, axis, [(i, (i + step) % n) for i in range(n)])  66.6 us
    pallas_call x1, Pallas kernels, order(): pl.pallas_call(order_kernel, out_shape=jax.ShapeDtypeStruct((16, 256, 256...  64.9 us
    ppermute x38, starting transfers between devices, shift(): return lax.ppermute(a, axis, [(i, (i + step) % n) for i in range(n)])  62 us
    pallas_call x6, Pallas kernels, partial_matmul(): pl.pallas_call(lambda *refs: partial_kernel(steps, counts, n, groups, has...  28.2 us
    pallas_call x1, Pallas kernels, attend(): pl.pallas_call(attend_kernel, out_shape=jax.ShapeDtypeStruct((2, 512, DH)...  9.8 us
    unnamed x70, local copies, waits for them, and re-layouts  8.99 us
    pallas_call x1, Pallas kernels, dense(): pl.pallas_call(dense_kernel, out_shape=jax.ShapeDtypeStruct((3, 2 * BLK,...  7.42 us
    all_to_all x1, starting transfers between devices, body(): w_cols = lax.all_to_all(ordered, ('y', 'x'), 0, 0, tiled=True)  5.32 us
  transfers between devices with their start and end apart: 41, of which 21 were waited for; matrix products, arithmetic and copies ran while one was open for 1% of the time, Pallas kernels for 35%

profile of v1, /device:TPU:24, one launch (start us, length us, event | category | flops | bytes accessed | tf_op | source)
XLA Modules:
  0.0 262.9 jit_solution(5138644303101548415)
XLA Ops:
  4.3 1.8 collective-permute-start.2
  6.3 1.8 collective-permute-start.4
  15.8 2.5 collective-permute-start.9
  18.4 2.2 collective-permute-start.6
  21.8 9.2 %collective-permute-done.8 = bf16[1024,256]{1,0:T(8,128)(2,1)S(1)} collective-permute-done((bf16[1024,256]{1,0:T(8,128)(2,1)S(1)}, bf16[1024,256]{1,0:T(8,128)(2,1)S(1)}, u32[]{:S(2)}, u32[]{:S(2)}) %collective-permute-start.8) | collective-permute-done | bytes 524320 | tf_op jit(solution)/shard_map/ppermute | solution.py:20
  31.1 9.4 %collective-permute-start.10 = (bf16[1024,256]{1,0:T(8,128)(2,1)S(1)}, bf16[1024,256]{1,0:T(8,128)(2,1)}, u32[]{:S(2)}, u32[]{:S(2)}) collective-permute-start(bf16[1024,256]{1,0:T(8,128)(2,1)S(1)} %pad_maximum_fusion), channel_id=1, source_target_pairs={{0,8},{4,12},{8,0},{12,4},{1,9},{5,13},{9,1},{13,5},{2,10},{6,14},... | collective-permute-start | bytes 1572872 | tf_op jit(solution)/shard_map/ppermute | solution.py:20
  40.5 64.9 %order.1 = bf16[16,256,256]{2,1,0:T(8,128)(2,1)} custom-call(bf16[256,4096]{1,0:T(8,128)(2,1)} %w_ref.1), custom_call_target="tpu_custom_call" | custom-call | tf_op jit(solution)/shard_map/order/pallas_call | solution.py:174
  107.1 2.3 all-reduce.refs_0_
  109.5 4.6 %project0.1.refs_5_ = f32[512,768]{1,0:T(8,128)} custom-call(bf16[4,256,256]{2,1,0:T(8,128)(2,1)} %bitcast.41, bf16[4,256,256]{2,1,0:T(8,128)(2,1)} %bitcast.40, bf16[3,4096,256]{2,1,0:T(8,128)(2,1)} %bitcast.34), custom_call_target="tpu_custom_call" | custom-call | tf_op jit(solution)/shard_map/project0/pallas_call | solution.py:128
  115.1 7.5 %project1.1.refs_3_ = f32[512,768]{1,0:T(8,128)} custom-call(bf16[4,256,256]{2,1,0:T(8,128)(2,1)} %bitcast.47, bf16[4,256,256]{2,1,0:T(8,128)(2,1)} %bitcast.6.refs_1_, bf16[4,256,256]{2,1,0:T(8,128)(2,1)} %bitcast.44, bf16[4,256,256]{2,1,0:T(8,128)(2,1)} %bitcast.45, bf16[3,4096,256]{2,1,0:T(8,128)(2,1)} %bitcast.35, f32[512,768]{1,0:T(8,128)} %project0.1.refs_5_), custom_call_target="tpu_custom_call" | custom-call | tf_op jit(solution)/shard_map/project1/pallas_call | solution.py:128
  123.4 5.0 %project3.1 = (bf16[3,512,128]{2,1,0:T(8,128)(2,1)}, bf16[3,512,128]{2,1,0:T(8,128)(2,1)}) custom-call(bf16[4,256,256]{2,1,0:T(8,128)(2,1)} %bitcast.9.refs_0_, bf16[4,256,256]{2,1,0:T(8,128)(2,1)} %bitcast.46, bf16[3,4096,256]{2,1,0:T(8,128)(2,1)} %bitcast.36, f32[512,768]{1,0:T(8,128)} %project1.1.refs_3_), custom_call_target="tpu_custom_call" | custom-call | tf_op jit(solution)/shard_map/project3/pallas_call | solution.py:128
  130.5 2.2 collective-permute-start.20
  132.7 4.0 %collective-permute-start.21 = (bf16[1024,128]{1,0:T(8,128)(2,1)S(1)}, bf16[1024,128]{1,0:T(8,128)(2,1)S(1)}, u32[]{:S(2)}, u32[]{:S(2)}) collective-permute-start(bf16[1024,128]{1,0:T(8,128)(2,1)S(1)} %pad_maximum_fusion.5.refs_10_.refs_13_), channel_id=1, source_target_pairs={{0,224},{32,0},{64,32},{96,64},{128,96},{160,128},{192,160},{224,1... | collective-permute-start | bytes 786440 | tf_op jit(solution)/shard_map/ppermute | solution.py:20
  136.8 3.2 %collective-permute-start.14 = (bf16[1024,128]{1,0:T(8,128)(2,1)S(1)}, bf16[1024,128]{1,0:T(8,128)(2,1)S(1)}, u32[]{:S(2)}, u32[]{:S(2)}) collective-permute-start(bf16[1024,128]{1,0:T(8,128)(2,1)S(1)} %pad_maximum_fusion.4.refs_3_.refs_5_), channel_id=1, source_target_pairs={{0,224},{32,0},{64,32},{96,64},{128,96},{160,128},{192,160},{224,1... | collective-permute-start | bytes 786440 | tf_op jit(solution)/shard_map/ppermute | solution.py:20
  140.0 3.6 %collective-permute-done.20.refs_11_.refs_14_ = bf16[1024,128]{1,0:T(8,128)(2,1)S(1)} collective-permute-done((bf16[1024,128]{1,0:T(8,128)(2,1)S(1)}, bf16[1024,128]{1,0:T(8,128)(2,1)S(1)}, u32[]{:S(2)}, u32[]{:S(2)}) %collective-permute-start.20) | collective-permute-done | bytes 262176 | tf_op jit(solution)/shard_map/ppermute | solution.py:20
  143.7 5.2 %collective-permute-done.13.refs_4_.refs_6_ = bf16[1024,128]{1,0:T(8,128)(2,1)S(1)} collective-permute-done((bf16[1024,128]{1,0:T(8,128)(2,1)S(1)}, bf16[1024,128]{1,0:T(8,128)(2,1)S(1)}, u32[]{:S(2)}, u32[]{:S(2)}) %collective-permute-start.13) | collective-permute-done | bytes 262176 | tf_op jit(solution)/shard_map/ppermute | solution.py:20
  150.2 5.3 %all-to-all-start = ((bf16[16,256,256]{2,1,0:T(8,128)(2,1)}), bf16[16,256,256]{2,1,0:T(8,128)(2,1)S(1)}, u32[]{:S(2)}, u32[]{:S(2)}) async-start(bf16[16,256,256]{2,1,0:T(8,128)(2,1)} %order.1), calls=%async_computation | async-start | bytes 4194304 | tf_op jit(solution)/shard_map/all_to_all | solution.py:356
  155.6 2.4 collective-permute-start.23
  158.0 3.3 %collective-permute-start.16 = (bf16[1024,128]{1,0:T(8,128)(2,1)}, bf16[1024,128]{1,0:T(8,128)(2,1)S(1)}, u32[]{:S(2)}, u32[]{:S(2)}) collective-permute-start(bf16[1024,128]{1,0:T(8,128)(2,1)} %copy-done.11), channel_id=1, source_target_pairs={{0,224},{32,0},{64,32},{96,64},{128,96},{160,128},{192,160},{224,1... | collective-permute-start | bytes 786440 | tf_op jit(solution)/shard_map/ppermute | solution.py:20
  161.3 3.6 %collective-permute-done.23.refs_14_.refs_17_ = bf16[1024,128]{1,0:T(8,128)(2,1)S(1)} collective-permute-done((bf16[1024,128]{1,0:T(8,128)(2,1)S(1)}, bf16[1024,128]{1,0:T(8,128)(2,1)S(1)}, u32[]{:S(2)}, u32[]{:S(2)}) %collective-permute-start.23) | collective-permute-done | bytes 262176 | tf_op jit(solution)/shard_map/ppermute | solution.py:20
  164.9 3.5 %collective-permute-start.25 = (bf16[1024,128]{1,0:T(8,128)(2,1)S(1)}, bf16[1024,128]{1,0:T(8,128)(2,1)S(1)}, u32[]{:S(2)}, u32[]{:S(2)}) collective-permute-start(bf16[1024,128]{1,0:T(8,128)(2,1)S(1)} %collective-permute-done.23.refs_14_.refs_17_), channel_id=1, source_target_pairs={{0,224},{32,0},{64,32},{96,64},{128,96},{160,128},{192,160},{224,1... | collective-permute-start | bytes 786440 | tf_op jit(solution)/shard_map/ppermute | solution.py:20
  168.7 5.6 %collective-permute-done.22.refs_13_.refs_16_ = bf16[1024,128]{1,0:T(8,128)(2,1)S(1)} collective-permute-done((bf16[1024,128]{1,0:T(8,128)(2,1)S(1)}, bf16[1024,128]{1,0:T(8,128)(2,1)S(1)}, u32[]{:S(2)}, u32[]{:S(2)}) %collective-permute-start.22) | collective-permute-done | bytes 262176 | tf_op jit(solution)/shard_map/ppermute | solution.py:20
  174.3 3.2 %collective-permute-start.18 = (bf16[1024,128]{1,0:T(8,128)(2,1)S(1)}, bf16[1024,128]{1,0:T(8,128)(2,1)S(1)}, u32[]{:S(2)}, u32[]{:S(2)}) collective-permute-start(bf16[1024,128]{1,0:T(8,128)(2,1)S(1)} %collective-permute-done.16.refs_7_.refs_9_), channel_id=1, source_target_pairs={{0,224},{32,0},{64,32},{96,64},{128,96},{160,128},{192,160},{224,1... | collective-permute-start | bytes 786440 | tf_op jit(solution)/shard_map/ppermute | solution.py:20
  180.0 5.5 %collective-permute-done.24.refs_15_.refs_18_ = bf16[1024,128]{1,0:T(8,128)(2,1)S(1)} collective-permute-done((bf16[1024,128]{1,0:T(8,128)(2,1)S(1)}, bf16[1024,128]{1,0:T(8,128)(2,1)S(1)}, u32[]{:S(2)}, u32[]{:S(2)}) %collective-permute-start.24) | collective-permute-done | bytes 262176 | tf_op jit(solution)/shard_map/ppermute | solution.py:20
  186.9 7.4 %dense.1.refs_21_ = f32[3,128,128]{2,1,0:T(8,128)} custom-call(s32[2]{0:T(128)} %refs_1_.1, bf16[3,512,128]{2,1,0:T(8,128)(2,1)} %get-tuple-element.55.refs_1_.refs_3_, bf16[3,512,128]{2,1,0:T(8,128)(2,1)} %copy-done.1, bf16[1024,128]{1,0:T(8,128)(2,1)} %copy-done.3, bf16[1024,128]{1,0:T(8,128)(2,1)} %copy-done.10, bf16[1024,128]{1,0:T(8,128)(2,1)} %copy-done.11, ...), custom_call_target="tpu_custom_call" | custom-call | tf_op jit(solution)/shard_map/dense/pallas_call | solution.py:307
  195.9 9.8 %attend.1 = bf16[2,512,128]{2,1,0:T(8,128)(2,1)} custom-call(s32[96]{0:T(128)} %all-reduce.refs_0_, s32[2]{0:T(128)} %refs_1_.1, s32[2]{0:T(128)} %refs_2_.1, bf16[3,512,128]{2,1,0:T(8,128)(2,1)} %get-tuple-element.55.refs_1_.refs_3_, bf16[3,512,128]{2,1,0:T(8,128)(2,1)} %copy-done.1, bf16[1024,128]{1,0:T(8,128)(2,1)} %copy-done.3, ...), custom_call_target="tpu_custom_call" | custom-call | tf_op jit(solution)/shard_map/attend/pallas_call | solution.py:325
  219.5 3.4 %collective-permute-done.32 = bf16[256,256]{1,0:T(8,128)(2,1)S(1)} collective-permute-done((bf16[256,256]{1,0:T(8,128)(2,1)S(1)}, bf16[256,256]{1,0:T(8,128)(2,1)S(1)}, u32[]{:S(2)}, u32[]{:S(2)}) %collective-permute-start.32) | collective-permute-done | bytes 131104 | tf_op jit(solution)/shard_map/ppermute | solution.py:20
  223.4 2.9 %collective-permute-start.39 = (bf16[1024,256]{1,0:T(8,128)(2,1)S(1)}, bf16[1024,256]{1,0:T(8,128)(2,1)S(1)}, u32[]{:S(2)}, u32[]{:S(2)}) collective-permute-start(bf16[1024,256]{1,0:T(8,128)(2,1)S(1)} %pad_maximum_fusion.3), channel_id=1, source_target_pairs={{0,3},{1,0},{2,1},{3,2},{4,7},{5,4},{6,5},{7,6},{8,11},{9,8},{10,9... | collective-permute-start | bytes 1572872 | tf_op jit(solution)/shard_map/ppermute | solution.py:20
  228.8 19.2 %collective-permute-done.38 = bf16[1024,256]{1,0:T(8,128)(2,1)S(1)} collective-permute-done((bf16[1024,256]{1,0:T(8,128)(2,1)S(1)}, bf16[1024,256]{1,0:T(8,128)(2,1)S(1)}, u32[]{:S(2)}, u32[]{:S(2)}) %collective-permute-start.38) | collective-permute-done | bytes 524320 | tf_op jit(solution)/shard_map/ppermute | solution.py:20
  248.0 3.3 %output0.1.refs_5_ = f32[512,256]{1,0:T(8,128)} custom-call(bf16[4,256,256]{2,1,0:T(8,128)(2,1)} %bitcast.43, bf16[4,256,256]{2,1,0:T(8,128)(2,1)} %bitcast.42, bf16[1,4096,256]{2,1,0:T(8,128)(2,1)} %bitcast.37), custom_call_target="tpu_custom_call" | custom-call | tf_op jit(solution)/shard_map/output0/pallas_call | solution.py:128
  252.6 4.6 %output1.1.refs_3_ = f32[512,256]{1,0:T(8,128)} custom-call(bf16[4,256,256]{2,1,0:T(8,128)(2,1)} %bitcast.51, bf16[4,256,256]{2,1,0:T(8,128)(2,1)} %bitcast.53, bf16[4,256,256]{2,1,0:T(8,128)(2,1)} %bitcast.48, bf16[4,256,256]{2,1,0:T(8,128)(2,1)} %bitcast.49, bf16[1,4096,256]{2,1,0:T(8,128)(2,1)} %bitcast.38, f32[512,256]{1,0:T(8,128)} %output0.1.refs_5_), custom_call_target="tpu_custom_call" | custom-call | tf_op jit(solution)/shard_map/output1/pallas_call | solution.py:128
  259.5 3.2 %output3.1 = bf16[512,256]{1,0:T(8,128)(2,1)} custom-call(bf16[4,256,256]{2,1,0:T(8,128)(2,1)} %bitcast.52, bf16[4,256,256]{2,1,0:T(8,128)(2,1)} %bitcast.50, bf16[1,4096,256]{2,1,0:T(8,128)(2,1)} %bitcast.39, f32[512,256]{1,0:T(8,128)} %output1.1.refs_3_), custom_call_target="tpu_custom_call" | custom-call | tf_op jit(solution)/shard_map/output3/pallas_call | solution.py:128
  (142 shorter events, 45.6 us)
Async XLA Ops:
  6.3 7.3 %collective-permute-start.4 = (bf16[256,256]{1,0:T(8,128)(2,1)S(1)}, bf16[256,256]{1,0:T(8,128)(2,1)S(1)}, u32[]{:S(2)}, u32[]{:S(2)}) collective-permute-start(bf16[256,256]{1,0:T(8,128)(2,1)S(1)} %get-tuple-element.83), channel_id=1, source_target_pairs={{0,12},{4,0},{8,4},{12,8},{1,13},{5,1},{9,5},{13,9},{2,14},{6,2},{... | collective-permute-start | bytes 393224 | tf_op jit(solution)/shard_map/ppermute | solution.py:20
  15.0 16.0 %collective-permute-start.8 = (bf16[1024,256]{1,0:T(8,128)(2,1)S(1)}, bf16[1024,256]{1,0:T(8,128)(2,1)S(1)}, u32[]{:S(2)}, u32[]{:S(2)}) collective-permute-start(bf16[1024,256]{1,0:T(8,128)(2,1)S(1)} %pad_maximum_fusion.1), channel_id=1, source_target_pairs={{0,1},{1,2},{2,3},{3,0},{4,5},{5,6},{6,7},{7,4},{8,9},{9,10},{10,1... | collective-permute-start | bytes 1572872 | tf_op jit(solution)/shard_map/ppermute | solution.py:20
  15.8 98.2 %collective-permute-start.9 = (bf16[1024,256]{1,0:T(8,128)(2,1)S(1)}, bf16[1024,256]{1,0:T(8,128)(2,1)S(1)}, u32[]{:S(2)}, u32[]{:S(2)}) collective-permute-start(bf16[1024,256]{1,0:T(8,128)(2,1)S(1)} %pad_maximum_fusion.1), channel_id=1, source_target_pairs={{0,3},{1,0},{2,1},{3,2},{4,7},{5,4},{6,5},{7,6},{8,11},{9,8},{10,9... | collective-permute-start | bytes 1572872 | tf_op jit(solution)/shard_map/ppermute | solution.py:20
  18.4 95.7 %collective-permute-start.6 = (bf16[1024,256]{1,0:T(8,128)(2,1)S(1)}, bf16[1024,256]{1,0:T(8,128)(2,1)S(1)}, u32[]{:S(2)}, u32[]{:S(2)}) collective-permute-start(bf16[1024,256]{1,0:T(8,128)(2,1)S(1)} %pad_maximum_fusion), channel_id=1, source_target_pairs={{0,4},{4,8},{8,12},{12,0},{1,5},{5,9},{9,13},{13,1},{2,6},{6,10},{... | collective-permute-start | bytes 1572872 | tf_op jit(solution)/shard_map/ppermute | solution.py:20
  20.6 93.5 %collective-permute-start.7 = (bf16[1024,256]{1,0:T(8,128)(2,1)S(1)}, bf16[1024,256]{1,0:T(8,128)(2,1)}, u32[]{:S(2)}, u32[]{:S(2)}) collective-permute-start(bf16[1024,256]{1,0:T(8,128)(2,1)S(1)} %pad_maximum_fusion), channel_id=1, source_target_pairs={{0,12},{4,0},{8,4},{12,8},{1,13},{5,1},{9,5},{13,9},{2,14},{6,2},{... | collective-permute-start | bytes 1572872 | tf_op jit(solution)/shard_map/ppermute | solution.py:20
  20.6 102.0 %collective-permute-start.11 = (bf16[1024,256]{1,0:T(8,128)(2,1)S(1)}, bf16[1024,256]{1,0:T(8,128)(2,1)S(1)}, u32[]{:S(2)}, u32[]{:S(2)}) collective-permute-start(bf16[1024,256]{1,0:T(8,128)(2,1)S(1)} %pad_maximum_fusion.1), channel_id=1, source_target_pairs={{0,2},{1,3},{2,0},{3,1},{4,6},{5,7},{6,4},{7,5},{8,10},{9,11},{10,... | collective-permute-start | bytes 1572872 | tf_op jit(solution)/shard_map/ppermute | solution.py:20
  31.1 91.5 %collective-permute-start.10 = (bf16[1024,256]{1,0:T(8,128)(2,1)S(1)}, bf16[1024,256]{1,0:T(8,128)(2,1)}, u32[]{:S(2)}, u32[]{:S(2)}) collective-permute-start(bf16[1024,256]{1,0:T(8,128)(2,1)S(1)} %pad_maximum_fusion), channel_id=1, source_target_pairs={{0,8},{4,12},{8,0},{12,4},{1,9},{5,13},{9,1},{13,5},{2,10},{6,14},... | collective-permute-start | bytes 1572872 | tf_op jit(solution)/shard_map/ppermute | solution.py:20
  130.5 13.2 %collective-permute-start.20 = (bf16[1024,128]{1,0:T(8,128)(2,1)S(1)}, bf16[1024,128]{1,0:T(8,128)(2,1)S(1)}, u32[]{:S(2)}, u32[]{:S(2)}) collective-permute-start(bf16[1024,128]{1,0:T(8,128)(2,1)S(1)} %pad_maximum_fusion.5.refs_10_.refs_13_), channel_id=1, source_target_pairs={{0,32},{32,64},{64,96},{96,128},{128,160},{160,192},{192,224},{224... | collective-permute-start | bytes 786440 | tf_op jit(solution)/shard_map/ppermute | solution.py:20
  132.7 11.0 %collective-permute-start.21 = (bf16[1024,128]{1,0:T(8,128)(2,1)S(1)}, bf16[1024,128]{1,0:T(8,128)(2,1)S(1)}, u32[]{:S(2)}, u32[]{:S(2)}) collective-permute-start(bf16[1024,128]{1,0:T(8,128)(2,1)S(1)} %pad_maximum_fusion.5.refs_10_.refs_13_), channel_id=1, source_target_pairs={{0,224},{32,0},{64,32},{96,64},{128,96},{160,128},{192,160},{224,1... | collective-permute-start | bytes 786440 | tf_op jit(solution)/shard_map/ppermute | solution.py:20
  136.7 12.1 %collective-permute-start.13 = (bf16[1024,128]{1,0:T(8,128)(2,1)S(1)}, bf16[1024,128]{1,0:T(8,128)(2,1)S(1)}, u32[]{:S(2)}, u32[]{:S(2)}) collective-permute-start(bf16[1024,128]{1,0:T(8,128)(2,1)S(1)} %pad_maximum_fusion.4.refs_3_.refs_5_), channel_id=1, source_target_pairs={{0,32},{32,64},{64,96},{96,128},{128,160},{160,192},{192,224},{224... | collective-permute-start | bytes 786440 | tf_op jit(solution)/shard_map/ppermute | solution.py:20
  136.8 12.0 %collective-permute-start.14 = (bf16[1024,128]{1,0:T(8,128)(2,1)S(1)}, bf16[1024,128]{1,0:T(8,128)(2,1)S(1)}, u32[]{:S(2)}, u32[]{:S(2)}) collective-permute-start(bf16[1024,128]{1,0:T(8,128)(2,1)S(1)} %pad_maximum_fusion.4.refs_3_.refs_5_), channel_id=1, source_target_pairs={{0,224},{32,0},{64,32},{96,64},{128,96},{160,128},{192,160},{224,1... | collective-permute-start | bytes 786440 | tf_op jit(solution)/shard_map/ppermute | solution.py:20
  150.2 44.1 %all-to-all-start = ((bf16[16,256,256]{2,1,0:T(8,128)(2,1)}), bf16[16,256,256]{2,1,0:T(8,128)(2,1)S(1)}, u32[]{:S(2)}, u32[]{:S(2)}) async-start(bf16[16,256,256]{2,1,0:T(8,128)(2,1)} %order.1), calls=%async_computation | async-start | bytes 4194304 | tf_op jit(solution)/shard_map/all_to_all | solution.py:356
  155.6 9.3 %collective-permute-start.23 = (bf16[1024,128]{1,0:T(8,128)(2,1)S(1)}, bf16[1024,128]{1,0:T(8,128)(2,1)S(1)}, u32[]{:S(2)}, u32[]{:S(2)}) collective-permute-start(bf16[1024,128]{1,0:T(8,128)(2,1)S(1)} %collective-permute-done.21.refs_12_.refs_15_), channel_id=1, source_target_pairs={{0,224},{32,0},{64,32},{96,64},{128,96},{160,128},{192,160},{224,1... | collective-permute-start | bytes 786440 | tf_op jit(solution)/shard_map/ppermute | solution.py:20
  158.0 10.7 %collective-permute-start.15 = (bf16[1024,128]{1,0:T(8,128)(2,1)}, bf16[1024,128]{1,0:T(8,128)(2,1)S(1)}, u32[]{:S(2)}, u32[]{:S(2)}) collective-permute-start(bf16[1024,128]{1,0:T(8,128)(2,1)} %copy-done.10), channel_id=1, source_target_pairs={{0,32},{32,64},{64,96},{96,128},{128,160},{160,192},{192,224},{224... | collective-permute-start | bytes 786440 | tf_op jit(solution)/shard_map/ppermute | solution.py:20
  158.0 16.3 %collective-permute-start.22 = (bf16[1024,128]{1,0:T(8,128)(2,1)S(1)}, bf16[1024,128]{1,0:T(8,128)(2,1)S(1)}, u32[]{:S(2)}, u32[]{:S(2)}) collective-permute-start(bf16[1024,128]{1,0:T(8,128)(2,1)S(1)} %collective-permute-done.20.refs_11_.refs_14_), channel_id=1, source_target_pairs={{0,32},{32,64},{64,96},{96,128},{128,160},{160,192},{192,224},{224... | collective-permute-start | bytes 786440 | tf_op jit(solution)/shard_map/ppermute | solution.py:20
  158.0 16.3 %collective-permute-start.16 = (bf16[1024,128]{1,0:T(8,128)(2,1)}, bf16[1024,128]{1,0:T(8,128)(2,1)S(1)}, u32[]{:S(2)}, u32[]{:S(2)}) collective-permute-start(bf16[1024,128]{1,0:T(8,128)(2,1)} %copy-done.11), channel_id=1, source_target_pairs={{0,224},{32,0},{64,32},{96,64},{128,96},{160,128},{192,160},{224,1... | collective-permute-start | bytes 786440 | tf_op jit(solution)/shard_map/ppermute | solution.py:20
  164.9 12.6 %collective-permute-start.25 = (bf16[1024,128]{1,0:T(8,128)(2,1)S(1)}, bf16[1024,128]{1,0:T(8,128)(2,1)S(1)}, u32[]{:S(2)}, u32[]{:S(2)}) collective-permute-start(bf16[1024,128]{1,0:T(8,128)(2,1)S(1)} %collective-permute-done.23.refs_14_.refs_17_), channel_id=1, source_target_pairs={{0,224},{32,0},{64,32},{96,64},{128,96},{160,128},{192,160},{224,1... | collective-permute-start | bytes 786440 | tf_op jit(solution)/shard_map/ppermute | solution.py:20
  168.7 11.3 %collective-permute-start.17 = (bf16[1024,128]{1,0:T(8,128)(2,1)S(1)}, bf16[1024,128]{1,0:T(8,128)(2,1)}, u32[]{:S(2)}, u32[]{:S(2)}) collective-permute-start(bf16[1024,128]{1,0:T(8,128)(2,1)S(1)} %collective-permute-done.15.refs_6_.refs_8_), channel_id=1, source_target_pairs={{0,32},{32,64},{64,96},{96,128},{128,160},{160,192},{192,224},{224... | collective-permute-start | bytes 786440 | tf_op jit(solution)/shard_map/ppermute | solution.py:20
  174.3 11.2 %collective-permute-start.24 = (bf16[1024,128]{1,0:T(8,128)(2,1)S(1)}, bf16[1024,128]{1,0:T(8,128)(2,1)S(1)}, u32[]{:S(2)}, u32[]{:S(2)}) collective-permute-start(bf16[1024,128]{1,0:T(8,128)(2,1)S(1)} %collective-permute-done.22.refs_13_.refs_16_), channel_id=1, source_target_pairs={{0,32},{32,64},{64,96},{96,128},{128,160},{160,192},{192,224},{224... | collective-permute-start | bytes 786440 | tf_op jit(solution)/shard_map/ppermute | solution.py:20
  174.3 11.2 %collective-permute-start.18 = (bf16[1024,128]{1,0:T(8,128)(2,1)S(1)}, bf16[1024,128]{1,0:T(8,128)(2,1)S(1)}, u32[]{:S(2)}, u32[]{:S(2)}) collective-permute-start(bf16[1024,128]{1,0:T(8,128)(2,1)S(1)} %collective-permute-done.16.refs_7_.refs_9_), channel_id=1, source_target_pairs={{0,224},{32,0},{64,32},{96,64},{128,96},{160,128},{192,160},{224,1... | collective-permute-start | bytes 786440 | tf_op jit(solution)/shard_map/ppermute | solution.py:20
  177.5 16.9 %collective-permute-start.26 = (bf16[1024,128]{1,0:T(8,128)(2,1)S(1)}, bf16[1024,128]{1,0:T(8,128)(2,1)S(1)}, u32[]{:S(2)}, u32[]{:S(2)}) collective-permute-start(bf16[1024,128]{1,0:T(8,128)(2,1)S(1)} %collective-permute-done.25.refs_16_.refs_19_), channel_id=1, source_target_pairs={{0,224},{32,0},{64,32},{96,64},{128,96},{160,128},{192,160},{224,1... | collective-permute-start | bytes 786440 | tf_op jit(solution)/shard_map/ppermute | solution.py:20
  180.0 14.4 %collective-permute-start.19 = (bf16[1024,128]{1,0:T(8,128)(2,1)}, bf16[1024,128]{1,0:T(8,128)(2,1)S(1)}, u32[]{:S(2)}, u32[]{:S(2)}) collective-permute-start(bf16[1024,128]{1,0:T(8,128)(2,1)} %collective-permute-done.17.refs_8_.refs_10_), channel_id=1, source_target_pairs={{0,32},{32,64},{64,96},{96,128},{128,160},{160,192},{192,224},{224... | collective-permute-start | bytes 786440 | tf_op jit(solution)/shard_map/ppermute | solution.py:20
  210.0 7.4 %collective-permute-start.29 = (bf16[256,256]{1,0:T(8,128)(2,1)S(1)}, bf16[256,256]{1,0:T(8,128)(2,1)S(1)}, u32[]{:S(2)}, u32[]{:S(2)}) collective-permute-start(bf16[256,256]{1,0:T(8,128)(2,1)S(1)} %get-tuple-element.80), channel_id=1, source_target_pairs={{0,3},{1,0},{2,1},{3,2},{4,7},{5,4},{6,5},{7,6},{8,11},{9,8},{10,9... | collective-permute-start | bytes 393224 | tf_op jit(solution)/shard_map/ppermute | solution.py:20
  211.7 7.2 %collective-permute-start.30 = (bf16[256,256]{1,0:T(8,128)(2,1)S(1)}, bf16[256,256]{1,0:T(8,128)(2,1)S(1)}, u32[]{:S(2)}, u32[]{:S(2)}) collective-permute-start(bf16[256,256]{1,0:T(8,128)(2,1)S(1)} %get-tuple-element.80), channel_id=1, source_target_pairs={{0,2},{1,3},{2,0},{3,1},{4,6},{5,7},{6,4},{7,5},{8,10},{9,11},{10,... | collective-permute-start | bytes 393224 | tf_op jit(solution)/shard_map/ppermute | solution.py:20
  214.0 8.9 %collective-permute-start.32 = (bf16[256,256]{1,0:T(8,128)(2,1)S(1)}, bf16[256,256]{1,0:T(8,128)(2,1)S(1)}, u32[]{:S(2)}, u32[]{:S(2)}) collective-permute-start(bf16[256,256]{1,0:T(8,128)(2,1)S(1)} %get-tuple-element.79), channel_id=1, source_target_pairs={{0,12},{4,0},{8,4},{12,8},{1,13},{5,1},{9,5},{13,9},{2,14},{6,2},{... | collective-permute-start | bytes 393224 | tf_op jit(solution)/shard_map/ppermute | solution.py:20
  215.5 7.4 %collective-permute-start.33 = (bf16[256,256]{1,0:T(8,128)(2,1)S(1)}, bf16[256,256]{1,0:T(8,128)(2,1)S(1)}, u32[]{:S(2)}, u32[]{:S(2)}) collective-permute-start(bf16[256,256]{1,0:T(8,128)(2,1)S(1)} %get-tuple-element.79), channel_id=1, source_target_pairs={{0,8},{4,12},{8,0},{12,4},{1,9},{5,13},{9,1},{13,5},{2,10},{6,14},... | collective-permute-start | bytes 393224 | tf_op jit(solution)/shard_map/ppermute | solution.py:20
  223.0 25.0 %collective-permute-start.38 = (bf16[1024,256]{1,0:T(8,128)(2,1)S(1)}, bf16[1024,256]{1,0:T(8,128)(2,1)S(1)}, u32[]{:S(2)}, u32[]{:S(2)}) collective-permute-start(bf16[1024,256]{1,0:T(8,128)(2,1)S(1)} %pad_maximum_fusion.3), channel_id=1, source_target_pairs={{0,1},{1,2},{2,3},{3,0},{4,5},{5,6},{6,7},{7,4},{8,9},{9,10},{10,1... | collective-permute-start | bytes 1572872 | tf_op jit(solution)/shard_map/ppermute | solution.py:20
  223.4 27.9 %collective-permute-start.39 = (bf16[1024,256]{1,0:T(8,128)(2,1)S(1)}, bf16[1024,256]{1,0:T(8,128)(2,1)S(1)}, u32[]{:S(2)}, u32[]{:S(2)}) collective-permute-start(bf16[1024,256]{1,0:T(8,128)(2,1)S(1)} %pad_maximum_fusion.3), channel_id=1, source_target_pairs={{0,3},{1,0},{2,1},{3,2},{4,7},{5,4},{6,5},{7,6},{8,11},{9,8},{10,9... | collective-permute-start | bytes 1572872 | tf_op jit(solution)/shard_map/ppermute | solution.py:20
  226.4 25.0 %collective-permute-start.36 = (bf16[1024,256]{1,0:T(8,128)(2,1)S(1)}, bf16[1024,256]{1,0:T(8,128)(2,1)S(1)}, u32[]{:S(2)}, u32[]{:S(2)}) collective-permute-start(bf16[1024,256]{1,0:T(8,128)(2,1)S(1)} %pad_maximum_fusion.2), channel_id=1, source_target_pairs={{0,4},{4,8},{8,12},{12,0},{1,5},{5,9},{9,13},{13,1},{2,6},{6,10},{... | collective-permute-start | bytes 1572872 | tf_op jit(solution)/shard_map/ppermute | solution.py:20
  227.4 24.0 %collective-permute-start.37 = (bf16[1024,256]{1,0:T(8,128)(2,1)S(1)}, bf16[1024,256]{1,0:T(8,128)(2,1)S(1)}, u32[]{:S(2)}, u32[]{:S(2)}) collective-permute-start(bf16[1024,256]{1,0:T(8,128)(2,1)S(1)} %pad_maximum_fusion.2), channel_id=1, source_target_pairs={{0,12},{4,0},{8,4},{12,8},{1,13},{5,1},{9,5},{13,9},{2,14},{6,2},{... | collective-permute-start | bytes 1572872 | tf_op jit(solution)/shard_map/ppermute | solution.py:20
  228.5 28.7 %collective-permute-start.35 = (bf16[1024,256]{1,0:T(8,128)(2,1)S(1)}, bf16[1024,256]{1,0:T(8,128)(2,1)S(1)}, u32[]{:S(2)}, u32[]{:S(2)}) collective-permute-start(bf16[1024,256]{1,0:T(8,128)(2,1)S(1)} %pad_maximum_fusion.3), channel_id=1, source_target_pairs={{0,2},{1,3},{2,0},{3,1},{4,6},{5,7},{6,4},{7,5},{8,10},{9,11},{10,... | collective-permute-start | bytes 1572872 | tf_op jit(solution)/shard_map/ppermute | solution.py:20
  248.0 10.7 %collective-permute-start.34 = (bf16[1024,256]{1,0:T(8,128)(2,1)S(1)}, bf16[1024,256]{1,0:T(8,128)(2,1)S(1)}, u32[]{:S(2)}, u32[]{:S(2)}) collective-permute-start(bf16[1024,256]{1,0:T(8,128)(2,1)S(1)} %pad_maximum_fusion.2), channel_id=1, source_target_pairs={{0,8},{4,12},{8,0},{12,4},{1,9},{5,13},{9,1},{13,5},{2,10},{6,14},... | collective-permute-start | bytes 1572872 | tf_op jit(solution)/shard_map/ppermute | solution.py:20
  (42 other events, 653.9 us)

commit v2 on v1

--- a/solution.py
+++ b/solution.py
@@ -28,21 +28,20 @@
     n = a.shape[0] // 2
     parts = ((a[:n], "x", "y"), (a[n:], "y", "x"))
     around = lax.optimization_barrier([around4(part, first) for part, first, _ in parts])
-    near, next_to, across = [], [], []
+    near, next_to = [], []
     for (part, _, second), others in zip(parts, around):
         stack = jnp.concatenate([part, *others], axis=0)
-        low, high, far = around4(stack, second)
         near.append(stack)
-        next_to.append((low, high))
-        across.append(far)
+        next_to.append([shift(stack, second, 1), shift(stack, second, -1)])
 
     def blocks(v):
         return v.reshape(-1, n, 256)
 
     sums = partial_matmul((0,), [[blocks(v)] for v in near], w, None, name)
-    next_to, sums, extra = lax.optimization_barrier((next_to, sums, extra))
-    sums = partial_matmul((1, 2), [[blocks(v) for v in f] for f in next_to], w, sums, name)
-    across, sums = lax.optimization_barrier((across, sums))
+    lows = [f[0] for f in next_to]
+    near, lows, sums, extra = lax.optimization_barrier((near, lows, sums, extra))
+    across = [shift(v, second, 2) for v, (_, _, second) in zip(near, parts)]
+    sums = partial_matmul((1, 2), [[blocks(v), blocks(f[1])] for v, f in zip(lows, next_to)], w, sums, name)
     out = partial_matmul((3,), [[blocks(v)] for v in across], w, sums, name, finish, out_shape)
     return out, extra
 
@@ -174,18 +173,18 @@
     return pl.pallas_call(
         order_kernel,
         out_shape=jax.ShapeDtypeStruct((16, 256, 256), jnp.bfloat16),
-        in_specs=[ANY],
+        in_specs=[VMEM],
         out_specs=ANY,
         scratch_shapes=[pltpu.SemaphoreType.DMA((2, 16))],
+        compiler_params=PARAMS,
         name="order",
     )(w_out).reshape(4096, 256)
 
 
-def z_ring(a, last):
+def z_ring(a):
     f1, b1 = shift(a, "z", 1), shift(a, "z", -1)
     f2, b2 = shift(f1, "z", 1), shift(b1, "z", -1)
-    f3, b3 = shift(f2, "z", 1), shift(b2, "z", -1)
-    return [a, f1, b1, f2, b2, f3, b3, shift(f3 if last > 0 else b3, "z", last)]
+    return [a, f1, b1, f2, b2, shift(f2, "z", 1), shift(b2, "z", -1)]
 
 
 SLOTS = (0, 7, 1, 6, 2, 5, 3, 4)
@@ -249,7 +248,7 @@
     def _():
         query = jnp.concatenate([q_buf[side, pl.ds(row, BLK)] for side, row in rows_of], axis=0)
         state = (dense_ref[0], dense_ref[1], dense_ref[2])
-        _, total, acc = dense_step(query, k_buf[4], v_buf[4], state)
+        _, total, acc = lax.fori_loop(3, 6, lambda i, state: dense_step(query, k_buf[i], v_buf[i], state), state)
         result = (acc / total).astype(jnp.bfloat16)
         for k, (side, row) in enumerate(rows_of):
 
@@ -280,8 +279,8 @@
 
 def dense_kernel(*refs):
     glob_ref, mine_ref, theirs_ref = refs[:3]
-    k_refs, v_refs = refs[3:10], refs[10:17]
-    o_ref, k_buf, v_buf, q_buf, sem = refs[17:]
+    k_refs, v_refs = refs[3:8], refs[8:13]
+    o_ref, k_buf, v_buf, q_buf, sem = refs[13:]
     _, owned, rows_of = owned_globals(glob_ref)
 
     @pl.when(owned[0] | owned[1])
@@ -297,7 +296,7 @@
         query = jnp.concatenate([q_buf[side, pl.ds(row, BLK)] for side, row in rows_of], axis=0)
         shape = (2 * BLK, DH)
         init = (jnp.full(shape, NEG, jnp.float32), jnp.zeros(shape, jnp.float32), jnp.zeros(shape, jnp.float32))
-        state = lax.fori_loop(0, 7, lambda i, state: dense_step(query, k_buf[i], v_buf[i], state), init)
+        state = lax.fori_loop(0, 5, lambda i, state: dense_step(query, k_buf[i], v_buf[i], state), init)
         for i, value in enumerate(state):
             o_ref[i] = value
 
@@ -307,17 +306,17 @@
     return pl.pallas_call(
         dense_kernel,
         out_shape=jax.ShapeDtypeStruct((3, 2 * BLK, DH), jnp.float32),
-        in_specs=[SMEM] + [ANY] * 16,
+        in_specs=[SMEM] + [ANY] * 12,
         out_specs=VMEM,
         scratch_shapes=[
-            pltpu.VMEM((7, 1024, DH), bf16),
-            pltpu.VMEM((7, 1024, DH), bf16),
+            pltpu.VMEM((5, 1024, DH), bf16),
+            pltpu.VMEM((5, 1024, DH), bf16),
             pltpu.VMEM((2, 512, DH), bf16),
-            pltpu.SemaphoreType.DMA((16,)),
+            pltpu.SemaphoreType.DMA((12,)),
         ],
         compiler_params=PARAMS,
         name="dense",
-    )(glob, mine, theirs, *keys[:7], *values[:7])
+    )(glob, mine, theirs, *keys[:5], *values[:5])
 
 
 def attend(rand, glob, radius, mine, theirs, keys, values, started):
@@ -344,19 +343,23 @@
 
 def body(tokens, w_qkv, w_out, rand_blocks, glob_blocks, window_radius):
     bf16 = jnp.bfloat16
-    rand = lax.all_gather(rand_blocks.reshape(-1), "core", axis=0, tiled=True)
     part = jax.ShapeDtypeStruct((3, 512, DH), bf16)
-    (mine, send), (ordered, rand) = plane_matmul(
-        tokens, w_qkv.transpose(1, 0, 2), split_heads, (part, part), "project", (order(w_out), rand)
+    (mine, send), ordered = plane_matmul(
+        tokens, w_qkv.transpose(1, 0, 2), split_heads, (part, part), "project", order(w_out)
     )
     theirs = swap(send)
-    keys = z_ring(jnp.concatenate([mine[1], theirs[1]], axis=0), 1)
-    values = z_ring(jnp.concatenate([mine[2], theirs[2]], axis=0), -1)
-    ordered, _ = lax.optimization_barrier((ordered, (keys[1:3], values[1:3])))
+    keys = z_ring(jnp.concatenate([mine[1], theirs[1]], axis=0))
+    values = z_ring(jnp.concatenate([mine[2], theirs[2]], axis=0))
+    ordered, _ = lax.optimization_barrier((ordered, send))
+    rand, _ = lax.optimization_barrier((rand_blocks.reshape(-1), keys[1:3]))
+    rand = lax.all_gather(rand, "core", axis=0, tiled=True)
     w_cols = lax.all_to_all(ordered, ("y", "x"), 0, 0, tiled=True)
     started = dense(glob_blocks, mine, theirs, keys, values)
-    started, w_cols = lax.optimization_barrier((started, w_cols))
+    keys[5], values[6], started, rand = lax.optimization_barrier((keys[5], values[6], started, rand))
+    keys.append(shift(keys[5], "z", 1))
+    values.append(shift(values[6], "z", -1))
     att = attend(rand, glob_blocks, window_radius, mine, theirs, keys, values, started)
+    att, w_cols = lax.optimization_barrier((att, w_cols))
     attended = jnp.concatenate([att[0], swap(att[1])], axis=1)
     out = jax.ShapeDtypeStruct((512, 256), bf16)
     return plane_matmul(attended, w_cols[None], round_out, out, "output")[0]

time: 262 us -> 185 us (0.71)
  Pallas kernels: 110 us -> 41.9 us
  starting transfers between devices: 67.9 us -> 63.7 us
  local copies, waits for them, and re-layouts: 12.1 us -> 8.55 us
    pallas_call x1, Pallas kernels: 64.9 us -> 3.22 us  [order(): pl.pallas_call(order_kernel, out_shape=jax.ShapeDtypeStruct((16, 256, 256...]
    pallas_call x1, Pallas kernels: 7.42 us -> 1.48 us  [dense(): pl.pallas_call(dense_kernel, out_shape=jax.ShapeDtypeStruct((3, 2 * BLK,...]
    ppermute x38, starting transfers between devices: 62 us -> 58.6 us  [shift(): return lax.ppermute(a, axis, [(i, (i + step) % n) for i in range(n)])]
    ppermute x38, waiting for transfers between devices: 66.6 us -> 63.3 us  [shift(): return lax.ppermute(a, axis, [(i, (i + step) % n) for i in range(n)])]
    unnamed x70 -> x64, local copies, waits for them, and re-layouts: 8.99 us -> 6.14 us
  transfers between devices with their start and end apart: 41 -> 41, of which waited for: 21 -> 22; matrix products, arithmetic and copies ran while one was open for 1% -> 1% of each run, Pallas kernels for 35% -> 18%
where the time goes in v2:
time: 185 us; the launch traced here: 184 us
  waiting for transfers between devices  66.3 us (36%)
  starting transfers between devices  63.7 us (34%)
  Pallas kernels  41.9 us (23%)
  local copies, waits for them, and re-layouts  8.55 us (5%)
  blocking collectives  2.38 us (1%)
    ppermute x38, waiting for transfers between devices, shift(): return lax.ppermute(a, axis, [(i, (i + step) % n) for i in range(n)])  63.3 us
    ppermute x38, starting transfers between devices, shift(): return lax.ppermute(a, axis, [(i, (i + step) % n) for i in range(n)])  58.6 us
    pallas_call x6, Pallas kernels, partial_matmul(): pl.pallas_call(lambda *refs: partial_kernel(steps, counts, n, groups, has...  28 us
    pallas_call x1, Pallas kernels, attend(): pl.pallas_call(attend_kernel, out_shape=jax.ShapeDtypeStruct((2, 512, DH)...  9.16 us
    unnamed x64, local copies, waits for them, and re-layouts  6.14 us
    all_to_all x1, starting transfers between devices, body(): w_cols = lax.all_to_all(ordered, ('y', 'x'), 0, 0, tiled=True)  4.67 us
  transfers between devices with their start and end apart: 41, of which 22 were waited for; matrix products, arithmetic and copies ran while one was open for 1% of the time, Pallas kernels for 18%

profile of v2, /device:TPU:24, one launch (start us, length us, event | category | flops | bytes accessed | tf_op | source)
XLA Modules:
  0.0 184.3 jit_solution(1575916881792784450)
XLA Ops:
  2.6 1.7 collective-permute-start.1
  4.3 1.8 collective-permute-start.2
  6.3 1.8 collective-permute-start.4
  17.3 3.2 %order.1 = bf16[16,256,256]{2,1,0:T(8,128)(2,1)} custom-call(bf16[256,4096]{1,0:T(8,128)(2,1)} %w_ref.1), custom_call_target="tpu_custom_call" | custom-call | tf_op jit(solution)/shard_map/order/pallas_call | solution.py:173
  20.6 3.3 %collective-permute-start.11 = (bf16[1024,256]{1,0:T(8,128)(2,1)S(1)}, bf16[1024,256]{1,0:T(8,128)(2,1)S(1)}, u32[]{:S(2)}, u32[]{:S(2)}) collective-permute-start(bf16[1024,256]{1,0:T(8,128)(2,1)S(1)} %pad_maximum_fusion.1), channel_id=1, source_target_pairs={{0,3},{1,0},{2,1},{3,2},{4,7},{5,4},{6,5},{7,6},{8,11},{9,8},{10,9... | collective-permute-start | bytes 1572872 | tf_op jit(solution)/shard_map/ppermute | solution.py:20
  23.9 4.6 %project0.1.refs_5_ = f32[512,768]{1,0:T(8,128)} custom-call(bf16[4,256,256]{2,1,0:T(8,128)(2,1)} %bitcast.42, bf16[4,256,256]{2,1,0:T(8,128)(2,1)} %bitcast.40, bf16[3,4096,256]{2,1,0:T(8,128)(2,1)} %bitcast.34), custom_call_target="tpu_custom_call" | custom-call | tf_op jit(solution)/shard_map/project0/pallas_call | solution.py:127
  31.4 12.1 %collective-permute-done.11 = bf16[1024,256]{1,0:T(8,128)(2,1)S(1)} collective-permute-done((bf16[1024,256]{1,0:T(8,128)(2,1)S(1)}, bf16[1024,256]{1,0:T(8,128)(2,1)S(1)}, u32[]{:S(2)}, u32[]{:S(2)}) %collective-permute-start.11) | collective-permute-done | bytes 524320 | tf_op jit(solution)/shard_map/ppermute | solution.py:20
  43.5 3.4 %collective-permute-done.10 = bf16[1024,256]{1,0:T(8,128)(2,1)S(1)} collective-permute-done((bf16[1024,256]{1,0:T(8,128)(2,1)S(1)}, bf16[1024,256]{1,0:T(8,128)(2,1)S(1)}, u32[]{:S(2)}, u32[]{:S(2)}) %collective-permute-start.10) | collective-permute-done | bytes 524320 | tf_op jit(solution)/shard_map/ppermute | solution.py:20
  47.7 7.5 %project1.1.refs_3_ = f32[512,768]{1,0:T(8,128)} custom-call(bf16[4,256,256]{2,1,0:T(8,128)(2,1)} %bitcast.46, bf16[4,256,256]{2,1,0:T(8,128)(2,1)} %bitcast.52, bf16[4,256,256]{2,1,0:T(8,128)(2,1)} %bitcast.44, bf16[4,256,256]{2,1,0:T(8,128)(2,1)} %bitcast.48, bf16[3,4096,256]{2,1,0:T(8,128)(2,1)} %bitcast.35, f32[512,768]{1,0:T(8,128)} %project0.1.refs_5_), custom_call_target="tpu_custom_call" | custom-call | tf_op jit(solution)/shard_map/project1/pallas_call | solution.py:127
  56.2 5.0 %project3.1 = (bf16[3,512,128]{2,1,0:T(8,128)(2,1)}, bf16[3,512,128]{2,1,0:T(8,128)(2,1)}) custom-call(bf16[4,256,256]{2,1,0:T(8,128)(2,1)} %bitcast.50, bf16[4,256,256]{2,1,0:T(8,128)(2,1)} %bitcast.54, bf16[3,4096,256]{2,1,0:T(8,128)(2,1)} %bitcast.36, f32[512,768]{1,0:T(8,128)} %project1.1.refs_3_), custom_call_target="tpu_custom_call" | custom-call | tf_op jit(solution)/shard_map/project3/pallas_call | solution.py:127
  61.2 4.7 %all-to-all-start = ((bf16[16,256,256]{2,1,0:T(8,128)(2,1)}), bf16[16,256,256]{2,1,0:T(8,128)(2,1)S(1)}, u32[]{:S(2)}, u32[]{:S(2)}) async-start(bf16[16,256,256]{2,1,0:T(8,128)(2,1)} %order.1), calls=%async_computation | async-start | bytes 4194304 | tf_op jit(solution)/shard_map/all_to_all | solution.py:356
  67.8 5.9 %collective-permute-start.16 = (bf16[1024,128]{1,0:T(8,128)(2,1)S(1)}, bf16[1024,128]{1,0:T(8,128)(2,1)S(1)}, u32[]{:S(2)}, u32[]{:S(2)}) collective-permute-start(bf16[1024,128]{1,0:T(8,128)(2,1)S(1)} %pad_maximum_fusion.5.refs_8_.refs_13_), channel_id=1, source_target_pairs={{0,224},{32,0},{64,32},{96,64},{128,96},{160,128},{192,160},{224,1... | collective-permute-start | bytes 786440 | tf_op jit(solution)/shard_map/ppermute | solution.py:20
  74.1 3.2 %collective-permute-start.19 = (bf16[1024,128]{1,0:T(8,128)(2,1)S(1)}, bf16[1024,128]{1,0:T(8,128)(2,1)}, u32[]{:S(2)}, u32[]{:S(2)}) collective-permute-start(bf16[1024,128]{1,0:T(8,128)(2,1)S(1)} %pad_maximum_fusion.4.refs_3_.refs_5_), channel_id=1, source_target_pairs={{0,224},{32,0},{64,32},{96,64},{128,96},{160,128},{192,160},{224,1... | collective-permute-start | bytes 786440 | tf_op jit(solution)/shard_map/ppermute | solution.py:20
  77.3 3.0 %collective-permute-done.16.refs_10_.refs_15_ = bf16[1024,128]{1,0:T(8,128)(2,1)S(1)} collective-permute-done((bf16[1024,128]{1,0:T(8,128)(2,1)S(1)}, bf16[1024,128]{1,0:T(8,128)(2,1)S(1)}, u32[]{:S(2)}, u32[]{:S(2)}) %collective-permute-start.16) | collective-permute-done | bytes 262176 | tf_op jit(solution)/shard_map/ppermute | solution.py:20
  80.4 3.7 %collective-permute-start.17 = (bf16[1024,128]{1,0:T(8,128)(2,1)S(1)}, bf16[1024,128]{1,0:T(8,128)(2,1)}, u32[]{:S(2)}, u32[]{:S(2)}) collective-permute-start(bf16[1024,128]{1,0:T(8,128)(2,1)S(1)} %collective-permute-done.16.refs_10_.refs_15_), channel_id=1, source_target_pairs={{0,224},{32,0},{64,32},{96,64},{128,96},{160,128},{192,160},{224,1... | collective-permute-start | bytes 786440 | tf_op jit(solution)/shard_map/ppermute | solution.py:20
  84.4 5.7 %collective-permute-done.21.refs_9_.refs_14_ = bf16[1024,128]{1,0:T(8,128)(2,1)} collective-permute-done((bf16[1024,128]{1,0:T(8,128)(2,1)S(1)}, bf16[1024,128]{1,0:T(8,128)(2,1)}, u32[]{:S(2)}, u32[]{:S(2)}) %collective-permute-start.21) | collective-permute-done | bytes 262176 | tf_op jit(solution)/shard_map/ppermute | solution.py:20
  90.1 3.2 %collective-permute-start.20 = (bf16[1024,128]{1,0:T(8,128)(2,1)}, bf16[1024,128]{1,0:T(8,128)(2,1)}, u32[]{:S(2)}, u32[]{:S(2)}) collective-permute-start(bf16[1024,128]{1,0:T(8,128)(2,1)} %collective-permute-done.19.refs_5_.refs_7_), channel_id=1, source_target_pairs={{0,224},{32,0},{64,32},{96,64},{128,96},{160,128},{192,160},{224,1... | collective-permute-start | bytes 786440 | tf_op jit(solution)/shard_map/ppermute | solution.py:20
  97.5 2.4 %all-reduce.refs_0_ = s32[96]{0:T(128)} all-reduce(s32[96]{0:T(128)S(1)} %dynamic-update-slice), channel_id=1, replica_groups=mesh['z'=8,'core'=2,'y'=4,'x'=4] {'core'}, use_global_device_ids=true, to_apply=%add | all-reduce | flops 96 | bytes 768 | tf_op jit(solution)/shard_map/optimization_barrier | solution.py:358
  101.3 3.2 %collective-permute-start.23 = (bf16[1024,128]{1,0:T(8,128)(2,1)}, bf16[1024,128]{1,0:T(8,128)(2,1)S(1)}, u32[]{:S(2)}, u32[]{:S(2)}) collective-permute-start(bf16[1024,128]{1,0:T(8,128)(2,1)} %collective-permute-done.20.refs_7_.refs_9_), channel_id=1, source_target_pairs={{0,224},{32,0},{64,32},{96,64},{128,96},{160,128},{192,160},{224,1... | collective-permute-start | bytes 786440 | tf_op jit(solution)/shard_map/ppermute | solution.py:20
  107.0 4.4 %collective-permute-start.26 = (bf16[1024,128]{1,0:T(8,128)(2,1)}, bf16[1024,128]{1,0:T(8,128)(2,1)S(1)}, u32[]{:S(2)}, u32[]{:S(2)}) collective-permute-start(bf16[1024,128]{1,0:T(8,128)(2,1)} %collective-permute-done.18.refs_19_), channel_id=1, source_target_pairs={{0,224},{32,0},{64,32},{96,64},{128,96},{160,128},{192,160},{224,1... | collective-permute-start | bytes 786440 | tf_op jit(solution)/shard_map/ppermute | solution.py:20
  111.3 6.2 %collective-permute-done.24.refs_12_ = bf16[1024,128]{1,0:T(8,128)(2,1)S(1)} collective-permute-done((bf16[1024,128]{1,0:T(8,128)(2,1)}, bf16[1024,128]{1,0:T(8,128)(2,1)S(1)}, u32[]{:S(2)}, u32[]{:S(2)}) %collective-permute-start.24) | collective-permute-done | bytes 262176 | tf_op jit(solution)/shard_map/ppermute | solution.py:20
  118.9 9.2 %attend.1 = bf16[2,512,128]{2,1,0:T(8,128)(2,1)} custom-call(s32[96]{0:T(128)} %all-reduce.refs_0_, s32[2]{0:T(128)} %refs_1_.1, s32[2]{0:T(128)} %refs_2_.1, bf16[3,512,128]{2,1,0:T(8,128)(2,1)} %get-tuple-element.49.refs_1_.refs_3_, bf16[3,512,128]{2,1,0:T(8,128)(2,1)} %copy-done.2, bf16[1024,128]{1,0:T(8,128)(2,1)} %copy-done.4, ...), custom_call_target="tpu_custom_call" | custom-call | tf_op jit(solution)/shard_map/attend/pallas_call | solution.py:324
  132.7 1.8 collective-permute-start.29
  134.4 1.8 collective-permute-start.30
  142.2 3.4 %collective-permute-done.32 = bf16[256,256]{1,0:T(8,128)(2,1)S(1)} collective-permute-done((bf16[256,256]{1,0:T(8,128)(2,1)S(1)}, bf16[256,256]{1,0:T(8,128)(2,1)S(1)}, u32[]{:S(2)}, u32[]{:S(2)}) %collective-permute-start.32) | collective-permute-done | bytes 131104 | tf_op jit(solution)/shard_map/ppermute | solution.py:20
  147.5 2.7 %collective-permute-start.39 = (bf16[1024,256]{1,0:T(8,128)(2,1)S(1)}, bf16[1024,256]{1,0:T(8,128)(2,1)S(1)}, u32[]{:S(2)}, u32[]{:S(2)}) collective-permute-start(bf16[1024,256]{1,0:T(8,128)(2,1)S(1)} %pad_maximum_fusion.3), channel_id=1, source_target_pairs={{0,3},{1,0},{2,1},{3,2},{4,7},{5,4},{6,5},{7,6},{8,11},{9,8},{10,9... | collective-permute-start | bytes 1572872 | tf_op jit(solution)/shard_map/ppermute | solution.py:20
  151.2 3.1 %output0.1.refs_5_ = f32[512,256]{1,0:T(8,128)} custom-call(bf16[4,256,256]{2,1,0:T(8,128)(2,1)} %bitcast.43, bf16[4,256,256]{2,1,0:T(8,128)(2,1)} %bitcast.41, bf16[1,4096,256]{2,1,0:T(8,128)(2,1)} %bitcast.37), custom_call_target="tpu_custom_call" | custom-call | tf_op jit(solution)/shard_map/output0/pallas_call | solution.py:127
  154.3 5.1 %collective-permute-done.35 = bf16[1024,256]{1,0:T(8,128)(2,1)S(1)} collective-permute-done((bf16[1024,256]{1,0:T(8,128)(2,1)S(1)}, bf16[1024,256]{1,0:T(8,128)(2,1)S(1)}, u32[]{:S(2)}, u32[]{:S(2)}) %collective-permute-start.35) | collective-permute-done | bytes 524320 | tf_op jit(solution)/shard_map/ppermute | solution.py:20
  160.3 1.7 collective-permute-start.37
  162.1 12.3 %collective-permute-done.38 = bf16[1024,256]{1,0:T(8,128)(2,1)S(1)} collective-permute-done((bf16[1024,256]{1,0:T(8,128)(2,1)S(1)}, bf16[1024,256]{1,0:T(8,128)(2,1)S(1)}, u32[]{:S(2)}, u32[]{:S(2)}) %collective-permute-start.38) | collective-permute-done | bytes 524320 | tf_op jit(solution)/shard_map/ppermute | solution.py:20
  175.2 4.6 %output1.1.refs_3_ = f32[512,256]{1,0:T(8,128)} custom-call(bf16[4,256,256]{2,1,0:T(8,128)(2,1)} %bitcast.47, bf16[4,256,256]{2,1,0:T(8,128)(2,1)} %bitcast.53, bf16[4,256,256]{2,1,0:T(8,128)(2,1)} %bitcast.45, bf16[4,256,256]{2,1,0:T(8,128)(2,1)} %bitcast.49, bf16[1,4096,256]{2,1,0:T(8,128)(2,1)} %bitcast.38, f32[512,256]{1,0:T(8,128)} %output0.1.refs_5_), custom_call_target="tpu_custom_call" | custom-call | tf_op jit(solution)/shard_map/output1/pallas_call | solution.py:127
  180.9 3.2 %output3.1 = bf16[512,256]{1,0:T(8,128)(2,1)} custom-call(bf16[4,256,256]{2,1,0:T(8,128)(2,1)} %bitcast.51, bf16[4,256,256]{2,1,0:T(8,128)(2,1)} %bitcast.55, bf16[1,4096,256]{2,1,0:T(8,128)(2,1)} %bitcast.39, f32[512,256]{1,0:T(8,128)} %output1.1.refs_3_), custom_call_target="tpu_custom_call" | custom-call | tf_op jit(solution)/shard_map/output3/pallas_call | solution.py:127
  (136 shorter events, 44.1 us)
Async XLA Ops:
  6.3 7.3 %collective-permute-start.4 = (bf16[256,256]{1,0:T(8,128)(2,1)S(1)}, bf16[256,256]{1,0:T(8,128)(2,1)S(1)}, u32[]{:S(2)}, u32[]{:S(2)}) collective-permute-start(bf16[256,256]{1,0:T(8,128)(2,1)S(1)} %get-tuple-element.79), channel_id=1, source_target_pairs={{0,12},{4,0},{8,4},{12,8},{1,13},{5,1},{9,5},{13,9},{2,14},{6,2},{... | collective-permute-start | bytes 393224 | tf_op jit(solution)/shard_map/ppermute | solution.py:20
  15.0 13.4 %collective-permute-start.7 = (bf16[1024,256]{1,0:T(8,128)(2,1)S(1)}, bf16[1024,256]{1,0:T(8,128)(2,1)S(1)}, u32[]{:S(2)}, u32[]{:S(2)}) collective-permute-start(bf16[1024,256]{1,0:T(8,128)(2,1)S(1)} %pad_maximum_fusion.1), channel_id=1, source_target_pairs={{0,1},{1,2},{2,3},{3,0},{4,5},{5,6},{6,7},{7,4},{8,9},{9,10},{10,1... | collective-permute-start | bytes 1572872 | tf_op jit(solution)/shard_map/ppermute | solution.py:20
  15.9 12.6 %collective-permute-start.6 = (bf16[1024,256]{1,0:T(8,128)(2,1)S(1)}, bf16[1024,256]{1,0:T(8,128)(2,1)S(1)}, u32[]{:S(2)}, u32[]{:S(2)}) collective-permute-start(bf16[1024,256]{1,0:T(8,128)(2,1)S(1)} %pad_maximum_fusion), channel_id=1, source_target_pairs={{0,4},{4,8},{8,12},{12,0},{1,5},{5,9},{9,13},{13,1},{2,6},{6,10},{... | collective-permute-start | bytes 1572872 | tf_op jit(solution)/shard_map/ppermute | solution.py:20
  20.6 22.9 %collective-permute-start.11 = (bf16[1024,256]{1,0:T(8,128)(2,1)S(1)}, bf16[1024,256]{1,0:T(8,128)(2,1)S(1)}, u32[]{:S(2)}, u32[]{:S(2)}) collective-permute-start(bf16[1024,256]{1,0:T(8,128)(2,1)S(1)} %pad_maximum_fusion.1), channel_id=1, source_target_pairs={{0,3},{1,0},{2,1},{3,2},{4,7},{5,4},{6,5},{7,6},{8,11},{9,8},{10,9... | collective-permute-start | bytes 1572872 | tf_op jit(solution)/shard_map/ppermute | solution.py:20
  23.9 23.0 %collective-permute-start.10 = (bf16[1024,256]{1,0:T(8,128)(2,1)S(1)}, bf16[1024,256]{1,0:T(8,128)(2,1)S(1)}, u32[]{:S(2)}, u32[]{:S(2)}) collective-permute-start(bf16[1024,256]{1,0:T(8,128)(2,1)S(1)} %pad_maximum_fusion), channel_id=1, source_target_pairs={{0,12},{4,0},{8,4},{12,8},{1,13},{5,1},{9,5},{13,9},{2,14},{6,2},{... | collective-permute-start | bytes 1572872 | tf_op jit(solution)/shard_map/ppermute | solution.py:20
  28.5 26.7 %collective-permute-start.8 = (bf16[1024,256]{1,0:T(8,128)(2,1)}, bf16[1024,256]{1,0:T(8,128)(2,1)S(1)}, u32[]{:S(2)}, u32[]{:S(2)}) collective-permute-start(bf16[1024,256]{1,0:T(8,128)(2,1)} %copy-done.7), channel_id=1, source_target_pairs={{0,8},{4,12},{8,0},{12,4},{1,9},{5,13},{9,1},{13,5},{2,10},{6,14},... | collective-permute-start | bytes 1572872 | tf_op jit(solution)/shard_map/ppermute | solution.py:20
  30.2 25.1 %collective-permute-start.9 = (bf16[1024,256]{1,0:T(8,128)(2,1)}, bf16[1024,256]{1,0:T(8,128)(2,1)S(1)}, u32[]{:S(2)}, u32[]{:S(2)}) collective-permute-start(bf16[1024,256]{1,0:T(8,128)(2,1)} %copy-done.5), channel_id=1, source_target_pairs={{0,2},{1,3},{2,0},{3,1},{4,6},{5,7},{6,4},{7,5},{8,10},{9,11},{10,... | collective-permute-start | bytes 1572872 | tf_op jit(solution)/shard_map/ppermute | solution.py:20
  61.2 66.9 %all-to-all-start = ((bf16[16,256,256]{2,1,0:T(8,128)(2,1)}), bf16[16,256,256]{2,1,0:T(8,128)(2,1)S(1)}, u32[]{:S(2)}, u32[]{:S(2)}) async-start(bf16[16,256,256]{2,1,0:T(8,128)(2,1)} %order.1), calls=%async_computation | async-start | bytes 4194304 | tf_op jit(solution)/shard_map/all_to_all | solution.py:356
  67.8 12.6 %collective-permute-start.16 = (bf16[1024,128]{1,0:T(8,128)(2,1)S(1)}, bf16[1024,128]{1,0:T(8,128)(2,1)S(1)}, u32[]{:S(2)}, u32[]{:S(2)}) collective-permute-start(bf16[1024,128]{1,0:T(8,128)(2,1)S(1)} %pad_maximum_fusion.5.refs_8_.refs_13_), channel_id=1, source_target_pairs={{0,224},{32,0},{64,32},{96,64},{128,96},{160,128},{192,160},{224,1... | collective-permute-start | bytes 786440 | tf_op jit(solution)/shard_map/ppermute | solution.py:20
  73.7 10.7 %collective-permute-start.13 = (bf16[1024,128]{1,0:T(8,128)(2,1)S(1)}, bf16[1024,128]{1,0:T(8,128)(2,1)S(1)}, u32[]{:S(2)}, u32[]{:S(2)}) collective-permute-start(bf16[1024,128]{1,0:T(8,128)(2,1)S(1)} %pad_maximum_fusion.4.refs_3_.refs_5_), channel_id=1, source_target_pairs={{0,32},{32,64},{64,96},{96,128},{128,160},{160,192},{192,224},{224... | collective-permute-start | bytes 786440 | tf_op jit(solution)/shard_map/ppermute | solution.py:20
  74.0 16.1 %collective-permute-start.21 = (bf16[1024,128]{1,0:T(8,128)(2,1)S(1)}, bf16[1024,128]{1,0:T(8,128)(2,1)}, u32[]{:S(2)}, u32[]{:S(2)}) collective-permute-start(bf16[1024,128]{1,0:T(8,128)(2,1)S(1)} %pad_maximum_fusion.5.refs_8_.refs_13_), channel_id=1, source_target_pairs={{0,32},{32,64},{64,96},{96,128},{128,160},{160,192},{192,224},{224... | collective-permute-start | bytes 786440 | tf_op jit(solution)/shard_map/ppermute | solution.py:20
  74.1 16.0 %collective-permute-start.19 = (bf16[1024,128]{1,0:T(8,128)(2,1)S(1)}, bf16[1024,128]{1,0:T(8,128)(2,1)}, u32[]{:S(2)}, u32[]{:S(2)}) collective-permute-start(bf16[1024,128]{1,0:T(8,128)(2,1)S(1)} %pad_maximum_fusion.4.refs_3_.refs_5_), channel_id=1, source_target_pairs={{0,224},{32,0},{64,32},{96,64},{128,96},{160,128},{192,160},{224,1... | collective-permute-start | bytes 786440 | tf_op jit(solution)/shard_map/ppermute | solution.py:20
  80.4 13.0 %collective-permute-start.17 = (bf16[1024,128]{1,0:T(8,128)(2,1)S(1)}, bf16[1024,128]{1,0:T(8,128)(2,1)}, u32[]{:S(2)}, u32[]{:S(2)}) collective-permute-start(bf16[1024,128]{1,0:T(8,128)(2,1)S(1)} %collective-permute-done.16.refs_10_.refs_15_), channel_id=1, source_target_pairs={{0,224},{32,0},{64,32},{96,64},{128,96},{160,128},{192,160},{224,1... | collective-permute-start | bytes 786440 | tf_op jit(solution)/shard_map/ppermute | solution.py:20
  84.4 11.3 %collective-permute-start.14 = (bf16[1024,128]{1,0:T(8,128)(2,1)S(1)}, bf16[1024,128]{1,0:T(8,128)(2,1)}, u32[]{:S(2)}, u32[]{:S(2)}) collective-permute-start(bf16[1024,128]{1,0:T(8,128)(2,1)S(1)} %collective-permute-done.13.refs_4_.refs_6_), channel_id=1, source_target_pairs={{0,32},{32,64},{64,96},{96,128},{128,160},{160,192},{192,224},{224... | collective-permute-start | bytes 786440 | tf_op jit(solution)/shard_map/ppermute | solution.py:20
  90.1 11.2 %collective-permute-start.22 = (bf16[1024,128]{1,0:T(8,128)(2,1)}, bf16[1024,128]{1,0:T(8,128)(2,1)}, u32[]{:S(2)}, u32[]{:S(2)}) collective-permute-start(bf16[1024,128]{1,0:T(8,128)(2,1)} %collective-permute-done.21.refs_9_.refs_14_), channel_id=1, source_target_pairs={{0,32},{32,64},{64,96},{96,128},{128,160},{160,192},{192,224},{224... | collective-permute-start | bytes 786440 | tf_op jit(solution)/shard_map/ppermute | solution.py:20
  90.1 11.2 %collective-permute-start.20 = (bf16[1024,128]{1,0:T(8,128)(2,1)}, bf16[1024,128]{1,0:T(8,128)(2,1)}, u32[]{:S(2)}, u32[]{:S(2)}) collective-permute-start(bf16[1024,128]{1,0:T(8,128)(2,1)} %collective-permute-done.19.refs_5_.refs_7_), channel_id=1, source_target_pairs={{0,224},{32,0},{64,32},{96,64},{128,96},{160,128},{192,160},{224,1... | collective-permute-start | bytes 786440 | tf_op jit(solution)/shard_map/ppermute | solution.py:20
  93.3 12.7 %collective-permute-start.18 = (bf16[1024,128]{1,0:T(8,128)(2,1)}, bf16[1024,128]{1,0:T(8,128)(2,1)}, u32[]{:S(2)}, u32[]{:S(2)}) collective-permute-start(bf16[1024,128]{1,0:T(8,128)(2,1)} %collective-permute-done.17.refs_12_.refs_17_), channel_id=1, source_target_pairs={{0,224},{32,0},{64,32},{96,64},{128,96},{160,128},{192,160},{224,1... | collective-permute-start | bytes 786440 | tf_op jit(solution)/shard_map/ppermute | solution.py:20
  95.7 11.2 %collective-permute-start.15 = (bf16[1024,128]{1,0:T(8,128)(2,1)}, bf16[1024,128]{1,0:T(8,128)(2,1)}, u32[]{:S(2)}, u32[]{:S(2)}) collective-permute-start(bf16[1024,128]{1,0:T(8,128)(2,1)} %collective-permute-done.14.refs_6_.refs_8_), channel_id=1, source_target_pairs={{0,32},{32,64},{64,96},{96,128},{128,160},{160,192},{192,224},{224... | collective-permute-start | bytes 786440 | tf_op jit(solution)/shard_map/ppermute | solution.py:20
  101.3 10.0 %collective-permute-start.25 = (bf16[1024,128]{1,0:T(8,128)(2,1)}, bf16[1024,128]{1,0:T(8,128)(2,1)S(1)}, u32[]{:S(2)}, u32[]{:S(2)}) collective-permute-start(bf16[1024,128]{1,0:T(8,128)(2,1)} %collective-permute-done.22.refs_11_.refs_16_), channel_id=1, source_target_pairs={{0,32},{32,64},{64,96},{96,128},{128,160},{160,192},{192,224},{224... | collective-permute-start | bytes 786440 | tf_op jit(solution)/shard_map/ppermute | solution.py:20
  101.3 10.0 %collective-permute-start.23 = (bf16[1024,128]{1,0:T(8,128)(2,1)}, bf16[1024,128]{1,0:T(8,128)(2,1)S(1)}, u32[]{:S(2)}, u32[]{:S(2)}) collective-permute-start(bf16[1024,128]{1,0:T(8,128)(2,1)} %collective-permute-done.20.refs_7_.refs_9_), channel_id=1, source_target_pairs={{0,224},{32,0},{64,32},{96,64},{128,96},{160,128},{192,160},{224,1... | collective-permute-start | bytes 786440 | tf_op jit(solution)/shard_map/ppermute | solution.py:20
  107.0 10.5 %collective-permute-start.24 = (bf16[1024,128]{1,0:T(8,128)(2,1)}, bf16[1024,128]{1,0:T(8,128)(2,1)S(1)}, u32[]{:S(2)}, u32[]{:S(2)}) collective-permute-start(bf16[1024,128]{1,0:T(8,128)(2,1)} %collective-permute-done.15.refs_10_), channel_id=1, source_target_pairs={{0,32},{32,64},{64,96},{96,128},{128,160},{160,192},{192,224},{224... | collective-permute-start | bytes 786440 | tf_op jit(solution)/shard_map/ppermute | solution.py:20
  107.0 10.6 %collective-permute-start.26 = (bf16[1024,128]{1,0:T(8,128)(2,1)}, bf16[1024,128]{1,0:T(8,128)(2,1)S(1)}, u32[]{:S(2)}, u32[]{:S(2)}) collective-permute-start(bf16[1024,128]{1,0:T(8,128)(2,1)} %collective-permute-done.18.refs_19_), channel_id=1, source_target_pairs={{0,224},{32,0},{64,32},{96,64},{128,96},{160,128},{192,160},{224,1... | collective-permute-start | bytes 786440 | tf_op jit(solution)/shard_map/ppermute | solution.py:20
  132.7 7.4 %collective-permute-start.29 = (bf16[256,256]{1,0:T(8,128)(2,1)S(1)}, bf16[256,256]{1,0:T(8,128)(2,1)S(1)}, u32[]{:S(2)}, u32[]{:S(2)}) collective-permute-start(bf16[256,256]{1,0:T(8,128)(2,1)S(1)} %get-tuple-element.76), channel_id=1, source_target_pairs={{0,3},{1,0},{2,1},{3,2},{4,7},{5,4},{6,5},{7,6},{8,11},{9,8},{10,9... | collective-permute-start | bytes 393224 | tf_op jit(solution)/shard_map/ppermute | solution.py:20
  134.4 7.2 %collective-permute-start.30 = (bf16[256,256]{1,0:T(8,128)(2,1)S(1)}, bf16[256,256]{1,0:T(8,128)(2,1)S(1)}, u32[]{:S(2)}, u32[]{:S(2)}) collective-permute-start(bf16[256,256]{1,0:T(8,128)(2,1)S(1)} %get-tuple-element.76), channel_id=1, source_target_pairs={{0,2},{1,3},{2,0},{3,1},{4,6},{5,7},{6,4},{7,5},{8,10},{9,11},{10,... | collective-permute-start | bytes 393224 | tf_op jit(solution)/shard_map/ppermute | solution.py:20
  136.8 8.9 %collective-permute-start.32 = (bf16[256,256]{1,0:T(8,128)(2,1)S(1)}, bf16[256,256]{1,0:T(8,128)(2,1)S(1)}, u32[]{:S(2)}, u32[]{:S(2)}) collective-permute-start(bf16[256,256]{1,0:T(8,128)(2,1)S(1)} %get-tuple-element.75), channel_id=1, source_target_pairs={{0,12},{4,0},{8,4},{12,8},{1,13},{5,1},{9,5},{13,9},{2,14},{6,2},{... | collective-permute-start | bytes 393224 | tf_op jit(solution)/shard_map/ppermute | solution.py:20
  138.2 7.4 %collective-permute-start.33 = (bf16[256,256]{1,0:T(8,128)(2,1)S(1)}, bf16[256,256]{1,0:T(8,128)(2,1)S(1)}, u32[]{:S(2)}, u32[]{:S(2)}) collective-permute-start(bf16[256,256]{1,0:T(8,128)(2,1)S(1)} %get-tuple-element.75), channel_id=1, source_target_pairs={{0,8},{4,12},{8,0},{12,4},{1,9},{5,13},{9,1},{13,5},{2,10},{6,14},... | collective-permute-start | bytes 393224 | tf_op jit(solution)/shard_map/ppermute | solution.py:20
  145.7 13.7 %collective-permute-start.35 = (bf16[1024,256]{1,0:T(8,128)(2,1)S(1)}, bf16[1024,256]{1,0:T(8,128)(2,1)S(1)}, u32[]{:S(2)}, u32[]{:S(2)}) collective-permute-start(bf16[1024,256]{1,0:T(8,128)(2,1)S(1)} %pad_maximum_fusion.3), channel_id=1, source_target_pairs={{0,1},{1,2},{2,3},{3,0},{4,5},{5,6},{6,7},{7,4},{8,9},{9,10},{10,1... | collective-permute-start | bytes 1572872 | tf_op jit(solution)/shard_map/ppermute | solution.py:20
  146.2 13.3 %collective-permute-start.34 = (bf16[1024,256]{1,0:T(8,128)(2,1)S(1)}, bf16[1024,256]{1,0:T(8,128)(2,1)S(1)}, u32[]{:S(2)}, u32[]{:S(2)}) collective-permute-start(bf16[1024,256]{1,0:T(8,128)(2,1)S(1)} %pad_maximum_fusion.2), channel_id=1, source_target_pairs={{0,4},{4,8},{8,12},{12,0},{1,5},{5,9},{9,13},{13,1},{2,6},{6,10},{... | collective-permute-start | bytes 1572872 | tf_op jit(solution)/shard_map/ppermute | solution.py:20
  147.5 14.6 %collective-permute-start.39 = (bf16[1024,256]{1,0:T(8,128)(2,1)S(1)}, bf16[1024,256]{1,0:T(8,128)(2,1)S(1)}, u32[]{:S(2)}, u32[]{:S(2)}) collective-permute-start(bf16[1024,256]{1,0:T(8,128)(2,1)S(1)} %pad_maximum_fusion.3), channel_id=1, source_target_pairs={{0,3},{1,0},{2,1},{3,2},{4,7},{5,4},{6,5},{7,6},{8,11},{9,8},{10,9... | collective-permute-start | bytes 1572872 | tf_op jit(solution)/shard_map/ppermute | solution.py:20
  150.1 24.3 %collective-permute-start.38 = (bf16[1024,256]{1,0:T(8,128)(2,1)S(1)}, bf16[1024,256]{1,0:T(8,128)(2,1)S(1)}, u32[]{:S(2)}, u32[]{:S(2)}) collective-permute-start(bf16[1024,256]{1,0:T(8,128)(2,1)S(1)} %pad_maximum_fusion.2), channel_id=1, source_target_pairs={{0,12},{4,0},{8,4},{12,8},{1,13},{5,1},{9,5},{13,9},{2,14},{6,2},{... | collective-permute-start | bytes 1572872 | tf_op jit(solution)/shard_map/ppermute | solution.py:20
  159.5 20.4 %collective-permute-start.36 = (bf16[1024,256]{1,0:T(8,128)(2,1)}, bf16[1024,256]{1,0:T(8,128)(2,1)S(1)}, u32[]{:S(2)}, u32[]{:S(2)}) collective-permute-start(bf16[1024,256]{1,0:T(8,128)(2,1)} %copy-done.8), channel_id=1, source_target_pairs={{0,8},{4,12},{8,0},{12,4},{1,9},{5,13},{9,1},{13,5},{2,10},{6,14},... | collective-permute-start | bytes 1572872 | tf_op jit(solution)/shard_map/ppermute | solution.py:20
  160.3 19.5 %collective-permute-start.37 = (bf16[1024,256]{1,0:T(8,128)(2,1)}, bf16[1024,256]{1,0:T(8,128)(2,1)S(1)}, u32[]{:S(2)}, u32[]{:S(2)}) collective-permute-start(bf16[1024,256]{1,0:T(8,128)(2,1)} %copy-done.6), channel_id=1, source_target_pairs={{0,2},{1,3},{2,0},{3,1},{4,6},{5,7},{6,4},{7,5},{8,10},{9,11},{10,... | collective-permute-start | bytes 1572872 | tf_op jit(solution)/shard_map/ppermute | solution.py:20
  (39 other events, 409.9 us)

commit v3 on v2

--- a/solution.py
+++ b/solution.py
@@ -24,34 +24,34 @@
     return [shift(a, axis, 1), shift(a, axis, -1), shift(a, axis, 2)]
 
 
-def plane_matmul(a, w, finish, out_shape, name, extra=()):
+def plane_matmul(a, w, finish, out_shape, name, more=(), extra=()):
     n = a.shape[0] // 2
-    parts = ((a[:n], "x", "y"), (a[n:], "y", "x"))
-    around = lax.optimization_barrier([around4(part, first) for part, first, _ in parts])
-    near, next_to = [], []
-    for (part, _, second), others in zip(parts, around):
-        stack = jnp.concatenate([part, *others], axis=0)
-        near.append(stack)
-        next_to.append([shift(stack, second, 1), shift(stack, second, -1)])
+    others = around4(a[n:], "y")
+    by_x = lax.all_gather(a[:n], "x", axis=0, tiled=True)
+    by_x, others = lax.optimization_barrier((by_x, others))
+    near = [by_x, jnp.concatenate([a[n:], *others], axis=0)]
+    far = [(shift(stack, second, 1), shift(stack, second, -1)) for stack, second in zip(near, "yx")]
 
     def blocks(v):
         return v.reshape(-1, n, 256)
 
     sums = partial_matmul((0,), [[blocks(v)] for v in near], w, None, name)
-    lows = [f[0] for f in next_to]
-    near, lows, sums, extra = lax.optimization_barrier((near, lows, sums, extra))
-    across = [shift(v, second, 2) for v, (_, _, second) in zip(near, parts)]
-    sums = partial_matmul((1, 2), [[blocks(v), blocks(f[1])] for v, f in zip(lows, next_to)], w, sums, name)
-    out = partial_matmul((3,), [[blocks(v)] for v in across], w, sums, name, finish, out_shape)
+    far, sums, extra = lax.optimization_barrier((far, sums, extra))
+    last = []
+    for (low, high), second in zip(far, "yx"):
+        last.append((shift(low[: 2 * n], second, 1), shift(high[2 * n :], second, -1)))
+    sums = partial_matmul((1, 2), [[blocks(v) for v in f] for f in far], w, sums, name)
+    out = partial_matmul((3,), [[blocks(v) for v in f] for f in last], w, sums, name, finish, out_shape, more)
     return out, extra
 
 
-def partial_kernel(steps, counts, n, groups, has_sums, finish, *refs):
+def partial_kernel(steps, counts, n, groups, has_sums, n_more, finish, *refs):
     n_x = sum(len(c) for c in counts)
     x_refs, w_ref = refs[:n_x], refs[n_x]
     sums_ref = refs[n_x + 1] if has_sums else None
     x_buf, w_buf, acc, x_sem, w_sem, s_sem = refs[-6:]
-    outs = refs[n_x + 1 + has_sums : -6]
+    more = refs[n_x + 1 + has_sums : n_x + 1 + has_sums + n_more]
+    outs = refs[n_x + 1 + has_sums + n_more : -6]
     y = lax.axis_index("y")
     x = lax.axis_index("x")
     x_copies = []
@@ -76,8 +76,10 @@
     for half in range(2):
         for k, step in enumerate(steps):
             for j in range(NXY):
-                iy, ix = (step, j) if half == 0 else (j, step)
-                owner = lax.rem(y + OFFS[iy] + NXY, NXY) * NXY + lax.rem(x + OFFS[ix] + NXY, NXY)
+                if half == 0:
+                    owner = lax.rem(y + OFFS[step] + NXY, NXY) * NXY + j
+                else:
+                    owner = lax.rem(y + OFFS[j] + NXY, NXY) * NXY + lax.rem(x + OFFS[step] + NXY, NXY)
                 w_copy(half * n_steps + k, j, owner).start()
         for copy, owner_half in zip(x_copies, [h for h in range(2) for _ in counts[h]]):
             if owner_half == half:
@@ -87,72 +89,76 @@
     for copy in x_copies:
         copy.wait()
 
-    def multiply(part, carry):
+    def multiply(i, carry):
+        part, g = i // groups, lax.rem(i, groups)
         half, k = part // n_steps, lax.rem(part, n_steps)
-        for j in range(NXY):
-            w_copy(part, j, 0).wait()
+
+        @pl.when(g == 0)
+        def _():
+            for j in range(NXY):
+                w_copy(part, j, 0).wait()
+
         rows = jnp.concatenate([x_buf[half, NXY * k + j] for j in range(NXY)], axis=1)
         span = pl.ds(pl.multiple_of(half * n, n), n)
-        for g in range(groups):
-            cols = slice(g * 256, (g + 1) * 256)
-            value = jnp.dot(rows, w_buf[part, g], preferred_element_type=jnp.float32)
-            if has_sums:
-                value = acc[span, cols] + value
-            acc[span, cols] = value
+        value = jnp.dot(rows, w_buf[part, g], preferred_element_type=jnp.float32)
+        if has_sums:
+            value = acc[g, span] + value
+        acc[g, span] = value
         return carry
 
-    lax.fori_loop(0, 2 * n_steps, multiply, 0)
+    lax.fori_loop(0, 2 * n_steps * groups, multiply, 0)
     if finish is None:
         copy = pltpu.make_async_copy(acc, outs[0], s_sem)
         copy.start()
         copy.wait()
     else:
-        finish(acc, *outs)
-
-
-ANY = pl.BlockSpec(memory_space=pl.ANY)
+        finish(acc, *more, *outs)
+
+
+HBM = pl.BlockSpec(memory_space=pltpu.HBM)
 VMEM = pl.BlockSpec(memory_space=pltpu.VMEM)
 SMEM = pl.BlockSpec(memory_space=pltpu.SMEM)
 PARAMS = pltpu.CompilerParams(vmem_limit_bytes=56 * 1024 * 1024)
 
 
-def partial_matmul(steps, halves, w, sums, name, finish=None, out_shape=None):
+def partial_matmul(steps, halves, w, sums, name, finish=None, out_shape=None, more=()):
     counts = [[v.shape[0] for v in half] for half in halves]
     xs = [v for half in halves for v in half]
     n, groups = xs[0].shape[1], w.shape[0]
-    total = jax.ShapeDtypeStruct((2 * n, 256 * groups), jnp.float32)
+    total = jax.ShapeDtypeStruct((groups, 2 * n, 256), jnp.float32)
     has_sums = sums is not None
     operands = [*xs, w] + ([sums] if has_sums else [])
     bf16 = jnp.bfloat16
     return pl.pallas_call(
-        lambda *refs: partial_kernel(steps, counts, n, groups, has_sums, finish, *refs),
+        lambda *refs: partial_kernel(steps, counts, n, groups, has_sums, len(more), finish, *refs),
         out_shape=total if finish is None else out_shape,
-        in_specs=[ANY] * len(operands),
-        out_specs=ANY if finish is None else jax.tree.map(lambda _: VMEM, out_shape),
+        in_specs=[HBM] * len(operands) + [VMEM] * len(more),
+        out_specs=HBM if finish is None else jax.tree.map(lambda _: VMEM, out_shape),
         scratch_shapes=[
             pltpu.VMEM((2, NXY * len(steps), n, 256), bf16),
             pltpu.VMEM((2 * len(steps), groups, 1024, 256), bf16),
-            pltpu.VMEM((2 * n, 256 * groups), jnp.float32),
+            pltpu.VMEM((groups, 2 * n, 256), jnp.float32),
             pltpu.SemaphoreType.DMA((len(xs),)),
             pltpu.SemaphoreType.DMA((2 * len(steps), NXY)),
             pltpu.SemaphoreType.DMA(()),
         ],
         compiler_params=PARAMS,
         name=name + str(steps[0]),
-    )(*operands)
-
-
-def split_heads(acc, mine_ref, send_ref):
+    )(*operands, *more)
+
+
+def split_heads(acc, ids_ref, mine_ref, send_ref):
     first = lax.axis_index("core") == 0
     for g in range(3):
-        h0 = acc[:, g * 256 : g * 256 + DH].astype(jnp.bfloat16)
-        h1 = acc[:, g * 256 + DH : (g + 1) * 256].astype(jnp.bfloat16)
+        h0 = acc[g, :, :DH].astype(jnp.bfloat16)
+        h1 = acc[g, :, DH:].astype(jnp.bfloat16)
         mine_ref[g] = jnp.where(first, h0, h1)
-        send_ref[g] = jnp.where(first, h1, h0)
+        send_ref[g * 512 : (g + 1) * 512] = jnp.where(first, h1, h0)
+    send_ref[3 * 512 :] = ids_ref[...]
 
 
 def round_out(acc, o_ref):
-    o_ref[...] = acc[...].astype(jnp.bfloat16)
+    o_ref[...] = acc[0].astype(jnp.bfloat16)
 
 
 def order_kernel(w_ref, o_ref, sem):
@@ -174,7 +180,7 @@
         order_kernel,
         out_shape=jax.ShapeDtypeStruct((16, 256, 256), jnp.bfloat16),
         in_specs=[VMEM],
-        out_specs=ANY,
+        out_specs=HBM,
         scratch_shapes=[pltpu.SemaphoreType.DMA((2, 16))],
         compiler_params=PARAMS,
         name="order",
@@ -194,7 +200,7 @@
     rand_ref, glob_ref, radius_ref, mine_ref, theirs_ref = refs[:5]
     k_refs, v_refs, dense_ref = refs[5:13], refs[13:21], refs[21]
     o_ref, k_buf, v_buf, q_buf, sem = refs[22:]
-    copies = [(mine_ref.at[0], q_buf.at[0]), (theirs_ref.at[0], q_buf.at[1])]
+    copies = [(mine_ref.at[0], q_buf.at[0]), (theirs_ref.at[pl.ds(0, 512)], q_buf.at[1])]
     for arrays, buf in ((k_refs, k_buf), (v_refs, v_buf)):
         copies += [(array, buf.at[slot]) for array, slot in zip(arrays, SLOTS)]
     copies = [pltpu.make_async_copy(src, dst, sem.at[i]) for i, (src, dst) in enumerate(copies)]
@@ -218,7 +224,7 @@
 
     def one_block(side, j):
         block = z * 16 + lax.rem(core + side, 2) * 8 + j
-        base = lax.rem(core + side, 2) * 48 + (j * 2 + core) * 3
+        base = side * 48 + (j * 2 + core) * 3
         ids = [jnp.maximum(block - 1, 0), block, jnp.minimum(block + 1, 127)]
         ids += [rand_ref[base + r] for r in range(3)] + [glob_ref[g] for g in range(2)]
         places = [place(i) for i in ids]
@@ -285,7 +291,7 @@
 
     @pl.when(owned[0] | owned[1])
     def _():
-        copies = [(mine_ref.at[0], q_buf.at[0]), (theirs_ref.at[0], q_buf.at[1])]
+        copies = [(mine_ref.at[0], q_buf.at[0]), (theirs_ref.at[pl.ds(0, 512)], q_buf.at[1])]
         for arrays, buf in ((k_refs, k_buf), (v_refs, v_buf)):
             copies += [(array, buf.at[i]) for i, array in enumerate(arrays)]
         copies = [pltpu.make_async_copy(src, dst, sem.at[i]) for i, (src, dst) in enumerate(copies)]
@@ -306,7 +312,7 @@
     return pl.pallas_call(
         dense_kernel,
         out_shape=jax.ShapeDtypeStruct((3, 2 * BLK, DH), jnp.float32),
-        in_specs=[SMEM] + [ANY] * 12,
+        in_specs=[SMEM] + [HBM] * 12,
         out_specs=VMEM,
         scratch_shapes=[
             pltpu.VMEM((5, 1024, DH), bf16),
@@ -324,7 +330,7 @@
     return pl.pallas_call(
         attend_kernel,
         out_shape=jax.ShapeDtypeStruct((2, 512, DH), bf16),
-        in_specs=[SMEM] * 3 + [ANY] * 18 + [VMEM],
+        in_specs=[SMEM] * 3 + [HBM] * 18 + [VMEM],
         out_specs=VMEM,
         scratch_shapes=[
             pltpu.VMEM((NZ, 1024, DH), bf16),
@@ -343,16 +349,18 @@
 
 def body(tokens, w_qkv, w_out, rand_blocks, glob_blocks, window_radius):
     bf16 = jnp.bfloat16
-    part = jax.ShapeDtypeStruct((3, 512, DH), bf16)
+    rand = rand_blocks.reshape(-1)
+    ids = jnp.pad(rand.astype(bf16)[None], ((0, 15), (0, DH - 48)))
+    shapes = (jax.ShapeDtypeStruct((3, 512, DH), bf16), jax.ShapeDtypeStruct((3 * 512 + 16, DH), bf16))
     (mine, send), ordered = plane_matmul(
-        tokens, w_qkv.transpose(1, 0, 2), split_heads, (part, part), "project", order(w_out)
+        tokens, w_qkv.transpose(1, 0, 2), split_heads, shapes, "project", (ids,), order(w_out)
     )
     theirs = swap(send)
-    keys = z_ring(jnp.concatenate([mine[1], theirs[1]], axis=0))
-    values = z_ring(jnp.concatenate([mine[2], theirs[2]], axis=0))
+    keys = z_ring(jnp.concatenate([mine[1], theirs[512:1024]], axis=0))
+    values = z_ring(jnp.concatenate([mine[2], theirs[1024:1536]], axis=0))
     ordered, _ = lax.optimization_barrier((ordered, send))
-    rand, _ = lax.optimization_barrier((rand_blocks.reshape(-1), keys[1:3]))
-    rand = lax.all_gather(rand, "core", axis=0, tiled=True)
+    ids, _ = lax.optimization_barrier((theirs[1536:], keys[1:3]))
+    rand = jnp.concatenate([rand, ids[0, :48].astype(jnp.int32)])
     w_cols = lax.all_to_all(ordered, ("y", "x"), 0, 0, tiled=True)
     started = dense(glob_blocks, mine, theirs, keys, values)
     keys[5], values[6], started, rand = lax.optimization_barrier((keys[5], values[6], started, rand))

time: 185 us -> 179 us (0.968); the launches traced: 184 us -> 176 us
  waiting for transfers between devices: 66.3 us -> 20.7 us
  blocking collectives: 2.38 us -> 26.2 us
  starting transfers between devices: 63.7 us -> 71.9 us
  Pallas kernels: 41.9 us -> 45.6 us
    ppermute x38 -> x36, waiting for transfers between devices: 63.3 us -> 19.4 us  [shift(): return lax.ppermute(a, axis, [(i, (i + step) % n) for i in range(n)])]
    all_gather x0 -> x2, blocking collectives: none -> 26.2 us  [plane_matmul(): by_x = lax.all_gather(a[:n], 'x', axis=0, tiled=True)]
    ppermute x38 -> x36, starting transfers between devices: 58.6 us -> 64.5 us  [shift(): return lax.ppermute(a, axis, [(i, (i + step) % n) for i in range(n)])]
    pallas_call x6, Pallas kernels: 28 us -> 31.8 us  [partial_matmul(): pl.pallas_call(lambda *refs: partial_kernel(steps, counts, n, groups, has...]
    all_to_all x1, starting transfers between devices: 4.67 us -> 7.27 us  [body(): w_cols = lax.all_to_all(ordered, ('y', 'x'), 0, 0, tiled=True)]
    slice x1 -> x11, local copies, waits for them, and re-layouts: 0.98 us -> 3.4 us  [the longest x4 1.62 us: plane_matmul(): high[2 * n:]]
    optimization_barrier x1 -> x0, blocking collectives: 2.38 us -> none  [body(): lax.optimization_barrier((keys[5], values[6], started, rand))]
    unnamed x64 -> x73, local copies, waits for them, and re-layouts: 6.14 us -> 4.06 us
  transfers between devices with their start and end apart: 41 -> 39, of which waited for: 22 -> 11; matrix products, arithmetic and copies ran while one was open for 1% -> 1% of each run, Pallas kernels for 18% -> 20%
where the time goes in v3:
time: 179 us; the launch traced here: 176 us
  starting transfers between devices  71.9 us (40%)
  Pallas kernels  45.6 us (25%)
  blocking collectives  26.2 us (15%)
  waiting for transfers between devices  20.7 us (12%)
  local copies, waits for them, and re-layouts  9.66 us (5%)
    ppermute x36, starting transfers between devices, shift(): return lax.ppermute(a, axis, [(i, (i + step) % n) for i in range(n)])  64.5 us
    pallas_call x6, Pallas kernels, partial_matmul(): pl.pallas_call(lambda *refs: partial_kernel(steps, counts, n, groups, has...  31.8 us
    all_gather x2, blocking collectives, plane_matmul(): by_x = lax.all_gather(a[:n], 'x', axis=0, tiled=True)  26.2 us
    ppermute x36, waiting for transfers between devices, shift(): return lax.ppermute(a, axis, [(i, (i + step) % n) for i in range(n)])  19.4 us
    pallas_call x1, Pallas kernels, attend(): pl.pallas_call(attend_kernel, out_shape=jax.ShapeDtypeStruct((2, 512, DH)...  9.1 us
    all_to_all x1, starting transfers between devices, body(): w_cols = lax.all_to_all(ordered, ('y', 'x'), 0, 0, tiled=True)  7.27 us
    unnamed x73, local copies, waits for them, and re-layouts  4.06 us
  transfers between devices with their start and end apart: 39, of which 11 were waited for; matrix products, arithmetic and copies ran while one was open for 1% of the time, Pallas kernels for 20%

profile of v3, /device:TPU:24, one launch (start us, length us, event | category | flops | bytes accessed | tf_op | source)
XLA Modules:
  0.0 175.7 jit_solution(13233090273987044066)
XLA Ops:
  5.5 13.1 %all_gather.6 = bf16[1024,256]{1,0:T(8,128)(2,1)S(1)} all-gather(bf16[256,256]{1,0:T(8,128)(2,1)S(1)} %get-tuple-element.72), channel_id=1, replica_groups=mesh['z'=8,'core'=2,'y'=4,'x'=4] {'x'}, dimensions={0}, use_global_device_ids=true | all-gather | bytes 655360 | tf_op jit(solution)/shard_map/all_gather | solution.py:30
  18.7 3.3 %collective-permute-start.6 = (bf16[1024,256]{1,0:T(8,128)(2,1)S(1)}, bf16[1024,256]{1,0:T(8,128)(2,1)S(1)}, u32[]{:S(2)}, u32[]{:S(2)}) collective-permute-start(bf16[1024,256]{1,0:T(8,128)(2,1)S(1)} %pad_maximum_fusion), channel_id=1, source_target_pairs={{0,3},{1,0},{2,1},{3,2},{4,7},{5,4},{6,5},{7,6},{8,11},{9,8},{10,9... | collective-permute-start | bytes 1572872 | tf_op jit(solution)/shard_map/ppermute | solution.py:20
  22.1 3.2 %collective-permute-start.3 = (bf16[1024,256]{1,0:T(8,128)(2,1)S(1)}, bf16[1024,256]{1,0:T(8,128)(2,1)S(1)}, u32[]{:S(2)}, u32[]{:S(2)}) collective-permute-start(bf16[1024,256]{1,0:T(8,128)(2,1)S(1)} %all_gather.6), channel_id=1, source_target_pairs={{0,4},{4,8},{8,12},{12,0},{1,5},{5,9},{9,13},{13,1},{2,6},{6,10},{... | collective-permute-start | bytes 1572872 | tf_op jit(solution)/shard_map/ppermute | solution.py:20
  25.3 3.2 %order.1 = bf16[16,256,256]{2,1,0:T(8,128)(2,1)} custom-call(bf16[256,4096]{1,0:T(8,128)(2,1)} %w_ref.1), custom_call_target="tpu_custom_call" | custom-call | tf_op jit(solution)/shard_map/order/pallas_call | solution.py:179
  28.5 5.4 %project0.1.refs_5_ = f32[3,512,256]{2,1,0:T(8,128)} custom-call(bf16[4,256,256]{2,1,0:T(8,128)(2,1)} %bitcast.42, bf16[4,256,256]{2,1,0:T(8,128)(2,1)} %bitcast.44, bf16[3,4096,256]{2,1,0:T(8,128)(2,1)} %bitcast.36), custom_call_target="tpu_custom_call" | custom-call | tf_op jit(solution)/shard_map/project0/pallas_call | solution.py:132
  36.3 3.2 %collective-permute-start.10 = (bf16[512,256]{1,0:T(8,128)(2,1)}, bf16[512,256]{1,0:T(8,128)(2,1)S(1)}, u32[]{:S(2)}, u32[]{:S(2)}) collective-permute-start(bf16[512,256]{1,0:T(8,128)(2,1)} %slice.67), channel_id=1, source_target_pairs={{0,3},{1,0},{2,1},{3,2},{4,7},{5,4},{6,5},{7,6},{8,11},{9,8},{10,9... | collective-permute-start | bytes 786440 | tf_op jit(solution)/shard_map/ppermute | solution.py:20
  39.6 3.2 %collective-permute-start.7 = (bf16[512,256]{1,0:T(8,128)(2,1)S(1)}, bf16[512,256]{1,0:T(8,128)(2,1)S(1)}, u32[]{:S(2)}, u32[]{:S(2)}) collective-permute-start(bf16[512,256]{1,0:T(8,128)(2,1)S(1)} %slice.64), channel_id=1, source_target_pairs={{0,4},{4,8},{8,12},{12,0},{1,5},{5,9},{9,13},{13,1},{2,6},{6,10},{... | collective-permute-start | bytes 786440 | tf_op jit(solution)/shard_map/ppermute | solution.py:20
  43.6 9.1 %project1.1.refs_5_ = f32[3,512,256]{2,1,0:T(8,128)} custom-call(bf16[4,256,256]{2,1,0:T(8,128)(2,1)} %bitcast.49, bf16[4,256,256]{2,1,0:T(8,128)(2,1)} %bitcast.48, bf16[4,256,256]{2,1,0:T(8,128)(2,1)} %bitcast.47, bf16[4,256,256]{2,1,0:T(8,128)(2,1)} %bitcast.46, bf16[3,4096,256]{2,1,0:T(8,128)(2,1)} %bitcast.37, f32[3,512,256]{2,1,0:T(8,128)} %project0.1.refs_5_), custom_call_target="tpu_custom_call" | custom-call | tf_op jit(solution)/shard_map/project1/pallas_call | solution.py:132
  53.7 6.4 %project3.1 = (bf16[3,512,128]{2,1,0:T(8,128)(2,1)}, bf16[1552,128]{1,0:T(8,128)(2,1)}) custom-call(bf16[2,256,256]{2,1,0:T(8,128)(2,1)} %bitcast.57, bf16[2,256,256]{2,1,0:T(8,128)(2,1)} %bitcast.56, bf16[2,256,256]{2,1,0:T(8,128)(2,1)} %bitcast.55, bf16[2,256,256]{2,1,0:T(8,128)(2,1)} %bitcast.54, bf16[3,4096,256]{2,1,0:T(8,128)(2,1)} %bitcast.38, ...), custom_call_target="tpu_custom_call" | custom-call | tf_op jit(solution)/shard_map/project3/pallas_call | solution.py:132
  60.2 7.3 %all-to-all-start = ((bf16[16,256,256]{2,1,0:T(8,128)(2,1)}), bf16[16,256,256]{2,1,0:T(8,128)(2,1)S(1)}, u32[]{:S(2)}, u32[]{:S(2)}) async-start(bf16[16,256,256]{2,1,0:T(8,128)(2,1)} %order.1), calls=%async_computation | async-start | bytes 4194304 | tf_op jit(solution)/shard_map/all_to_all | solution.py:364
  67.6 2.0 %collective-permute-start.12 = (bf16[1024,128]{1,0:T(8,128)(2,1)S(1)}, bf16[1024,128]{1,0:T(8,128)(2,1)S(1)}, u32[]{:S(2)}, u32[]{:S(2)}) collective-permute-start(bf16[1024,128]{1,0:T(8,128)(2,1)S(1)} %pad_maximum_fusion.2.refs_3_.refs_5_), channel_id=1, source_target_pairs={{0,32},{32,64},{64,96},{96,128},{128,160},{160,192},{192,224},{224... | collective-permute-start | bytes 786440 | tf_op jit(solution)/shard_map/ppermute | solution.py:20
  69.6 4.2 %collective-permute-start.15 = (bf16[1024,128]{1,0:T(8,128)(2,1)S(1)}, bf16[1024,128]{1,0:T(8,128)(2,1)S(1)}, u32[]{:S(2)}, u32[]{:S(2)}) collective-permute-start(bf16[1024,128]{1,0:T(8,128)(2,1)S(1)} %pad_maximum_fusion.3.refs_8_.refs_13_), channel_id=1, source_target_pairs={{0,224},{32,0},{64,32},{96,64},{128,96},{160,128},{192,160},{224,1... | collective-permute-start | bytes 786440 | tf_op jit(solution)/shard_map/ppermute | solution.py:20
  73.8 2.0 %collective-permute-start.18 = (bf16[1024,128]{1,0:T(8,128)(2,1)S(1)}, bf16[1024,128]{1,0:T(8,128)(2,1)}, u32[]{:S(2)}, u32[]{:S(2)}) collective-permute-start(bf16[1024,128]{1,0:T(8,128)(2,1)S(1)} %pad_maximum_fusion.2.refs_3_.refs_5_), channel_id=1, source_target_pairs={{0,224},{32,0},{64,32},{96,64},{128,96},{160,128},{192,160},{224,1... | collective-permute-start | bytes 786440 | tf_op jit(solution)/shard_map/ppermute | solution.py:20
  75.9 4.8 %collective-permute-done.12.refs_4_.refs_6_ = bf16[1024,128]{1,0:T(8,128)(2,1)S(1)} collective-permute-done((bf16[1024,128]{1,0:T(8,128)(2,1)S(1)}, bf16[1024,128]{1,0:T(8,128)(2,1)S(1)}, u32[]{:S(2)}, u32[]{:S(2)}) %collective-permute-start.12) | collective-permute-done | bytes 262176 | tf_op jit(solution)/shard_map/ppermute | solution.py:20
  80.7 3.6 %collective-permute-start.16 = (bf16[1024,128]{1,0:T(8,128)(2,1)S(1)}, bf16[1024,128]{1,0:T(8,128)(2,1)}, u32[]{:S(2)}, u32[]{:S(2)}) collective-permute-start(bf16[1024,128]{1,0:T(8,128)(2,1)S(1)} %collective-permute-done.15.refs_10_.refs_15_), channel_id=1, source_target_pairs={{0,224},{32,0},{64,32},{96,64},{128,96},{160,128},{192,160},{224,1... | collective-permute-start | bytes 786440 | tf_op jit(solution)/shard_map/ppermute | solution.py:20
  86.2 3.8 %collective-permute-start.19 = (bf16[1024,128]{1,0:T(8,128)(2,1)}, bf16[1024,128]{1,0:T(8,128)(2,1)S(1)}, u32[]{:S(2)}, u32[]{:S(2)}) collective-permute-start(bf16[1024,128]{1,0:T(8,128)(2,1)} %collective-permute-done.18.refs_5_.refs_7_), channel_id=1, source_target_pairs={{0,224},{32,0},{64,32},{96,64},{128,96},{160,128},{192,160},{224,1... | collective-permute-start | bytes 786440 | tf_op jit(solution)/shard_map/ppermute | solution.py:20
  91.8 3.8 %collective-permute-start.17 = (bf16[1024,128]{1,0:T(8,128)(2,1)}, bf16[1024,128]{1,0:T(8,128)(2,1)S(1)}, u32[]{:S(2)}, u32[]{:S(2)}) collective-permute-start(bf16[1024,128]{1,0:T(8,128)(2,1)} %collective-permute-done.16.refs_12_.refs_17_), channel_id=1, source_target_pairs={{0,224},{32,0},{64,32},{96,64},{128,96},{160,128},{192,160},{224,1... | collective-permute-start | bytes 786440 | tf_op jit(solution)/shard_map/ppermute | solution.py:20
  97.5 3.6 %collective-permute-start.22 = (bf16[1024,128]{1,0:T(8,128)(2,1)S(1)}, bf16[1024,128]{1,0:T(8,128)(2,1)S(1)}, u32[]{:S(2)}, u32[]{:S(2)}) collective-permute-start(bf16[1024,128]{1,0:T(8,128)(2,1)S(1)} %collective-permute-done.19.refs_7_.refs_9_), channel_id=1, source_target_pairs={{0,224},{32,0},{64,32},{96,64},{128,96},{160,128},{192,160},{224,1... | collective-permute-start | bytes 786440 | tf_op jit(solution)/shard_map/ppermute | solution.py:20
  103.7 6.9 %collective-permute-start.25 = (bf16[1024,128]{1,0:T(8,128)(2,1)S(1)}, bf16[1024,128]{1,0:T(8,128)(2,1)S(1)}, u32[]{:S(2)}, u32[]{:S(2)}) collective-permute-start(bf16[1024,128]{1,0:T(8,128)(2,1)S(1)} %collective-permute-done.17.refs_19_), channel_id=1, source_target_pairs={{0,224},{32,0},{64,32},{96,64},{128,96},{160,128},{192,160},{224,1... | collective-permute-start | bytes 786440 | tf_op jit(solution)/shard_map/ppermute | solution.py:20
  110.6 4.2 %collective-permute-done.23.refs_12_ = bf16[1024,128]{1,0:T(8,128)(2,1)S(1)} collective-permute-done((bf16[1024,128]{1,0:T(8,128)(2,1)S(1)}, bf16[1024,128]{1,0:T(8,128)(2,1)S(1)}, u32[]{:S(2)}, u32[]{:S(2)}) %collective-permute-start.23) | collective-permute-done | bytes 262176 | tf_op jit(solution)/shard_map/ppermute | solution.py:20
  116.3 9.1 %attend.1 = bf16[2,512,128]{2,1,0:T(8,128)(2,1)} custom-call(s32[96]{0:T(128)} %pad_add_fusion.refs_0_, s32[2]{0:T(128)} %refs_1_.1, s32[2]{0:T(128)} %refs_2_.1, bf16[3,512,128]{2,1,0:T(8,128)(2,1)} %get-tuple-element.43.refs_1_.refs_3_, bf16[1552,128]{1,0:T(8,128)(2,1)} %copy-done.1, bf16[1024,128]{1,0:T(8,128)(2,1)} %copy-done.3, ...), custom_call_target="tpu_custom_call" | custom-call | tf_op jit(solution)/shard_map/attend/pallas_call | solution.py:330
  130.0 3.2 %collective-permute-start.27 = (bf16[256,256]{1,0:T(8,128)(2,1)S(1)}, bf16[256,256]{1,0:T(8,128)(2,1)S(1)}, u32[]{:S(2)}, u32[]{:S(2)}) collective-permute-start(bf16[256,256]{1,0:T(8,128)(2,1)S(1)} %get-tuple-element.67), channel_id=1, source_target_pairs={{0,4},{4,8},{8,12},{12,0},{1,5},{5,9},{9,13},{13,1},{2,6},{6,10},{... | collective-permute-start | bytes 393224 | tf_op jit(solution)/shard_map/ppermute | solution.py:20
  133.2 13.1 %all_gather.7 = bf16[1024,256]{1,0:T(8,128)(2,1)S(1)} all-gather(bf16[256,256]{1,0:T(8,128)(2,1)S(1)} %get-tuple-element.68), channel_id=1, replica_groups=mesh['z'=8,'core'=2,'y'=4,'x'=4] {'x'}, dimensions={0}, use_global_device_ids=true | all-gather | bytes 655360 | tf_op jit(solution)/shard_map/all_gather | solution.py:30
  146.3 3.1 %collective-permute-start.33 = (bf16[1024,256]{1,0:T(8,128)(2,1)S(1)}, bf16[1024,256]{1,0:T(8,128)(2,1)S(1)}, u32[]{:S(2)}, u32[]{:S(2)}) collective-permute-start(bf16[1024,256]{1,0:T(8,128)(2,1)S(1)} %pad_maximum_fusion.1), channel_id=1, source_target_pairs={{0,3},{1,0},{2,1},{3,2},{4,7},{5,4},{6,5},{7,6},{8,11},{9,8},{10,9... | collective-permute-start | bytes 1572872 | tf_op jit(solution)/shard_map/ppermute | solution.py:20
  149.4 3.2 %collective-permute-start.30 = (bf16[1024,256]{1,0:T(8,128)(2,1)S(1)}, bf16[1024,256]{1,0:T(8,128)(2,1)S(1)}, u32[]{:S(2)}, u32[]{:S(2)}) collective-permute-start(bf16[1024,256]{1,0:T(8,128)(2,1)S(1)} %all_gather.7), channel_id=1, source_target_pairs={{0,4},{4,8},{8,12},{12,0},{1,5},{5,9},{9,13},{13,1},{2,6},{6,10},{... | collective-permute-start | bytes 1572872 | tf_op jit(solution)/shard_map/ppermute | solution.py:20
  152.7 3.2 %output0.1.refs_5_ = f32[1,512,256]{2,1,0:T(8,128)} custom-call(bf16[4,256,256]{2,1,0:T(8,128)(2,1)} %bitcast.43, bf16[4,256,256]{2,1,0:T(8,128)(2,1)} %bitcast.45, bf16[1,4096,256]{2,1,0:T(8,128)(2,1)} %bitcast.39), custom_call_target="tpu_custom_call" | custom-call | tf_op jit(solution)/shard_map/output0/pallas_call | solution.py:132
  155.8 2.6 %collective-permute-done.33 = bf16[1024,256]{1,0:T(8,128)(2,1)S(1)} collective-permute-done((bf16[1024,256]{1,0:T(8,128)(2,1)S(1)}, bf16[1024,256]{1,0:T(8,128)(2,1)S(1)}, u32[]{:S(2)}, u32[]{:S(2)}) %collective-permute-start.33) | collective-permute-done | bytes 524320 | tf_op jit(solution)/shard_map/ppermute | solution.py:20
  158.4 1.8 %collective-permute-done.32 = bf16[1024,256]{1,0:T(8,128)(2,1)S(1)} collective-permute-done((bf16[1024,256]{1,0:T(8,128)(2,1)S(1)}, bf16[1024,256]{1,0:T(8,128)(2,1)S(1)}, u32[]{:S(2)}, u32[]{:S(2)}) %collective-permute-start.32) | collective-permute-done | bytes 524320 | tf_op jit(solution)/shard_map/ppermute | solution.py:20
  161.2 2.2 %collective-permute-start.37 = (bf16[512,256]{1,0:T(8,128)(2,1)S(1)}, bf16[512,256]{1,0:T(8,128)(2,1)S(1)}, u32[]{:S(2)}, u32[]{:S(2)}) collective-permute-start(bf16[512,256]{1,0:T(8,128)(2,1)S(1)} %slice.81), channel_id=1, source_target_pairs={{0,3},{1,0},{2,1},{3,2},{4,7},{5,4},{6,5},{7,6},{8,11},{9,8},{10,9... | collective-permute-start | bytes 786440 | tf_op jit(solution)/shard_map/ppermute | solution.py:20
  163.4 3.2 %collective-permute-start.34 = (bf16[512,256]{1,0:T(8,128)(2,1)S(1)}, bf16[512,256]{1,0:T(8,128)(2,1)S(1)}, u32[]{:S(2)}, u32[]{:S(2)}) collective-permute-start(bf16[512,256]{1,0:T(8,128)(2,1)S(1)} %slice.78), channel_id=1, source_target_pairs={{0,4},{4,8},{8,12},{12,0},{1,5},{5,9},{9,13},{13,1},{2,6},{6,10},{... | collective-permute-start | bytes 786440 | tf_op jit(solution)/shard_map/ppermute | solution.py:20
  166.7 4.7 %output1.1.refs_5_ = f32[1,512,256]{2,1,0:T(8,128)} custom-call(bf16[4,256,256]{2,1,0:T(8,128)(2,1)} %bitcast.53, bf16[4,256,256]{2,1,0:T(8,128)(2,1)} %bitcast.52, bf16[4,256,256]{2,1,0:T(8,128)(2,1)} %bitcast.51, bf16[4,256,256]{2,1,0:T(8,128)(2,1)} %bitcast.50, bf16[1,4096,256]{2,1,0:T(8,128)(2,1)} %bitcast.40, f32[1,512,256]{2,1,0:T(8,128)} %output0.1.refs_5_), custom_call_target="tpu_custom_call" | custom-call | tf_op jit(solution)/shard_map/output1/pallas_call | solution.py:132
  172.3 3.2 %output3.1 = bf16[512,256]{1,0:T(8,128)(2,1)} custom-call(bf16[2,256,256]{2,1,0:T(8,128)(2,1)} %bitcast.61, bf16[2,256,256]{2,1,0:T(8,128)(2,1)} %bitcast.60, bf16[2,256,256]{2,1,0:T(8,128)(2,1)} %bitcast.59, bf16[2,256,256]{2,1,0:T(8,128)(2,1)} %bitcast.58, bf16[1,4096,256]{2,1,0:T(8,128)(2,1)} %bitcast.41, f32[1,512,256]{2,1,0:T(8,128)} %output1.1.refs_5_), custom_call_target="tpu_custom_call" | custom-call | tf_op jit(solution)/shard_map/output3/pallas_call | solution.py:132
  (155 shorter events, 25.9 us)
Async XLA Ops:
  1.0 17.7 %collective-permute-start.2 = (bf16[256,256]{1,0:T(8,128)(2,1)S(1)}, bf16[256,256]{1,0:T(8,128)(2,1)S(1)}, u32[]{:S(2)}, u32[]{:S(2)}) collective-permute-start(bf16[256,256]{1,0:T(8,128)(2,1)S(1)} %get-tuple-element.71), channel_id=1, source_target_pairs={{0,8},{4,12},{8,0},{12,4},{1,9},{5,13},{9,1},{13,5},{2,10},{6,14},... | collective-permute-start | bytes 393224 | tf_op jit(solution)/shard_map/ppermute | solution.py:20
  2.3 16.4 %collective-permute-start.1 = (bf16[256,256]{1,0:T(8,128)(2,1)S(1)}, bf16[256,256]{1,0:T(8,128)(2,1)S(1)}, u32[]{:S(2)}, u32[]{:S(2)}) collective-permute-start(bf16[256,256]{1,0:T(8,128)(2,1)S(1)} %get-tuple-element.71), channel_id=1, source_target_pairs={{0,12},{4,0},{8,4},{12,8},{1,13},{5,1},{9,5},{13,9},{2,14},{6,2},{... | collective-permute-start | bytes 393224 | tf_op jit(solution)/shard_map/ppermute | solution.py:20
  3.9 14.8 %collective-permute-start = (bf16[256,256]{1,0:T(8,128)(2,1)S(1)}, bf16[256,256]{1,0:T(8,128)(2,1)S(1)}, u32[]{:S(2)}, u32[]{:S(2)}) collective-permute-start(bf16[256,256]{1,0:T(8,128)(2,1)S(1)} %get-tuple-element.71), channel_id=1, source_target_pairs={{0,4},{4,8},{8,12},{12,0},{1,5},{5,9},{9,13},{13,1},{2,6},{6,10},{... | collective-permute-start | bytes 393224 | tf_op jit(solution)/shard_map/ppermute | solution.py:20
  18.7 15.2 %collective-permute-start.6 = (bf16[1024,256]{1,0:T(8,128)(2,1)S(1)}, bf16[1024,256]{1,0:T(8,128)(2,1)S(1)}, u32[]{:S(2)}, u32[]{:S(2)}) collective-permute-start(bf16[1024,256]{1,0:T(8,128)(2,1)S(1)} %pad_maximum_fusion), channel_id=1, source_target_pairs={{0,3},{1,0},{2,1},{3,2},{4,7},{5,4},{6,5},{7,6},{8,11},{9,8},{10,9... | collective-permute-start | bytes 1572872 | tf_op jit(solution)/shard_map/ppermute | solution.py:20
  22.1 11.9 %collective-permute-start.5 = (bf16[1024,256]{1,0:T(8,128)(2,1)S(1)}, bf16[1024,256]{1,0:T(8,128)(2,1)S(1)}, u32[]{:S(2)}, u32[]{:S(2)}) collective-permute-start(bf16[1024,256]{1,0:T(8,128)(2,1)S(1)} %pad_maximum_fusion), channel_id=1, source_target_pairs={{0,1},{1,2},{2,3},{3,0},{4,5},{5,6},{6,7},{7,4},{8,9},{9,10},{10,1... | collective-permute-start | bytes 1572872 | tf_op jit(solution)/shard_map/ppermute | solution.py:20
  22.1 11.9 %collective-permute-start.4 = (bf16[1024,256]{1,0:T(8,128)(2,1)S(1)}, bf16[1024,256]{1,0:T(8,128)(2,1)S(1)}, u32[]{:S(2)}, u32[]{:S(2)}) collective-permute-start(bf16[1024,256]{1,0:T(8,128)(2,1)S(1)} %all_gather.6), channel_id=1, source_target_pairs={{0,12},{4,0},{8,4},{12,8},{1,13},{5,1},{9,5},{13,9},{2,14},{6,2},{... | collective-permute-start | bytes 1572872 | tf_op jit(solution)/shard_map/ppermute | solution.py:20
  22.1 11.9 %collective-permute-start.3 = (bf16[1024,256]{1,0:T(8,128)(2,1)S(1)}, bf16[1024,256]{1,0:T(8,128)(2,1)S(1)}, u32[]{:S(2)}, u32[]{:S(2)}) collective-permute-start(bf16[1024,256]{1,0:T(8,128)(2,1)S(1)} %all_gather.6), channel_id=1, source_target_pairs={{0,4},{4,8},{8,12},{12,0},{1,5},{5,9},{9,13},{13,1},{2,6},{6,10},{... | collective-permute-start | bytes 1572872 | tf_op jit(solution)/shard_map/ppermute | solution.py:20
  36.3 16.4 %collective-permute-start.10 = (bf16[512,256]{1,0:T(8,128)(2,1)}, bf16[512,256]{1,0:T(8,128)(2,1)S(1)}, u32[]{:S(2)}, u32[]{:S(2)}) collective-permute-start(bf16[512,256]{1,0:T(8,128)(2,1)} %slice.67), channel_id=1, source_target_pairs={{0,3},{1,0},{2,1},{3,2},{4,7},{5,4},{6,5},{7,6},{8,11},{9,8},{10,9... | collective-permute-start | bytes 786440 | tf_op jit(solution)/shard_map/ppermute | solution.py:20
  39.6 13.2 %collective-permute-start.9 = (bf16[512,256]{1,0:T(8,128)(2,1)}, bf16[512,256]{1,0:T(8,128)(2,1)S(1)}, u32[]{:S(2)}, u32[]{:S(2)}) collective-permute-start(bf16[512,256]{1,0:T(8,128)(2,1)} %slice.66), channel_id=1, source_target_pairs={{0,1},{1,2},{2,3},{3,0},{4,5},{5,6},{6,7},{7,4},{8,9},{9,10},{10,1... | collective-permute-start | bytes 786440 | tf_op jit(solution)/shard_map/ppermute | solution.py:20
  39.6 13.2 %collective-permute-start.8 = (bf16[512,256]{1,0:T(8,128)(2,1)}, bf16[512,256]{1,0:T(8,128)(2,1)S(1)}, u32[]{:S(2)}, u32[]{:S(2)}) collective-permute-start(bf16[512,256]{1,0:T(8,128)(2,1)} %slice.65), channel_id=1, source_target_pairs={{0,12},{4,0},{8,4},{12,8},{1,13},{5,1},{9,5},{13,9},{2,14},{6,2},{... | collective-permute-start | bytes 786440 | tf_op jit(solution)/shard_map/ppermute | solution.py:20
  39.6 13.2 %collective-permute-start.7 = (bf16[512,256]{1,0:T(8,128)(2,1)S(1)}, bf16[512,256]{1,0:T(8,128)(2,1)S(1)}, u32[]{:S(2)}, u32[]{:S(2)}) collective-permute-start(bf16[512,256]{1,0:T(8,128)(2,1)S(1)} %slice.64), channel_id=1, source_target_pairs={{0,4},{4,8},{8,12},{12,0},{1,5},{5,9},{9,13},{13,1},{2,6},{6,10},{... | collective-permute-start | bytes 786440 | tf_op jit(solution)/shard_map/ppermute | solution.py:20
  60.2 65.2 %all-to-all-start = ((bf16[16,256,256]{2,1,0:T(8,128)(2,1)}), bf16[16,256,256]{2,1,0:T(8,128)(2,1)S(1)}, u32[]{:S(2)}, u32[]{:S(2)}) async-start(bf16[16,256,256]{2,1,0:T(8,128)(2,1)} %order.1), calls=%async_computation | async-start | bytes 4194304 | tf_op jit(solution)/shard_map/all_to_all | solution.py:364
  67.6 13.1 %collective-permute-start.12 = (bf16[1024,128]{1,0:T(8,128)(2,1)S(1)}, bf16[1024,128]{1,0:T(8,128)(2,1)S(1)}, u32[]{:S(2)}, u32[]{:S(2)}) collective-permute-start(bf16[1024,128]{1,0:T(8,128)(2,1)S(1)} %pad_maximum_fusion.2.refs_3_.refs_5_), channel_id=1, source_target_pairs={{0,32},{32,64},{64,96},{96,128},{128,160},{160,192},{192,224},{224... | collective-permute-start | bytes 786440 | tf_op jit(solution)/shard_map/ppermute | solution.py:20
  69.6 11.0 %collective-permute-start.15 = (bf16[1024,128]{1,0:T(8,128)(2,1)S(1)}, bf16[1024,128]{1,0:T(8,128)(2,1)S(1)}, u32[]{:S(2)}, u32[]{:S(2)}) collective-permute-start(bf16[1024,128]{1,0:T(8,128)(2,1)S(1)} %pad_maximum_fusion.3.refs_8_.refs_13_), channel_id=1, source_target_pairs={{0,224},{32,0},{64,32},{96,64},{128,96},{160,128},{192,160},{224,1... | collective-permute-start | bytes 786440 | tf_op jit(solution)/shard_map/ppermute | solution.py:20
  73.8 12.3 %collective-permute-start.18 = (bf16[1024,128]{1,0:T(8,128)(2,1)S(1)}, bf16[1024,128]{1,0:T(8,128)(2,1)}, u32[]{:S(2)}, u32[]{:S(2)}) collective-permute-start(bf16[1024,128]{1,0:T(8,128)(2,1)S(1)} %pad_maximum_fusion.2.refs_3_.refs_5_), channel_id=1, source_target_pairs={{0,224},{32,0},{64,32},{96,64},{128,96},{160,128},{192,160},{224,1... | collective-permute-start | bytes 786440 | tf_op jit(solution)/shard_map/ppermute | solution.py:20
  75.9 14.1 %collective-permute-start.20 = (bf16[1024,128]{1,0:T(8,128)(2,1)S(1)}, bf16[1024,128]{1,0:T(8,128)(2,1)}, u32[]{:S(2)}, u32[]{:S(2)}) collective-permute-start(bf16[1024,128]{1,0:T(8,128)(2,1)S(1)} %pad_maximum_fusion.3.refs_8_.refs_13_), channel_id=1, source_target_pairs={{0,32},{32,64},{64,96},{96,128},{128,160},{160,192},{192,224},{224... | collective-permute-start | bytes 786440 | tf_op jit(solution)/shard_map/ppermute | solution.py:20
  80.7 10.6 %collective-permute-start.13 = (bf16[1024,128]{1,0:T(8,128)(2,1)S(1)}, bf16[1024,128]{1,0:T(8,128)(2,1)}, u32[]{:S(2)}, u32[]{:S(2)}) collective-permute-start(bf16[1024,128]{1,0:T(8,128)(2,1)S(1)} %collective-permute-done.12.refs_4_.refs_6_), channel_id=1, source_target_pairs={{0,32},{32,64},{64,96},{96,128},{128,160},{160,192},{192,224},{224... | collective-permute-start | bytes 786440 | tf_op jit(solution)/shard_map/ppermute | solution.py:20
  80.7 11.1 %collective-permute-start.16 = (bf16[1024,128]{1,0:T(8,128)(2,1)S(1)}, bf16[1024,128]{1,0:T(8,128)(2,1)}, u32[]{:S(2)}, u32[]{:S(2)}) collective-permute-start(bf16[1024,128]{1,0:T(8,128)(2,1)S(1)} %collective-permute-done.15.refs_10_.refs_15_), channel_id=1, source_target_pairs={{0,224},{32,0},{64,32},{96,64},{128,96},{160,128},{192,160},{224,1... | collective-permute-start | bytes 786440 | tf_op jit(solution)/shard_map/ppermute | solution.py:20
  86.2 11.3 %collective-permute-start.19 = (bf16[1024,128]{1,0:T(8,128)(2,1)}, bf16[1024,128]{1,0:T(8,128)(2,1)S(1)}, u32[]{:S(2)}, u32[]{:S(2)}) collective-permute-start(bf16[1024,128]{1,0:T(8,128)(2,1)} %collective-permute-done.18.refs_5_.refs_7_), channel_id=1, source_target_pairs={{0,224},{32,0},{64,32},{96,64},{128,96},{160,128},{192,160},{224,1... | collective-permute-start | bytes 786440 | tf_op jit(solution)/shard_map/ppermute | solution.py:20
  90.0 11.1 %collective-permute-start.21 = (bf16[1024,128]{1,0:T(8,128)(2,1)}, bf16[1024,128]{1,0:T(8,128)(2,1)S(1)}, u32[]{:S(2)}, u32[]{:S(2)}) collective-permute-start(bf16[1024,128]{1,0:T(8,128)(2,1)} %collective-permute-done.20.refs_9_.refs_14_), channel_id=1, source_target_pairs={{0,32},{32,64},{64,96},{96,128},{128,160},{160,192},{192,224},{224... | collective-permute-start | bytes 786440 | tf_op jit(solution)/shard_map/ppermute | solution.py:20
  91.3 12.2 %collective-permute-start.14 = (bf16[1024,128]{1,0:T(8,128)(2,1)}, bf16[1024,128]{1,0:T(8,128)(2,1)S(1)}, u32[]{:S(2)}, u32[]{:S(2)}) collective-permute-start(bf16[1024,128]{1,0:T(8,128)(2,1)} %collective-permute-done.13.refs_6_.refs_8_), channel_id=1, source_target_pairs={{0,32},{32,64},{64,96},{96,128},{128,160},{160,192},{192,224},{224... | collective-permute-start | bytes 786440 | tf_op jit(solution)/shard_map/ppermute | solution.py:20
  91.8 11.7 %collective-permute-start.17 = (bf16[1024,128]{1,0:T(8,128)(2,1)}, bf16[1024,128]{1,0:T(8,128)(2,1)S(1)}, u32[]{:S(2)}, u32[]{:S(2)}) collective-permute-start(bf16[1024,128]{1,0:T(8,128)(2,1)} %collective-permute-done.16.refs_12_.refs_17_), channel_id=1, source_target_pairs={{0,224},{32,0},{64,32},{96,64},{128,96},{160,128},{192,160},{224,1... | collective-permute-start | bytes 786440 | tf_op jit(solution)/shard_map/ppermute | solution.py:20
  97.5 13.1 %collective-permute-start.22 = (bf16[1024,128]{1,0:T(8,128)(2,1)S(1)}, bf16[1024,128]{1,0:T(8,128)(2,1)S(1)}, u32[]{:S(2)}, u32[]{:S(2)}) collective-permute-start(bf16[1024,128]{1,0:T(8,128)(2,1)S(1)} %collective-permute-done.19.refs_7_.refs_9_), channel_id=1, source_target_pairs={{0,224},{32,0},{64,32},{96,64},{128,96},{160,128},{192,160},{224,1... | collective-permute-start | bytes 786440 | tf_op jit(solution)/shard_map/ppermute | solution.py:20
  103.5 11.4 %collective-permute-start.23 = (bf16[1024,128]{1,0:T(8,128)(2,1)S(1)}, bf16[1024,128]{1,0:T(8,128)(2,1)S(1)}, u32[]{:S(2)}, u32[]{:S(2)}) collective-permute-start(bf16[1024,128]{1,0:T(8,128)(2,1)S(1)} %collective-permute-done.14.refs_10_), channel_id=1, source_target_pairs={{0,32},{32,64},{64,96},{96,128},{128,160},{160,192},{192,224},{224... | collective-permute-start | bytes 786440 | tf_op jit(solution)/shard_map/ppermute | solution.py:20
  103.7 11.2 %collective-permute-start.25 = (bf16[1024,128]{1,0:T(8,128)(2,1)S(1)}, bf16[1024,128]{1,0:T(8,128)(2,1)S(1)}, u32[]{:S(2)}, u32[]{:S(2)}) collective-permute-start(bf16[1024,128]{1,0:T(8,128)(2,1)S(1)} %collective-permute-done.17.refs_19_), channel_id=1, source_target_pairs={{0,224},{32,0},{64,32},{96,64},{128,96},{160,128},{192,160},{224,1... | collective-permute-start | bytes 786440 | tf_op jit(solution)/shard_map/ppermute | solution.py:20
  128.2 18.1 %collective-permute-start.29 = (bf16[256,256]{1,0:T(8,128)(2,1)S(1)}, bf16[256,256]{1,0:T(8,128)(2,1)S(1)}, u32[]{:S(2)}, u32[]{:S(2)}) collective-permute-start(bf16[256,256]{1,0:T(8,128)(2,1)S(1)} %get-tuple-element.67), channel_id=1, source_target_pairs={{0,8},{4,12},{8,0},{12,4},{1,9},{5,13},{9,1},{13,5},{2,10},{6,14},... | collective-permute-start | bytes 393224 | tf_op jit(solution)/shard_map/ppermute | solution.py:20
  130.0 16.3 %collective-permute-start.28 = (bf16[256,256]{1,0:T(8,128)(2,1)S(1)}, bf16[256,256]{1,0:T(8,128)(2,1)S(1)}, u32[]{:S(2)}, u32[]{:S(2)}) collective-permute-start(bf16[256,256]{1,0:T(8,128)(2,1)S(1)} %get-tuple-element.67), channel_id=1, source_target_pairs={{0,12},{4,0},{8,4},{12,8},{1,13},{5,1},{9,5},{13,9},{2,14},{6,2},{... | collective-permute-start | bytes 393224 | tf_op jit(solution)/shard_map/ppermute | solution.py:20
  130.0 16.3 %collective-permute-start.27 = (bf16[256,256]{1,0:T(8,128)(2,1)S(1)}, bf16[256,256]{1,0:T(8,128)(2,1)S(1)}, u32[]{:S(2)}, u32[]{:S(2)}) collective-permute-start(bf16[256,256]{1,0:T(8,128)(2,1)S(1)} %get-tuple-element.67), channel_id=1, source_target_pairs={{0,4},{4,8},{8,12},{12,0},{1,5},{5,9},{9,13},{13,1},{2,6},{6,10},{... | collective-permute-start | bytes 393224 | tf_op jit(solution)/shard_map/ppermute | solution.py:20
  146.3 12.1 %collective-permute-start.33 = (bf16[1024,256]{1,0:T(8,128)(2,1)S(1)}, bf16[1024,256]{1,0:T(8,128)(2,1)S(1)}, u32[]{:S(2)}, u32[]{:S(2)}) collective-permute-start(bf16[1024,256]{1,0:T(8,128)(2,1)S(1)} %pad_maximum_fusion.1), channel_id=1, source_target_pairs={{0,3},{1,0},{2,1},{3,2},{4,7},{5,4},{6,5},{7,6},{8,11},{9,8},{10,9... | collective-permute-start | bytes 1572872 | tf_op jit(solution)/shard_map/ppermute | solution.py:20
  149.4 10.8 %collective-permute-start.32 = (bf16[1024,256]{1,0:T(8,128)(2,1)S(1)}, bf16[1024,256]{1,0:T(8,128)(2,1)S(1)}, u32[]{:S(2)}, u32[]{:S(2)}) collective-permute-start(bf16[1024,256]{1,0:T(8,128)(2,1)S(1)} %pad_maximum_fusion.1), channel_id=1, source_target_pairs={{0,1},{1,2},{2,3},{3,0},{4,5},{5,6},{6,7},{7,4},{8,9},{9,10},{10,1... | collective-permute-start | bytes 1572872 | tf_op jit(solution)/shard_map/ppermute | solution.py:20
  149.4 11.7 %collective-permute-start.31 = (bf16[1024,256]{1,0:T(8,128)(2,1)S(1)}, bf16[1024,256]{1,0:T(8,128)(2,1)S(1)}, u32[]{:S(2)}, u32[]{:S(2)}) collective-permute-start(bf16[1024,256]{1,0:T(8,128)(2,1)S(1)} %all_gather.7), channel_id=1, source_target_pairs={{0,12},{4,0},{8,4},{12,8},{1,13},{5,1},{9,5},{13,9},{2,14},{6,2},{... | collective-permute-start | bytes 1572872 | tf_op jit(solution)/shard_map/ppermute | solution.py:20
  149.4 11.7 %collective-permute-start.30 = (bf16[1024,256]{1,0:T(8,128)(2,1)S(1)}, bf16[1024,256]{1,0:T(8,128)(2,1)S(1)}, u32[]{:S(2)}, u32[]{:S(2)}) collective-permute-start(bf16[1024,256]{1,0:T(8,128)(2,1)S(1)} %all_gather.7), channel_id=1, source_target_pairs={{0,4},{4,8},{8,12},{12,0},{1,5},{5,9},{9,13},{13,1},{2,6},{6,10},{... | collective-permute-start | bytes 1572872 | tf_op jit(solution)/shard_map/ppermute | solution.py:20
  (43 other events, 375.8 us)

commit v4 on v3

--- a/solution.py
+++ b/solution.py
@@ -89,24 +89,20 @@
     for copy in x_copies:
         copy.wait()
 
-    def multiply(i, carry):
-        part, g = i // groups, lax.rem(i, groups)
+    def multiply(part, carry):
         half, k = part // n_steps, lax.rem(part, n_steps)
-
-        @pl.when(g == 0)
-        def _():
-            for j in range(NXY):
-                w_copy(part, j, 0).wait()
-
+        for j in range(NXY):
+            w_copy(part, j, 0).wait()
         rows = jnp.concatenate([x_buf[half, NXY * k + j] for j in range(NXY)], axis=1)
         span = pl.ds(pl.multiple_of(half * n, n), n)
-        value = jnp.dot(rows, w_buf[part, g], preferred_element_type=jnp.float32)
-        if has_sums:
-            value = acc[g, span] + value
-        acc[g, span] = value
+        for g in range(groups):
+            value = jnp.dot(rows, w_buf[part, g], preferred_element_type=jnp.float32)
+            if has_sums:
+                value = acc[g, span] + value
+            acc[g, span] = value
         return carry
 
-    lax.fori_loop(0, 2 * n_steps * groups, multiply, 0)
+    lax.fori_loop(0, 2 * n_steps, multiply, 0)
     if finish is None:
         copy = pltpu.make_async_copy(acc, outs[0], s_sem)
         copy.start()
@@ -147,14 +143,20 @@
     )(*operands, *more)
 
 
-def split_heads(acc, ids_ref, mine_ref, send_ref):
+def split_heads(acc, ids_ref, q_ref, kv_ref, send_q_ref, send_kv_ref):
     first = lax.axis_index("core") == 0
     for g in range(3):
         h0 = acc[g, :, :DH].astype(jnp.bfloat16)
         h1 = acc[g, :, DH:].astype(jnp.bfloat16)
-        mine_ref[g] = jnp.where(first, h0, h1)
-        send_ref[g * 512 : (g + 1) * 512] = jnp.where(first, h1, h0)
-    send_ref[3 * 512 :] = ids_ref[...]
+        mine = jnp.where(first, h0, h1)
+        other = jnp.where(first, h1, h0)
+        if g == 0:
+            q_ref[...] = mine
+            send_q_ref[:512] = other
+        else:
+            kv_ref[g - 1] = mine
+            send_kv_ref[g - 1] = other
+    send_q_ref[512:] = ids_ref[...]
 
 
 def round_out(acc, o_ref):
@@ -198,11 +200,12 @@
 
 def attend_kernel(*refs):
     rand_ref, glob_ref, radius_ref, mine_ref, theirs_ref = refs[:5]
-    k_refs, v_refs, dense_ref = refs[5:13], refs[13:21], refs[21]
-    o_ref, k_buf, v_buf, q_buf, sem = refs[22:]
-    copies = [(mine_ref.at[0], q_buf.at[0]), (theirs_ref.at[pl.ds(0, 512)], q_buf.at[1])]
-    for arrays, buf in ((k_refs, k_buf), (v_refs, v_buf)):
-        copies += [(array, buf.at[slot]) for array, slot in zip(arrays, SLOTS)]
+    rings, dense_ref = (refs[5:13], refs[13:21]), refs[21]
+    o_refs = refs[22:24]
+    kv_buf, q_buf, sem = refs[24:]
+    copies = [(mine_ref, q_buf.at[0]), (theirs_ref.at[pl.ds(0, 512)], q_buf.at[1])]
+    for side, arrays in enumerate(rings):
+        copies += [(array, kv_buf.at[slot, side]) for array, slot in zip(arrays, SLOTS)]
     copies = [pltpu.make_async_copy(src, dst, sem.at[i]) for i, (src, dst) in enumerate(copies)]
     for copy in copies:
         copy.start()
@@ -217,7 +220,7 @@
     def place(block):
         slot = lax.rem(block // 16 - z + NZ, NZ)
         side = lax.rem(block // 8 + core, 2)
-        return slot, pl.multiple_of(side * 512 + lax.rem(block, 8) * BLK, BLK)
+        return slot, side, pl.multiple_of(lax.rem(block, 8) * BLK, BLK)
 
     column = lax.broadcasted_iota(jnp.int32, (BLK, 8 * BLK), 1) // BLK
     nt = (((1,), (1,)), ((), ()))
@@ -228,8 +231,8 @@
         ids = [jnp.maximum(block - 1, 0), block, jnp.minimum(block + 1, 127)]
         ids += [rand_ref[base + r] for r in range(3)] + [glob_ref[g] for g in range(2)]
         places = [place(i) for i in ids]
-        keys = jnp.concatenate([k_buf[slot, pl.ds(row, BLK)] for slot, row in places], axis=0)
-        values = jnp.concatenate([v_buf[slot, pl.ds(row, BLK)] for slot, row in places], axis=0)
+        keys = jnp.concatenate([kv_buf[slot, owner, 0, pl.ds(row, BLK)] for slot, owner, row in places], axis=0)
+        values = jnp.concatenate([kv_buf[slot, owner, 1, pl.ds(row, BLK)] for slot, owner, row in places], axis=0)
         mine = pl.ds(pl.multiple_of(j * BLK, BLK), BLK)
         scores = lax.dot_general(q_buf[side, mine], keys, nt, preferred_element_type=jnp.float32) * scale
         low_off = jnp.where((radius >= 1) & (block > 0), -1, 0)
@@ -239,14 +242,16 @@
         probs = jnp.exp(scores - top)
         total = jnp.sum(probs, axis=1, keepdims=True)
         acc = jnp.dot(probs.astype(jnp.bfloat16), values, preferred_element_type=jnp.float32)
-        o_ref[side, mine] = (acc / total).astype(jnp.bfloat16)
-
-    def four_blocks(i, carry):
-        for u in range(4):
-            one_block(i // 2, lax.rem(i, 2) * 4 + u)
-        return carry
-
-    lax.fori_loop(0, 4, four_blocks, 0)
+        o_refs[side][mine] = (acc / total).astype(jnp.bfloat16)
+
+    for side in range(2):
+
+        def four_blocks(i, carry, side=side):
+            for u in range(4):
+                one_block(side, i * 4 + u)
+            return carry
+
+        lax.fori_loop(0, 2, four_blocks, 0)
 
     glob, owned, rows_of = owned_globals(glob_ref)
 
@@ -254,13 +259,15 @@
     def _():
         query = jnp.concatenate([q_buf[side, pl.ds(row, BLK)] for side, row in rows_of], axis=0)
         state = (dense_ref[0], dense_ref[1], dense_ref[2])
-        _, total, acc = lax.fori_loop(3, 6, lambda i, state: dense_step(query, k_buf[i], v_buf[i], state), state)
+        _, total, acc = lax.fori_loop(3, 6, lambda i, state: dense_step(query, kv_buf.at[i], state), state)
         result = (acc / total).astype(jnp.bfloat16)
         for k, (side, row) in enumerate(rows_of):
 
-            @pl.when(owned[k])
-            def _(k=k, side=side, row=row):
-                o_ref[side, pl.ds(row, BLK)] = result[k * BLK : (k + 1) * BLK]
+            for which in range(2):
+
+                @pl.when(owned[k] & (side == which))
+                def _(k=k, which=which, row=row):
+                    o_refs[which][pl.ds(row, BLK)] = result[k * BLK : (k + 1) * BLK]
 
 
 def owned_globals(glob_ref):
@@ -271,8 +278,10 @@
     return glob, [g // 16 == z for g in glob], rows_of
 
 
-def dense_step(query, keys, values, state):
+def dense_step(query, kv_ref, state):
     top, total, acc = state
+    keys = jnp.concatenate([kv_ref[0, 0], kv_ref[1, 0]], axis=0)
+    values = jnp.concatenate([kv_ref[0, 1], kv_ref[1, 1]], axis=0)
     scores = lax.dot_general(query, keys, (((1,), (1,)), ((), ())), preferred_element_type=jnp.float32)
     scores = scores * (1.0 / math.sqrt(DH))
     new = jnp.maximum(top, jnp.max(scores, axis=1, keepdims=True))
@@ -285,15 +294,15 @@
 
 def dense_kernel(*refs):
     glob_ref, mine_ref, theirs_ref = refs[:3]
-    k_refs, v_refs = refs[3:8], refs[8:13]
-    o_ref, k_buf, v_buf, q_buf, sem = refs[13:]
+    rings = refs[3:8], refs[8:13]
+    o_ref, kv_buf, q_buf, sem = refs[13:]
     _, owned, rows_of = owned_globals(glob_ref)
 
     @pl.when(owned[0] | owned[1])
     def _():
-        copies = [(mine_ref.at[0], q_buf.at[0]), (theirs_ref.at[pl.ds(0, 512)], q_buf.at[1])]
-        for arrays, buf in ((k_refs, k_buf), (v_refs, v_buf)):
-            copies += [(array, buf.at[i]) for i, array in enumerate(arrays)]
+        copies = [(mine_ref, q_buf.at[0]), (theirs_ref.at[pl.ds(0, 512)], q_buf.at[1])]
+        for side, arrays in enumerate(rings):
+            copies += [(array, kv_buf.at[i, side]) for i, array in enumerate(arrays)]
         copies = [pltpu.make_async_copy(src, dst, sem.at[i]) for i, (src, dst) in enumerate(copies)]
         for copy in copies:
             copy.start()
@@ -302,12 +311,12 @@
         query = jnp.concatenate([q_buf[side, pl.ds(row, BLK)] for side, row in rows_of], axis=0)
         shape = (2 * BLK, DH)
         init = (jnp.full(shape, NEG, jnp.float32), jnp.zeros(shape, jnp.float32), jnp.zeros(shape, jnp.float32))
-        state = lax.fori_loop(0, 5, lambda i, state: dense_step(query, k_buf[i], v_buf[i], state), init)
+        state = lax.fori_loop(0, 5, lambda i, state: dense_step(query, kv_buf.at[i], state), init)
         for i, value in enumerate(state):
             o_ref[i] = value
 
 
-def dense(glob, mine, theirs, keys, values):
+def dense(glob, mine, theirs, own, other):
     bf16 = jnp.bfloat16
     return pl.pallas_call(
         dense_kernel,
@@ -315,32 +324,30 @@
         in_specs=[SMEM] + [HBM] * 12,
         out_specs=VMEM,
         scratch_shapes=[
-            pltpu.VMEM((5, 1024, DH), bf16),
-            pltpu.VMEM((5, 1024, DH), bf16),
+            pltpu.VMEM((5, 2, 2, 512, DH), bf16),
             pltpu.VMEM((2, 512, DH), bf16),
             pltpu.SemaphoreType.DMA((12,)),
         ],
         compiler_params=PARAMS,
         name="dense",
-    )(glob, mine, theirs, *keys[:5], *values[:5])
-
-
-def attend(rand, glob, radius, mine, theirs, keys, values, started):
+    )(glob, mine, theirs, *own[:5], *other[:5])
+
+
+def attend(rand, glob, radius, mine, theirs, own, other, started):
     bf16 = jnp.bfloat16
     return pl.pallas_call(
         attend_kernel,
-        out_shape=jax.ShapeDtypeStruct((2, 512, DH), bf16),
+        out_shape=(jax.ShapeDtypeStruct((512, DH), bf16),) * 2,
         in_specs=[SMEM] * 3 + [HBM] * 18 + [VMEM],
-        out_specs=VMEM,
+        out_specs=(VMEM, VMEM),
         scratch_shapes=[
-            pltpu.VMEM((NZ, 1024, DH), bf16),
-            pltpu.VMEM((NZ, 1024, DH), bf16),
+            pltpu.VMEM((NZ, 2, 2, 512, DH), bf16),
             pltpu.VMEM((2, 512, DH), bf16),
             pltpu.SemaphoreType.DMA((18,)),
         ],
         compiler_params=PARAMS,
         name="attend",
-    )(rand, glob, radius, mine, theirs, *keys, *values, started)
+    )(rand, glob, radius, mine, theirs, *own, *other, started)
 
 
 def swap(a):
@@ -351,26 +358,27 @@
     bf16 = jnp.bfloat16
     rand = rand_blocks.reshape(-1)
     ids = jnp.pad(rand.astype(bf16)[None], ((0, 15), (0, DH - 48)))
-    shapes = (jax.ShapeDtypeStruct((3, 512, DH), bf16), jax.ShapeDtypeStruct((3 * 512 + 16, DH), bf16))
-    (mine, send), ordered = plane_matmul(
+    heads = jax.ShapeDtypeStruct((2, 512, DH), bf16)
+    shapes = (jax.ShapeDtypeStruct((512, DH), bf16), heads, jax.ShapeDtypeStruct((528, DH), bf16), heads)
+    (mine, own, send_q, send_kv), ordered = plane_matmul(
         tokens, w_qkv.transpose(1, 0, 2), split_heads, shapes, "project", (ids,), order(w_out)
     )
-    theirs = swap(send)
-    keys = z_ring(jnp.concatenate([mine[1], theirs[512:1024]], axis=0))
-    values = z_ring(jnp.concatenate([mine[2], theirs[1024:1536]], axis=0))
-    ordered, _ = lax.optimization_barrier((ordered, send))
-    ids, _ = lax.optimization_barrier((theirs[1536:], keys[1:3]))
+    own = z_ring(own)
+    other = swap(send_kv)
+    ordered, _ = lax.optimization_barrier((ordered, other))
+    w_cols = lax.all_to_all(ordered, ("y", "x"), 0, 0, tiled=True)
+    other = z_ring(other)
+    theirs = swap(send_q)
+    ids, _ = lax.optimization_barrier((theirs[512:], own[1:3]))
     rand = jnp.concatenate([rand, ids[0, :48].astype(jnp.int32)])
-    w_cols = lax.all_to_all(ordered, ("y", "x"), 0, 0, tiled=True)
-    started = dense(glob_blocks, mine, theirs, keys, values)
-    keys[5], values[6], started, rand = lax.optimization_barrier((keys[5], values[6], started, rand))
-    keys.append(shift(keys[5], "z", 1))
-    values.append(shift(values[6], "z", -1))
-    att = attend(rand, glob_blocks, window_radius, mine, theirs, keys, values, started)
-    att, w_cols = lax.optimization_barrier((att, w_cols))
+    started = dense(glob_blocks, mine, theirs, own, other)
+    own[5], other[6], started, rand = lax.optimization_barrier((own[5], other[6], started, rand))
+    own.append(shift(own[5], "z", 1))
+    other.append(shift(other[6], "z", -1))
+    att = attend(rand, glob_blocks, window_radius, mine, theirs, own, other, started)
     attended = jnp.concatenate([att[0], swap(att[1])], axis=1)
     out = jax.ShapeDtypeStruct((512, 256), bf16)
-    return plane_matmul(attended, w_cols[None], round_out, out, "output")[0]
+    return plane_matmul(attended, w_cols[None], round_out, out, "output", (), w_cols)[0]
 
 
 def solution(mesh):

time: 179 us -> 174 us (0.972); the launches traced: 176 us -> 173 us
  starting transfers between devices: 71.9 us -> 60.7 us
  waiting for transfers between devices: 20.7 us -> 27.8 us
  local copies, waits for them, and re-layouts: 9.66 us -> 14.3 us
  Pallas kernels: 45.6 us -> 42.5 us
    ppermute x36, starting transfers between devices: 64.5 us -> 55.5 us  [shift(): return lax.ppermute(a, axis, [(i, (i + step) % n) for i in range(n)])]
    ppermute x36, waiting for transfers between devices: 19.4 us -> 27.2 us  [shift(): return lax.ppermute(a, axis, [(i, (i + step) % n) for i in range(n)])]
    pallas_call x6, Pallas kernels: 31.8 us -> 28.6 us  [partial_matmul(): pl.pallas_call(lambda *refs: partial_kernel(steps, counts, n, groups, has...]
    all_to_all x1, starting transfers between devices: 7.27 us -> 5.04 us  [body(): w_cols = lax.all_to_all(ordered, ('y', 'x'), 0, 0, tiled=True)]
    unnamed x73 -> x66, local copies, waits for them, and re-layouts: 4.06 us -> 6.27 us
    slice x4, local copies, waits for them, and re-layouts: 0.77 us -> 2.71 us  [plane_matmul(): low[:2 * n]]
    slice x4, local copies, waits for them, and re-layouts: 1.62 us -> 3.41 us  [plane_matmul(): high[2 * n:]]
  transfers between devices with their start and end apart: 39 -> 40, of which waited for: 11 -> 11; matrix products, arithmetic and copies ran while one was open for 1% -> 4% of each run, Pallas kernels for 20% -> 20%
where the time goes in v4:
time: 174 us; the launch traced here: 173 us
  starting transfers between devices  60.7 us (35%)
  Pallas kernels  42.5 us (24%)
  waiting for transfers between devices  27.8 us (16%)
  blocking collectives  26 us (15%)
  local copies, waits for them, and re-layouts  14.3 us (8%)
    ppermute x36, starting transfers between devices, shift(): return lax.ppermute(a, axis, [(i, (i + step) % n) for i in range(n)])  55.5 us
    pallas_call x6, Pallas kernels, partial_matmul(): pl.pallas_call(lambda *refs: partial_kernel(steps, counts, n, groups, has...  28.6 us
    ppermute x36, waiting for transfers between devices, shift(): return lax.ppermute(a, axis, [(i, (i + step) % n) for i in range(n)])  27.2 us
    all_gather x2, blocking collectives, plane_matmul(): by_x = lax.all_gather(a[:n], 'x', axis=0, tiled=True)  26 us
    pallas_call x1, Pallas kernels, attend(): pl.pallas_call(attend_kernel, out_shape=(jax.ShapeDtypeStruct((512, DH),...  9.16 us
    unnamed x66, local copies, waits for them, and re-layouts  6.27 us
    all_to_all x1, starting transfers between devices, body(): w_cols = lax.all_to_all(ordered, ('y', 'x'), 0, 0, tiled=True)  5.04 us
  transfers between devices with their start and end apart: 40, of which 11 were waited for; matrix products, arithmetic and copies ran while one was open for 4% of the time, Pallas kernels for 20%

profile of v4, /device:TPU:24, one launch (start us, length us, event | category | flops | bytes accessed | tf_op | source)
XLA Modules:
  0.0 172.7 jit_solution(17929303293457370064)
XLA Ops:
  1.0 2.0 %collective-permute-start = (bf16[256,256]{1,0:T(8,128)(2,1)S(1)}, bf16[256,256]{1,0:T(8,128)(2,1)S(1)}, u32[]{:S(2)}, u32[]{:S(2)}) collective-permute-start(bf16[256,256]{1,0:T(8,128)(2,1)S(1)} %get-tuple-element.69), channel_id=1, source_target_pairs={{0,4},{4,8},{8,12},{12,0},{1,5},{5,9},{9,13},{13,1},{2,6},{6,10},{... | collective-permute-start | bytes 393224 | tf_op jit(solution)/shard_map/ppermute | solution.py:20
  4.6 12.9 %all_gather.6 = bf16[1024,256]{1,0:T(8,128)(2,1)S(1)} all-gather(bf16[256,256]{1,0:T(8,128)(2,1)S(1)} %get-tuple-element.70), channel_id=1, replica_groups=mesh['z'=8,'core'=2,'y'=4,'x'=4] {'x'}, dimensions={0}, use_global_device_ids=true | all-gather | bytes 655360 | tf_op jit(solution)/shard_map/all_gather | solution.py:30
  17.5 2.2 %collective-permute-start.5 = (bf16[1024,256]{1,0:T(8,128)(2,1)S(1)}, bf16[1024,256]{1,0:T(8,128)(2,1)S(1)}, u32[]{:S(2)}, u32[]{:S(2)}) collective-permute-start(bf16[1024,256]{1,0:T(8,128)(2,1)S(1)} %pad_maximum_fusion), channel_id=1, source_target_pairs={{0,1},{1,2},{2,3},{3,0},{4,5},{5,6},{6,7},{7,4},{8,9},{9,10},{10,1... | collective-permute-start | bytes 1572872 | tf_op jit(solution)/shard_map/ppermute | solution.py:20
  20.8 2.2 %collective-permute-start.3 = (bf16[1024,256]{1,0:T(8,128)(2,1)S(1)}, bf16[1024,256]{1,0:T(8,128)(2,1)S(1)}, u32[]{:S(2)}, u32[]{:S(2)}) collective-permute-start(bf16[1024,256]{1,0:T(8,128)(2,1)S(1)} %all_gather.6), channel_id=1, source_target_pairs={{0,4},{4,8},{8,12},{12,0},{1,5},{5,9},{9,13},{13,1},{2,6},{6,10},{... | collective-permute-start | bytes 1572872 | tf_op jit(solution)/shard_map/ppermute | solution.py:20
  24.1 3.2 %order.1 = bf16[16,256,256]{2,1,0:T(8,128)(2,1)} custom-call(bf16[256,4096]{1,0:T(8,128)(2,1)} %w_ref.1), custom_call_target="tpu_custom_call" | custom-call | tf_op jit(solution)/shard_map/order/pallas_call | solution.py:181
  27.3 4.6 %project0.1.refs_5_ = f32[3,512,256]{2,1,0:T(8,128)} custom-call(bf16[4,256,256]{2,1,0:T(8,128)(2,1)} %bitcast.34, bf16[4,256,256]{2,1,0:T(8,128)(2,1)} %bitcast.36, bf16[3,4096,256]{2,1,0:T(8,128)(2,1)} %bitcast.27), custom_call_target="tpu_custom_call" | custom-call | tf_op jit(solution)/shard_map/project0/pallas_call | solution.py:128
  32.0 2.8 %collective-permute-done.4 = bf16[1024,256]{1,0:T(8,128)(2,1)S(1)} collective-permute-done((bf16[1024,256]{1,0:T(8,128)(2,1)S(1)}, bf16[1024,256]{1,0:T(8,128)(2,1)S(1)}, u32[]{:S(2)}, u32[]{:S(2)}) %collective-permute-start.4) | collective-permute-done | bytes 524320 | tf_op jit(solution)/shard_map/ppermute | solution.py:20
  39.2 3.2 %collective-permute-start.10 = (bf16[512,256]{1,0:T(8,128)(2,1)}, bf16[512,256]{1,0:T(8,128)(2,1)S(1)}, u32[]{:S(2)}, u32[]{:S(2)}) collective-permute-start(bf16[512,256]{1,0:T(8,128)(2,1)} %slice.49), channel_id=1, source_target_pairs={{0,3},{1,0},{2,1},{3,2},{4,7},{5,4},{6,5},{7,6},{8,11},{9,8},{10,9... | collective-permute-start | bytes 786440 | tf_op jit(solution)/shard_map/ppermute | solution.py:20
  43.3 7.5 %project1.1.refs_5_ = f32[3,512,256]{2,1,0:T(8,128)} custom-call(bf16[4,256,256]{2,1,0:T(8,128)(2,1)} %bitcast.39, bf16[4,256,256]{2,1,0:T(8,128)(2,1)} %bitcast.40, bf16[4,256,256]{2,1,0:T(8,128)(2,1)} %bitcast.37, bf16[4,256,256]{2,1,0:T(8,128)(2,1)} %bitcast.38, bf16[3,4096,256]{2,1,0:T(8,128)(2,1)} %bitcast.28, f32[3,512,256]{2,1,0:T(8,128)} %project0.1.refs_5_), custom_call_target="tpu_custom_call" | custom-call | tf_op jit(solution)/shard_map/project1/pallas_call | solution.py:128
  51.8 5.6 %project3.1 = (bf16[512,128]{1,0:T(8,128)(2,1)}, bf16[2,512,128]{2,1,0:T(8,128)(2,1)}, bf16[528,128]{1,0:T(8,128)(2,1)}, bf16[2,512,128]{2,1,0:T(8,128)(2,1)}) custom-call(bf16[2,256,256]{2,1,0:T(8,128)(2,1)} %bitcast.41, bf16[2,256,256]{2,1,0:T(8,128)(2,1)} %bitcast.42, bf16[2,256,256]{2,1,0:T(8,128)(2,1)} %bitcast.43, bf16[2,256,256]{2,1,0:T(8,128)(2,1)} %bitcast.44, ...), custom_call_target="tpu_custom_call" | custom-call | tf_op jit(solution)/shard_map/project3/pallas_call | solution.py:128
  57.5 2.0 %collective-permute-start.11 = (bf16[2,512,128]{2,1,0:T(8,128)(2,1)}, bf16[2,512,128]{2,1,0:T(8,128)(2,1)S(1)}, u32[]{:S(2)}, u32[]{:S(2)}) collective-permute-start(bf16[2,512,128]{2,1,0:T(8,128)(2,1)} %get-tuple-element.45.refs_3_.refs_5_), channel_id=1, source_target_pairs={{0,32},{32,64},{64,96},{96,128},{128,160},{160,192},{192,224},{224... | collective-permute-start | bytes 786440 | tf_op jit(solution)/shard_map/ppermute | solution.py:20
  59.5 5.6 %collective-permute-start.15 = (bf16[2,512,128]{2,1,0:T(8,128)(2,1)S(1)}, bf16[2,512,128]{2,1,0:T(8,128)(2,1)S(1)}, u32[]{:S(2)}, u32[]{:S(2)}) collective-permute-start(bf16[2,512,128]{2,1,0:T(8,128)(2,1)S(1)} %collective-permute-done.14.refs_8_.refs_13_), channel_id=1, source_target_pairs={{0,224},{32,0},{64,32},{96,64},{128,96},{160,128},{192,160},{224,1... | collective-permute-start | bytes 786440 | tf_op jit(solution)/shard_map/ppermute | solution.py:20
  67.1 3.7 %collective-permute-done.11.refs_4_.refs_6_ = bf16[2,512,128]{2,1,0:T(8,128)(2,1)S(1)} collective-permute-done((bf16[2,512,128]{2,1,0:T(8,128)(2,1)}, bf16[2,512,128]{2,1,0:T(8,128)(2,1)S(1)}, u32[]{:S(2)}, u32[]{:S(2)}) %collective-permute-start.11) | collective-permute-done | bytes 262176 | tf_op jit(solution)/shard_map/ppermute | solution.py:20
  71.7 3.7 %collective-permute-start.16 = (bf16[2,512,128]{2,1,0:T(8,128)(2,1)S(1)}, bf16[2,512,128]{2,1,0:T(8,128)(2,1)}, u32[]{:S(2)}, u32[]{:S(2)}) collective-permute-start(bf16[2,512,128]{2,1,0:T(8,128)(2,1)S(1)} %collective-permute-done.15.refs_10_.refs_15_), channel_id=1, source_target_pairs={{0,224},{32,0},{64,32},{96,64},{128,96},{160,128},{192,160},{224,1... | collective-permute-start | bytes 786440 | tf_op jit(solution)/shard_map/ppermute | solution.py:20
  75.4 5.0 %all-to-all-start = ((bf16[16,256,256]{2,1,0:T(8,128)(2,1)}), bf16[16,256,256]{2,1,0:T(8,128)(2,1)S(1)}, u32[]{:S(2)}, u32[]{:S(2)}) async-start(bf16[16,256,256]{2,1,0:T(8,128)(2,1)} %order.1), calls=%async_computation | async-start | bytes 4194304 | tf_op jit(solution)/shard_map/all_to_all | solution.py:369
  82.9 3.7 %collective-permute-start.17 = (bf16[2,512,128]{2,1,0:T(8,128)(2,1)}, bf16[2,512,128]{2,1,0:T(8,128)(2,1)S(1)}, u32[]{:S(2)}, u32[]{:S(2)}) collective-permute-start(bf16[2,512,128]{2,1,0:T(8,128)(2,1)} %collective-permute-done.16.refs_12_.refs_17_), channel_id=1, source_target_pairs={{0,224},{32,0},{64,32},{96,64},{128,96},{160,128},{192,160},{224,1... | collective-permute-start | bytes 786440 | tf_op jit(solution)/shard_map/ppermute | solution.py:20
  87.2 2.7 %collective-permute-done.20.refs_7_.refs_9_ = bf16[2,512,128]{2,1,0:T(8,128)(2,1)S(1)} collective-permute-done((bf16[2,512,128]{2,1,0:T(8,128)(2,1)S(1)}, bf16[2,512,128]{2,1,0:T(8,128)(2,1)S(1)}, u32[]{:S(2)}, u32[]{:S(2)}) %collective-permute-start.20) | collective-permute-done | bytes 262176 | tf_op jit(solution)/shard_map/ppermute | solution.py:20
  89.9 2.2 %collective-permute-start.23 = (bf16[2,512,128]{2,1,0:T(8,128)(2,1)S(1)}, bf16[2,512,128]{2,1,0:T(8,128)(2,1)S(1)}, u32[]{:S(2)}, u32[]{:S(2)}) collective-permute-start(bf16[2,512,128]{2,1,0:T(8,128)(2,1)S(1)} %collective-permute-done.20.refs_7_.refs_9_), channel_id=1, source_target_pairs={{0,224},{32,0},{64,32},{96,64},{128,96},{160,128},{192,160},{224,1... | collective-permute-start | bytes 786440 | tf_op jit(solution)/shard_map/ppermute | solution.py:20
  94.3 3.2 %collective-permute-done.13.refs_10_ = bf16[2,512,128]{2,1,0:T(8,128)(2,1)S(1)} collective-permute-done((bf16[2,512,128]{2,1,0:T(8,128)(2,1)}, bf16[2,512,128]{2,1,0:T(8,128)(2,1)S(1)}, u32[]{:S(2)}, u32[]{:S(2)}) %collective-permute-start.13) | collective-permute-done | bytes 262176 | tf_op jit(solution)/shard_map/ppermute | solution.py:20
  97.7 3.9 %collective-permute-start.26 = (bf16[2,512,128]{2,1,0:T(8,128)(2,1)S(1)}, bf16[2,512,128]{2,1,0:T(8,128)(2,1)S(1)}, u32[]{:S(2)}, u32[]{:S(2)}) collective-permute-start(bf16[2,512,128]{2,1,0:T(8,128)(2,1)S(1)} %collective-permute-done.17.refs_19_), channel_id=1, source_target_pairs={{0,224},{32,0},{64,32},{96,64},{128,96},{160,128},{192,160},{224,1... | collective-permute-start | bytes 786440 | tf_op jit(solution)/shard_map/ppermute | solution.py:20
  102.9 4.5 %collective-permute-done.24.refs_12_ = bf16[2,512,128]{2,1,0:T(8,128)(2,1)S(1)} collective-permute-done((bf16[2,512,128]{2,1,0:T(8,128)(2,1)S(1)}, bf16[2,512,128]{2,1,0:T(8,128)(2,1)S(1)}, u32[]{:S(2)}, u32[]{:S(2)}) %collective-permute-start.24) | collective-permute-done | bytes 262176 | tf_op jit(solution)/shard_map/ppermute | solution.py:20
  108.8 9.2 %attend.1 = (bf16[512,128]{1,0:T(8,128)(2,1)}, bf16[512,128]{1,0:T(8,128)(2,1)}) custom-call(s32[96]{0:T(128)} %pad_add_fusion.refs_0_, s32[2]{0:T(128)} %refs_1_.1, s32[2]{0:T(128)} %refs_2_.1, bf16[512,128]{1,0:T(8,128)(2,1)} %get-tuple-element.47.refs_1_.refs_3_, bf16[528,128]{1,0:T(8,128)(2,1)} %copy-done.16, ...), custom_call_target="tpu_custom_call" | custom-call | tf_op jit(solution)/shard_map/attend/pallas_call | solution.py:338
  123.2 13.1 %all_gather.7 = bf16[1024,256]{1,0:T(8,128)(2,1)S(1)} all-gather(bf16[256,256]{1,0:T(8,128)(2,1)S(1)} %get-tuple-element.68), channel_id=1, replica_groups=mesh['z'=8,'core'=2,'y'=4,'x'=4] {'x'}, dimensions={0}, use_global_device_ids=true | all-gather | bytes 655360 | tf_op jit(solution)/shard_map/all_gather | solution.py:30
  136.4 2.1 %collective-permute-start.33 = (bf16[1024,256]{1,0:T(8,128)(2,1)S(1)}, bf16[1024,256]{1,0:T(8,128)(2,1)}, u32[]{:S(2)}, u32[]{:S(2)}) collective-permute-start(bf16[1024,256]{1,0:T(8,128)(2,1)S(1)} %pad_maximum_fusion.1), channel_id=1, source_target_pairs={{0,1},{1,2},{2,3},{3,0},{4,5},{5,6},{6,7},{7,4},{8,9},{9,10},{10,1... | collective-permute-start | bytes 1572872 | tf_op jit(solution)/shard_map/ppermute | solution.py:20
  139.7 2.1 %collective-permute-start.31 = (bf16[1024,256]{1,0:T(8,128)(2,1)S(1)}, bf16[1024,256]{1,0:T(8,128)(2,1)}, u32[]{:S(2)}, u32[]{:S(2)}) collective-permute-start(bf16[1024,256]{1,0:T(8,128)(2,1)S(1)} %all_gather.7), channel_id=1, source_target_pairs={{0,4},{4,8},{8,12},{12,0},{1,5},{5,9},{9,13},{13,1},{2,6},{6,10},{... | collective-permute-start | bytes 1572872 | tf_op jit(solution)/shard_map/ppermute | solution.py:20
  143.1 3.1 %output0.1.refs_5_ = f32[1,512,256]{2,1,0:T(8,128)} custom-call(bf16[4,256,256]{2,1,0:T(8,128)(2,1)} %bitcast.33, bf16[4,256,256]{2,1,0:T(8,128)(2,1)} %bitcast.35, bf16[1,4096,256]{2,1,0:T(8,128)(2,1)} %bitcast.30), custom_call_target="tpu_custom_call" | custom-call | tf_op jit(solution)/shard_map/output0/pallas_call | solution.py:128
  146.2 3.5 %collective-permute-done.33 = bf16[1024,256]{1,0:T(8,128)(2,1)} collective-permute-done((bf16[1024,256]{1,0:T(8,128)(2,1)S(1)}, bf16[1024,256]{1,0:T(8,128)(2,1)}, u32[]{:S(2)}, u32[]{:S(2)}) %collective-permute-start.33) | collective-permute-done | bytes 524320 | tf_op jit(solution)/shard_map/ppermute | solution.py:20
  151.2 3.0 %collective-permute-done.32 = bf16[1024,256]{1,0:T(8,128)(2,1)} collective-permute-done((bf16[1024,256]{1,0:T(8,128)(2,1)S(1)}, bf16[1024,256]{1,0:T(8,128)(2,1)}, u32[]{:S(2)}, u32[]{:S(2)}) %collective-permute-start.32) | collective-permute-done | bytes 524320 | tf_op jit(solution)/shard_map/ppermute | solution.py:20
  156.6 1.8 %collective-permute-start.36 = (bf16[512,256]{1,0:T(8,128)(2,1)S(1)}, bf16[512,256]{1,0:T(8,128)(2,1)S(1)}, u32[]{:S(2)}, u32[]{:S(2)}) collective-permute-start(bf16[512,256]{1,0:T(8,128)(2,1)S(1)} %slice.55), channel_id=1, source_target_pairs={{0,12},{4,0},{8,4},{12,8},{1,13},{5,1},{9,5},{13,9},{2,14},{6,2},{... | collective-permute-start | bytes 786440 | tf_op jit(solution)/shard_map/ppermute | solution.py:20
  160.4 3.3 %collective-permute-start.38 = (bf16[512,256]{1,0:T(8,128)(2,1)S(1)}, bf16[512,256]{1,0:T(8,128)(2,1)S(1)}, u32[]{:S(2)}, u32[]{:S(2)}) collective-permute-start(bf16[512,256]{1,0:T(8,128)(2,1)S(1)} %slice.57), channel_id=1, source_target_pairs={{0,3},{1,0},{2,1},{3,2},{4,7},{5,4},{6,5},{7,6},{8,11},{9,8},{10,9... | collective-permute-start | bytes 786440 | tf_op jit(solution)/shard_map/ppermute | solution.py:20
  163.7 4.7 %output1.1.refs_5_ = f32[1,512,256]{2,1,0:T(8,128)} custom-call(bf16[4,256,256]{2,1,0:T(8,128)(2,1)} %bitcast.21.refs_0_, bf16[4,256,256]{2,1,0:T(8,128)(2,1)} %bitcast.22.refs_1_, bf16[4,256,256]{2,1,0:T(8,128)(2,1)} %bitcast.23.refs_2_, bf16[4,256,256]{2,1,0:T(8,128)(2,1)} %bitcast.24.refs_3_, bf16[1,4096,256]{2,1,0:T(8,128)(2,1)} %bitcast.31, ...), custom_call_target="tpu_custom_call" | custom-call | tf_op jit(solution)/shard_map/output1/pallas_call | solution.py:128
  169.4 3.2 %output3.1 = bf16[512,256]{1,0:T(8,128)(2,1)} custom-call(bf16[2,256,256]{2,1,0:T(8,128)(2,1)} %bitcast.45, bf16[2,256,256]{2,1,0:T(8,128)(2,1)} %bitcast.46, bf16[2,256,256]{2,1,0:T(8,128)(2,1)} %bitcast.47, bf16[2,256,256]{2,1,0:T(8,128)(2,1)} %bitcast.48, bf16[1,4096,256]{2,1,0:T(8,128)(2,1)} %bitcast.32, f32[1,512,256]{2,1,0:T(8,128)} %output1.1.refs_5_), custom_call_target="tpu_custom_call" | custom-call | tf_op jit(solution)/shard_map/output3/pallas_call | solution.py:128
  (146 shorter events, 36.5 us)
Async XLA Ops:
  1.0 16.5 %collective-permute-start = (bf16[256,256]{1,0:T(8,128)(2,1)S(1)}, bf16[256,256]{1,0:T(8,128)(2,1)S(1)}, u32[]{:S(2)}, u32[]{:S(2)}) collective-permute-start(bf16[256,256]{1,0:T(8,128)(2,1)S(1)} %get-tuple-element.69), channel_id=1, source_target_pairs={{0,4},{4,8},{8,12},{12,0},{1,5},{5,9},{9,13},{13,1},{2,6},{6,10},{... | collective-permute-start | bytes 393224 | tf_op jit(solution)/shard_map/ppermute | solution.py:20
  3.0 14.4 %collective-permute-start.1 = (bf16[256,256]{1,0:T(8,128)(2,1)S(1)}, bf16[256,256]{1,0:T(8,128)(2,1)S(1)}, u32[]{:S(2)}, u32[]{:S(2)}) collective-permute-start(bf16[256,256]{1,0:T(8,128)(2,1)S(1)} %get-tuple-element.69), channel_id=1, source_target_pairs={{0,12},{4,0},{8,4},{12,8},{1,13},{5,1},{9,5},{13,9},{2,14},{6,2},{... | collective-permute-start | bytes 393224 | tf_op jit(solution)/shard_map/ppermute | solution.py:20
  3.1 14.4 %collective-permute-start.2 = (bf16[256,256]{1,0:T(8,128)(2,1)S(1)}, bf16[256,256]{1,0:T(8,128)(2,1)S(1)}, u32[]{:S(2)}, u32[]{:S(2)}) collective-permute-start(bf16[256,256]{1,0:T(8,128)(2,1)S(1)} %get-tuple-element.69), channel_id=1, source_target_pairs={{0,8},{4,12},{8,0},{12,4},{1,9},{5,13},{9,1},{13,5},{2,10},{6,14},... | collective-permute-start | bytes 393224 | tf_op jit(solution)/shard_map/ppermute | solution.py:20
  17.5 14.4 %collective-permute-start.5 = (bf16[1024,256]{1,0:T(8,128)(2,1)S(1)}, bf16[1024,256]{1,0:T(8,128)(2,1)S(1)}, u32[]{:S(2)}, u32[]{:S(2)}) collective-permute-start(bf16[1024,256]{1,0:T(8,128)(2,1)S(1)} %pad_maximum_fusion), channel_id=1, source_target_pairs={{0,1},{1,2},{2,3},{3,0},{4,5},{5,6},{6,7},{7,4},{8,9},{9,10},{10,1... | collective-permute-start | bytes 1572872 | tf_op jit(solution)/shard_map/ppermute | solution.py:20
  19.7 12.2 %collective-permute-start.6 = (bf16[1024,256]{1,0:T(8,128)(2,1)S(1)}, bf16[1024,256]{1,0:T(8,128)(2,1)S(1)}, u32[]{:S(2)}, u32[]{:S(2)}) collective-permute-start(bf16[1024,256]{1,0:T(8,128)(2,1)S(1)} %pad_maximum_fusion), channel_id=1, source_target_pairs={{0,3},{1,0},{2,1},{3,2},{4,7},{5,4},{6,5},{7,6},{8,11},{9,8},{10,9... | collective-permute-start | bytes 1572872 | tf_op jit(solution)/shard_map/ppermute | solution.py:20
  20.8 11.2 %collective-permute-start.3 = (bf16[1024,256]{1,0:T(8,128)(2,1)S(1)}, bf16[1024,256]{1,0:T(8,128)(2,1)S(1)}, u32[]{:S(2)}, u32[]{:S(2)}) collective-permute-start(bf16[1024,256]{1,0:T(8,128)(2,1)S(1)} %all_gather.6), channel_id=1, source_target_pairs={{0,4},{4,8},{8,12},{12,0},{1,5},{5,9},{9,13},{13,1},{2,6},{6,10},{... | collective-permute-start | bytes 1572872 | tf_op jit(solution)/shard_map/ppermute | solution.py:20
  23.0 11.8 %collective-permute-start.4 = (bf16[1024,256]{1,0:T(8,128)(2,1)S(1)}, bf16[1024,256]{1,0:T(8,128)(2,1)S(1)}, u32[]{:S(2)}, u32[]{:S(2)}) collective-permute-start(bf16[1024,256]{1,0:T(8,128)(2,1)S(1)} %all_gather.6), channel_id=1, source_target_pairs={{0,12},{4,0},{8,4},{12,8},{1,13},{5,1},{9,5},{13,9},{2,14},{6,2},{... | collective-permute-start | bytes 1572872 | tf_op jit(solution)/shard_map/ppermute | solution.py:20
  34.9 15.9 %collective-permute-start.7 = (bf16[512,256]{1,0:T(8,128)(2,1)S(1)}, bf16[512,256]{1,0:T(8,128)(2,1)S(1)}, u32[]{:S(2)}, u32[]{:S(2)}) collective-permute-start(bf16[512,256]{1,0:T(8,128)(2,1)S(1)} %slice.46), channel_id=1, source_target_pairs={{0,4},{4,8},{8,12},{12,0},{1,5},{5,9},{9,13},{13,1},{2,6},{6,10},{... | collective-permute-start | bytes 786440 | tf_op jit(solution)/shard_map/ppermute | solution.py:20
  36.0 14.8 %collective-permute-start.8 = (bf16[512,256]{1,0:T(8,128)(2,1)}, bf16[512,256]{1,0:T(8,128)(2,1)S(1)}, u32[]{:S(2)}, u32[]{:S(2)}) collective-permute-start(bf16[512,256]{1,0:T(8,128)(2,1)} %slice.47), channel_id=1, source_target_pairs={{0,12},{4,0},{8,4},{12,8},{1,13},{5,1},{9,5},{13,9},{2,14},{6,2},{... | collective-permute-start | bytes 786440 | tf_op jit(solution)/shard_map/ppermute | solution.py:20
  38.5 12.4 %collective-permute-start.9 = (bf16[512,256]{1,0:T(8,128)(2,1)}, bf16[512,256]{1,0:T(8,128)(2,1)S(1)}, u32[]{:S(2)}, u32[]{:S(2)}) collective-permute-start(bf16[512,256]{1,0:T(8,128)(2,1)} %slice.48), channel_id=1, source_target_pairs={{0,1},{1,2},{2,3},{3,0},{4,5},{5,6},{6,7},{7,4},{8,9},{9,10},{10,1... | collective-permute-start | bytes 786440 | tf_op jit(solution)/shard_map/ppermute | solution.py:20
  39.2 11.6 %collective-permute-start.10 = (bf16[512,256]{1,0:T(8,128)(2,1)}, bf16[512,256]{1,0:T(8,128)(2,1)S(1)}, u32[]{:S(2)}, u32[]{:S(2)}) collective-permute-start(bf16[512,256]{1,0:T(8,128)(2,1)} %slice.49), channel_id=1, source_target_pairs={{0,3},{1,0},{2,1},{3,2},{4,7},{5,4},{6,5},{7,6},{8,11},{9,8},{10,9... | collective-permute-start | bytes 786440 | tf_op jit(solution)/shard_map/ppermute | solution.py:20
  57.5 13.3 %collective-permute-start.11 = (bf16[2,512,128]{2,1,0:T(8,128)(2,1)}, bf16[2,512,128]{2,1,0:T(8,128)(2,1)S(1)}, u32[]{:S(2)}, u32[]{:S(2)}) collective-permute-start(bf16[2,512,128]{2,1,0:T(8,128)(2,1)} %get-tuple-element.45.refs_3_.refs_5_), channel_id=1, source_target_pairs={{0,32},{32,64},{64,96},{96,128},{128,160},{160,192},{192,224},{224... | collective-permute-start | bytes 786440 | tf_op jit(solution)/shard_map/ppermute | solution.py:20
  59.5 12.3 %collective-permute-start.15 = (bf16[2,512,128]{2,1,0:T(8,128)(2,1)S(1)}, bf16[2,512,128]{2,1,0:T(8,128)(2,1)S(1)}, u32[]{:S(2)}, u32[]{:S(2)}) collective-permute-start(bf16[2,512,128]{2,1,0:T(8,128)(2,1)S(1)} %collective-permute-done.14.refs_8_.refs_13_), channel_id=1, source_target_pairs={{0,224},{32,0},{64,32},{96,64},{128,96},{160,128},{192,160},{224,1... | collective-permute-start | bytes 786440 | tf_op jit(solution)/shard_map/ppermute | solution.py:20
  65.0 15.6 %collective-permute-start.19 = (bf16[2,512,128]{2,1,0:T(8,128)(2,1)}, bf16[2,512,128]{2,1,0:T(8,128)(2,1)S(1)}, u32[]{:S(2)}, u32[]{:S(2)}) collective-permute-start(bf16[2,512,128]{2,1,0:T(8,128)(2,1)} %get-tuple-element.45.refs_3_.refs_5_), channel_id=1, source_target_pairs={{0,224},{32,0},{64,32},{96,64},{128,96},{160,128},{192,160},{224,1... | collective-permute-start | bytes 786440 | tf_op jit(solution)/shard_map/ppermute | solution.py:20
  66.1 15.4 %collective-permute-start.21 = (bf16[2,512,128]{2,1,0:T(8,128)(2,1)S(1)}, bf16[2,512,128]{2,1,0:T(8,128)(2,1)S(1)}, u32[]{:S(2)}, u32[]{:S(2)}) collective-permute-start(bf16[2,512,128]{2,1,0:T(8,128)(2,1)S(1)} %collective-permute-done.14.refs_8_.refs_13_), channel_id=1, source_target_pairs={{0,32},{32,64},{64,96},{96,128},{128,160},{160,192},{192,224},{224... | collective-permute-start | bytes 786440 | tf_op jit(solution)/shard_map/ppermute | solution.py:20
  70.8 12.1 %collective-permute-start.12 = (bf16[2,512,128]{2,1,0:T(8,128)(2,1)S(1)}, bf16[2,512,128]{2,1,0:T(8,128)(2,1)}, u32[]{:S(2)}, u32[]{:S(2)}) collective-permute-start(bf16[2,512,128]{2,1,0:T(8,128)(2,1)S(1)} %collective-permute-done.11.refs_4_.refs_6_), channel_id=1, source_target_pairs={{0,32},{32,64},{64,96},{96,128},{128,160},{160,192},{192,224},{224... | collective-permute-start | bytes 786440 | tf_op jit(solution)/shard_map/ppermute | solution.py:20
  71.7 11.2 %collective-permute-start.16 = (bf16[2,512,128]{2,1,0:T(8,128)(2,1)S(1)}, bf16[2,512,128]{2,1,0:T(8,128)(2,1)}, u32[]{:S(2)}, u32[]{:S(2)}) collective-permute-start(bf16[2,512,128]{2,1,0:T(8,128)(2,1)S(1)} %collective-permute-done.15.refs_10_.refs_15_), channel_id=1, source_target_pairs={{0,224},{32,0},{64,32},{96,64},{128,96},{160,128},{192,160},{224,1... | collective-permute-start | bytes 786440 | tf_op jit(solution)/shard_map/ppermute | solution.py:20
  75.4 66.4 %all-to-all-start = ((bf16[16,256,256]{2,1,0:T(8,128)(2,1)}), bf16[16,256,256]{2,1,0:T(8,128)(2,1)S(1)}, u32[]{:S(2)}, u32[]{:S(2)}) async-start(bf16[16,256,256]{2,1,0:T(8,128)(2,1)} %order.1), calls=%async_computation | async-start | bytes 4194304 | tf_op jit(solution)/shard_map/all_to_all | solution.py:369
  81.5 10.7 %collective-permute-start.22 = (bf16[2,512,128]{2,1,0:T(8,128)(2,1)S(1)}, bf16[2,512,128]{2,1,0:T(8,128)(2,1)S(1)}, u32[]{:S(2)}, u32[]{:S(2)}) collective-permute-start(bf16[2,512,128]{2,1,0:T(8,128)(2,1)S(1)} %collective-permute-done.21.refs_9_.refs_14_), channel_id=1, source_target_pairs={{0,32},{32,64},{64,96},{96,128},{128,160},{160,192},{192,224},{224... | collective-permute-start | bytes 786440 | tf_op jit(solution)/shard_map/ppermute | solution.py:20
  82.8 14.7 %collective-permute-start.13 = (bf16[2,512,128]{2,1,0:T(8,128)(2,1)}, bf16[2,512,128]{2,1,0:T(8,128)(2,1)S(1)}, u32[]{:S(2)}, u32[]{:S(2)}) collective-permute-start(bf16[2,512,128]{2,1,0:T(8,128)(2,1)} %collective-permute-done.12.refs_6_.refs_8_), channel_id=1, source_target_pairs={{0,32},{32,64},{64,96},{96,128},{128,160},{160,192},{192,224},{224... | collective-permute-start | bytes 786440 | tf_op jit(solution)/shard_map/ppermute | solution.py:20
  82.9 14.6 %collective-permute-start.17 = (bf16[2,512,128]{2,1,0:T(8,128)(2,1)}, bf16[2,512,128]{2,1,0:T(8,128)(2,1)S(1)}, u32[]{:S(2)}, u32[]{:S(2)}) collective-permute-start(bf16[2,512,128]{2,1,0:T(8,128)(2,1)} %collective-permute-done.16.refs_12_.refs_17_), channel_id=1, source_target_pairs={{0,224},{32,0},{64,32},{96,64},{128,96},{160,128},{192,160},{224,1... | collective-permute-start | bytes 786440 | tf_op jit(solution)/shard_map/ppermute | solution.py:20
  89.9 11.7 %collective-permute-start.23 = (bf16[2,512,128]{2,1,0:T(8,128)(2,1)S(1)}, bf16[2,512,128]{2,1,0:T(8,128)(2,1)S(1)}, u32[]{:S(2)}, u32[]{:S(2)}) collective-permute-start(bf16[2,512,128]{2,1,0:T(8,128)(2,1)S(1)} %collective-permute-done.20.refs_7_.refs_9_), channel_id=1, source_target_pairs={{0,224},{32,0},{64,32},{96,64},{128,96},{160,128},{192,160},{224,1... | collective-permute-start | bytes 786440 | tf_op jit(solution)/shard_map/ppermute | solution.py:20
  92.1 10.8 %collective-permute-start.25 = (bf16[2,512,128]{2,1,0:T(8,128)(2,1)S(1)}, bf16[2,512,128]{2,1,0:T(8,128)(2,1)S(1)}, u32[]{:S(2)}, u32[]{:S(2)}) collective-permute-start(bf16[2,512,128]{2,1,0:T(8,128)(2,1)S(1)} %collective-permute-done.22.refs_11_.refs_16_), channel_id=1, source_target_pairs={{0,32},{32,64},{64,96},{96,128},{128,160},{160,192},{192,224},{224... | collective-permute-start | bytes 786440 | tf_op jit(solution)/shard_map/ppermute | solution.py:20
  119.7 16.6 %collective-permute-start.28 = (bf16[256,256]{1,0:T(8,128)(2,1)S(1)}, bf16[256,256]{1,0:T(8,128)(2,1)S(1)}, u32[]{:S(2)}, u32[]{:S(2)}) collective-permute-start(bf16[256,256]{1,0:T(8,128)(2,1)S(1)} %get-tuple-element.67), channel_id=1, source_target_pairs={{0,4},{4,8},{8,12},{12,0},{1,5},{5,9},{9,13},{13,1},{2,6},{6,10},{... | collective-permute-start | bytes 393224 | tf_op jit(solution)/shard_map/ppermute | solution.py:20
  120.2 16.1 %collective-permute-start.29 = (bf16[256,256]{1,0:T(8,128)(2,1)S(1)}, bf16[256,256]{1,0:T(8,128)(2,1)S(1)}, u32[]{:S(2)}, u32[]{:S(2)}) collective-permute-start(bf16[256,256]{1,0:T(8,128)(2,1)S(1)} %get-tuple-element.67), channel_id=1, source_target_pairs={{0,12},{4,0},{8,4},{12,8},{1,13},{5,1},{9,5},{13,9},{2,14},{6,2},{... | collective-permute-start | bytes 393224 | tf_op jit(solution)/shard_map/ppermute | solution.py:20
  121.8 14.5 %collective-permute-start.30 = (bf16[256,256]{1,0:T(8,128)(2,1)S(1)}, bf16[256,256]{1,0:T(8,128)(2,1)S(1)}, u32[]{:S(2)}, u32[]{:S(2)}) collective-permute-start(bf16[256,256]{1,0:T(8,128)(2,1)S(1)} %get-tuple-element.67), channel_id=1, source_target_pairs={{0,8},{4,12},{8,0},{12,4},{1,9},{5,13},{9,1},{13,5},{2,10},{6,14},... | collective-permute-start | bytes 393224 | tf_op jit(solution)/shard_map/ppermute | solution.py:20
  136.4 13.4 %collective-permute-start.33 = (bf16[1024,256]{1,0:T(8,128)(2,1)S(1)}, bf16[1024,256]{1,0:T(8,128)(2,1)}, u32[]{:S(2)}, u32[]{:S(2)}) collective-permute-start(bf16[1024,256]{1,0:T(8,128)(2,1)S(1)} %pad_maximum_fusion.1), channel_id=1, source_target_pairs={{0,1},{1,2},{2,3},{3,0},{4,5},{5,6},{6,7},{7,4},{8,9},{9,10},{10,1... | collective-permute-start | bytes 1572872 | tf_op jit(solution)/shard_map/ppermute | solution.py:20
  138.4 11.3 %collective-permute-start.34 = (bf16[1024,256]{1,0:T(8,128)(2,1)S(1)}, bf16[1024,256]{1,0:T(8,128)(2,1)}, u32[]{:S(2)}, u32[]{:S(2)}) collective-permute-start(bf16[1024,256]{1,0:T(8,128)(2,1)S(1)} %pad_maximum_fusion.1), channel_id=1, source_target_pairs={{0,3},{1,0},{2,1},{3,2},{4,7},{5,4},{6,5},{7,6},{8,11},{9,8},{10,9... | collective-permute-start | bytes 1572872 | tf_op jit(solution)/shard_map/ppermute | solution.py:20
  139.7 11.5 %collective-permute-start.31 = (bf16[1024,256]{1,0:T(8,128)(2,1)S(1)}, bf16[1024,256]{1,0:T(8,128)(2,1)}, u32[]{:S(2)}, u32[]{:S(2)}) collective-permute-start(bf16[1024,256]{1,0:T(8,128)(2,1)S(1)} %all_gather.7), channel_id=1, source_target_pairs={{0,4},{4,8},{8,12},{12,0},{1,5},{5,9},{9,13},{13,1},{2,6},{6,10},{... | collective-permute-start | bytes 1572872 | tf_op jit(solution)/shard_map/ppermute | solution.py:20
  141.8 12.5 %collective-permute-start.32 = (bf16[1024,256]{1,0:T(8,128)(2,1)S(1)}, bf16[1024,256]{1,0:T(8,128)(2,1)}, u32[]{:S(2)}, u32[]{:S(2)}) collective-permute-start(bf16[1024,256]{1,0:T(8,128)(2,1)S(1)} %all_gather.7), channel_id=1, source_target_pairs={{0,12},{4,0},{8,4},{12,8},{1,13},{5,1},{9,5},{13,9},{2,14},{6,2},{... | collective-permute-start | bytes 1572872 | tf_op jit(solution)/shard_map/ppermute | solution.py:20
  155.2 13.1 %collective-permute-start.35 = (bf16[512,256]{1,0:T(8,128)(2,1)S(1)}, bf16[512,256]{1,0:T(8,128)(2,1)S(1)}, u32[]{:S(2)}, u32[]{:S(2)}) collective-permute-start(bf16[512,256]{1,0:T(8,128)(2,1)S(1)} %slice.54), channel_id=1, source_target_pairs={{0,4},{4,8},{8,12},{12,0},{1,5},{5,9},{9,13},{13,1},{2,6},{6,10},{... | collective-permute-start | bytes 786440 | tf_op jit(solution)/shard_map/ppermute | solution.py:20
  156.6 11.8 %collective-permute-start.36 = (bf16[512,256]{1,0:T(8,128)(2,1)S(1)}, bf16[512,256]{1,0:T(8,128)(2,1)S(1)}, u32[]{:S(2)}, u32[]{:S(2)}) collective-permute-start(bf16[512,256]{1,0:T(8,128)(2,1)S(1)} %slice.55), channel_id=1, source_target_pairs={{0,12},{4,0},{8,4},{12,8},{1,13},{5,1},{9,5},{13,9},{2,14},{6,2},{... | collective-permute-start | bytes 786440 | tf_op jit(solution)/shard_map/ppermute | solution.py:20
  (40 other events, 238.5 us)

commit v5 on v4

--- a/solution.py
+++ b/solution.py
@@ -27,7 +27,7 @@
 def plane_matmul(a, w, finish, out_shape, name, more=(), extra=()):
     n = a.shape[0] // 2
     others = around4(a[n:], "y")
-    by_x = lax.all_gather(a[:n], "x", axis=0, tiled=True)
+    by_x = lax.all_to_all(jnp.concatenate([a[:n]] * NXY, axis=0), "x", 0, 0, tiled=True)
     by_x, others = lax.optimization_barrier((by_x, others))
     near = [by_x, jnp.concatenate([a[n:], *others], axis=0)]
     far = [(shift(stack, second, 1), shift(stack, second, -1)) for stack, second in zip(near, "yx")]
@@ -70,9 +70,10 @@
             w_ref.at[:, pl.ds(row, 256)], w_buf.at[part, :, pl.ds(j * 256, 256)], w_sem.at[part, j]
         )
 
+    for copy in x_copies:
+        copy.start()
     if has_sums:
         sums_copy = pltpu.make_async_copy(sums_ref, acc, s_sem)
-        sums_copy.start()
     for half in range(2):
         for k, step in enumerate(steps):
             for j in range(NXY):
@@ -81,11 +82,8 @@
                 else:
                     owner = lax.rem(y + OFFS[j] + NXY, NXY) * NXY + lax.rem(x + OFFS[step] + NXY, NXY)
                 w_copy(half * n_steps + k, j, owner).start()
-        for copy, owner_half in zip(x_copies, [h for h in range(2) for _ in counts[h]]):
-            if owner_half == half:
-                copy.start()
-    if has_sums:
-        sums_copy.wait()
+        if has_sums and half == 0:
+            sums_copy.start()
     for copy in x_copies:
         copy.wait()
 
@@ -95,6 +93,12 @@
             w_copy(part, j, 0).wait()
         rows = jnp.concatenate([x_buf[half, NXY * k + j] for j in range(NXY)], axis=1)
         span = pl.ds(pl.multiple_of(half * n, n), n)
+        if has_sums:
+
+            @pl.when(part == 0)
+            def _():
+                sums_copy.wait()
+
         for g in range(groups):
             value = jnp.dot(rows, w_buf[part, g], preferred_element_type=jnp.float32)
             if has_sums:
@@ -346,6 +350,7 @@
             pltpu.SemaphoreType.DMA((18,)),
         ],
         compiler_params=PARAMS,
+        cost_estimate=pl.CostEstimate(flops=14000000000, transcendentals=0, bytes_accessed=28000000),
         name="attend",
     )(rand, glob, radius, mine, theirs, *own, *other, started)
 
@@ -376,9 +381,10 @@
     own.append(shift(own[5], "z", 1))
     other.append(shift(other[6], "z", -1))
     att = attend(rand, glob_blocks, window_radius, mine, theirs, own, other, started)
+    att, w_cols = lax.optimization_barrier((att, w_cols))
     attended = jnp.concatenate([att[0], swap(att[1])], axis=1)
     out = jax.ShapeDtypeStruct((512, 256), bf16)
-    return plane_matmul(attended, w_cols[None], round_out, out, "output", (), w_cols)[0]
+    return plane_matmul(attended, w_cols[None], round_out, out, "output")[0]
 
 
 def solution(mesh):

time: 174 us -> 168 us (0.966)
  blocking collectives: 26 us -> 0 us
  waiting for transfers between devices: 27.8 us -> 39 us
  starting transfers between devices: 60.7 us -> 67.1 us
  Pallas kernels: 42.5 us -> 48.6 us
  local copies, waits for them, and re-layouts: 14.3 us -> 9.34 us
    all_gather x2 -> x0, blocking collectives: 26 us -> none  [plane_matmul(): by_x = lax.all_gather(a[:n], 'x', axis=0, tiled=True)]
    ppermute x36, waiting for transfers between devices: 27.2 us -> 38.3 us  [shift(): return lax.ppermute(a, axis, [(i, (i + step) % n) for i in range(n)])]
    all_to_all x0 -> x2, starting transfers between devices: none -> 8.54 us  [plane_matmul(): lax.all_to_all(jnp.concatenate([a[:n]] * NXY, axis=0), 'x', 0, 0, tiled=T...]
    pallas_call x1, Pallas kernels: 1.49 us -> 5.98 us  [dense(): pl.pallas_call(dense_kernel, out_shape=jax.ShapeDtypeStruct((3, 2 * BLK,...]
    ppermute x36, starting transfers between devices: 55.5 us -> 53.3 us  [shift(): return lax.ppermute(a, axis, [(i, (i + step) % n) for i in range(n)])]
    slice x4, local copies, waits for them, and re-layouts: 3.41 us -> 1.49 us  [plane_matmul(): high[2 * n:]]
    slice x4, local copies, waits for them, and re-layouts: 2.71 us -> 0.8 us  [plane_matmul(): low[:2 * n]]
    unnamed x66 -> x74, local copies, waits for them, and re-layouts: 6.27 us -> 5.12 us
  transfers between devices with their start and end apart: 40 -> 42, of which waited for: 11 -> 18; matrix products, arithmetic and copies ran while one was open for 4% -> 3% of each run, Pallas kernels for 20% -> 24%
where the time goes in v5:
time: 168 us; the launch traced here: 167 us
  starting transfers between devices  67.1 us (40%)
  Pallas kernels  48.6 us (29%)
  waiting for transfers between devices  39 us (23%)
  local copies, waits for them, and re-layouts  9.34 us (6%)
  other arithmetic  2.41 us (1%)
    ppermute x36, starting transfers between devices, shift(): return lax.ppermute(a, axis, [(i, (i + step) % n) for i in range(n)])  53.3 us
    ppermute x36, waiting for transfers between devices, shift(): return lax.ppermute(a, axis, [(i, (i + step) % n) for i in range(n)])  38.3 us
    pallas_call x6, Pallas kernels, partial_matmul(): pl.pallas_call(lambda *refs: partial_kernel(steps, counts, n, groups, has...  28.6 us
    pallas_call x1, Pallas kernels, attend(): pl.pallas_call(attend_kernel, out_shape=(jax.ShapeDtypeStruct((512, DH),...  10.9 us
    all_to_all x2, starting transfers between devices, plane_matmul(): lax.all_to_all(jnp.concatenate([a[:n]] * NXY, axis=0), 'x', 0, 0, tiled=T...  8.54 us
    pallas_call x1, Pallas kernels, dense(): pl.pallas_call(dense_kernel, out_shape=jax.ShapeDtypeStruct((3, 2 * BLK,...  5.98 us
    unnamed x74, local copies, waits for them, and re-layouts  5.12 us
    all_to_all x1, starting transfers between devices, body(): w_cols = lax.all_to_all(ordered, ('y', 'x'), 0, 0, tiled=True)  5.07 us
  transfers between devices with their start and end apart: 42, of which 18 were waited for; matrix products, arithmetic and copies ran while one was open for 3% of the time, Pallas kernels for 24%

profile of v5, /device:TPU:24, one launch (start us, length us, event | category | flops | bytes accessed | tf_op | source)
XLA Modules:
  0.0 167.2 jit_solution(2978886238826391109)
XLA Ops:
  1.8 4.3 %all-to-all-start = ((bf16[4,256,256]{2,1,0:T(8,128)(2,1)}), bf16[4,256,256]{2,1,0:T(8,128)(2,1)S(1)}, u32[]{:S(2)}, u32[]{:S(2)}) async-start(bf16[4,256,256]{2,1,0:T(8,128)(2,1)} %bitcast), calls=%async_computation | async-start | bytes 1048576 | tf_op jit(solution)/shard_map/all_to_all | solution.py:30
  9.4 2.8 %collective-permute-done = bf16[256,256]{1,0:T(8,128)(2,1)S(1)} collective-permute-done((bf16[256,256]{1,0:T(8,128)(2,1)S(1)}, bf16[256,256]{1,0:T(8,128)(2,1)S(1)}, u32[]{:S(2)}, u32[]{:S(2)}) %collective-permute-start) | collective-permute-done | bytes 131104 | tf_op jit(solution)/shard_map/ppermute | solution.py:20
  12.2 3.7 %collective-permute-done.1 = bf16[256,256]{1,0:T(8,128)(2,1)S(1)} collective-permute-done((bf16[256,256]{1,0:T(8,128)(2,1)S(1)}, bf16[256,256]{1,0:T(8,128)(2,1)S(1)}, u32[]{:S(2)}, u32[]{:S(2)}) %collective-permute-start.1) | collective-permute-done | bytes 131104 | tf_op jit(solution)/shard_map/ppermute | solution.py:20
  16.0 1.9 %collective-permute-start.5 = (bf16[1024,256]{1,0:T(8,128)(2,1)S(1)}, bf16[1024,256]{1,0:T(8,128)(2,1)S(1)}, u32[]{:S(2)}, u32[]{:S(2)}) collective-permute-start(bf16[1024,256]{1,0:T(8,128)(2,1)S(1)} %pad_maximum_fusion.1), channel_id=1, source_target_pairs={{0,1},{1,2},{2,3},{3,0},{4,5},{5,6},{6,7},{7,4},{8,9},{9,10},{10,1... | collective-permute-start | bytes 1572872 | tf_op jit(solution)/shard_map/ppermute | solution.py:20
  21.3 3.2 %order.1 = bf16[16,256,256]{2,1,0:T(8,128)(2,1)} custom-call(bf16[256,4096]{1,0:T(8,128)(2,1)} %w_ref.1), custom_call_target="tpu_custom_call" | custom-call | tf_op jit(solution)/shard_map/order/pallas_call | solution.py:185
  24.5 4.5 %project0.1.refs_5_ = f32[3,512,256]{2,1,0:T(8,128)} custom-call(bf16[4,256,256]{2,1,0:T(8,128)(2,1)} %copy-done.1, bf16[4,256,256]{2,1,0:T(8,128)(2,1)} %bitcast.42, bf16[3,4096,256]{2,1,0:T(8,128)(2,1)} %bitcast.32), custom_call_target="tpu_custom_call" | custom-call | tf_op jit(solution)/shard_map/project0/pallas_call | solution.py:132
  30.9 2.0 %collective-permute-done.4 = bf16[1024,256]{1,0:T(8,128)(2,1)S(1)} collective-permute-done((bf16[1024,256]{1,0:T(8,128)(2,1)S(1)}, bf16[1024,256]{1,0:T(8,128)(2,1)S(1)}, u32[]{:S(2)}, u32[]{:S(2)}) %collective-permute-start.4) | collective-permute-done | bytes 524320 | tf_op jit(solution)/shard_map/ppermute | solution.py:20
  37.7 2.8 %collective-permute-start.10 = (bf16[512,256]{1,0:T(8,128)(2,1)}, bf16[512,256]{1,0:T(8,128)(2,1)S(1)}, u32[]{:S(2)}, u32[]{:S(2)}) collective-permute-start(bf16[512,256]{1,0:T(8,128)(2,1)} %slice.49), channel_id=1, source_target_pairs={{0,3},{1,0},{2,1},{3,2},{4,7},{5,4},{6,5},{7,6},{8,11},{9,8},{10,9... | collective-permute-start | bytes 786440 | tf_op jit(solution)/shard_map/ppermute | solution.py:20
  41.3 7.6 %project1.1.refs_5_ = f32[3,512,256]{2,1,0:T(8,128)} custom-call(bf16[4,256,256]{2,1,0:T(8,128)(2,1)} %bitcast.46, bf16[4,256,256]{2,1,0:T(8,128)(2,1)} %bitcast.47, bf16[4,256,256]{2,1,0:T(8,128)(2,1)} %bitcast.44, bf16[4,256,256]{2,1,0:T(8,128)(2,1)} %bitcast.45, bf16[3,4096,256]{2,1,0:T(8,128)(2,1)} %bitcast.33, f32[3,512,256]{2,1,0:T(8,128)} %project0.1.refs_5_), custom_call_target="tpu_custom_call" | custom-call | tf_op jit(solution)/shard_map/project1/pallas_call | solution.py:132
  49.9 5.5 %project3.1 = (bf16[512,128]{1,0:T(8,128)(2,1)}, bf16[2,512,128]{2,1,0:T(8,128)(2,1)}, bf16[528,128]{1,0:T(8,128)(2,1)}, bf16[2,512,128]{2,1,0:T(8,128)(2,1)}) custom-call(bf16[2,256,256]{2,1,0:T(8,128)(2,1)} %bitcast.52, bf16[2,256,256]{2,1,0:T(8,128)(2,1)} %bitcast.53, bf16[2,256,256]{2,1,0:T(8,128)(2,1)} %bitcast.54, bf16[2,256,256]{2,1,0:T(8,128)(2,1)} %bitcast.55, ...), custom_call_target="tpu_custom_call" | custom-call | tf_op jit(solution)/shard_map/project3/pallas_call | solution.py:132
  55.5 2.4 %collective-permute-start.11 = (bf16[2,512,128]{2,1,0:T(8,128)(2,1)}, bf16[2,512,128]{2,1,0:T(8,128)(2,1)S(1)}, u32[]{:S(2)}, u32[]{:S(2)}) collective-permute-start(bf16[2,512,128]{2,1,0:T(8,128)(2,1)} %get-tuple-element.48.refs_3_.refs_5_), channel_id=1, source_target_pairs={{0,32},{32,64},{64,96},{96,128},{128,160},{160,192},{192,224},{224... | collective-permute-start | bytes 786440 | tf_op jit(solution)/shard_map/ppermute | solution.py:20
  57.9 5.6 %collective-permute-start.15 = (bf16[2,512,128]{2,1,0:T(8,128)(2,1)S(1)}, bf16[2,512,128]{2,1,0:T(8,128)(2,1)S(1)}, u32[]{:S(2)}, u32[]{:S(2)}) collective-permute-start(bf16[2,512,128]{2,1,0:T(8,128)(2,1)S(1)} %collective-permute-done.14.refs_8_.refs_13_), channel_id=1, source_target_pairs={{0,224},{32,0},{64,32},{96,64},{128,96},{160,128},{192,160},{224,1... | collective-permute-start | bytes 786440 | tf_op jit(solution)/shard_map/ppermute | solution.py:20
  65.5 3.7 %collective-permute-done.11.refs_4_.refs_6_ = bf16[2,512,128]{2,1,0:T(8,128)(2,1)S(1)} collective-permute-done((bf16[2,512,128]{2,1,0:T(8,128)(2,1)}, bf16[2,512,128]{2,1,0:T(8,128)(2,1)S(1)}, u32[]{:S(2)}, u32[]{:S(2)}) %collective-permute-start.11) | collective-permute-done | bytes 262176 | tf_op jit(solution)/shard_map/ppermute | solution.py:20
  70.2 3.7 %collective-permute-start.16 = (bf16[2,512,128]{2,1,0:T(8,128)(2,1)S(1)}, bf16[2,512,128]{2,1,0:T(8,128)(2,1)}, u32[]{:S(2)}, u32[]{:S(2)}) collective-permute-start(bf16[2,512,128]{2,1,0:T(8,128)(2,1)S(1)} %collective-permute-done.15.refs_10_.refs_15_), channel_id=1, source_target_pairs={{0,224},{32,0},{64,32},{96,64},{128,96},{160,128},{192,160},{224,1... | collective-permute-start | bytes 786440 | tf_op jit(solution)/shard_map/ppermute | solution.py:20
  73.9 5.1 %all-to-all-start.1 = ((bf16[16,256,256]{2,1,0:T(8,128)(2,1)}), bf16[16,256,256]{2,1,0:T(8,128)(2,1)S(1)}, u32[]{:S(2)}, u32[]{:S(2)}) async-start(bf16[16,256,256]{2,1,0:T(8,128)(2,1)} %order.1), calls=%async_computation.1 | async-start | bytes 4194304 | tf_op jit(solution)/shard_map/all_to_all | solution.py:374
  81.4 3.7 %collective-permute-start.17 = (bf16[2,512,128]{2,1,0:T(8,128)(2,1)}, bf16[2,512,128]{2,1,0:T(8,128)(2,1)S(1)}, u32[]{:S(2)}, u32[]{:S(2)}) collective-permute-start(bf16[2,512,128]{2,1,0:T(8,128)(2,1)} %collective-permute-done.16.refs_12_.refs_17_), channel_id=1, source_target_pairs={{0,224},{32,0},{64,32},{96,64},{128,96},{160,128},{192,160},{224,1... | collective-permute-start | bytes 786440 | tf_op jit(solution)/shard_map/ppermute | solution.py:20
  85.7 2.7 %collective-permute-done.20.refs_7_.refs_9_ = bf16[2,512,128]{2,1,0:T(8,128)(2,1)S(1)} collective-permute-done((bf16[2,512,128]{2,1,0:T(8,128)(2,1)S(1)}, bf16[2,512,128]{2,1,0:T(8,128)(2,1)S(1)}, u32[]{:S(2)}, u32[]{:S(2)}) %collective-permute-start.20) | collective-permute-done | bytes 262176 | tf_op jit(solution)/shard_map/ppermute | solution.py:20
  88.4 2.2 %collective-permute-start.23 = (bf16[2,512,128]{2,1,0:T(8,128)(2,1)S(1)}, bf16[2,512,128]{2,1,0:T(8,128)(2,1)S(1)}, u32[]{:S(2)}, u32[]{:S(2)}) collective-permute-start(bf16[2,512,128]{2,1,0:T(8,128)(2,1)S(1)} %collective-permute-done.20.refs_7_.refs_9_), channel_id=1, source_target_pairs={{0,224},{32,0},{64,32},{96,64},{128,96},{160,128},{192,160},{224,1... | collective-permute-start | bytes 786440 | tf_op jit(solution)/shard_map/ppermute | solution.py:20
  91.3 6.0 %dense.1.refs_21_ = f32[3,128,128]{2,1,0:T(8,128)} custom-call(s32[2]{0:T(128)} %refs_1_.1, bf16[512,128]{1,0:T(8,128)(2,1)} %get-tuple-element.50.refs_1_.refs_3_, bf16[528,128]{1,0:T(8,128)(2,1)} %copy-done.28, bf16[2,512,128]{2,1,0:T(8,128)(2,1)} %get-tuple-element.48.refs_3_.refs_5_, bf16[2,512,128]{2,1,0:T(8,128)(2,1)} %copy-done.14, ...), custom_call_target="tpu_custom_call" | custom-call | tf_op jit(solution)/shard_map/dense/pallas_call | solution.py:325
  97.4 3.2 %collective-permute-start.26 = (bf16[2,512,128]{2,1,0:T(8,128)(2,1)S(1)}, bf16[2,512,128]{2,1,0:T(8,128)(2,1)S(1)}, u32[]{:S(2)}, u32[]{:S(2)}) collective-permute-start(bf16[2,512,128]{2,1,0:T(8,128)(2,1)S(1)} %collective-permute-done.17.refs_19_), channel_id=1, source_target_pairs={{0,224},{32,0},{64,32},{96,64},{128,96},{160,128},{192,160},{224,1... | collective-permute-start | bytes 786440 | tf_op jit(solution)/shard_map/ppermute | solution.py:20
  100.7 5.1 %collective-permute-done.24.refs_12_ = bf16[2,512,128]{2,1,0:T(8,128)(2,1)S(1)} collective-permute-done((bf16[2,512,128]{2,1,0:T(8,128)(2,1)S(1)}, bf16[2,512,128]{2,1,0:T(8,128)(2,1)S(1)}, u32[]{:S(2)}, u32[]{:S(2)}) %collective-permute-start.24) | collective-permute-done | bytes 262176 | tf_op jit(solution)/shard_map/ppermute | solution.py:20
  107.3 10.9 %attend.1 = (bf16[512,128]{1,0:T(8,128)(2,1)}, bf16[512,128]{1,0:T(8,128)(2,1)}) custom-call(s32[96]{0:T(128)} %pad_add_fusion.refs_0_, s32[2]{0:T(128)} %refs_1_.1, s32[2]{0:T(128)} %refs_2_.1, bf16[512,128]{1,0:T(8,128)(2,1)} %get-tuple-element.50.refs_1_.refs_3_, bf16[528,128]{1,0:T(8,128)(2,1)} %copy-done.28, ...), custom_call_target="tpu_custom_call" | custom-call | flops 14000000000 | bytes 28000000 | tf_op jit(solution)/shard_map/attend/pallas_call | solution.py:342
  120.7 4.2 %all-to-all-start.2 = ((bf16[4,256,256]{2,1,0:T(8,128)(2,1)}), bf16[4,256,256]{2,1,0:T(8,128)(2,1)S(1)}, u32[]{:S(2)}, u32[]{:S(2)}) async-start(bf16[4,256,256]{2,1,0:T(8,128)(2,1)} %bitcast.17), calls=%async_computation.2 | async-start | bytes 1048576 | tf_op jit(solution)/shard_map/all_to_all | solution.py:30
  128.4 2.7 %collective-permute-done.28 = bf16[256,256]{1,0:T(8,128)(2,1)S(1)} collective-permute-done((bf16[256,256]{1,0:T(8,128)(2,1)S(1)}, bf16[256,256]{1,0:T(8,128)(2,1)S(1)}, u32[]{:S(2)}, u32[]{:S(2)}) %collective-permute-start.28) | collective-permute-done | bytes 131104 | tf_op jit(solution)/shard_map/ppermute | solution.py:20
  131.1 3.4 %collective-permute-done.29 = bf16[256,256]{1,0:T(8,128)(2,1)S(1)} collective-permute-done((bf16[256,256]{1,0:T(8,128)(2,1)S(1)}, bf16[256,256]{1,0:T(8,128)(2,1)S(1)}, u32[]{:S(2)}, u32[]{:S(2)}) %collective-permute-start.29) | collective-permute-done | bytes 131104 | tf_op jit(solution)/shard_map/ppermute | solution.py:20
  140.1 3.1 %output0.1.refs_5_ = f32[1,512,256]{2,1,0:T(8,128)} custom-call(bf16[4,256,256]{2,1,0:T(8,128)(2,1)} %copy-done.2, bf16[4,256,256]{2,1,0:T(8,128)(2,1)} %bitcast.43, bf16[1,4096,256]{2,1,0:T(8,128)(2,1)} %bitcast.35), custom_call_target="tpu_custom_call" | custom-call | tf_op jit(solution)/shard_map/output0/pallas_call | solution.py:132
  143.2 5.7 %collective-permute-done.33 = bf16[1024,256]{1,0:T(8,128)(2,1)S(1)} collective-permute-done((bf16[1024,256]{1,0:T(8,128)(2,1)S(1)}, bf16[1024,256]{1,0:T(8,128)(2,1)S(1)}, u32[]{:S(2)}, u32[]{:S(2)}) %collective-permute-start.33) | collective-permute-done | bytes 524320 | tf_op jit(solution)/shard_map/ppermute | solution.py:20
  150.4 2.1 %collective-permute-done.32 = bf16[1024,256]{1,0:T(8,128)(2,1)S(1)} collective-permute-done((bf16[1024,256]{1,0:T(8,128)(2,1)S(1)}, bf16[1024,256]{1,0:T(8,128)(2,1)S(1)}, u32[]{:S(2)}, u32[]{:S(2)}) %collective-permute-start.32) | collective-permute-done | bytes 524320 | tf_op jit(solution)/shard_map/ppermute | solution.py:20
  152.9 1.8 %collective-permute-start.36 = (bf16[512,256]{1,0:T(8,128)(2,1)S(1)}, bf16[512,256]{1,0:T(8,128)(2,1)S(1)}, u32[]{:S(2)}, u32[]{:S(2)}) collective-permute-start(bf16[512,256]{1,0:T(8,128)(2,1)S(1)} %slice.55), channel_id=1, source_target_pairs={{0,12},{4,0},{8,4},{12,8},{1,13},{5,1},{9,5},{13,9},{2,14},{6,2},{... | collective-permute-start | bytes 786440 | tf_op jit(solution)/shard_map/ppermute | solution.py:20
  155.1 3.1 %collective-permute-start.38 = (bf16[512,256]{1,0:T(8,128)(2,1)S(1)}, bf16[512,256]{1,0:T(8,128)(2,1)S(1)}, u32[]{:S(2)}, u32[]{:S(2)}) collective-permute-start(bf16[512,256]{1,0:T(8,128)(2,1)S(1)} %slice.57), channel_id=1, source_target_pairs={{0,3},{1,0},{2,1},{3,2},{4,7},{5,4},{6,5},{7,6},{8,11},{9,8},{10,9... | collective-permute-start | bytes 786440 | tf_op jit(solution)/shard_map/ppermute | solution.py:20
  158.2 4.7 %output1.1.refs_5_ = f32[1,512,256]{2,1,0:T(8,128)} custom-call(bf16[4,256,256]{2,1,0:T(8,128)(2,1)} %bitcast.50, bf16[4,256,256]{2,1,0:T(8,128)(2,1)} %bitcast.51, bf16[4,256,256]{2,1,0:T(8,128)(2,1)} %bitcast.48, bf16[4,256,256]{2,1,0:T(8,128)(2,1)} %bitcast.49, bf16[1,4096,256]{2,1,0:T(8,128)(2,1)} %bitcast.36, f32[1,512,256]{2,1,0:T(8,128)} %output0.1.refs_5_), custom_call_target="tpu_custom_call" | custom-call | tf_op jit(solution)/shard_map/output1/pallas_call | solution.py:132
  163.9 3.2 %output3.1 = bf16[512,256]{1,0:T(8,128)(2,1)} custom-call(bf16[2,256,256]{2,1,0:T(8,128)(2,1)} %bitcast.56, bf16[2,256,256]{2,1,0:T(8,128)(2,1)} %bitcast.57, bf16[2,256,256]{2,1,0:T(8,128)(2,1)} %bitcast.58, bf16[2,256,256]{2,1,0:T(8,128)(2,1)} %bitcast.59, bf16[1,4096,256]{2,1,0:T(8,128)(2,1)} %bitcast.37, f32[1,512,256]{2,1,0:T(8,128)} %output1.1.refs_5_), custom_call_target="tpu_custom_call" | custom-call | tf_op jit(solution)/shard_map/output3/pallas_call | solution.py:132
  (158 shorter events, 40.1 us)
Async XLA Ops:
  1.8 14.1 %all-to-all-start = ((bf16[4,256,256]{2,1,0:T(8,128)(2,1)}), bf16[4,256,256]{2,1,0:T(8,128)(2,1)S(1)}, u32[]{:S(2)}, u32[]{:S(2)}) async-start(bf16[4,256,256]{2,1,0:T(8,128)(2,1)} %bitcast), calls=%async_computation | async-start | bytes 1048576 | tf_op jit(solution)/shard_map/all_to_all | solution.py:30
  7.4 8.5 %collective-permute-start.1 = (bf16[256,256]{1,0:T(8,128)(2,1)S(1)}, bf16[256,256]{1,0:T(8,128)(2,1)S(1)}, u32[]{:S(2)}, u32[]{:S(2)}) collective-permute-start(bf16[256,256]{1,0:T(8,128)(2,1)S(1)} %get-tuple-element.75), channel_id=1, source_target_pairs={{0,12},{4,0},{8,4},{12,8},{1,13},{5,1},{9,5},{13,9},{2,14},{6,2},{... | collective-permute-start | bytes 393224 | tf_op jit(solution)/shard_map/ppermute | solution.py:20
  16.0 13.5 %collective-permute-start.5 = (bf16[1024,256]{1,0:T(8,128)(2,1)S(1)}, bf16[1024,256]{1,0:T(8,128)(2,1)S(1)}, u32[]{:S(2)}, u32[]{:S(2)}) collective-permute-start(bf16[1024,256]{1,0:T(8,128)(2,1)S(1)} %pad_maximum_fusion.1), channel_id=1, source_target_pairs={{0,1},{1,2},{2,3},{3,0},{4,5},{5,6},{6,7},{7,4},{8,9},{9,10},{10,1... | collective-permute-start | bytes 1572872 | tf_op jit(solution)/shard_map/ppermute | solution.py:20
  17.9 11.7 %collective-permute-start.6 = (bf16[1024,256]{1,0:T(8,128)(2,1)S(1)}, bf16[1024,256]{1,0:T(8,128)(2,1)S(1)}, u32[]{:S(2)}, u32[]{:S(2)}) collective-permute-start(bf16[1024,256]{1,0:T(8,128)(2,1)S(1)} %pad_maximum_fusion.1), channel_id=1, source_target_pairs={{0,3},{1,0},{2,1},{3,2},{4,7},{5,4},{6,5},{7,6},{8,11},{9,8},{10,9... | collective-permute-start | bytes 1572872 | tf_op jit(solution)/shard_map/ppermute | solution.py:20
  19.3 11.6 %collective-permute-start.3 = (bf16[1024,256]{1,0:T(8,128)(2,1)S(1)}, bf16[1024,256]{1,0:T(8,128)(2,1)S(1)}, u32[]{:S(2)}, u32[]{:S(2)}) collective-permute-start(bf16[1024,256]{1,0:T(8,128)(2,1)S(1)} %bitcast.38), channel_id=1, source_target_pairs={{0,4},{4,8},{8,12},{12,0},{1,5},{5,9},{9,13},{13,1},{2,6},{6,10},{... | collective-permute-start | bytes 1572872 | tf_op jit(solution)/shard_map/ppermute | solution.py:20
  20.4 12.5 %collective-permute-start.4 = (bf16[1024,256]{1,0:T(8,128)(2,1)S(1)}, bf16[1024,256]{1,0:T(8,128)(2,1)S(1)}, u32[]{:S(2)}, u32[]{:S(2)}) collective-permute-start(bf16[1024,256]{1,0:T(8,128)(2,1)S(1)} %bitcast.39), channel_id=1, source_target_pairs={{0,12},{4,0},{8,4},{12,8},{1,13},{5,1},{9,5},{13,9},{2,14},{6,2},{... | collective-permute-start | bytes 1572872 | tf_op jit(solution)/shard_map/ppermute | solution.py:20
  33.0 16.0 %collective-permute-start.7 = (bf16[512,256]{1,0:T(8,128)(2,1)S(1)}, bf16[512,256]{1,0:T(8,128)(2,1)S(1)}, u32[]{:S(2)}, u32[]{:S(2)}) collective-permute-start(bf16[512,256]{1,0:T(8,128)(2,1)S(1)} %slice.46), channel_id=1, source_target_pairs={{0,4},{4,8},{8,12},{12,0},{1,5},{5,9},{9,13},{13,1},{2,6},{6,10},{... | collective-permute-start | bytes 786440 | tf_op jit(solution)/shard_map/ppermute | solution.py:20
  34.1 14.9 %collective-permute-start.8 = (bf16[512,256]{1,0:T(8,128)(2,1)}, bf16[512,256]{1,0:T(8,128)(2,1)S(1)}, u32[]{:S(2)}, u32[]{:S(2)}) collective-permute-start(bf16[512,256]{1,0:T(8,128)(2,1)} %slice.47), channel_id=1, source_target_pairs={{0,12},{4,0},{8,4},{12,8},{1,13},{5,1},{9,5},{13,9},{2,14},{6,2},{... | collective-permute-start | bytes 786440 | tf_op jit(solution)/shard_map/ppermute | solution.py:20
  36.5 12.4 %collective-permute-start.9 = (bf16[512,256]{1,0:T(8,128)(2,1)}, bf16[512,256]{1,0:T(8,128)(2,1)S(1)}, u32[]{:S(2)}, u32[]{:S(2)}) collective-permute-start(bf16[512,256]{1,0:T(8,128)(2,1)} %slice.48), channel_id=1, source_target_pairs={{0,1},{1,2},{2,3},{3,0},{4,5},{5,6},{6,7},{7,4},{8,9},{9,10},{10,1... | collective-permute-start | bytes 786440 | tf_op jit(solution)/shard_map/ppermute | solution.py:20
  37.7 11.3 %collective-permute-start.10 = (bf16[512,256]{1,0:T(8,128)(2,1)}, bf16[512,256]{1,0:T(8,128)(2,1)S(1)}, u32[]{:S(2)}, u32[]{:S(2)}) collective-permute-start(bf16[512,256]{1,0:T(8,128)(2,1)} %slice.49), channel_id=1, source_target_pairs={{0,3},{1,0},{2,1},{3,2},{4,7},{5,4},{6,5},{7,6},{8,11},{9,8},{10,9... | collective-permute-start | bytes 786440 | tf_op jit(solution)/shard_map/ppermute | solution.py:20
  55.5 13.7 %collective-permute-start.11 = (bf16[2,512,128]{2,1,0:T(8,128)(2,1)}, bf16[2,512,128]{2,1,0:T(8,128)(2,1)S(1)}, u32[]{:S(2)}, u32[]{:S(2)}) collective-permute-start(bf16[2,512,128]{2,1,0:T(8,128)(2,1)} %get-tuple-element.48.refs_3_.refs_5_), channel_id=1, source_target_pairs={{0,32},{32,64},{64,96},{96,128},{128,160},{160,192},{192,224},{224... | collective-permute-start | bytes 786440 | tf_op jit(solution)/shard_map/ppermute | solution.py:20
  57.9 12.3 %collective-permute-start.15 = (bf16[2,512,128]{2,1,0:T(8,128)(2,1)S(1)}, bf16[2,512,128]{2,1,0:T(8,128)(2,1)S(1)}, u32[]{:S(2)}, u32[]{:S(2)}) collective-permute-start(bf16[2,512,128]{2,1,0:T(8,128)(2,1)S(1)} %collective-permute-done.14.refs_8_.refs_13_), channel_id=1, source_target_pairs={{0,224},{32,0},{64,32},{96,64},{128,96},{160,128},{192,160},{224,1... | collective-permute-start | bytes 786440 | tf_op jit(solution)/shard_map/ppermute | solution.py:20
  63.5 15.7 %collective-permute-start.19 = (bf16[2,512,128]{2,1,0:T(8,128)(2,1)}, bf16[2,512,128]{2,1,0:T(8,128)(2,1)S(1)}, u32[]{:S(2)}, u32[]{:S(2)}) collective-permute-start(bf16[2,512,128]{2,1,0:T(8,128)(2,1)} %get-tuple-element.48.refs_3_.refs_5_), channel_id=1, source_target_pairs={{0,224},{32,0},{64,32},{96,64},{128,96},{160,128},{192,160},{224,1... | collective-permute-start | bytes 786440 | tf_op jit(solution)/shard_map/ppermute | solution.py:20
  64.5 15.4 %collective-permute-start.21 = (bf16[2,512,128]{2,1,0:T(8,128)(2,1)S(1)}, bf16[2,512,128]{2,1,0:T(8,128)(2,1)S(1)}, u32[]{:S(2)}, u32[]{:S(2)}) collective-permute-start(bf16[2,512,128]{2,1,0:T(8,128)(2,1)S(1)} %collective-permute-done.14.refs_8_.refs_13_), channel_id=1, source_target_pairs={{0,32},{32,64},{64,96},{96,128},{128,160},{160,192},{192,224},{224... | collective-permute-start | bytes 786440 | tf_op jit(solution)/shard_map/ppermute | solution.py:20
  69.2 12.1 %collective-permute-start.12 = (bf16[2,512,128]{2,1,0:T(8,128)(2,1)S(1)}, bf16[2,512,128]{2,1,0:T(8,128)(2,1)}, u32[]{:S(2)}, u32[]{:S(2)}) collective-permute-start(bf16[2,512,128]{2,1,0:T(8,128)(2,1)S(1)} %collective-permute-done.11.refs_4_.refs_6_), channel_id=1, source_target_pairs={{0,32},{32,64},{64,96},{96,128},{128,160},{160,192},{192,224},{224... | collective-permute-start | bytes 786440 | tf_op jit(solution)/shard_map/ppermute | solution.py:20
  70.2 11.2 %collective-permute-start.16 = (bf16[2,512,128]{2,1,0:T(8,128)(2,1)S(1)}, bf16[2,512,128]{2,1,0:T(8,128)(2,1)}, u32[]{:S(2)}, u32[]{:S(2)}) collective-permute-start(bf16[2,512,128]{2,1,0:T(8,128)(2,1)S(1)} %collective-permute-done.15.refs_10_.refs_15_), channel_id=1, source_target_pairs={{0,224},{32,0},{64,32},{96,64},{128,96},{160,128},{192,160},{224,1... | collective-permute-start | bytes 786440 | tf_op jit(solution)/shard_map/ppermute | solution.py:20
  73.9 44.3 %all-to-all-start.1 = ((bf16[16,256,256]{2,1,0:T(8,128)(2,1)}), bf16[16,256,256]{2,1,0:T(8,128)(2,1)S(1)}, u32[]{:S(2)}, u32[]{:S(2)}) async-start(bf16[16,256,256]{2,1,0:T(8,128)(2,1)} %order.1), calls=%async_computation.1 | async-start | bytes 4194304 | tf_op jit(solution)/shard_map/all_to_all | solution.py:374
  79.2 9.2 %collective-permute-start.20 = (bf16[2,512,128]{2,1,0:T(8,128)(2,1)S(1)}, bf16[2,512,128]{2,1,0:T(8,128)(2,1)S(1)}, u32[]{:S(2)}, u32[]{:S(2)}) collective-permute-start(bf16[2,512,128]{2,1,0:T(8,128)(2,1)S(1)} %collective-permute-done.19.refs_5_.refs_7_), channel_id=1, source_target_pairs={{0,224},{32,0},{64,32},{96,64},{128,96},{160,128},{192,160},{224,1... | collective-permute-start | bytes 786440 | tf_op jit(solution)/shard_map/ppermute | solution.py:20
  79.9 10.6 %collective-permute-start.22 = (bf16[2,512,128]{2,1,0:T(8,128)(2,1)S(1)}, bf16[2,512,128]{2,1,0:T(8,128)(2,1)S(1)}, u32[]{:S(2)}, u32[]{:S(2)}) collective-permute-start(bf16[2,512,128]{2,1,0:T(8,128)(2,1)S(1)} %collective-permute-done.21.refs_9_.refs_14_), channel_id=1, source_target_pairs={{0,32},{32,64},{64,96},{96,128},{128,160},{160,192},{192,224},{224... | collective-permute-start | bytes 786440 | tf_op jit(solution)/shard_map/ppermute | solution.py:20
  81.3 16.0 %collective-permute-start.13 = (bf16[2,512,128]{2,1,0:T(8,128)(2,1)}, bf16[2,512,128]{2,1,0:T(8,128)(2,1)S(1)}, u32[]{:S(2)}, u32[]{:S(2)}) collective-permute-start(bf16[2,512,128]{2,1,0:T(8,128)(2,1)} %collective-permute-done.12.refs_6_.refs_8_), channel_id=1, source_target_pairs={{0,32},{32,64},{64,96},{96,128},{128,160},{160,192},{192,224},{224... | collective-permute-start | bytes 786440 | tf_op jit(solution)/shard_map/ppermute | solution.py:20
  81.4 15.9 %collective-permute-start.17 = (bf16[2,512,128]{2,1,0:T(8,128)(2,1)}, bf16[2,512,128]{2,1,0:T(8,128)(2,1)S(1)}, u32[]{:S(2)}, u32[]{:S(2)}) collective-permute-start(bf16[2,512,128]{2,1,0:T(8,128)(2,1)} %collective-permute-done.16.refs_12_.refs_17_), channel_id=1, source_target_pairs={{0,224},{32,0},{64,32},{96,64},{128,96},{160,128},{192,160},{224,1... | collective-permute-start | bytes 786440 | tf_op jit(solution)/shard_map/ppermute | solution.py:20
  88.4 12.2 %collective-permute-start.23 = (bf16[2,512,128]{2,1,0:T(8,128)(2,1)S(1)}, bf16[2,512,128]{2,1,0:T(8,128)(2,1)S(1)}, u32[]{:S(2)}, u32[]{:S(2)}) collective-permute-start(bf16[2,512,128]{2,1,0:T(8,128)(2,1)S(1)} %collective-permute-done.20.refs_7_.refs_9_), channel_id=1, source_target_pairs={{0,224},{32,0},{64,32},{96,64},{128,96},{160,128},{192,160},{224,1... | collective-permute-start | bytes 786440 | tf_op jit(solution)/shard_map/ppermute | solution.py:20
  90.6 10.1 %collective-permute-start.25 = (bf16[2,512,128]{2,1,0:T(8,128)(2,1)S(1)}, bf16[2,512,128]{2,1,0:T(8,128)(2,1)S(1)}, u32[]{:S(2)}, u32[]{:S(2)}) collective-permute-start(bf16[2,512,128]{2,1,0:T(8,128)(2,1)S(1)} %collective-permute-done.22.refs_11_.refs_16_), channel_id=1, source_target_pairs={{0,32},{32,64},{64,96},{96,128},{128,160},{160,192},{192,224},{224... | collective-permute-start | bytes 786440 | tf_op jit(solution)/shard_map/ppermute | solution.py:20
  97.3 8.6 %collective-permute-start.24 = (bf16[2,512,128]{2,1,0:T(8,128)(2,1)S(1)}, bf16[2,512,128]{2,1,0:T(8,128)(2,1)S(1)}, u32[]{:S(2)}, u32[]{:S(2)}) collective-permute-start(bf16[2,512,128]{2,1,0:T(8,128)(2,1)S(1)} %collective-permute-done.13.refs_10_), channel_id=1, source_target_pairs={{0,32},{32,64},{64,96},{96,128},{128,160},{160,192},{192,224},{224... | collective-permute-start | bytes 786440 | tf_op jit(solution)/shard_map/ppermute | solution.py:20
  120.7 14.0 %all-to-all-start.2 = ((bf16[4,256,256]{2,1,0:T(8,128)(2,1)}), bf16[4,256,256]{2,1,0:T(8,128)(2,1)S(1)}, u32[]{:S(2)}, u32[]{:S(2)}) async-start(bf16[4,256,256]{2,1,0:T(8,128)(2,1)} %bitcast.17), calls=%async_computation.2 | async-start | bytes 1048576 | tf_op jit(solution)/shard_map/all_to_all | solution.py:30
  125.4 9.0 %collective-permute-start.29 = (bf16[256,256]{1,0:T(8,128)(2,1)S(1)}, bf16[256,256]{1,0:T(8,128)(2,1)S(1)}, u32[]{:S(2)}, u32[]{:S(2)}) collective-permute-start(bf16[256,256]{1,0:T(8,128)(2,1)S(1)} %get-tuple-element.73), channel_id=1, source_target_pairs={{0,12},{4,0},{8,4},{12,8},{1,13},{5,1},{9,5},{13,9},{2,14},{6,2},{... | collective-permute-start | bytes 393224 | tf_op jit(solution)/shard_map/ppermute | solution.py:20
  134.8 14.1 %collective-permute-start.33 = (bf16[1024,256]{1,0:T(8,128)(2,1)S(1)}, bf16[1024,256]{1,0:T(8,128)(2,1)S(1)}, u32[]{:S(2)}, u32[]{:S(2)}) collective-permute-start(bf16[1024,256]{1,0:T(8,128)(2,1)S(1)} %pad_maximum_fusion.3), channel_id=1, source_target_pairs={{0,1},{1,2},{2,3},{3,0},{4,5},{5,6},{6,7},{7,4},{8,9},{9,10},{10,1... | collective-permute-start | bytes 1572872 | tf_op jit(solution)/shard_map/ppermute | solution.py:20
  136.5 12.4 %collective-permute-start.34 = (bf16[1024,256]{1,0:T(8,128)(2,1)S(1)}, bf16[1024,256]{1,0:T(8,128)(2,1)S(1)}, u32[]{:S(2)}, u32[]{:S(2)}) collective-permute-start(bf16[1024,256]{1,0:T(8,128)(2,1)S(1)} %pad_maximum_fusion.3), channel_id=1, source_target_pairs={{0,3},{1,0},{2,1},{3,2},{4,7},{5,4},{6,5},{7,6},{8,11},{9,8},{10,9... | collective-permute-start | bytes 1572872 | tf_op jit(solution)/shard_map/ppermute | solution.py:20
  138.1 12.3 %collective-permute-start.31 = (bf16[1024,256]{1,0:T(8,128)(2,1)S(1)}, bf16[1024,256]{1,0:T(8,128)(2,1)S(1)}, u32[]{:S(2)}, u32[]{:S(2)}) collective-permute-start(bf16[1024,256]{1,0:T(8,128)(2,1)S(1)} %bitcast.40), channel_id=1, source_target_pairs={{0,4},{4,8},{8,12},{12,0},{1,5},{5,9},{9,13},{13,1},{2,6},{6,10},{... | collective-permute-start | bytes 1572872 | tf_op jit(solution)/shard_map/ppermute | solution.py:20
  139.1 13.4 %collective-permute-start.32 = (bf16[1024,256]{1,0:T(8,128)(2,1)S(1)}, bf16[1024,256]{1,0:T(8,128)(2,1)S(1)}, u32[]{:S(2)}, u32[]{:S(2)}) collective-permute-start(bf16[1024,256]{1,0:T(8,128)(2,1)S(1)} %bitcast.41), channel_id=1, source_target_pairs={{0,12},{4,0},{8,4},{12,8},{1,13},{5,1},{9,5},{13,9},{2,14},{6,2},{... | collective-permute-start | bytes 1572872 | tf_op jit(solution)/shard_map/ppermute | solution.py:20
  152.5 10.4 %collective-permute-start.35 = (bf16[512,256]{1,0:T(8,128)(2,1)S(1)}, bf16[512,256]{1,0:T(8,128)(2,1)S(1)}, u32[]{:S(2)}, u32[]{:S(2)}) collective-permute-start(bf16[512,256]{1,0:T(8,128)(2,1)S(1)} %slice.54), channel_id=1, source_target_pairs={{0,4},{4,8},{8,12},{12,0},{1,5},{5,9},{9,13},{13,1},{2,6},{6,10},{... | collective-permute-start | bytes 786440 | tf_op jit(solution)/shard_map/ppermute | solution.py:20
  152.9 10.0 %collective-permute-start.36 = (bf16[512,256]{1,0:T(8,128)(2,1)S(1)}, bf16[512,256]{1,0:T(8,128)(2,1)S(1)}, u32[]{:S(2)}, u32[]{:S(2)}) collective-permute-start(bf16[512,256]{1,0:T(8,128)(2,1)S(1)} %slice.55), channel_id=1, source_target_pairs={{0,12},{4,0},{8,4},{12,8},{1,13},{5,1},{9,5},{13,9},{2,14},{6,2},{... | collective-permute-start | bytes 786440 | tf_op jit(solution)/shard_map/ppermute | solution.py:20
  (46 other events, 293.3 us)

commit v6 on v5

--- a/solution.py
+++ b/solution.py
@@ -24,7 +24,7 @@
     return [shift(a, axis, 1), shift(a, axis, -1), shift(a, axis, 2)]
 
 
-def plane_matmul(a, w, finish, out_shape, name, more=(), extra=()):
+def plane_matmul(a, w, finish, out_shape, name, more=(), extra=(), halves=True):
     n = a.shape[0] // 2
     others = around4(a[n:], "y")
     by_x = lax.all_to_all(jnp.concatenate([a[:n]] * NXY, axis=0), "x", 0, 0, tiled=True)
@@ -39,7 +39,10 @@
     far, sums, extra = lax.optimization_barrier((far, sums, extra))
     last = []
     for (low, high), second in zip(far, "yx"):
-        last.append((shift(low[: 2 * n], second, 1), shift(high[2 * n :], second, -1)))
+        if halves:
+            last.append((shift(low[: 2 * n], second, 1), shift(high[2 * n :], second, -1)))
+        else:
+            last.append((shift(low, second, 1),))
     sums = partial_matmul((1, 2), [[blocks(v) for v in f] for f in far], w, sums, name)
     out = partial_matmul((3,), [[blocks(v) for v in f] for f in last], w, sums, name, finish, out_shape, more)
     return out, extra
@@ -206,7 +209,7 @@
     rand_ref, glob_ref, radius_ref, mine_ref, theirs_ref = refs[:5]
     rings, dense_ref = (refs[5:13], refs[13:21]), refs[21]
     o_refs = refs[22:24]
-    kv_buf, q_buf, sem = refs[24:]
+    kv_buf, q_buf, o_buf, sem = refs[24:]
     copies = [(mine_ref, q_buf.at[0]), (theirs_ref.at[pl.ds(0, 512)], q_buf.at[1])]
     for side, arrays in enumerate(rings):
         copies += [(array, kv_buf.at[slot, side]) for array, slot in zip(arrays, SLOTS)]
@@ -237,7 +240,7 @@
         places = [place(i) for i in ids]
         keys = jnp.concatenate([kv_buf[slot, owner, 0, pl.ds(row, BLK)] for slot, owner, row in places], axis=0)
         values = jnp.concatenate([kv_buf[slot, owner, 1, pl.ds(row, BLK)] for slot, owner, row in places], axis=0)
-        mine = pl.ds(pl.multiple_of(j * BLK, BLK), BLK)
+        mine = pl.ds(j * BLK, BLK)
         scores = lax.dot_general(q_buf[side, mine], keys, nt, preferred_element_type=jnp.float32) * scale
         low_off = jnp.where((radius >= 1) & (block > 0), -1, 0)
         high_off = jnp.where((radius >= 1) & (block < 127), -1, 2)
@@ -246,16 +249,14 @@
         probs = jnp.exp(scores - top)
         total = jnp.sum(probs, axis=1, keepdims=True)
         acc = jnp.dot(probs.astype(jnp.bfloat16), values, preferred_element_type=jnp.float32)
-        o_refs[side][mine] = (acc / total).astype(jnp.bfloat16)
-
-    for side in range(2):
-
-        def four_blocks(i, carry, side=side):
-            for u in range(4):
-                one_block(side, i * 4 + u)
-            return carry
-
-        lax.fori_loop(0, 2, four_blocks, 0)
+        o_buf[side, mine] = (acc / total).astype(jnp.bfloat16)
+
+    def eight_blocks(side, carry):
+        for j in range(8):
+            one_block(side, j)
+        return carry
+
+    lax.fori_loop(0, 2, eight_blocks, 0)
 
     glob, owned, rows_of = owned_globals(glob_ref)
 
@@ -267,11 +268,12 @@
         result = (acc / total).astype(jnp.bfloat16)
         for k, (side, row) in enumerate(rows_of):
 
-            for which in range(2):
-
-                @pl.when(owned[k] & (side == which))
-                def _(k=k, which=which, row=row):
-                    o_refs[which][pl.ds(row, BLK)] = result[k * BLK : (k + 1) * BLK]
+            @pl.when(owned[k])
+            def _(k=k, side=side, row=row):
+                o_buf[side, pl.ds(row, BLK)] = result[k * BLK : (k + 1) * BLK]
+
+    for side in range(2):
+        o_refs[side][...] = o_buf[side]
 
 
 def owned_globals(glob_ref):
@@ -347,6 +349,7 @@
         scratch_shapes=[
             pltpu.VMEM((NZ, 2, 2, 512, DH), bf16),
             pltpu.VMEM((2, 512, DH), bf16),
+            pltpu.VMEM((2, 512, DH), bf16),
             pltpu.SemaphoreType.DMA((18,)),
         ],
         compiler_params=PARAMS,
@@ -366,7 +369,7 @@
     heads = jax.ShapeDtypeStruct((2, 512, DH), bf16)
     shapes = (jax.ShapeDtypeStruct((512, DH), bf16), heads, jax.ShapeDtypeStruct((528, DH), bf16), heads)
     (mine, own, send_q, send_kv), ordered = plane_matmul(
-        tokens, w_qkv.transpose(1, 0, 2), split_heads, shapes, "project", (ids,), order(w_out)
+        tokens, w_qkv.transpose(1, 0, 2), split_heads, shapes, "project", (ids,), order(w_out), False
     )
     own = z_ring(own)
     other = swap(send_kv)

time: 168 us -> 163 us (0.970)
  waiting for transfers between devices: 39 us -> 45.9 us
  Pallas kernels: 48.6 us -> 41.8 us
  starting transfers between devices: 67.1 us -> 63.8 us
  local copies, waits for them, and re-layouts: 9.34 us -> 6.99 us
    ppermute x36 -> x34, waiting for transfers between devices: 38.3 us -> 45.2 us  [shift(): return lax.ppermute(a, axis, [(i, (i + step) % n) for i in range(n)])]
    pallas_call x1, Pallas kernels: 5.98 us -> 1.49 us  [dense(): pl.pallas_call(dense_kernel, out_shape=jax.ShapeDtypeStruct((3, 2 * BLK,...]
    ppermute x36 -> x34, starting transfers between devices: 53.3 us -> 49.7 us  [shift(): return lax.ppermute(a, axis, [(i, (i + step) % n) for i in range(n)])]
    pallas_call x1, Pallas kernels: 10.9 us -> 8.52 us  [attend(): pl.pallas_call(attend_kernel, out_shape=(jax.ShapeDtypeStruct((512, DH),...]
    unnamed x74 -> x70, local copies, waits for them, and re-layouts: 5.12 us -> 4.98 us
  transfers between devices with their start and end apart: 42 -> 40, of which waited for: 18 -> 21; matrix products, arithmetic and copies ran while one was open for 3% -> 2% of each run, Pallas kernels for 24% -> 21%
where the time goes in v6:
time: 163 us; the launch traced here: 161 us
  starting transfers between devices  63.8 us (39%)
  waiting for transfers between devices  45.9 us (28%)
  Pallas kernels  41.8 us (26%)
  local copies, waits for them, and re-layouts  6.99 us (4%)
  other arithmetic  2.36 us (1%)
    ppermute x34, starting transfers between devices, shift(): return lax.ppermute(a, axis, [(i, (i + step) % n) for i in range(n)])  49.7 us
    ppermute x34, waiting for transfers between devices, shift(): return lax.ppermute(a, axis, [(i, (i + step) % n) for i in range(n)])  45.2 us
    pallas_call x6, Pallas kernels, partial_matmul(): pl.pallas_call(lambda *refs: partial_kernel(steps, counts, n, groups, has...  28.6 us
    all_to_all x2, starting transfers between devices, plane_matmul(): lax.all_to_all(jnp.concatenate([a[:n]] * NXY, axis=0), 'x', 0, 0, tiled=T...  8.53 us
    pallas_call x1, Pallas kernels, attend(): pl.pallas_call(attend_kernel, out_shape=(jax.ShapeDtypeStruct((512, DH),...  8.52 us
    all_to_all x1, starting transfers between devices, body(): w_cols = lax.all_to_all(ordered, ('y', 'x'), 0, 0, tiled=True)  5.36 us
    unnamed x70, local copies, waits for them, and re-layouts  4.98 us
  transfers between devices with their start and end apart: 40, of which 21 were waited for; matrix products, arithmetic and copies ran while one was open for 2% of the time, Pallas kernels for 21%

profile of v6, /device:TPU:24, one launch (start us, length us, event | category | flops | bytes accessed | tf_op | source)
XLA Modules:
  0.0 161.4 jit_solution(10588979503906044672)
XLA Ops:
  1.8 4.3 %all-to-all-start = ((bf16[4,256,256]{2,1,0:T(8,128)(2,1)}), bf16[4,256,256]{2,1,0:T(8,128)(2,1)S(1)}, u32[]{:S(2)}, u32[]{:S(2)}) async-start(bf16[4,256,256]{2,1,0:T(8,128)(2,1)} %bitcast), calls=%async_computation | async-start | bytes 1048576 | tf_op jit(solution)/shard_map/all_to_all | solution.py:30
  9.4 2.8 %collective-permute-done = bf16[256,256]{1,0:T(8,128)(2,1)S(1)} collective-permute-done((bf16[256,256]{1,0:T(8,128)(2,1)S(1)}, bf16[256,256]{1,0:T(8,128)(2,1)S(1)}, u32[]{:S(2)}, u32[]{:S(2)}) %collective-permute-start) | collective-permute-done | bytes 131104 | tf_op jit(solution)/shard_map/ppermute | solution.py:20
  12.2 3.7 %collective-permute-done.1 = bf16[256,256]{1,0:T(8,128)(2,1)S(1)} collective-permute-done((bf16[256,256]{1,0:T(8,128)(2,1)S(1)}, bf16[256,256]{1,0:T(8,128)(2,1)S(1)}, u32[]{:S(2)}, u32[]{:S(2)}) %collective-permute-start.1) | collective-permute-done | bytes 131104 | tf_op jit(solution)/shard_map/ppermute | solution.py:20
  16.0 1.9 %collective-permute-start.5 = (bf16[1024,256]{1,0:T(8,128)(2,1)S(1)}, bf16[1024,256]{1,0:T(8,128)(2,1)S(1)}, u32[]{:S(2)}, u32[]{:S(2)}) collective-permute-start(bf16[1024,256]{1,0:T(8,128)(2,1)S(1)} %pad_maximum_fusion.1), channel_id=1, source_target_pairs={{0,1},{1,2},{2,3},{3,0},{4,5},{5,6},{6,7},{7,4},{8,9},{9,10},{10,1... | collective-permute-start | bytes 1572872 | tf_op jit(solution)/shard_map/ppermute | solution.py:20
  21.3 3.2 %order.1 = bf16[16,256,256]{2,1,0:T(8,128)(2,1)} custom-call(bf16[256,4096]{1,0:T(8,128)(2,1)} %w_ref.1), custom_call_target="tpu_custom_call" | custom-call | tf_op jit(solution)/shard_map/order/pallas_call | solution.py:188
  24.6 4.5 %project0.1.refs_5_ = f32[3,512,256]{2,1,0:T(8,128)} custom-call(bf16[4,256,256]{2,1,0:T(8,128)(2,1)} %copy-done.1, bf16[4,256,256]{2,1,0:T(8,128)(2,1)} %bitcast.40, bf16[3,4096,256]{2,1,0:T(8,128)(2,1)} %bitcast.30), custom_call_target="tpu_custom_call" | custom-call | tf_op jit(solution)/shard_map/project0/pallas_call | solution.py:135
  30.9 2.0 %collective-permute-done.4 = bf16[1024,256]{1,0:T(8,128)(2,1)S(1)} collective-permute-done((bf16[1024,256]{1,0:T(8,128)(2,1)S(1)}, bf16[1024,256]{1,0:T(8,128)(2,1)S(1)}, u32[]{:S(2)}, u32[]{:S(2)}) %collective-permute-start.4) | collective-permute-done | bytes 524320 | tf_op jit(solution)/shard_map/ppermute | solution.py:20
  34.6 7.6 %project1.1.refs_3_ = f32[3,512,256]{2,1,0:T(8,128)} custom-call(bf16[4,256,256]{2,1,0:T(8,128)(2,1)} %bitcast.48, bf16[4,256,256]{2,1,0:T(8,128)(2,1)} %bitcast.49, bf16[4,256,256]{2,1,0:T(8,128)(2,1)} %bitcast.46, bf16[4,256,256]{2,1,0:T(8,128)(2,1)} %bitcast.47, bf16[3,4096,256]{2,1,0:T(8,128)(2,1)} %bitcast.31, f32[3,512,256]{2,1,0:T(8,128)} %project0.1.refs_5_), custom_call_target="tpu_custom_call" | custom-call | tf_op jit(solution)/shard_map/project1/pallas_call | solution.py:135
  45.7 5.5 %project3.1 = (bf16[512,128]{1,0:T(8,128)(2,1)}, bf16[2,512,128]{2,1,0:T(8,128)(2,1)}, bf16[528,128]{1,0:T(8,128)(2,1)}, bf16[2,512,128]{2,1,0:T(8,128)(2,1)}) custom-call(bf16[4,256,256]{2,1,0:T(8,128)(2,1)} %bitcast.50, bf16[4,256,256]{2,1,0:T(8,128)(2,1)} %bitcast.51, bf16[3,4096,256]{2,1,0:T(8,128)(2,1)} %bitcast.32, f32[3,512,256]{2,1,0:T(8,128)} %project1.1.refs_3_, ...), custom_call_target="tpu_custom_call" | custom-call | tf_op jit(solution)/shard_map/project3/pallas_call | solution.py:135
  51.3 3.2 %collective-permute-start.9 = (bf16[2,512,128]{2,1,0:T(8,128)(2,1)}, bf16[2,512,128]{2,1,0:T(8,128)(2,1)S(1)}, u32[]{:S(2)}, u32[]{:S(2)}) collective-permute-start(bf16[2,512,128]{2,1,0:T(8,128)(2,1)} %get-tuple-element.48.refs_3_.refs_5_), channel_id=1, source_target_pairs={{0,32},{32,64},{64,96},{96,128},{128,160},{160,192},{192,224},{224... | collective-permute-start | bytes 786440 | tf_op jit(solution)/shard_map/ppermute | solution.py:20
  54.5 5.6 %collective-permute-start.13 = (bf16[2,512,128]{2,1,0:T(8,128)(2,1)S(1)}, bf16[2,512,128]{2,1,0:T(8,128)(2,1)S(1)}, u32[]{:S(2)}, u32[]{:S(2)}) collective-permute-start(bf16[2,512,128]{2,1,0:T(8,128)(2,1)S(1)} %collective-permute-done.12.refs_8_.refs_13_), channel_id=1, source_target_pairs={{0,224},{32,0},{64,32},{96,64},{128,96},{160,128},{192,160},{224,1... | collective-permute-start | bytes 786440 | tf_op jit(solution)/shard_map/ppermute | solution.py:20
  62.1 3.7 %collective-permute-done.9.refs_4_.refs_6_ = bf16[2,512,128]{2,1,0:T(8,128)(2,1)S(1)} collective-permute-done((bf16[2,512,128]{2,1,0:T(8,128)(2,1)}, bf16[2,512,128]{2,1,0:T(8,128)(2,1)S(1)}, u32[]{:S(2)}, u32[]{:S(2)}) %collective-permute-start.9) | collective-permute-done | bytes 262176 | tf_op jit(solution)/shard_map/ppermute | solution.py:20
  66.8 3.7 %collective-permute-start.14 = (bf16[2,512,128]{2,1,0:T(8,128)(2,1)S(1)}, bf16[2,512,128]{2,1,0:T(8,128)(2,1)}, u32[]{:S(2)}, u32[]{:S(2)}) collective-permute-start(bf16[2,512,128]{2,1,0:T(8,128)(2,1)S(1)} %collective-permute-done.13.refs_10_.refs_15_), channel_id=1, source_target_pairs={{0,224},{32,0},{64,32},{96,64},{128,96},{160,128},{192,160},{224,1... | collective-permute-start | bytes 786440 | tf_op jit(solution)/shard_map/ppermute | solution.py:20
  70.5 5.4 %all-to-all-start.1 = ((bf16[16,256,256]{2,1,0:T(8,128)(2,1)}), bf16[16,256,256]{2,1,0:T(8,128)(2,1)S(1)}, u32[]{:S(2)}, u32[]{:S(2)}) async-start(bf16[16,256,256]{2,1,0:T(8,128)(2,1)} %order.1), calls=%async_computation.1 | async-start | bytes 4194304 | tf_op jit(solution)/shard_map/all_to_all | solution.py:377
  78.3 3.4 %collective-permute-start.15 = (bf16[2,512,128]{2,1,0:T(8,128)(2,1)}, bf16[2,512,128]{2,1,0:T(8,128)(2,1)S(1)}, u32[]{:S(2)}, u32[]{:S(2)}) collective-permute-start(bf16[2,512,128]{2,1,0:T(8,128)(2,1)} %collective-permute-done.14.refs_12_.refs_17_), channel_id=1, source_target_pairs={{0,224},{32,0},{64,32},{96,64},{128,96},{160,128},{192,160},{224,1... | collective-permute-start | bytes 786440 | tf_op jit(solution)/shard_map/ppermute | solution.py:20
  82.2 3.1 %collective-permute-done.18.refs_7_.refs_9_ = bf16[2,512,128]{2,1,0:T(8,128)(2,1)S(1)} collective-permute-done((bf16[2,512,128]{2,1,0:T(8,128)(2,1)S(1)}, bf16[2,512,128]{2,1,0:T(8,128)(2,1)S(1)}, u32[]{:S(2)}, u32[]{:S(2)}) %collective-permute-start.18) | collective-permute-done | bytes 262176 | tf_op jit(solution)/shard_map/ppermute | solution.py:20
  85.3 1.9 %collective-permute-start.21 = (bf16[2,512,128]{2,1,0:T(8,128)(2,1)S(1)}, bf16[2,512,128]{2,1,0:T(8,128)(2,1)S(1)}, u32[]{:S(2)}, u32[]{:S(2)}) collective-permute-start(bf16[2,512,128]{2,1,0:T(8,128)(2,1)S(1)} %collective-permute-done.18.refs_7_.refs_9_), channel_id=1, source_target_pairs={{0,224},{32,0},{64,32},{96,64},{128,96},{160,128},{192,160},{224,1... | collective-permute-start | bytes 786440 | tf_op jit(solution)/shard_map/ppermute | solution.py:20
  89.5 3.4 %collective-permute-done.11.refs_10_ = bf16[2,512,128]{2,1,0:T(8,128)(2,1)S(1)} collective-permute-done((bf16[2,512,128]{2,1,0:T(8,128)(2,1)}, bf16[2,512,128]{2,1,0:T(8,128)(2,1)S(1)}, u32[]{:S(2)}, u32[]{:S(2)}) %collective-permute-start.11) | collective-permute-done | bytes 262176 | tf_op jit(solution)/shard_map/ppermute | solution.py:20
  93.1 3.6 %collective-permute-start.24 = (bf16[2,512,128]{2,1,0:T(8,128)(2,1)S(1)}, bf16[2,512,128]{2,1,0:T(8,128)(2,1)S(1)}, u32[]{:S(2)}, u32[]{:S(2)}) collective-permute-start(bf16[2,512,128]{2,1,0:T(8,128)(2,1)S(1)} %collective-permute-done.15.refs_19_), channel_id=1, source_target_pairs={{0,224},{32,0},{64,32},{96,64},{128,96},{160,128},{192,160},{224,1... | collective-permute-start | bytes 786440 | tf_op jit(solution)/shard_map/ppermute | solution.py:20
  98.1 4.4 %collective-permute-done.22.refs_12_ = bf16[2,512,128]{2,1,0:T(8,128)(2,1)S(1)} collective-permute-done((bf16[2,512,128]{2,1,0:T(8,128)(2,1)S(1)}, bf16[2,512,128]{2,1,0:T(8,128)(2,1)S(1)}, u32[]{:S(2)}, u32[]{:S(2)}) %collective-permute-start.22) | collective-permute-done | bytes 262176 | tf_op jit(solution)/shard_map/ppermute | solution.py:20
  103.9 8.5 %attend.1 = (bf16[512,128]{1,0:T(8,128)(2,1)}, bf16[512,128]{1,0:T(8,128)(2,1)}) custom-call(s32[96]{0:T(128)} %pad_add_fusion.refs_0_, s32[2]{0:T(128)} %refs_1_.1, s32[2]{0:T(128)} %refs_2_.1, bf16[512,128]{1,0:T(8,128)(2,1)} %get-tuple-element.50.refs_1_.refs_3_, bf16[528,128]{1,0:T(8,128)(2,1)} %copy-done.26, ...), custom_call_target="tpu_custom_call" | custom-call | flops 14000000000 | bytes 28000000 | tf_op jit(solution)/shard_map/attend/pallas_call | solution.py:344
  115.0 4.2 %all-to-all-start.2 = ((bf16[4,256,256]{2,1,0:T(8,128)(2,1)}), bf16[4,256,256]{2,1,0:T(8,128)(2,1)S(1)}, u32[]{:S(2)}, u32[]{:S(2)}) async-start(bf16[4,256,256]{2,1,0:T(8,128)(2,1)} %bitcast.15), calls=%async_computation.2 | async-start | bytes 1048576 | tf_op jit(solution)/shard_map/all_to_all | solution.py:30
  122.7 2.5 %collective-permute-done.26 = bf16[256,256]{1,0:T(8,128)(2,1)S(1)} collective-permute-done((bf16[256,256]{1,0:T(8,128)(2,1)S(1)}, bf16[256,256]{1,0:T(8,128)(2,1)S(1)}, u32[]{:S(2)}, u32[]{:S(2)}) %collective-permute-start.26) | collective-permute-done | bytes 131104 | tf_op jit(solution)/shard_map/ppermute | solution.py:20
  125.2 3.5 %collective-permute-done.27 = bf16[256,256]{1,0:T(8,128)(2,1)S(1)} collective-permute-done((bf16[256,256]{1,0:T(8,128)(2,1)S(1)}, bf16[256,256]{1,0:T(8,128)(2,1)S(1)}, u32[]{:S(2)}, u32[]{:S(2)}) %collective-permute-start.27) | collective-permute-done | bytes 131104 | tf_op jit(solution)/shard_map/ppermute | solution.py:20
  129.1 1.8 %collective-permute-start.31 = (bf16[1024,256]{1,0:T(8,128)(2,1)S(1)}, bf16[1024,256]{1,0:T(8,128)(2,1)S(1)}, u32[]{:S(2)}, u32[]{:S(2)}) collective-permute-start(bf16[1024,256]{1,0:T(8,128)(2,1)S(1)} %pad_maximum_fusion.3), channel_id=1, source_target_pairs={{0,1},{1,2},{2,3},{3,0},{4,5},{5,6},{6,7},{7,4},{8,9},{9,10},{10,1... | collective-permute-start | bytes 1572872 | tf_op jit(solution)/shard_map/ppermute | solution.py:20
  134.4 3.1 %output0.1.refs_5_ = f32[1,512,256]{2,1,0:T(8,128)} custom-call(bf16[4,256,256]{2,1,0:T(8,128)(2,1)} %copy-done.2, bf16[4,256,256]{2,1,0:T(8,128)(2,1)} %bitcast.41, bf16[1,4096,256]{2,1,0:T(8,128)(2,1)} %bitcast.33), custom_call_target="tpu_custom_call" | custom-call | tf_op jit(solution)/shard_map/output0/pallas_call | solution.py:135
  137.5 5.6 %collective-permute-done.31 = bf16[1024,256]{1,0:T(8,128)(2,1)S(1)} collective-permute-done((bf16[1024,256]{1,0:T(8,128)(2,1)S(1)}, bf16[1024,256]{1,0:T(8,128)(2,1)S(1)}, u32[]{:S(2)}, u32[]{:S(2)}) %collective-permute-start.31) | collective-permute-done | bytes 524320 | tf_op jit(solution)/shard_map/ppermute | solution.py:20
  144.7 2.0 %collective-permute-done.30 = bf16[1024,256]{1,0:T(8,128)(2,1)S(1)} collective-permute-done((bf16[1024,256]{1,0:T(8,128)(2,1)S(1)}, bf16[1024,256]{1,0:T(8,128)(2,1)S(1)}, u32[]{:S(2)}, u32[]{:S(2)}) %collective-permute-start.30) | collective-permute-done | bytes 524320 | tf_op jit(solution)/shard_map/ppermute | solution.py:20
  147.1 1.8 %collective-permute-start.34 = (bf16[512,256]{1,0:T(8,128)(2,1)S(1)}, bf16[512,256]{1,0:T(8,128)(2,1)S(1)}, u32[]{:S(2)}, u32[]{:S(2)}) collective-permute-start(bf16[512,256]{1,0:T(8,128)(2,1)S(1)} %slice.39), channel_id=1, source_target_pairs={{0,12},{4,0},{8,4},{12,8},{1,13},{5,1},{9,5},{13,9},{2,14},{6,2},{... | collective-permute-start | bytes 786440 | tf_op jit(solution)/shard_map/ppermute | solution.py:20
  149.3 3.1 %collective-permute-start.36 = (bf16[512,256]{1,0:T(8,128)(2,1)S(1)}, bf16[512,256]{1,0:T(8,128)(2,1)S(1)}, u32[]{:S(2)}, u32[]{:S(2)}) collective-permute-start(bf16[512,256]{1,0:T(8,128)(2,1)S(1)} %slice.41), channel_id=1, source_target_pairs={{0,3},{1,0},{2,1},{3,2},{4,7},{5,4},{6,5},{7,6},{8,11},{9,8},{10,9... | collective-permute-start | bytes 786440 | tf_op jit(solution)/shard_map/ppermute | solution.py:20
  152.4 4.7 %output1.1.refs_5_ = f32[1,512,256]{2,1,0:T(8,128)} custom-call(bf16[4,256,256]{2,1,0:T(8,128)(2,1)} %bitcast.44, bf16[4,256,256]{2,1,0:T(8,128)(2,1)} %bitcast.45, bf16[4,256,256]{2,1,0:T(8,128)(2,1)} %bitcast.42, bf16[4,256,256]{2,1,0:T(8,128)(2,1)} %bitcast.43, bf16[1,4096,256]{2,1,0:T(8,128)(2,1)} %bitcast.34, f32[1,512,256]{2,1,0:T(8,128)} %output0.1.refs_5_), custom_call_target="tpu_custom_call" | custom-call | tf_op jit(solution)/shard_map/output1/pallas_call | solution.py:135
  158.1 3.2 %output3.1 = bf16[512,256]{1,0:T(8,128)(2,1)} custom-call(bf16[2,256,256]{2,1,0:T(8,128)(2,1)} %bitcast.52, bf16[2,256,256]{2,1,0:T(8,128)(2,1)} %bitcast.53, bf16[2,256,256]{2,1,0:T(8,128)(2,1)} %bitcast.54, bf16[2,256,256]{2,1,0:T(8,128)(2,1)} %bitcast.55, bf16[1,4096,256]{2,1,0:T(8,128)(2,1)} %bitcast.35, f32[1,512,256]{2,1,0:T(8,128)} %output1.1.refs_5_), custom_call_target="tpu_custom_call" | custom-call | tf_op jit(solution)/shard_map/output3/pallas_call | solution.py:135
  (146 shorter events, 39.9 us)
Async XLA Ops:
  1.8 14.1 %all-to-all-start = ((bf16[4,256,256]{2,1,0:T(8,128)(2,1)}), bf16[4,256,256]{2,1,0:T(8,128)(2,1)S(1)}, u32[]{:S(2)}, u32[]{:S(2)}) async-start(bf16[4,256,256]{2,1,0:T(8,128)(2,1)} %bitcast), calls=%async_computation | async-start | bytes 1048576 | tf_op jit(solution)/shard_map/all_to_all | solution.py:30
  7.4 8.5 %collective-permute-start.1 = (bf16[256,256]{1,0:T(8,128)(2,1)S(1)}, bf16[256,256]{1,0:T(8,128)(2,1)S(1)}, u32[]{:S(2)}, u32[]{:S(2)}) collective-permute-start(bf16[256,256]{1,0:T(8,128)(2,1)S(1)} %get-tuple-element.75), channel_id=1, source_target_pairs={{0,12},{4,0},{8,4},{12,8},{1,13},{5,1},{9,5},{13,9},{2,14},{6,2},{... | collective-permute-start | bytes 393224 | tf_op jit(solution)/shard_map/ppermute | solution.py:20
  16.0 13.5 %collective-permute-start.5 = (bf16[1024,256]{1,0:T(8,128)(2,1)S(1)}, bf16[1024,256]{1,0:T(8,128)(2,1)S(1)}, u32[]{:S(2)}, u32[]{:S(2)}) collective-permute-start(bf16[1024,256]{1,0:T(8,128)(2,1)S(1)} %pad_maximum_fusion.1), channel_id=1, source_target_pairs={{0,1},{1,2},{2,3},{3,0},{4,5},{5,6},{6,7},{7,4},{8,9},{9,10},{10,1... | collective-permute-start | bytes 1572872 | tf_op jit(solution)/shard_map/ppermute | solution.py:20
  17.9 11.7 %collective-permute-start.6 = (bf16[1024,256]{1,0:T(8,128)(2,1)S(1)}, bf16[1024,256]{1,0:T(8,128)(2,1)S(1)}, u32[]{:S(2)}, u32[]{:S(2)}) collective-permute-start(bf16[1024,256]{1,0:T(8,128)(2,1)S(1)} %pad_maximum_fusion.1), channel_id=1, source_target_pairs={{0,3},{1,0},{2,1},{3,2},{4,7},{5,4},{6,5},{7,6},{8,11},{9,8},{10,9... | collective-permute-start | bytes 1572872 | tf_op jit(solution)/shard_map/ppermute | solution.py:20
  19.3 11.6 %collective-permute-start.3 = (bf16[1024,256]{1,0:T(8,128)(2,1)S(1)}, bf16[1024,256]{1,0:T(8,128)(2,1)S(1)}, u32[]{:S(2)}, u32[]{:S(2)}) collective-permute-start(bf16[1024,256]{1,0:T(8,128)(2,1)S(1)} %bitcast.36), channel_id=1, source_target_pairs={{0,4},{4,8},{8,12},{12,0},{1,5},{5,9},{9,13},{13,1},{2,6},{6,10},{... | collective-permute-start | bytes 1572872 | tf_op jit(solution)/shard_map/ppermute | solution.py:20
  20.4 12.5 %collective-permute-start.4 = (bf16[1024,256]{1,0:T(8,128)(2,1)S(1)}, bf16[1024,256]{1,0:T(8,128)(2,1)S(1)}, u32[]{:S(2)}, u32[]{:S(2)}) collective-permute-start(bf16[1024,256]{1,0:T(8,128)(2,1)S(1)} %bitcast.37), channel_id=1, source_target_pairs={{0,12},{4,0},{8,4},{12,8},{1,13},{5,1},{9,5},{13,9},{2,14},{6,2},{... | collective-permute-start | bytes 1572872 | tf_op jit(solution)/shard_map/ppermute | solution.py:20
  32.9 10.4 %collective-permute-start.7 = (bf16[1024,256]{1,0:T(8,128)(2,1)S(1)}, bf16[1024,256]{1,0:T(8,128)(2,1)S(1)}, u32[]{:S(2)}, u32[]{:S(2)}) collective-permute-start(bf16[1024,256]{1,0:T(8,128)(2,1)S(1)} %collective-permute-done.3), channel_id=1, source_target_pairs={{0,4},{4,8},{8,12},{12,0},{1,5},{5,9},{9,13},{13,1},{2,6},{6,10},{... | collective-permute-start | bytes 1572872 | tf_op jit(solution)/shard_map/ppermute | solution.py:20
  33.3 11.6 %collective-permute-start.8 = (bf16[1024,256]{1,0:T(8,128)(2,1)S(1)}, bf16[1024,256]{1,0:T(8,128)(2,1)S(1)}, u32[]{:S(2)}, u32[]{:S(2)}) collective-permute-start(bf16[1024,256]{1,0:T(8,128)(2,1)S(1)} %collective-permute-done.5), channel_id=1, source_target_pairs={{0,1},{1,2},{2,3},{3,0},{4,5},{5,6},{6,7},{7,4},{8,9},{9,10},{10,1... | collective-permute-start | bytes 1572872 | tf_op jit(solution)/shard_map/ppermute | solution.py:20
  51.3 14.5 %collective-permute-start.9 = (bf16[2,512,128]{2,1,0:T(8,128)(2,1)}, bf16[2,512,128]{2,1,0:T(8,128)(2,1)S(1)}, u32[]{:S(2)}, u32[]{:S(2)}) collective-permute-start(bf16[2,512,128]{2,1,0:T(8,128)(2,1)} %get-tuple-element.48.refs_3_.refs_5_), channel_id=1, source_target_pairs={{0,32},{32,64},{64,96},{96,128},{128,160},{160,192},{192,224},{224... | collective-permute-start | bytes 786440 | tf_op jit(solution)/shard_map/ppermute | solution.py:20
  54.5 12.3 %collective-permute-start.13 = (bf16[2,512,128]{2,1,0:T(8,128)(2,1)S(1)}, bf16[2,512,128]{2,1,0:T(8,128)(2,1)S(1)}, u32[]{:S(2)}, u32[]{:S(2)}) collective-permute-start(bf16[2,512,128]{2,1,0:T(8,128)(2,1)S(1)} %collective-permute-done.12.refs_8_.refs_13_), channel_id=1, source_target_pairs={{0,224},{32,0},{64,32},{96,64},{128,96},{160,128},{192,160},{224,1... | collective-permute-start | bytes 786440 | tf_op jit(solution)/shard_map/ppermute | solution.py:20
  60.1 16.0 %collective-permute-start.17 = (bf16[2,512,128]{2,1,0:T(8,128)(2,1)}, bf16[2,512,128]{2,1,0:T(8,128)(2,1)S(1)}, u32[]{:S(2)}, u32[]{:S(2)}) collective-permute-start(bf16[2,512,128]{2,1,0:T(8,128)(2,1)} %get-tuple-element.48.refs_3_.refs_5_), channel_id=1, source_target_pairs={{0,224},{32,0},{64,32},{96,64},{128,96},{160,128},{192,160},{224,1... | collective-permute-start | bytes 786440 | tf_op jit(solution)/shard_map/ppermute | solution.py:20
  61.1 15.7 %collective-permute-start.19 = (bf16[2,512,128]{2,1,0:T(8,128)(2,1)S(1)}, bf16[2,512,128]{2,1,0:T(8,128)(2,1)S(1)}, u32[]{:S(2)}, u32[]{:S(2)}) collective-permute-start(bf16[2,512,128]{2,1,0:T(8,128)(2,1)S(1)} %collective-permute-done.12.refs_8_.refs_13_), channel_id=1, source_target_pairs={{0,32},{32,64},{64,96},{96,128},{128,160},{160,192},{192,224},{224... | collective-permute-start | bytes 786440 | tf_op jit(solution)/shard_map/ppermute | solution.py:20
  65.8 12.4 %collective-permute-start.10 = (bf16[2,512,128]{2,1,0:T(8,128)(2,1)S(1)}, bf16[2,512,128]{2,1,0:T(8,128)(2,1)}, u32[]{:S(2)}, u32[]{:S(2)}) collective-permute-start(bf16[2,512,128]{2,1,0:T(8,128)(2,1)S(1)} %collective-permute-done.9.refs_4_.refs_6_), channel_id=1, source_target_pairs={{0,32},{32,64},{64,96},{96,128},{128,160},{160,192},{192,224},{224... | collective-permute-start | bytes 786440 | tf_op jit(solution)/shard_map/ppermute | solution.py:20
  66.8 11.5 %collective-permute-start.14 = (bf16[2,512,128]{2,1,0:T(8,128)(2,1)S(1)}, bf16[2,512,128]{2,1,0:T(8,128)(2,1)}, u32[]{:S(2)}, u32[]{:S(2)}) collective-permute-start(bf16[2,512,128]{2,1,0:T(8,128)(2,1)S(1)} %collective-permute-done.13.refs_10_.refs_15_), channel_id=1, source_target_pairs={{0,224},{32,0},{64,32},{96,64},{128,96},{160,128},{192,160},{224,1... | collective-permute-start | bytes 786440 | tf_op jit(solution)/shard_map/ppermute | solution.py:20
  70.5 42.0 %all-to-all-start.1 = ((bf16[16,256,256]{2,1,0:T(8,128)(2,1)}), bf16[16,256,256]{2,1,0:T(8,128)(2,1)S(1)}, u32[]{:S(2)}, u32[]{:S(2)}) async-start(bf16[16,256,256]{2,1,0:T(8,128)(2,1)} %order.1), calls=%async_computation.1 | async-start | bytes 4194304 | tf_op jit(solution)/shard_map/all_to_all | solution.py:377
  76.1 9.3 %collective-permute-start.18 = (bf16[2,512,128]{2,1,0:T(8,128)(2,1)S(1)}, bf16[2,512,128]{2,1,0:T(8,128)(2,1)S(1)}, u32[]{:S(2)}, u32[]{:S(2)}) collective-permute-start(bf16[2,512,128]{2,1,0:T(8,128)(2,1)S(1)} %collective-permute-done.17.refs_5_.refs_7_), channel_id=1, source_target_pairs={{0,224},{32,0},{64,32},{96,64},{128,96},{160,128},{192,160},{224,1... | collective-permute-start | bytes 786440 | tf_op jit(solution)/shard_map/ppermute | solution.py:20
  76.8 10.5 %collective-permute-start.20 = (bf16[2,512,128]{2,1,0:T(8,128)(2,1)S(1)}, bf16[2,512,128]{2,1,0:T(8,128)(2,1)S(1)}, u32[]{:S(2)}, u32[]{:S(2)}) collective-permute-start(bf16[2,512,128]{2,1,0:T(8,128)(2,1)S(1)} %collective-permute-done.19.refs_9_.refs_14_), channel_id=1, source_target_pairs={{0,32},{32,64},{64,96},{96,128},{128,160},{160,192},{192,224},{224... | collective-permute-start | bytes 786440 | tf_op jit(solution)/shard_map/ppermute | solution.py:20
  78.2 14.7 %collective-permute-start.11 = (bf16[2,512,128]{2,1,0:T(8,128)(2,1)}, bf16[2,512,128]{2,1,0:T(8,128)(2,1)S(1)}, u32[]{:S(2)}, u32[]{:S(2)}) collective-permute-start(bf16[2,512,128]{2,1,0:T(8,128)(2,1)} %collective-permute-done.10.refs_6_.refs_8_), channel_id=1, source_target_pairs={{0,32},{32,64},{64,96},{96,128},{128,160},{160,192},{192,224},{224... | collective-permute-start | bytes 786440 | tf_op jit(solution)/shard_map/ppermute | solution.py:20
  78.3 14.6 %collective-permute-start.15 = (bf16[2,512,128]{2,1,0:T(8,128)(2,1)}, bf16[2,512,128]{2,1,0:T(8,128)(2,1)S(1)}, u32[]{:S(2)}, u32[]{:S(2)}) collective-permute-start(bf16[2,512,128]{2,1,0:T(8,128)(2,1)} %collective-permute-done.14.refs_12_.refs_17_), channel_id=1, source_target_pairs={{0,224},{32,0},{64,32},{96,64},{128,96},{160,128},{192,160},{224,1... | collective-permute-start | bytes 786440 | tf_op jit(solution)/shard_map/ppermute | solution.py:20
  85.3 11.4 %collective-permute-start.21 = (bf16[2,512,128]{2,1,0:T(8,128)(2,1)S(1)}, bf16[2,512,128]{2,1,0:T(8,128)(2,1)S(1)}, u32[]{:S(2)}, u32[]{:S(2)}) collective-permute-start(bf16[2,512,128]{2,1,0:T(8,128)(2,1)S(1)} %collective-permute-done.18.refs_7_.refs_9_), channel_id=1, source_target_pairs={{0,224},{32,0},{64,32},{96,64},{128,96},{160,128},{192,160},{224,1... | collective-permute-start | bytes 786440 | tf_op jit(solution)/shard_map/ppermute | solution.py:20
  87.3 10.8 %collective-permute-start.23 = (bf16[2,512,128]{2,1,0:T(8,128)(2,1)S(1)}, bf16[2,512,128]{2,1,0:T(8,128)(2,1)S(1)}, u32[]{:S(2)}, u32[]{:S(2)}) collective-permute-start(bf16[2,512,128]{2,1,0:T(8,128)(2,1)S(1)} %collective-permute-done.20.refs_11_.refs_16_), channel_id=1, source_target_pairs={{0,32},{32,64},{64,96},{96,128},{128,160},{160,192},{192,224},{224... | collective-permute-start | bytes 786440 | tf_op jit(solution)/shard_map/ppermute | solution.py:20
  92.9 9.6 %collective-permute-start.22 = (bf16[2,512,128]{2,1,0:T(8,128)(2,1)S(1)}, bf16[2,512,128]{2,1,0:T(8,128)(2,1)S(1)}, u32[]{:S(2)}, u32[]{:S(2)}) collective-permute-start(bf16[2,512,128]{2,1,0:T(8,128)(2,1)S(1)} %collective-permute-done.11.refs_10_), channel_id=1, source_target_pairs={{0,32},{32,64},{64,96},{96,128},{128,160},{160,192},{192,224},{224... | collective-permute-start | bytes 786440 | tf_op jit(solution)/shard_map/ppermute | solution.py:20
  93.1 9.4 %collective-permute-start.24 = (bf16[2,512,128]{2,1,0:T(8,128)(2,1)S(1)}, bf16[2,512,128]{2,1,0:T(8,128)(2,1)S(1)}, u32[]{:S(2)}, u32[]{:S(2)}) collective-permute-start(bf16[2,512,128]{2,1,0:T(8,128)(2,1)S(1)} %collective-permute-done.15.refs_19_), channel_id=1, source_target_pairs={{0,224},{32,0},{64,32},{96,64},{128,96},{160,128},{192,160},{224,1... | collective-permute-start | bytes 786440 | tf_op jit(solution)/shard_map/ppermute | solution.py:20
  115.0 14.0 %all-to-all-start.2 = ((bf16[4,256,256]{2,1,0:T(8,128)(2,1)}), bf16[4,256,256]{2,1,0:T(8,128)(2,1)S(1)}, u32[]{:S(2)}, u32[]{:S(2)}) async-start(bf16[4,256,256]{2,1,0:T(8,128)(2,1)} %bitcast.15), calls=%async_computation.2 | async-start | bytes 1048576 | tf_op jit(solution)/shard_map/all_to_all | solution.py:30
  119.8 9.0 %collective-permute-start.27 = (bf16[256,256]{1,0:T(8,128)(2,1)S(1)}, bf16[256,256]{1,0:T(8,128)(2,1)S(1)}, u32[]{:S(2)}, u32[]{:S(2)}) collective-permute-start(bf16[256,256]{1,0:T(8,128)(2,1)S(1)} %get-tuple-element.73), channel_id=1, source_target_pairs={{0,12},{4,0},{8,4},{12,8},{1,13},{5,1},{9,5},{13,9},{2,14},{6,2},{... | collective-permute-start | bytes 393224 | tf_op jit(solution)/shard_map/ppermute | solution.py:20
  129.1 14.1 %collective-permute-start.31 = (bf16[1024,256]{1,0:T(8,128)(2,1)S(1)}, bf16[1024,256]{1,0:T(8,128)(2,1)S(1)}, u32[]{:S(2)}, u32[]{:S(2)}) collective-permute-start(bf16[1024,256]{1,0:T(8,128)(2,1)S(1)} %pad_maximum_fusion.3), channel_id=1, source_target_pairs={{0,1},{1,2},{2,3},{3,0},{4,5},{5,6},{6,7},{7,4},{8,9},{9,10},{10,1... | collective-permute-start | bytes 1572872 | tf_op jit(solution)/shard_map/ppermute | solution.py:20
  130.9 12.3 %collective-permute-start.32 = (bf16[1024,256]{1,0:T(8,128)(2,1)S(1)}, bf16[1024,256]{1,0:T(8,128)(2,1)S(1)}, u32[]{:S(2)}, u32[]{:S(2)}) collective-permute-start(bf16[1024,256]{1,0:T(8,128)(2,1)S(1)} %pad_maximum_fusion.3), channel_id=1, source_target_pairs={{0,3},{1,0},{2,1},{3,2},{4,7},{5,4},{6,5},{7,6},{8,11},{9,8},{10,9... | collective-permute-start | bytes 1572872 | tf_op jit(solution)/shard_map/ppermute | solution.py:20
  132.4 12.3 %collective-permute-start.29 = (bf16[1024,256]{1,0:T(8,128)(2,1)S(1)}, bf16[1024,256]{1,0:T(8,128)(2,1)S(1)}, u32[]{:S(2)}, u32[]{:S(2)}) collective-permute-start(bf16[1024,256]{1,0:T(8,128)(2,1)S(1)} %bitcast.38), channel_id=1, source_target_pairs={{0,4},{4,8},{8,12},{12,0},{1,5},{5,9},{9,13},{13,1},{2,6},{6,10},{... | collective-permute-start | bytes 1572872 | tf_op jit(solution)/shard_map/ppermute | solution.py:20
  133.4 13.3 %collective-permute-start.30 = (bf16[1024,256]{1,0:T(8,128)(2,1)S(1)}, bf16[1024,256]{1,0:T(8,128)(2,1)S(1)}, u32[]{:S(2)}, u32[]{:S(2)}) collective-permute-start(bf16[1024,256]{1,0:T(8,128)(2,1)S(1)} %bitcast.39), channel_id=1, source_target_pairs={{0,12},{4,0},{8,4},{12,8},{1,13},{5,1},{9,5},{13,9},{2,14},{6,2},{... | collective-permute-start | bytes 1572872 | tf_op jit(solution)/shard_map/ppermute | solution.py:20
  146.7 10.4 %collective-permute-start.33 = (bf16[512,256]{1,0:T(8,128)(2,1)S(1)}, bf16[512,256]{1,0:T(8,128)(2,1)S(1)}, u32[]{:S(2)}, u32[]{:S(2)}) collective-permute-start(bf16[512,256]{1,0:T(8,128)(2,1)S(1)} %slice.38), channel_id=1, source_target_pairs={{0,4},{4,8},{8,12},{12,0},{1,5},{5,9},{9,13},{13,1},{2,6},{6,10},{... | collective-permute-start | bytes 786440 | tf_op jit(solution)/shard_map/ppermute | solution.py:20
  147.1 10.0 %collective-permute-start.34 = (bf16[512,256]{1,0:T(8,128)(2,1)S(1)}, bf16[512,256]{1,0:T(8,128)(2,1)S(1)}, u32[]{:S(2)}, u32[]{:S(2)}) collective-permute-start(bf16[512,256]{1,0:T(8,128)(2,1)S(1)} %slice.39), channel_id=1, source_target_pairs={{0,12},{4,0},{8,4},{12,8},{1,13},{5,1},{9,5},{13,9},{2,14},{6,2},{... | collective-permute-start | bytes 786440 | tf_op jit(solution)/shard_map/ppermute | solution.py:20
  148.9 8.2 %collective-permute-start.35 = (bf16[512,256]{1,0:T(8,128)(2,1)S(1)}, bf16[512,256]{1,0:T(8,128)(2,1)S(1)}, u32[]{:S(2)}, u32[]{:S(2)}) collective-permute-start(bf16[512,256]{1,0:T(8,128)(2,1)S(1)} %slice.40), channel_id=1, source_target_pairs={{0,1},{1,2},{2,3},{3,0},{4,5},{5,6},{6,7},{7,4},{8,9},{9,10},{10,1... | collective-permute-start | bytes 786440 | tf_op jit(solution)/shard_map/ppermute | solution.py:20
  (42 other events, 248.8 us)

commit v7 on v6

--- a/solution.py
+++ b/solution.py
@@ -52,64 +52,43 @@
     n_x = sum(len(c) for c in counts)
     x_refs, w_ref = refs[:n_x], refs[n_x]
     sums_ref = refs[n_x + 1] if has_sums else None
-    x_buf, w_buf, acc, x_sem, w_sem, s_sem = refs[-6:]
+    acc, s_sem = refs[-2:]
     more = refs[n_x + 1 + has_sums : n_x + 1 + has_sums + n_more]
-    outs = refs[n_x + 1 + has_sums + n_more : -6]
+    outs = refs[n_x + 1 + has_sums + n_more : -2]
     y = lax.axis_index("y")
     x = lax.axis_index("x")
-    x_copies = []
+    n_steps = len(steps)
+    arrays = [[], []]
     i = 0
     for half in range(2):
-        at = 0
         for count in counts[half]:
-            x_copies.append(pltpu.make_async_copy(x_refs[i], x_buf.at[half, pl.ds(at, count)], x_sem.at[i]))
-            at += count
+            arrays[half] += [(x_refs[i], j) for j in range(count)]
             i += 1
-    n_steps = len(steps)
-
-    def w_copy(part, j, owner):
-        row = pl.multiple_of(owner * 256, 256)
-        return pltpu.make_async_copy(
-            w_ref.at[:, pl.ds(row, 256)], w_buf.at[part, :, pl.ds(j * 256, 256)], w_sem.at[part, j]
-        )
-
-    for copy in x_copies:
-        copy.start()
     if has_sums:
         sums_copy = pltpu.make_async_copy(sums_ref, acc, s_sem)
+        sums_copy.start()
     for half in range(2):
         for k, step in enumerate(steps):
+            blocks = arrays[half][NXY * k : NXY * (k + 1)]
+            rows = jnp.concatenate([ref[j] for ref, j in blocks], axis=1)
+            starts = []
             for j in range(NXY):
                 if half == 0:
                     owner = lax.rem(y + OFFS[step] + NXY, NXY) * NXY + j
                 else:
                     owner = lax.rem(y + OFFS[j] + NXY, NXY) * NXY + lax.rem(x + OFFS[step] + NXY, NXY)
-                w_copy(half * n_steps + k, j, owner).start()
-        if has_sums and half == 0:
-            sums_copy.start()
-    for copy in x_copies:
-        copy.wait()
-
-    def multiply(part, carry):
-        half, k = part // n_steps, lax.rem(part, n_steps)
-        for j in range(NXY):
-            w_copy(part, j, 0).wait()
-        rows = jnp.concatenate([x_buf[half, NXY * k + j] for j in range(NXY)], axis=1)
-        span = pl.ds(pl.multiple_of(half * n, n), n)
-        if has_sums:
-
-            @pl.when(part == 0)
-            def _():
+                starts.append(pl.multiple_of(owner * 256, 256))
+            if has_sums and half == 0 and k == 0:
                 sums_copy.wait()
-
-        for g in range(groups):
-            value = jnp.dot(rows, w_buf[part, g], preferred_element_type=jnp.float32)
-            if has_sums:
-                value = acc[g, span] + value
-            acc[g, span] = value
-        return carry
-
-    lax.fori_loop(0, 2 * n_steps, multiply, 0)
+            span = slice(half * n, (half + 1) * n)
+
+            def column(g, carry, rows=rows, starts=starts, span=span, first=k == 0 and not has_sums):
+                weights = jnp.concatenate([w_ref[g, pl.ds(start, 256)] for start in starts], axis=0)
+                value = jnp.dot(rows, weights, preferred_element_type=jnp.float32)
+                acc[g, span] = value if first else acc[g, span] + value
+                return carry
+
+            lax.fori_loop(0, groups, column, 0)
     if finish is None:
         copy = pltpu.make_async_copy(acc, outs[0], s_sem)
         copy.start()
@@ -121,7 +100,11 @@
 HBM = pl.BlockSpec(memory_space=pltpu.HBM)
 VMEM = pl.BlockSpec(memory_space=pltpu.VMEM)
 SMEM = pl.BlockSpec(memory_space=pltpu.SMEM)
-PARAMS = pltpu.CompilerParams(vmem_limit_bytes=56 * 1024 * 1024)
+PARAMS = pltpu.CompilerParams(vmem_limit_bytes=24 * 1024 * 1024)
+
+
+def in_vmem(a):
+    return pltpu.with_memory_space_constraint(a, pltpu.VMEM)
 
 
 def partial_matmul(steps, halves, w, sums, name, finish=None, out_shape=None, more=()):
@@ -130,19 +113,14 @@
     n, groups = xs[0].shape[1], w.shape[0]
     total = jax.ShapeDtypeStruct((groups, 2 * n, 256), jnp.float32)
     has_sums = sums is not None
-    operands = [*xs, w] + ([sums] if has_sums else [])
-    bf16 = jnp.bfloat16
+    operands = [in_vmem(v) for v in [*xs, w]] + ([sums] if has_sums else [])
     return pl.pallas_call(
         lambda *refs: partial_kernel(steps, counts, n, groups, has_sums, len(more), finish, *refs),
         out_shape=total if finish is None else out_shape,
-        in_specs=[HBM] * len(operands) + [VMEM] * len(more),
+        in_specs=[VMEM] * (len(xs) + 1) + [HBM] * has_sums + [VMEM] * len(more),
         out_specs=HBM if finish is None else jax.tree.map(lambda _: VMEM, out_shape),
         scratch_shapes=[
-            pltpu.VMEM((2, NXY * len(steps), n, 256), bf16),
-            pltpu.VMEM((2 * len(steps), groups, 1024, 256), bf16),
             pltpu.VMEM((groups, 2 * n, 256), jnp.float32),
-            pltpu.SemaphoreType.DMA((len(xs),)),
-            pltpu.SemaphoreType.DMA((2 * len(steps), NXY)),
             pltpu.SemaphoreType.DMA(()),
         ],
         compiler_params=PARAMS,
@@ -327,7 +305,7 @@
     return pl.pallas_call(
         dense_kernel,
         out_shape=jax.ShapeDtypeStruct((3, 2 * BLK, DH), jnp.float32),
-        in_specs=[SMEM] + [HBM] * 12,
+        in_specs=[SMEM] + [VMEM] * 12,
         out_specs=VMEM,
         scratch_shapes=[
             pltpu.VMEM((5, 2, 2, 512, DH), bf16),
@@ -336,7 +314,7 @@
         ],
         compiler_params=PARAMS,
         name="dense",
-    )(glob, mine, theirs, *own[:5], *other[:5])
+    )(glob, *map(in_vmem, [mine, theirs, *own[:5], *other[:5]]))
 
 
 def attend(rand, glob, radius, mine, theirs, own, other, started):
@@ -344,7 +322,7 @@
     return pl.pallas_call(
         attend_kernel,
         out_shape=(jax.ShapeDtypeStruct((512, DH), bf16),) * 2,
-        in_specs=[SMEM] * 3 + [HBM] * 18 + [VMEM],
+        in_specs=[SMEM] * 3 + [VMEM] * 19,
         out_specs=(VMEM, VMEM),
         scratch_shapes=[
             pltpu.VMEM((NZ, 2, 2, 512, DH), bf16),
@@ -355,7 +333,7 @@
         compiler_params=PARAMS,
         cost_estimate=pl.CostEstimate(flops=14000000000, transcendentals=0, bytes_accessed=28000000),
         name="attend",
-    )(rand, glob, radius, mine, theirs, *own, *other, started)
+    )(rand, glob, radius, in_vmem(mine), in_vmem(theirs), *map(in_vmem, [*own, *other]), started)
 
 
 def swap(a):

time: 163 us -> 160 us (0.982)
  Pallas kernels: 41.8 us -> 22 us
  local copies, waits for them, and re-layouts: 6.99 us -> 17.4 us
  waiting for transfers between devices: 45.9 us -> 52.1 us
    pallas_call x6, Pallas kernels: 28.6 us -> 13.3 us  [partial_matmul(): pl.pallas_call(lambda *refs: partial_kernel(steps, counts, n, groups, has...]
    unnamed x70 -> x34, local copies, waits for them, and re-layouts: 4.98 us -> 15.1 us
    ppermute x34, waiting for transfers between devices: 45.2 us -> 51.3 us  [shift(): return lax.ppermute(a, axis, [(i, (i + step) % n) for i in range(n)])]
    pallas_call x1, Pallas kernels: 3.21 us -> 0.65 us  [order(): pl.pallas_call(order_kernel, out_shape=jax.ShapeDtypeStruct((16, 256, 256...]
    pallas_call x1, Pallas kernels: 8.52 us -> 6.76 us  [attend(): pl.pallas_call(attend_kernel, out_shape=(jax.ShapeDtypeStruct((512, DH),...]
  transfers between devices with their start and end apart: 40 -> 40, of which waited for: 21 -> 24; matrix products, arithmetic and copies ran while one was open for 2% -> 2% of each run, Pallas kernels for 21% -> 11%
where the time goes in v7:
time: 160 us; the launch traced here: 157 us
  starting transfers between devices  63.3 us (40%)
  waiting for transfers between devices  52.1 us (33%)
  Pallas kernels  22 us (14%)
  local copies, waits for them, and re-layouts  17.4 us (11%)
  other arithmetic  1.83 us (1%)
    ppermute x34, waiting for transfers between devices, shift(): return lax.ppermute(a, axis, [(i, (i + step) % n) for i in range(n)])  51.3 us
    ppermute x34, starting transfers between devices, shift(): return lax.ppermute(a, axis, [(i, (i + step) % n) for i in range(n)])  48.6 us
    unnamed x34, local copies, waits for them, and re-layouts  15.1 us
    pallas_call x6, Pallas kernels, partial_matmul(): pl.pallas_call(lambda *refs: partial_kernel(steps, counts, n, groups, has...  13.3 us
    all_to_all x2, starting transfers between devices, plane_matmul(): lax.all_to_all(jnp.concatenate([a[:n]] * NXY, axis=0), 'x', 0, 0, tiled=T...  8.53 us
    pallas_call x1, Pallas kernels, attend(): pl.pallas_call(attend_kernel, out_shape=(jax.ShapeDtypeStruct((512, DH),...  6.76 us
    all_to_all x1, starting transfers between devices, body(): w_cols = lax.all_to_all(ordered, ('y', 'x'), 0, 0, tiled=True)  6.1 us
  transfers between devices with their start and end apart: 40, of which 24 were waited for; matrix products, arithmetic and copies ran while one was open for 2% of the time, Pallas kernels for 11%

profile of v7, /device:TPU:24, one launch (start us, length us, event | category | flops | bytes accessed | tf_op | source)
XLA Modules:
  0.0 157.0 jit_solution(4467705302973240995)
XLA Ops:
  2.0 4.3 %all-to-all-start = ((bf16[4,256,256]{2,1,0:T(8,128)(2,1)}), bf16[4,256,256]{2,1,0:T(8,128)(2,1)S(1)}, u32[]{:S(2)}, u32[]{:S(2)}) async-start(bf16[4,256,256]{2,1,0:T(8,128)(2,1)} %bitcast), calls=%async_computation | async-start | bytes 1048576 | tf_op jit(solution)/shard_map/all_to_all | solution.py:30
  9.5 2.8 %collective-permute-done = bf16[256,256]{1,0:T(8,128)(2,1)S(1)} collective-permute-done((bf16[256,256]{1,0:T(8,128)(2,1)S(1)}, bf16[256,256]{1,0:T(8,128)(2,1)S(1)}, u32[]{:S(2)}, u32[]{:S(2)}) %collective-permute-start) | collective-permute-done | bytes 131104 | tf_op jit(solution)/shard_map/ppermute | solution.py:20
  12.4 3.7 %collective-permute-done.1 = bf16[256,256]{1,0:T(8,128)(2,1)S(1)} collective-permute-done((bf16[256,256]{1,0:T(8,128)(2,1)S(1)}, bf16[256,256]{1,0:T(8,128)(2,1)S(1)}, u32[]{:S(2)}, u32[]{:S(2)}) %collective-permute-start.1) | collective-permute-done | bytes 131104 | tf_op jit(solution)/shard_map/ppermute | solution.py:20
  16.1 1.9 %collective-permute-start.5 = (bf16[1024,256]{1,0:T(8,128)(2,1)S(1)}, bf16[1024,256]{1,0:T(8,128)(2,1)S(1)}, u32[]{:S(2)}, u32[]{:S(2)}) collective-permute-start(bf16[1024,256]{1,0:T(8,128)(2,1)S(1)} %pad_maximum_fusion.1), channel_id=1, source_target_pairs={{0,1},{1,2},{2,3},{3,0},{4,5},{5,6},{6,7},{7,4},{8,9},{9,10},{10,1... | collective-permute-start | bytes 1572872 | tf_op jit(solution)/shard_map/ppermute | solution.py:20
  23.5 2.8 %copy-done = bf16[4096,3,256]{2,0,1:T(8,128)(2,1)S(1)} copy-done((bf16[4096,3,256]{2,0,1:T(8,128)(2,1)S(1)}, bf16[4096,3,256]{2,0,1:T(8,128)(2,1)}, u32[]{:S(2)}) %copy-start) | copy-done | bytes 6291480
  26.2 2.0 %project0.1.refs_5_ = f32[3,512,256]{2,1,0:T(8,128)S(1)} custom-call(bf16[4,256,256]{2,1,0:T(8,128)(2,1)S(1)} %all-to-all-done, bf16[4,256,256]{2,1,0:T(8,128)(2,1)S(1)} %bitcast.40, bf16[3,4096,256]{2,1,0:T(8,128)(2,1)S(1)} %bitcast.30), custom_call_target="tpu_custom_call" | custom-call | tf_op jit(solution)/shard_map/project0/pallas_call | solution.py:117
  31.1 1.9 %collective-permute-done.4 = bf16[1024,256]{1,0:T(8,128)(2,1)S(1)} collective-permute-done((bf16[1024,256]{1,0:T(8,128)(2,1)S(1)}, bf16[1024,256]{1,0:T(8,128)(2,1)S(1)}, u32[]{:S(2)}, u32[]{:S(2)}) %collective-permute-start.4) | collective-permute-done | bytes 524320 | tf_op jit(solution)/shard_map/ppermute | solution.py:20
  34.9 2.8 %copy-done.1 = bf16[4096,3,256]{2,0,1:T(8,128)(2,1)S(1)} copy-done((bf16[4096,3,256]{2,0,1:T(8,128)(2,1)S(1)}, bf16[4096,3,256]{2,0,1:T(8,128)(2,1)}, u32[]{:S(2)}) %copy-start.1) | copy-done | bytes 6291480
  39.8 5.0 %project1.1.refs_3_ = f32[3,512,256]{2,1,0:T(8,128)S(1)} custom-call(bf16[4,256,256]{2,1,0:T(8,128)(2,1)} %bitcast.8.refs_0_, bf16[4,256,256]{2,1,0:T(8,128)(2,1)S(1)} %bitcast.48, bf16[4,256,256]{2,1,0:T(8,128)(2,1)S(1)} %bitcast.46, bf16[4,256,256]{2,1,0:T(8,128)(2,1)S(1)} %bitcast.47, bf16[3,4096,256]{2,1,0:T(8,128)(2,1)S(1)} %bitcast.31, ...), custom_call_target="tpu_custom_call" | custom-call | tf_op jit(solution)/shard_map/project1/pallas_call | solution.py:117
  45.9 3.7 %project3.1 = (bf16[512,128]{1,0:T(8,128)(2,1)S(1)}, bf16[2,512,128]{2,1,0:T(8,128)(2,1)S(1)}, bf16[528,128]{1,0:T(8,128)(2,1)}, bf16[2,512,128]{2,1,0:T(8,128)(2,1)S(1)}) custom-call(bf16[4,256,256]{2,1,0:T(8,128)(2,1)S(1)} %bitcast.49, bf16[4,256,256]{2,1,0:T(8,128)(2,1)} %bitcast.7.refs_1_, bf16[3,4096,256]{2,1,0:T(8,128)(2,1)S(1)} %bitcast.32, ...), custom_call_target="tpu_custom_call" | custom-call | tf_op jit(solution)/shard_map/project3/pallas_call | solution.py:117
  50.3 3.1 %collective-permute-start.9 = (bf16[2,512,128]{2,1,0:T(8,128)(2,1)S(1)}, bf16[2,512,128]{2,1,0:T(8,128)(2,1)S(1)}, u32[]{:S(2)}, u32[]{:S(2)}) collective-permute-start(bf16[2,512,128]{2,1,0:T(8,128)(2,1)S(1)} %get-tuple-element.48.refs_3_.refs_5_), channel_id=1, source_target_pairs={{0,32},{32,64},{64,96},{96,128},{128,160},{160,192},{192,224},{224... | collective-permute-start | bytes 786440 | tf_op jit(solution)/shard_map/ppermute | solution.py:20
  53.4 5.5 %collective-permute-start.13 = (bf16[2,512,128]{2,1,0:T(8,128)(2,1)S(1)}, bf16[2,512,128]{2,1,0:T(8,128)(2,1)S(1)}, u32[]{:S(2)}, u32[]{:S(2)}) collective-permute-start(bf16[2,512,128]{2,1,0:T(8,128)(2,1)S(1)} %collective-permute-done.12.refs_8_.refs_13_), channel_id=1, source_target_pairs={{0,224},{32,0},{64,32},{96,64},{128,96},{160,128},{192,160},{224,1... | collective-permute-start | bytes 786440 | tf_op jit(solution)/shard_map/ppermute | solution.py:20
  60.9 3.6 %collective-permute-done.9.refs_4_.refs_6_ = bf16[2,512,128]{2,1,0:T(8,128)(2,1)S(1)} collective-permute-done((bf16[2,512,128]{2,1,0:T(8,128)(2,1)S(1)}, bf16[2,512,128]{2,1,0:T(8,128)(2,1)S(1)}, u32[]{:S(2)}, u32[]{:S(2)}) %collective-permute-start.9) | collective-permute-done | bytes 262176 | tf_op jit(solution)/shard_map/ppermute | solution.py:20
  65.6 3.7 %collective-permute-start.14 = (bf16[2,512,128]{2,1,0:T(8,128)(2,1)S(1)}, bf16[2,512,128]{2,1,0:T(8,128)(2,1)}, u32[]{:S(2)}, u32[]{:S(2)}) collective-permute-start(bf16[2,512,128]{2,1,0:T(8,128)(2,1)S(1)} %collective-permute-done.13.refs_10_.refs_15_), channel_id=1, source_target_pairs={{0,224},{32,0},{64,32},{96,64},{128,96},{160,128},{192,160},{224,1... | collective-permute-start | bytes 786440 | tf_op jit(solution)/shard_map/ppermute | solution.py:20
  69.3 6.1 %all-to-all-start.1 = ((bf16[16,256,256]{2,1,0:T(8,128)(2,1)}), bf16[16,256,256]{2,1,0:T(8,128)(2,1)S(1)}, u32[]{:S(2)}, u32[]{:S(2)}) async-start(bf16[16,256,256]{2,1,0:T(8,128)(2,1)} %copy-done.2), calls=%async_computation.1 | async-start | bytes 4194304 | tf_op jit(solution)/shard_map/all_to_all | solution.py:355
  77.0 2.0 %collective-permute-start.20 = (bf16[2,512,128]{2,1,0:T(8,128)(2,1)}, bf16[2,512,128]{2,1,0:T(8,128)(2,1)S(1)}, u32[]{:S(2)}, u32[]{:S(2)}) collective-permute-start(bf16[2,512,128]{2,1,0:T(8,128)(2,1)} %collective-permute-done.19.refs_9_.refs_14_), channel_id=1, source_target_pairs={{0,32},{32,64},{64,96},{96,128},{128,160},{160,192},{192,224},{224... | collective-permute-start | bytes 786440 | tf_op jit(solution)/shard_map/ppermute | solution.py:20
  79.1 3.2 %collective-permute-start.15 = (bf16[2,512,128]{2,1,0:T(8,128)(2,1)}, bf16[2,512,128]{2,1,0:T(8,128)(2,1)S(1)}, u32[]{:S(2)}, u32[]{:S(2)}) collective-permute-start(bf16[2,512,128]{2,1,0:T(8,128)(2,1)} %collective-permute-done.14.refs_12_.refs_17_), channel_id=1, source_target_pairs={{0,224},{32,0},{64,32},{96,64},{128,96},{160,128},{192,160},{224,1... | collective-permute-start | bytes 786440 | tf_op jit(solution)/shard_map/ppermute | solution.py:20
  82.3 3.8 %collective-permute-done.18.refs_7_.refs_9_ = bf16[2,512,128]{2,1,0:T(8,128)(2,1)S(1)} collective-permute-done((bf16[2,512,128]{2,1,0:T(8,128)(2,1)S(1)}, bf16[2,512,128]{2,1,0:T(8,128)(2,1)S(1)}, u32[]{:S(2)}, u32[]{:S(2)}) %collective-permute-start.18) | collective-permute-done | bytes 262176 | tf_op jit(solution)/shard_map/ppermute | solution.py:20
  90.6 2.6 %collective-permute-done.11.refs_10_ = bf16[2,512,128]{2,1,0:T(8,128)(2,1)S(1)} collective-permute-done((bf16[2,512,128]{2,1,0:T(8,128)(2,1)}, bf16[2,512,128]{2,1,0:T(8,128)(2,1)S(1)}, u32[]{:S(2)}, u32[]{:S(2)}) %collective-permute-start.11) | collective-permute-done | bytes 262176 | tf_op jit(solution)/shard_map/ppermute | solution.py:20
  94.0 2.5 %collective-permute-start.24 = (bf16[2,512,128]{2,1,0:T(8,128)(2,1)S(1)}, bf16[2,512,128]{2,1,0:T(8,128)(2,1)S(1)}, u32[]{:S(2)}, u32[]{:S(2)}) collective-permute-start(bf16[2,512,128]{2,1,0:T(8,128)(2,1)S(1)} %collective-permute-done.15.refs_19_), channel_id=1, source_target_pairs={{0,224},{32,0},{64,32},{96,64},{128,96},{160,128},{192,160},{224,1... | collective-permute-start | bytes 786440 | tf_op jit(solution)/shard_map/ppermute | solution.py:20
  98.9 4.6 %collective-permute-done.22.refs_12_ = bf16[2,512,128]{2,1,0:T(8,128)(2,1)S(1)} collective-permute-done((bf16[2,512,128]{2,1,0:T(8,128)(2,1)S(1)}, bf16[2,512,128]{2,1,0:T(8,128)(2,1)S(1)}, u32[]{:S(2)}, u32[]{:S(2)}) %collective-permute-start.22) | collective-permute-done | bytes 262176 | tf_op jit(solution)/shard_map/ppermute | solution.py:20
  103.5 6.8 %attend.1 = (bf16[512,128]{1,0:T(8,128)(2,1)S(1)}, bf16[512,128]{1,0:T(8,128)(2,1)S(1)}) custom-call(s32[96]{0:T(128)S(1)} %pad_add_fusion.refs_0_, s32[2]{0:T(128)S(1)} %copy-done.12, s32[2]{0:T(128)S(1)} %copy-done.14, bf16[512,128]{1,0:T(8,128)(2,1)S(1)} %copy-done.10, bf16[528,128]{1,0:T(8,128)(2,1)S(1)} %collective-permute-done.16.refs_2_.refs_4_, ...), custom_call_target="tpu_custom_call" | custom-call | flops 14000000000 | bytes 28000000 | tf_op jit(solution)/shard_map/attend/pallas_call | solution.py:322
  114.1 4.2 %all-to-all-start.2 = ((bf16[4,256,256]{2,1,0:T(8,128)(2,1)}), bf16[4,256,256]{2,1,0:T(8,128)(2,1)S(1)}, u32[]{:S(2)}, u32[]{:S(2)}) async-start(bf16[4,256,256]{2,1,0:T(8,128)(2,1)} %bitcast.15), calls=%async_computation.2 | async-start | bytes 1048576 | tf_op jit(solution)/shard_map/all_to_all | solution.py:30
  121.8 2.5 %collective-permute-done.26 = bf16[256,256]{1,0:T(8,128)(2,1)S(1)} collective-permute-done((bf16[256,256]{1,0:T(8,128)(2,1)S(1)}, bf16[256,256]{1,0:T(8,128)(2,1)S(1)}, u32[]{:S(2)}, u32[]{:S(2)}) %collective-permute-start.26) | collective-permute-done | bytes 131104 | tf_op jit(solution)/shard_map/ppermute | solution.py:20
  124.3 3.5 %collective-permute-done.27 = bf16[256,256]{1,0:T(8,128)(2,1)S(1)} collective-permute-done((bf16[256,256]{1,0:T(8,128)(2,1)S(1)}, bf16[256,256]{1,0:T(8,128)(2,1)S(1)}, u32[]{:S(2)}, u32[]{:S(2)}) %collective-permute-start.27) | collective-permute-done | bytes 131104 | tf_op jit(solution)/shard_map/ppermute | solution.py:20
  128.1 1.8 %collective-permute-start.31 = (bf16[1024,256]{1,0:T(8,128)(2,1)S(1)}, bf16[1024,256]{1,0:T(8,128)(2,1)S(1)}, u32[]{:S(2)}, u32[]{:S(2)}) collective-permute-start(bf16[1024,256]{1,0:T(8,128)(2,1)S(1)} %pad_maximum_fusion.3), channel_id=1, source_target_pairs={{0,1},{1,2},{2,3},{3,0},{4,5},{5,6},{6,7},{7,4},{8,9},{9,10},{10,1... | collective-permute-start | bytes 1572872 | tf_op jit(solution)/shard_map/ppermute | solution.py:20
  134.0 8.3 %collective-permute-done.31 = bf16[1024,256]{1,0:T(8,128)(2,1)S(1)} collective-permute-done((bf16[1024,256]{1,0:T(8,128)(2,1)S(1)}, bf16[1024,256]{1,0:T(8,128)(2,1)S(1)}, u32[]{:S(2)}, u32[]{:S(2)}) %collective-permute-start.31) | collective-permute-done | bytes 524320 | tf_op jit(solution)/shard_map/ppermute | solution.py:20
  143.7 2.0 %collective-permute-done.30 = bf16[1024,256]{1,0:T(8,128)(2,1)S(1)} collective-permute-done((bf16[1024,256]{1,0:T(8,128)(2,1)S(1)}, bf16[1024,256]{1,0:T(8,128)(2,1)S(1)}, u32[]{:S(2)}, u32[]{:S(2)}) %collective-permute-start.30) | collective-permute-done | bytes 524320 | tf_op jit(solution)/shard_map/ppermute | solution.py:20
  146.1 1.8 %collective-permute-start.34 = (bf16[512,256]{1,0:T(8,128)(2,1)S(1)}, bf16[512,256]{1,0:T(8,128)(2,1)S(1)}, u32[]{:S(2)}, u32[]{:S(2)}) collective-permute-start(bf16[512,256]{1,0:T(8,128)(2,1)S(1)} %slice.39), channel_id=1, source_target_pairs={{0,12},{4,0},{8,4},{12,8},{1,13},{5,1},{9,5},{13,9},{2,14},{6,2},{... | collective-permute-start | bytes 786440 | tf_op jit(solution)/shard_map/ppermute | solution.py:20
  148.3 3.1 %collective-permute-start.36 = (bf16[512,256]{1,0:T(8,128)(2,1)S(1)}, bf16[512,256]{1,0:T(8,128)(2,1)S(1)}, u32[]{:S(2)}, u32[]{:S(2)}) collective-permute-start(bf16[512,256]{1,0:T(8,128)(2,1)S(1)} %slice.41), channel_id=1, source_target_pairs={{0,3},{1,0},{2,1},{3,2},{4,7},{5,4},{6,5},{7,6},{8,11},{9,8},{10,9... | collective-permute-start | bytes 786440 | tf_op jit(solution)/shard_map/ppermute | solution.py:20
  152.2 1.6 collective-permute-done.34
  153.8 1.8 %collective-permute-done.35 = bf16[512,256]{1,0:T(8,128)(2,1)S(1)} collective-permute-done((bf16[512,256]{1,0:T(8,128)(2,1)S(1)}, bf16[512,256]{1,0:T(8,128)(2,1)S(1)}, u32[]{:S(2)}, u32[]{:S(2)}) %collective-permute-start.35) | collective-permute-done | bytes 262176 | tf_op jit(solution)/shard_map/ppermute | solution.py:20
  (110 shorter events, 47.5 us)
Async XLA Ops:
  2.0 14.1 %all-to-all-start = ((bf16[4,256,256]{2,1,0:T(8,128)(2,1)}), bf16[4,256,256]{2,1,0:T(8,128)(2,1)S(1)}, u32[]{:S(2)}, u32[]{:S(2)}) async-start(bf16[4,256,256]{2,1,0:T(8,128)(2,1)} %bitcast), calls=%async_computation | async-start | bytes 1048576 | tf_op jit(solution)/shard_map/all_to_all | solution.py:30
  7.5 8.5 %collective-permute-start.1 = (bf16[256,256]{1,0:T(8,128)(2,1)S(1)}, bf16[256,256]{1,0:T(8,128)(2,1)S(1)}, u32[]{:S(2)}, u32[]{:S(2)}) collective-permute-start(bf16[256,256]{1,0:T(8,128)(2,1)S(1)} %get-tuple-element.75), channel_id=1, source_target_pairs={{0,12},{4,0},{8,4},{12,8},{1,13},{5,1},{9,5},{13,9},{2,14},{6,2},{... | collective-permute-start | bytes 393224 | tf_op jit(solution)/shard_map/ppermute | solution.py:20
  8.3 7.7 %collective-permute-start.2 = (bf16[256,256]{1,0:T(8,128)(2,1)S(1)}, bf16[256,256]{1,0:T(8,128)(2,1)S(1)}, u32[]{:S(2)}, u32[]{:S(2)}) collective-permute-start(bf16[256,256]{1,0:T(8,128)(2,1)S(1)} %get-tuple-element.75), channel_id=1, source_target_pairs={{0,8},{4,12},{8,0},{12,4},{1,9},{5,13},{9,1},{13,5},{2,10},{6,14},... | collective-permute-start | bytes 393224 | tf_op jit(solution)/shard_map/ppermute | solution.py:20
  16.1 13.5 %collective-permute-start.5 = (bf16[1024,256]{1,0:T(8,128)(2,1)S(1)}, bf16[1024,256]{1,0:T(8,128)(2,1)S(1)}, u32[]{:S(2)}, u32[]{:S(2)}) collective-permute-start(bf16[1024,256]{1,0:T(8,128)(2,1)S(1)} %pad_maximum_fusion.1), channel_id=1, source_target_pairs={{0,1},{1,2},{2,3},{3,0},{4,5},{5,6},{6,7},{7,4},{8,9},{9,10},{10,1... | collective-permute-start | bytes 1572872 | tf_op jit(solution)/shard_map/ppermute | solution.py:20
  18.0 11.7 %collective-permute-start.6 = (bf16[1024,256]{1,0:T(8,128)(2,1)S(1)}, bf16[1024,256]{1,0:T(8,128)(2,1)S(1)}, u32[]{:S(2)}, u32[]{:S(2)}) collective-permute-start(bf16[1024,256]{1,0:T(8,128)(2,1)S(1)} %pad_maximum_fusion.1), channel_id=1, source_target_pairs={{0,3},{1,0},{2,1},{3,2},{4,7},{5,4},{6,5},{7,6},{8,11},{9,8},{10,9... | collective-permute-start | bytes 1572872 | tf_op jit(solution)/shard_map/ppermute | solution.py:20
  19.4 11.7 %collective-permute-start.3 = (bf16[1024,256]{1,0:T(8,128)(2,1)S(1)}, bf16[1024,256]{1,0:T(8,128)(2,1)}, u32[]{:S(2)}, u32[]{:S(2)}) collective-permute-start(bf16[1024,256]{1,0:T(8,128)(2,1)S(1)} %bitcast.36), channel_id=1, source_target_pairs={{0,4},{4,8},{8,12},{12,0},{1,5},{5,9},{9,13},{13,1},{2,6},{6,10},{... | collective-permute-start | bytes 1572872 | tf_op jit(solution)/shard_map/ppermute | solution.py:20
  20.6 12.5 %collective-permute-start.4 = (bf16[1024,256]{1,0:T(8,128)(2,1)S(1)}, bf16[1024,256]{1,0:T(8,128)(2,1)S(1)}, u32[]{:S(2)}, u32[]{:S(2)}) collective-permute-start(bf16[1024,256]{1,0:T(8,128)(2,1)S(1)} %bitcast.37), channel_id=1, source_target_pairs={{0,12},{4,0},{8,4},{12,8},{1,13},{5,1},{9,5},{13,9},{2,14},{6,2},{... | collective-permute-start | bytes 1572872 | tf_op jit(solution)/shard_map/ppermute | solution.py:20
  33.9 11.0 %collective-permute-start.7 = (bf16[1024,256]{1,0:T(8,128)(2,1)}, bf16[1024,256]{1,0:T(8,128)(2,1)S(1)}, u32[]{:S(2)}, u32[]{:S(2)}) collective-permute-start(bf16[1024,256]{1,0:T(8,128)(2,1)} %collective-permute-done.3), channel_id=1, source_target_pairs={{0,4},{4,8},{8,12},{12,0},{1,5},{5,9},{9,13},{13,1},{2,6},{6,10},{... | collective-permute-start | bytes 1572872 | tf_op jit(solution)/shard_map/ppermute | solution.py:20
  34.3 11.7 %collective-permute-start.8 = (bf16[1024,256]{1,0:T(8,128)(2,1)S(1)}, bf16[1024,256]{1,0:T(8,128)(2,1)}, u32[]{:S(2)}, u32[]{:S(2)}) collective-permute-start(bf16[1024,256]{1,0:T(8,128)(2,1)S(1)} %collective-permute-done.5), channel_id=1, source_target_pairs={{0,1},{1,2},{2,3},{3,0},{4,5},{5,6},{6,7},{7,4},{8,9},{9,10},{10,1... | collective-permute-start | bytes 1572872 | tf_op jit(solution)/shard_map/ppermute | solution.py:20
  50.3 14.2 %collective-permute-start.9 = (bf16[2,512,128]{2,1,0:T(8,128)(2,1)S(1)}, bf16[2,512,128]{2,1,0:T(8,128)(2,1)S(1)}, u32[]{:S(2)}, u32[]{:S(2)}) collective-permute-start(bf16[2,512,128]{2,1,0:T(8,128)(2,1)S(1)} %get-tuple-element.48.refs_3_.refs_5_), channel_id=1, source_target_pairs={{0,32},{32,64},{64,96},{96,128},{128,160},{160,192},{192,224},{224... | collective-permute-start | bytes 786440 | tf_op jit(solution)/shard_map/ppermute | solution.py:20
  53.4 12.1 %collective-permute-start.13 = (bf16[2,512,128]{2,1,0:T(8,128)(2,1)S(1)}, bf16[2,512,128]{2,1,0:T(8,128)(2,1)S(1)}, u32[]{:S(2)}, u32[]{:S(2)}) collective-permute-start(bf16[2,512,128]{2,1,0:T(8,128)(2,1)S(1)} %collective-permute-done.12.refs_8_.refs_13_), channel_id=1, source_target_pairs={{0,224},{32,0},{64,32},{96,64},{128,96},{160,128},{192,160},{224,1... | collective-permute-start | bytes 786440 | tf_op jit(solution)/shard_map/ppermute | solution.py:20
  58.9 18.0 %collective-permute-start.17 = (bf16[2,512,128]{2,1,0:T(8,128)(2,1)S(1)}, bf16[2,512,128]{2,1,0:T(8,128)(2,1)S(1)}, u32[]{:S(2)}, u32[]{:S(2)}) collective-permute-start(bf16[2,512,128]{2,1,0:T(8,128)(2,1)S(1)} %get-tuple-element.48.refs_3_.refs_5_), channel_id=1, source_target_pairs={{0,224},{32,0},{64,32},{96,64},{128,96},{160,128},{192,160},{224,1... | collective-permute-start | bytes 786440 | tf_op jit(solution)/shard_map/ppermute | solution.py:20
  59.9 17.1 %collective-permute-start.19 = (bf16[2,512,128]{2,1,0:T(8,128)(2,1)S(1)}, bf16[2,512,128]{2,1,0:T(8,128)(2,1)}, u32[]{:S(2)}, u32[]{:S(2)}) collective-permute-start(bf16[2,512,128]{2,1,0:T(8,128)(2,1)S(1)} %collective-permute-done.12.refs_8_.refs_13_), channel_id=1, source_target_pairs={{0,32},{32,64},{64,96},{96,128},{128,160},{160,192},{192,224},{224... | collective-permute-start | bytes 786440 | tf_op jit(solution)/shard_map/ppermute | solution.py:20
  64.5 14.5 %collective-permute-start.10 = (bf16[2,512,128]{2,1,0:T(8,128)(2,1)S(1)}, bf16[2,512,128]{2,1,0:T(8,128)(2,1)}, u32[]{:S(2)}, u32[]{:S(2)}) collective-permute-start(bf16[2,512,128]{2,1,0:T(8,128)(2,1)S(1)} %collective-permute-done.9.refs_4_.refs_6_), channel_id=1, source_target_pairs={{0,32},{32,64},{64,96},{96,128},{128,160},{160,192},{192,224},{224... | collective-permute-start | bytes 786440 | tf_op jit(solution)/shard_map/ppermute | solution.py:20
  65.6 13.5 %collective-permute-start.14 = (bf16[2,512,128]{2,1,0:T(8,128)(2,1)S(1)}, bf16[2,512,128]{2,1,0:T(8,128)(2,1)}, u32[]{:S(2)}, u32[]{:S(2)}) collective-permute-start(bf16[2,512,128]{2,1,0:T(8,128)(2,1)S(1)} %collective-permute-done.13.refs_10_.refs_15_), channel_id=1, source_target_pairs={{0,224},{32,0},{64,32},{96,64},{128,96},{160,128},{192,160},{224,1... | collective-permute-start | bytes 786440 | tf_op jit(solution)/shard_map/ppermute | solution.py:20
  69.3 42.3 %all-to-all-start.1 = ((bf16[16,256,256]{2,1,0:T(8,128)(2,1)}), bf16[16,256,256]{2,1,0:T(8,128)(2,1)S(1)}, u32[]{:S(2)}, u32[]{:S(2)}) async-start(bf16[16,256,256]{2,1,0:T(8,128)(2,1)} %copy-done.2), calls=%async_computation.1 | async-start | bytes 4194304 | tf_op jit(solution)/shard_map/all_to_all | solution.py:355
  76.9 9.3 %collective-permute-start.18 = (bf16[2,512,128]{2,1,0:T(8,128)(2,1)S(1)}, bf16[2,512,128]{2,1,0:T(8,128)(2,1)S(1)}, u32[]{:S(2)}, u32[]{:S(2)}) collective-permute-start(bf16[2,512,128]{2,1,0:T(8,128)(2,1)S(1)} %collective-permute-done.17.refs_5_.refs_7_), channel_id=1, source_target_pairs={{0,224},{32,0},{64,32},{96,64},{128,96},{160,128},{192,160},{224,1... | collective-permute-start | bytes 786440 | tf_op jit(solution)/shard_map/ppermute | solution.py:20
  77.0 10.7 %collective-permute-start.20 = (bf16[2,512,128]{2,1,0:T(8,128)(2,1)}, bf16[2,512,128]{2,1,0:T(8,128)(2,1)S(1)}, u32[]{:S(2)}, u32[]{:S(2)}) collective-permute-start(bf16[2,512,128]{2,1,0:T(8,128)(2,1)} %collective-permute-done.19.refs_9_.refs_14_), channel_id=1, source_target_pairs={{0,32},{32,64},{64,96},{96,128},{128,160},{160,192},{192,224},{224... | collective-permute-start | bytes 786440 | tf_op jit(solution)/shard_map/ppermute | solution.py:20
  79.0 14.3 %collective-permute-start.11 = (bf16[2,512,128]{2,1,0:T(8,128)(2,1)}, bf16[2,512,128]{2,1,0:T(8,128)(2,1)S(1)}, u32[]{:S(2)}, u32[]{:S(2)}) collective-permute-start(bf16[2,512,128]{2,1,0:T(8,128)(2,1)} %collective-permute-done.10.refs_6_.refs_8_), channel_id=1, source_target_pairs={{0,32},{32,64},{64,96},{96,128},{128,160},{160,192},{192,224},{224... | collective-permute-start | bytes 786440 | tf_op jit(solution)/shard_map/ppermute | solution.py:20
  79.1 14.2 %collective-permute-start.15 = (bf16[2,512,128]{2,1,0:T(8,128)(2,1)}, bf16[2,512,128]{2,1,0:T(8,128)(2,1)S(1)}, u32[]{:S(2)}, u32[]{:S(2)}) collective-permute-start(bf16[2,512,128]{2,1,0:T(8,128)(2,1)} %collective-permute-done.14.refs_12_.refs_17_), channel_id=1, source_target_pairs={{0,224},{32,0},{64,32},{96,64},{128,96},{160,128},{192,160},{224,1... | collective-permute-start | bytes 786440 | tf_op jit(solution)/shard_map/ppermute | solution.py:20
  86.1 11.2 %collective-permute-start.21 = (bf16[2,512,128]{2,1,0:T(8,128)(2,1)S(1)}, bf16[2,512,128]{2,1,0:T(8,128)(2,1)S(1)}, u32[]{:S(2)}, u32[]{:S(2)}) collective-permute-start(bf16[2,512,128]{2,1,0:T(8,128)(2,1)S(1)} %collective-permute-done.18.refs_7_.refs_9_), channel_id=1, source_target_pairs={{0,224},{32,0},{64,32},{96,64},{128,96},{160,128},{192,160},{224,1... | collective-permute-start | bytes 786440 | tf_op jit(solution)/shard_map/ppermute | solution.py:20
  87.7 11.2 %collective-permute-start.23 = (bf16[2,512,128]{2,1,0:T(8,128)(2,1)S(1)}, bf16[2,512,128]{2,1,0:T(8,128)(2,1)S(1)}, u32[]{:S(2)}, u32[]{:S(2)}) collective-permute-start(bf16[2,512,128]{2,1,0:T(8,128)(2,1)S(1)} %collective-permute-done.20.refs_11_.refs_16_), channel_id=1, source_target_pairs={{0,32},{32,64},{64,96},{96,128},{128,160},{160,192},{192,224},{224... | collective-permute-start | bytes 786440 | tf_op jit(solution)/shard_map/ppermute | solution.py:20
  93.3 10.2 %collective-permute-start.22 = (bf16[2,512,128]{2,1,0:T(8,128)(2,1)S(1)}, bf16[2,512,128]{2,1,0:T(8,128)(2,1)S(1)}, u32[]{:S(2)}, u32[]{:S(2)}) collective-permute-start(bf16[2,512,128]{2,1,0:T(8,128)(2,1)S(1)} %collective-permute-done.11.refs_10_), channel_id=1, source_target_pairs={{0,32},{32,64},{64,96},{96,128},{128,160},{160,192},{192,224},{224... | collective-permute-start | bytes 786440 | tf_op jit(solution)/shard_map/ppermute | solution.py:20
  94.0 9.5 %collective-permute-start.24 = (bf16[2,512,128]{2,1,0:T(8,128)(2,1)S(1)}, bf16[2,512,128]{2,1,0:T(8,128)(2,1)S(1)}, u32[]{:S(2)}, u32[]{:S(2)}) collective-permute-start(bf16[2,512,128]{2,1,0:T(8,128)(2,1)S(1)} %collective-permute-done.15.refs_19_), channel_id=1, source_target_pairs={{0,224},{32,0},{64,32},{96,64},{128,96},{160,128},{192,160},{224,1... | collective-permute-start | bytes 786440 | tf_op jit(solution)/shard_map/ppermute | solution.py:20
  114.1 14.0 %all-to-all-start.2 = ((bf16[4,256,256]{2,1,0:T(8,128)(2,1)}), bf16[4,256,256]{2,1,0:T(8,128)(2,1)S(1)}, u32[]{:S(2)}, u32[]{:S(2)}) async-start(bf16[4,256,256]{2,1,0:T(8,128)(2,1)} %bitcast.15), calls=%async_computation.2 | async-start | bytes 1048576 | tf_op jit(solution)/shard_map/all_to_all | solution.py:30
  118.9 9.0 %collective-permute-start.27 = (bf16[256,256]{1,0:T(8,128)(2,1)S(1)}, bf16[256,256]{1,0:T(8,128)(2,1)S(1)}, u32[]{:S(2)}, u32[]{:S(2)}) collective-permute-start(bf16[256,256]{1,0:T(8,128)(2,1)S(1)} %get-tuple-element.73), channel_id=1, source_target_pairs={{0,12},{4,0},{8,4},{12,8},{1,13},{5,1},{9,5},{13,9},{2,14},{6,2},{... | collective-permute-start | bytes 393224 | tf_op jit(solution)/shard_map/ppermute | solution.py:20
  128.1 14.1 %collective-permute-start.31 = (bf16[1024,256]{1,0:T(8,128)(2,1)S(1)}, bf16[1024,256]{1,0:T(8,128)(2,1)S(1)}, u32[]{:S(2)}, u32[]{:S(2)}) collective-permute-start(bf16[1024,256]{1,0:T(8,128)(2,1)S(1)} %pad_maximum_fusion.3), channel_id=1, source_target_pairs={{0,1},{1,2},{2,3},{3,0},{4,5},{5,6},{6,7},{7,4},{8,9},{9,10},{10,1... | collective-permute-start | bytes 1572872 | tf_op jit(solution)/shard_map/ppermute | solution.py:20
  129.9 12.3 %collective-permute-start.32 = (bf16[1024,256]{1,0:T(8,128)(2,1)S(1)}, bf16[1024,256]{1,0:T(8,128)(2,1)S(1)}, u32[]{:S(2)}, u32[]{:S(2)}) collective-permute-start(bf16[1024,256]{1,0:T(8,128)(2,1)S(1)} %pad_maximum_fusion.3), channel_id=1, source_target_pairs={{0,3},{1,0},{2,1},{3,2},{4,7},{5,4},{6,5},{7,6},{8,11},{9,8},{10,9... | collective-permute-start | bytes 1572872 | tf_op jit(solution)/shard_map/ppermute | solution.py:20
  131.4 12.3 %collective-permute-start.29 = (bf16[1024,256]{1,0:T(8,128)(2,1)S(1)}, bf16[1024,256]{1,0:T(8,128)(2,1)S(1)}, u32[]{:S(2)}, u32[]{:S(2)}) collective-permute-start(bf16[1024,256]{1,0:T(8,128)(2,1)S(1)} %bitcast.38), channel_id=1, source_target_pairs={{0,4},{4,8},{8,12},{12,0},{1,5},{5,9},{9,13},{13,1},{2,6},{6,10},{... | collective-permute-start | bytes 1572872 | tf_op jit(solution)/shard_map/ppermute | solution.py:20
  132.4 13.3 %collective-permute-start.30 = (bf16[1024,256]{1,0:T(8,128)(2,1)S(1)}, bf16[1024,256]{1,0:T(8,128)(2,1)S(1)}, u32[]{:S(2)}, u32[]{:S(2)}) collective-permute-start(bf16[1024,256]{1,0:T(8,128)(2,1)S(1)} %bitcast.39), channel_id=1, source_target_pairs={{0,12},{4,0},{8,4},{12,8},{1,13},{5,1},{9,5},{13,9},{2,14},{6,2},{... | collective-permute-start | bytes 1572872 | tf_op jit(solution)/shard_map/ppermute | solution.py:20
  146.1 7.7 %collective-permute-start.34 = (bf16[512,256]{1,0:T(8,128)(2,1)S(1)}, bf16[512,256]{1,0:T(8,128)(2,1)S(1)}, u32[]{:S(2)}, u32[]{:S(2)}) collective-permute-start(bf16[512,256]{1,0:T(8,128)(2,1)S(1)} %slice.39), channel_id=1, source_target_pairs={{0,12},{4,0},{8,4},{12,8},{1,13},{5,1},{9,5},{13,9},{2,14},{6,2},{... | collective-permute-start | bytes 786440 | tf_op jit(solution)/shard_map/ppermute | solution.py:20
  148.0 7.7 %collective-permute-start.35 = (bf16[512,256]{1,0:T(8,128)(2,1)S(1)}, bf16[512,256]{1,0:T(8,128)(2,1)S(1)}, u32[]{:S(2)}, u32[]{:S(2)}) collective-permute-start(bf16[512,256]{1,0:T(8,128)(2,1)S(1)} %slice.40), channel_id=1, source_target_pairs={{0,1},{1,2},{2,3},{3,0},{4,5},{5,6},{6,7},{7,4},{8,9},{9,10},{10,1... | collective-permute-start | bytes 786440 | tf_op jit(solution)/shard_map/ppermute | solution.py:20
  (24 other events, 150.5 us)

commit v8 on v7

--- a/solution.py
+++ b/solution.py
@@ -26,6 +26,7 @@
 
 def plane_matmul(a, w, finish, out_shape, name, more=(), extra=(), halves=True):
     n = a.shape[0] // 2
+    w = in_vmem(w)
     others = around4(a[n:], "y")
     by_x = lax.all_to_all(jnp.concatenate([a[:n]] * NXY, axis=0), "x", 0, 0, tiled=True)
     by_x, others = lax.optimization_barrier((by_x, others))
@@ -52,9 +53,9 @@
     n_x = sum(len(c) for c in counts)
     x_refs, w_ref = refs[:n_x], refs[n_x]
     sums_ref = refs[n_x + 1] if has_sums else None
-    acc, s_sem = refs[-2:]
+    acc = refs[-1]
     more = refs[n_x + 1 + has_sums : n_x + 1 + has_sums + n_more]
-    outs = refs[n_x + 1 + has_sums + n_more : -2]
+    outs = refs[n_x + 1 + has_sums + n_more : -1]
     y = lax.axis_index("y")
     x = lax.axis_index("x")
     n_steps = len(steps)
@@ -64,9 +65,7 @@
         for count in counts[half]:
             arrays[half] += [(x_refs[i], j) for j in range(count)]
             i += 1
-    if has_sums:
-        sums_copy = pltpu.make_async_copy(sums_ref, acc, s_sem)
-        sums_copy.start()
+    acc = acc if finish is not None else outs[0]
     for half in range(2):
         for k, step in enumerate(steps):
             blocks = arrays[half][NXY * k : NXY * (k + 1)]
@@ -78,29 +77,27 @@
                 else:
                     owner = lax.rem(y + OFFS[j] + NXY, NXY) * NXY + lax.rem(x + OFFS[step] + NXY, NXY)
                 starts.append(pl.multiple_of(owner * 256, 256))
-            if has_sums and half == 0 and k == 0:
-                sums_copy.wait()
             span = slice(half * n, (half + 1) * n)
 
-            def column(g, carry, rows=rows, starts=starts, span=span, first=k == 0 and not has_sums):
+            def column(g, carry, rows=rows, starts=starts, span=span, first=k == 0):
                 weights = jnp.concatenate([w_ref[g, pl.ds(start, 256)] for start in starts], axis=0)
                 value = jnp.dot(rows, weights, preferred_element_type=jnp.float32)
-                acc[g, span] = value if first else acc[g, span] + value
+                if not first:
+                    value = acc[g, span] + value
+                elif has_sums:
+                    value = sums_ref[g, span] + value
+                acc[g, span] = value
                 return carry
 
             lax.fori_loop(0, groups, column, 0)
-    if finish is None:
-        copy = pltpu.make_async_copy(acc, outs[0], s_sem)
-        copy.start()
-        copy.wait()
-    else:
+    if finish is not None:
         finish(acc, *more, *outs)
 
 
 HBM = pl.BlockSpec(memory_space=pltpu.HBM)
 VMEM = pl.BlockSpec(memory_space=pltpu.VMEM)
 SMEM = pl.BlockSpec(memory_space=pltpu.SMEM)
-PARAMS = pltpu.CompilerParams(vmem_limit_bytes=24 * 1024 * 1024)
+PARAMS = pltpu.CompilerParams(vmem_limit_bytes=8 * 1024 * 1024)
 
 
 def in_vmem(a):
@@ -113,15 +110,14 @@
     n, groups = xs[0].shape[1], w.shape[0]
     total = jax.ShapeDtypeStruct((groups, 2 * n, 256), jnp.float32)
     has_sums = sums is not None
-    operands = [in_vmem(v) for v in [*xs, w]] + ([sums] if has_sums else [])
+    operands = [*(xs if finish is None else map(in_vmem, xs)), w] + ([in_vmem(sums)] if has_sums else [])
     return pl.pallas_call(
         lambda *refs: partial_kernel(steps, counts, n, groups, has_sums, len(more), finish, *refs),
         out_shape=total if finish is None else out_shape,
-        in_specs=[VMEM] * (len(xs) + 1) + [HBM] * has_sums + [VMEM] * len(more),
-        out_specs=HBM if finish is None else jax.tree.map(lambda _: VMEM, out_shape),
+        in_specs=[VMEM] * (len(operands) + len(more)),
+        out_specs=VMEM if finish is None else jax.tree.map(lambda _: VMEM, out_shape),
         scratch_shapes=[
             pltpu.VMEM((groups, 2 * n, 256), jnp.float32),
-            pltpu.SemaphoreType.DMA(()),
         ],
         compiler_params=PARAMS,
         name=name + str(steps[0]),
@@ -242,7 +238,7 @@
     def _():
         query = jnp.concatenate([q_buf[side, pl.ds(row, BLK)] for side, row in rows_of], axis=0)
         state = (dense_ref[0], dense_ref[1], dense_ref[2])
-        _, total, acc = lax.fori_loop(3, 6, lambda i, state: dense_step(query, kv_buf.at[i], state), state)
+        _, total, acc = dense_step(query, kv_buf.at[4], state)
         result = (acc / total).astype(jnp.bfloat16)
         for k, (side, row) in enumerate(rows_of):
 
@@ -250,8 +246,11 @@
             def _(k=k, side=side, row=row):
                 o_buf[side, pl.ds(row, BLK)] = result[k * BLK : (k + 1) * BLK]
 
-    for side in range(2):
-        o_refs[side][...] = o_buf[side]
+    copies = [pltpu.make_async_copy(o_buf.at[side], o_refs[side], sem.at[side]) for side in range(2)]
+    for copy in copies:
+        copy.start()
+    for copy in copies:
+        copy.wait()
 
 
 def owned_globals(glob_ref):
@@ -276,10 +275,11 @@
     return new, total, acc
 
 
-def dense_kernel(*refs):
+def dense_kernel(n, has_state, *refs):
     glob_ref, mine_ref, theirs_ref = refs[:3]
-    rings = refs[3:8], refs[8:13]
-    o_ref, kv_buf, q_buf, sem = refs[13:]
+    rings = refs[3 : 3 + n], refs[3 + n : 3 + 2 * n]
+    state_ref = refs[3 + 2 * n]
+    o_ref, kv_buf, q_buf, sem = refs[-4:]
     _, owned, rows_of = owned_globals(glob_ref)
 
     @pl.when(owned[0] | owned[1])
@@ -293,28 +293,33 @@
         for copy in copies:
             copy.wait()
         query = jnp.concatenate([q_buf[side, pl.ds(row, BLK)] for side, row in rows_of], axis=0)
-        shape = (2 * BLK, DH)
-        init = (jnp.full(shape, NEG, jnp.float32), jnp.zeros(shape, jnp.float32), jnp.zeros(shape, jnp.float32))
-        state = lax.fori_loop(0, 5, lambda i, state: dense_step(query, kv_buf.at[i], state), init)
+        if has_state:
+            init = (state_ref[0], state_ref[1], state_ref[2])
+        else:
+            zeros = jnp.zeros((2 * BLK, DH), jnp.float32)
+            init = (zeros + NEG, zeros, zeros)
+        state = lax.fori_loop(0, n, lambda i, state: dense_step(query, kv_buf.at[i], state), init)
         for i, value in enumerate(state):
             o_ref[i] = value
 
 
-def dense(glob, mine, theirs, own, other):
+def dense(glob, mine, theirs, own, other, state=None):
     bf16 = jnp.bfloat16
+    n = len(own)
+    has_state = state is not None
     return pl.pallas_call(
-        dense_kernel,
+        lambda *refs: dense_kernel(n, has_state, *refs),
         out_shape=jax.ShapeDtypeStruct((3, 2 * BLK, DH), jnp.float32),
-        in_specs=[SMEM] + [VMEM] * 12,
+        in_specs=[SMEM] + [HBM] * 2 + [VMEM] * (2 * n + has_state),
         out_specs=VMEM,
         scratch_shapes=[
-            pltpu.VMEM((5, 2, 2, 512, DH), bf16),
+            pltpu.VMEM((n, 2, 2, 512, DH), bf16),
             pltpu.VMEM((2, 512, DH), bf16),
-            pltpu.SemaphoreType.DMA((12,)),
+            pltpu.SemaphoreType.DMA((2 + 2 * n,)),
         ],
         compiler_params=PARAMS,
         name="dense",
-    )(glob, *map(in_vmem, [mine, theirs, *own[:5], *other[:5]]))
+    )(glob, mine, theirs, *map(in_vmem, [*own, *other]), *([state] if has_state else []))
 
 
 def attend(rand, glob, radius, mine, theirs, own, other, started):
@@ -322,8 +327,8 @@
     return pl.pallas_call(
         attend_kernel,
         out_shape=(jax.ShapeDtypeStruct((512, DH), bf16),) * 2,
-        in_specs=[SMEM] * 3 + [VMEM] * 19,
-        out_specs=(VMEM, VMEM),
+        in_specs=[SMEM] * 3 + [HBM] * 2 + [VMEM] * 17,
+        out_specs=(HBM, HBM),
         scratch_shapes=[
             pltpu.VMEM((NZ, 2, 2, 512, DH), bf16),
             pltpu.VMEM((2, 512, DH), bf16),
@@ -333,7 +338,7 @@
         compiler_params=PARAMS,
         cost_estimate=pl.CostEstimate(flops=14000000000, transcendentals=0, bytes_accessed=28000000),
         name="attend",
-    )(rand, glob, radius, in_vmem(mine), in_vmem(theirs), *map(in_vmem, [*own, *other]), started)
+    )(rand, glob, radius, mine, theirs, *map(in_vmem, [*own, *other]), started)
 
 
 def swap(a):
@@ -346,8 +351,8 @@
     ids = jnp.pad(rand.astype(bf16)[None], ((0, 15), (0, DH - 48)))
     heads = jax.ShapeDtypeStruct((2, 512, DH), bf16)
     shapes = (jax.ShapeDtypeStruct((512, DH), bf16), heads, jax.ShapeDtypeStruct((528, DH), bf16), heads)
-    (mine, own, send_q, send_kv), ordered = plane_matmul(
-        tokens, w_qkv.transpose(1, 0, 2), split_heads, shapes, "project", (ids,), order(w_out), False
+    (mine, own, send_q, send_kv), (ordered, rand) = plane_matmul(
+        tokens, w_qkv.transpose(1, 0, 2), split_heads, shapes, "project", (ids,), (order(w_out), rand), False
     )
     own = z_ring(own)
     other = swap(send_kv)
@@ -357,8 +362,9 @@
     theirs = swap(send_q)
     ids, _ = lax.optimization_barrier((theirs[512:], own[1:3]))
     rand = jnp.concatenate([rand, ids[0, :48].astype(jnp.int32)])
-    started = dense(glob_blocks, mine, theirs, own, other)
+    started = dense(glob_blocks, mine, theirs, own[:5], other[:5])
     own[5], other[6], started, rand = lax.optimization_barrier((own[5], other[6], started, rand))
+    started = dense(glob_blocks, mine, theirs, own[5:], other[5:], started)
     own.append(shift(own[5], "z", 1))
     other.append(shift(other[6], "z", -1))
     att = attend(rand, glob_blocks, window_radius, mine, theirs, own, other, started)

time: 160 us -> 156 us (0.975)
  local copies, waits for them, and re-layouts: 17.4 us -> 11.5 us
  waiting for transfers between devices: 52.1 us -> 55 us
    unnamed x34 -> x22, local copies, waits for them, and re-layouts: 15.1 us -> 9.91 us
    ppermute x34, waiting for transfers between devices: 51.3 us -> 54.1 us  [shift(): return lax.ppermute(a, axis, [(i, (i + step) % n) for i in range(n)])]
  transfers between devices with their start and end apart: 40 -> 40, of which waited for: 24 -> 25; matrix products, arithmetic and copies ran while one was open for 2% -> 1% of each run, Pallas kernels for 11% -> 12%
where the time goes in v8:
time: 156 us; the launch traced here: 154 us
  starting transfers between devices  62.8 us (40%)
  waiting for transfers between devices  55 us (35%)
  Pallas kernels  21.9 us (14%)
  local copies, waits for them, and re-layouts  11.5 us (7%)
  other arithmetic  2.75 us (2%)
    ppermute x34, waiting for transfers between devices, shift(): return lax.ppermute(a, axis, [(i, (i + step) % n) for i in range(n)])  54.1 us
    ppermute x34, starting transfers between devices, shift(): return lax.ppermute(a, axis, [(i, (i + step) % n) for i in range(n)])  48.7 us
    pallas_call x6, Pallas kernels, partial_matmul(): pl.pallas_call(lambda *refs: partial_kernel(steps, counts, n, groups, has...  12.1 us
    unnamed x22, local copies, waits for them, and re-layouts  9.91 us
    all_to_all x2, starting transfers between devices, plane_matmul(): lax.all_to_all(jnp.concatenate([a[:n]] * NXY, axis=0), 'x', 0, 0, tiled=T...  8.53 us
    pallas_call x1, Pallas kernels, attend(): pl.pallas_call(attend_kernel, out_shape=(jax.ShapeDtypeStruct((512, DH),...  7 us
    all_to_all x1, starting transfers between devices, body(): w_cols = lax.all_to_all(ordered, ('y', 'x'), 0, 0, tiled=True)  5.57 us
  transfers between devices with their start and end apart: 40, of which 25 were waited for; matrix products, arithmetic and copies ran while one was open for 1% of the time, Pallas kernels for 12%

profile of v8, /device:TPU:24, one launch (start us, length us, event | category | flops | bytes accessed | tf_op | source)
XLA Modules:
  0.0 154.1 jit_solution(2138558492467471596)
XLA Ops:
  2.0 4.3 %all-to-all-start = ((bf16[4,256,256]{2,1,0:T(8,128)(2,1)}), bf16[4,256,256]{2,1,0:T(8,128)(2,1)S(1)}, u32[]{:S(2)}, u32[]{:S(2)}) async-start(bf16[4,256,256]{2,1,0:T(8,128)(2,1)} %bitcast), calls=%async_computation | async-start | bytes 1048576 | tf_op jit(solution)/shard_map/all_to_all | solution.py:31
  9.5 2.8 %collective-permute-done = bf16[256,256]{1,0:T(8,128)(2,1)S(1)} collective-permute-done((bf16[256,256]{1,0:T(8,128)(2,1)S(1)}, bf16[256,256]{1,0:T(8,128)(2,1)S(1)}, u32[]{:S(2)}, u32[]{:S(2)}) %collective-permute-start) | collective-permute-done | bytes 131104 | tf_op jit(solution)/shard_map/ppermute | solution.py:20
  12.4 3.7 %collective-permute-done.1 = bf16[256,256]{1,0:T(8,128)(2,1)S(1)} collective-permute-done((bf16[256,256]{1,0:T(8,128)(2,1)S(1)}, bf16[256,256]{1,0:T(8,128)(2,1)S(1)}, u32[]{:S(2)}, u32[]{:S(2)}) %collective-permute-start.1) | collective-permute-done | bytes 131104 | tf_op jit(solution)/shard_map/ppermute | solution.py:20
  17.7 1.9 %collective-permute-start.5 = (bf16[1024,256]{1,0:T(8,128)(2,1)S(1)}, bf16[1024,256]{1,0:T(8,128)(2,1)}, u32[]{:S(2)}, u32[]{:S(2)}) collective-permute-start(bf16[1024,256]{1,0:T(8,128)(2,1)S(1)} %pad_maximum_fusion.1), channel_id=1, source_target_pairs={{0,1},{1,2},{2,3},{3,0},{4,5},{5,6},{6,7},{7,4},{8,9},{9,10},{10,1... | collective-permute-start | bytes 1572872 | tf_op jit(solution)/shard_map/ppermute | solution.py:20
  25.2 2.8 %copy-done = bf16[4096,3,256]{2,0,1:T(8,128)(2,1)S(1)} copy-done((bf16[4096,3,256]{2,0,1:T(8,128)(2,1)S(1)}, bf16[4096,3,256]{2,0,1:T(8,128)(2,1)}, u32[]{:S(2)}) %copy-start) | copy-done | bytes 6291480
  28.0 1.9 %project0.1.refs_5_ = f32[3,512,256]{2,1,0:T(8,128)S(1)} custom-call(bf16[4,256,256]{2,1,0:T(8,128)(2,1)S(1)} %all-to-all-done, bf16[4,256,256]{2,1,0:T(8,128)(2,1)S(1)} %bitcast.40, bf16[3,4096,256]{2,1,0:T(8,128)(2,1)S(1)} %bitcast.30), custom_call_target="tpu_custom_call" | custom-call | tf_op jit(solution)/shard_map/project0/pallas_call | solution.py:114
  32.7 2.0 %collective-permute-done.4 = bf16[1024,256]{1,0:T(8,128)(2,1)} collective-permute-done((bf16[1024,256]{1,0:T(8,128)(2,1)S(1)}, bf16[1024,256]{1,0:T(8,128)(2,1)}, u32[]{:S(2)}, u32[]{:S(2)}) %collective-permute-start.4) | collective-permute-done | bytes 524320 | tf_op jit(solution)/shard_map/ppermute | solution.py:20
  35.7 2.8 %copy-done.1 = bf16[4096,3,256]{2,0,1:T(8,128)(2,1)S(1)} copy-done((bf16[4096,3,256]{2,0,1:T(8,128)(2,1)S(1)}, bf16[4096,3,256]{2,0,1:T(8,128)(2,1)}, u32[]{:S(2)}) %copy-start.1) | copy-done | bytes 6291480
  38.5 5.3 %project1.1.refs_3_ = f32[3,512,256]{2,1,0:T(8,128)S(1)} custom-call(bf16[4,256,256]{2,1,0:T(8,128)(2,1)} %bitcast.8.refs_0_, bf16[4,256,256]{2,1,0:T(8,128)(2,1)} %bitcast.9.refs_1_, bf16[4,256,256]{2,1,0:T(8,128)(2,1)} %bitcast.10.refs_2_, bf16[4,256,256]{2,1,0:T(8,128)(2,1)} %bitcast.11.refs_3_, bf16[3,4096,256]{2,1,0:T(8,128)(2,1)S(1)} %bitcast.31, ...), custom_call_target="tpu_custom_call" | custom-call | tf_op jit(solution)/shard_map/project1/pallas_call | solution.py:114
  46.8 2.6 %project3.1 = (bf16[512,128]{1,0:T(8,128)(2,1)S(1)}, bf16[2,512,128]{2,1,0:T(8,128)(2,1)S(1)}, bf16[528,128]{1,0:T(8,128)(2,1)}, bf16[2,512,128]{2,1,0:T(8,128)(2,1)S(1)}) custom-call(bf16[4,256,256]{2,1,0:T(8,128)(2,1)S(1)} %bitcast.46, bf16[4,256,256]{2,1,0:T(8,128)(2,1)S(1)} %bitcast.47, bf16[3,4096,256]{2,1,0:T(8,128)(2,1)S(1)} %bitcast.32, ...), custom_call_target="tpu_custom_call" | custom-call | tf_op jit(solution)/shard_map/project3/pallas_call | solution.py:114
  49.4 3.1 %collective-permute-start.9 = (bf16[2,512,128]{2,1,0:T(8,128)(2,1)S(1)}, bf16[2,512,128]{2,1,0:T(8,128)(2,1)S(1)}, u32[]{:S(2)}, u32[]{:S(2)}) collective-permute-start(bf16[2,512,128]{2,1,0:T(8,128)(2,1)S(1)} %get-tuple-element.49.refs_3_.refs_5_), channel_id=1, source_target_pairs={{0,32},{32,64},{64,96},{96,128},{128,160},{160,192},{192,224},{224... | collective-permute-start | bytes 786440 | tf_op jit(solution)/shard_map/ppermute | solution.py:20
  52.5 5.5 %collective-permute-start.13 = (bf16[2,512,128]{2,1,0:T(8,128)(2,1)S(1)}, bf16[2,512,128]{2,1,0:T(8,128)(2,1)S(1)}, u32[]{:S(2)}, u32[]{:S(2)}) collective-permute-start(bf16[2,512,128]{2,1,0:T(8,128)(2,1)S(1)} %collective-permute-done.12.refs_8_.refs_13_), channel_id=1, source_target_pairs={{0,224},{32,0},{64,32},{96,64},{128,96},{160,128},{192,160},{224,1... | collective-permute-start | bytes 786440 | tf_op jit(solution)/shard_map/ppermute | solution.py:20
  60.0 3.6 %collective-permute-done.9.refs_4_.refs_6_ = bf16[2,512,128]{2,1,0:T(8,128)(2,1)S(1)} collective-permute-done((bf16[2,512,128]{2,1,0:T(8,128)(2,1)S(1)}, bf16[2,512,128]{2,1,0:T(8,128)(2,1)S(1)}, u32[]{:S(2)}, u32[]{:S(2)}) %collective-permute-start.9) | collective-permute-done | bytes 262176 | tf_op jit(solution)/shard_map/ppermute | solution.py:20
  64.7 3.7 %collective-permute-start.14 = (bf16[2,512,128]{2,1,0:T(8,128)(2,1)S(1)}, bf16[2,512,128]{2,1,0:T(8,128)(2,1)}, u32[]{:S(2)}, u32[]{:S(2)}) collective-permute-start(bf16[2,512,128]{2,1,0:T(8,128)(2,1)S(1)} %collective-permute-done.13.refs_10_.refs_15_), channel_id=1, source_target_pairs={{0,224},{32,0},{64,32},{96,64},{128,96},{160,128},{192,160},{224,1... | collective-permute-start | bytes 786440 | tf_op jit(solution)/shard_map/ppermute | solution.py:20
  68.4 5.6 %all-to-all-start.1 = ((bf16[16,256,256]{2,1,0:T(8,128)(2,1)}), bf16[16,256,256]{2,1,0:T(8,128)(2,1)S(1)}, u32[]{:S(2)}, u32[]{:S(2)}) async-start(bf16[16,256,256]{2,1,0:T(8,128)(2,1)} %copy-done.2), calls=%async_computation.1 | async-start | bytes 4194304 | tf_op jit(solution)/shard_map/all_to_all | solution.py:360
  74.1 2.0 %collective-permute-start.20 = (bf16[2,512,128]{2,1,0:T(8,128)(2,1)}, bf16[2,512,128]{2,1,0:T(8,128)(2,1)S(1)}, u32[]{:S(2)}, u32[]{:S(2)}) collective-permute-start(bf16[2,512,128]{2,1,0:T(8,128)(2,1)} %collective-permute-done.19.refs_9_.refs_14_), channel_id=1, source_target_pairs={{0,32},{32,64},{64,96},{96,128},{128,160},{160,192},{192,224},{224... | collective-permute-start | bytes 786440 | tf_op jit(solution)/shard_map/ppermute | solution.py:20
  76.2 3.2 %collective-permute-start.15 = (bf16[2,512,128]{2,1,0:T(8,128)(2,1)}, bf16[2,512,128]{2,1,0:T(8,128)(2,1)S(1)}, u32[]{:S(2)}, u32[]{:S(2)}) collective-permute-start(bf16[2,512,128]{2,1,0:T(8,128)(2,1)} %collective-permute-done.14.refs_12_.refs_17_), channel_id=1, source_target_pairs={{0,224},{32,0},{64,32},{96,64},{128,96},{160,128},{192,160},{224,1... | collective-permute-start | bytes 786440 | tf_op jit(solution)/shard_map/ppermute | solution.py:20
  79.4 4.0 %collective-permute-done.18.refs_7_.refs_9_ = bf16[2,512,128]{2,1,0:T(8,128)(2,1)S(1)} collective-permute-done((bf16[2,512,128]{2,1,0:T(8,128)(2,1)}, bf16[2,512,128]{2,1,0:T(8,128)(2,1)S(1)}, u32[]{:S(2)}, u32[]{:S(2)}) %collective-permute-start.18) | collective-permute-done | bytes 262176 | tf_op jit(solution)/shard_map/ppermute | solution.py:20
  86.8 3.5 %collective-permute-done.11.refs_3_.refs_10_ = bf16[2,512,128]{2,1,0:T(8,128)(2,1)S(1)} collective-permute-done((bf16[2,512,128]{2,1,0:T(8,128)(2,1)}, bf16[2,512,128]{2,1,0:T(8,128)(2,1)S(1)}, u32[]{:S(2)}, u32[]{:S(2)}) %collective-permute-start.11) | collective-permute-done | bytes 262176 | tf_op jit(solution)/shard_map/ppermute | solution.py:20
  91.1 2.5 %collective-permute-start.24 = (bf16[2,512,128]{2,1,0:T(8,128)(2,1)S(1)}, bf16[2,512,128]{2,1,0:T(8,128)(2,1)S(1)}, u32[]{:S(2)}, u32[]{:S(2)}) collective-permute-start(bf16[2,512,128]{2,1,0:T(8,128)(2,1)S(1)} %collective-permute-done.15.refs_6_.refs_19_), channel_id=1, source_target_pairs={{0,224},{32,0},{64,32},{96,64},{128,96},{160,128},{192,160},{224,1... | collective-permute-start | bytes 786440 | tf_op jit(solution)/shard_map/ppermute | solution.py:20
  96.8 3.7 %collective-permute-done.22.refs_12_ = bf16[2,512,128]{2,1,0:T(8,128)(2,1)S(1)} collective-permute-done((bf16[2,512,128]{2,1,0:T(8,128)(2,1)S(1)}, bf16[2,512,128]{2,1,0:T(8,128)(2,1)S(1)}, u32[]{:S(2)}, u32[]{:S(2)}) %collective-permute-start.22) | collective-permute-done | bytes 262176 | tf_op jit(solution)/shard_map/ppermute | solution.py:20
  100.6 7.0 %attend.1 = (bf16[512,128]{1,0:T(8,128)(2,1)S(1)}, bf16[512,128]{1,0:T(8,128)(2,1)S(1)}) custom-call(s32[96]{0:T(128)S(1)} %pad_add_fusion.refs_0_, s32[2]{0:T(128)S(1)} %copy-done.5, s32[2]{0:T(128)S(1)} %copy-done.7, bf16[512,128]{1,0:T(8,128)(2,1)S(1)} %get-tuple-element.51.refs_1_.refs_3_, bf16[528,128]{1,0:T(8,128)(2,1)S(1)} %collective-permute-done.16.refs_2_.refs_4_, ...), custom_call_target="tpu_custom_call" | custom-call | flops 14000000000 | bytes 28000000 | tf_op jit(solution)/shard_map/attend/pallas_call | solution.py:327
  111.4 4.2 %all-to-all-start.2 = ((bf16[4,256,256]{2,1,0:T(8,128)(2,1)}), bf16[4,256,256]{2,1,0:T(8,128)(2,1)S(1)}, u32[]{:S(2)}, u32[]{:S(2)}) async-start(bf16[4,256,256]{2,1,0:T(8,128)(2,1)} %bitcast.15), calls=%async_computation.2 | async-start | bytes 1048576 | tf_op jit(solution)/shard_map/all_to_all | solution.py:31
  119.1 2.5 %collective-permute-done.26 = bf16[256,256]{1,0:T(8,128)(2,1)S(1)} collective-permute-done((bf16[256,256]{1,0:T(8,128)(2,1)S(1)}, bf16[256,256]{1,0:T(8,128)(2,1)S(1)}, u32[]{:S(2)}, u32[]{:S(2)}) %collective-permute-start.26) | collective-permute-done | bytes 131104 | tf_op jit(solution)/shard_map/ppermute | solution.py:20
  121.6 3.6 %collective-permute-done.27 = bf16[256,256]{1,0:T(8,128)(2,1)S(1)} collective-permute-done((bf16[256,256]{1,0:T(8,128)(2,1)S(1)}, bf16[256,256]{1,0:T(8,128)(2,1)S(1)}, u32[]{:S(2)}, u32[]{:S(2)}) %collective-permute-start.27) | collective-permute-done | bytes 131104 | tf_op jit(solution)/shard_map/ppermute | solution.py:20
  125.4 1.8 %collective-permute-start.31 = (bf16[1024,256]{1,0:T(8,128)(2,1)S(1)}, bf16[1024,256]{1,0:T(8,128)(2,1)S(1)}, u32[]{:S(2)}, u32[]{:S(2)}) collective-permute-start(bf16[1024,256]{1,0:T(8,128)(2,1)S(1)} %pad_maximum_fusion.3), channel_id=1, source_target_pairs={{0,1},{1,2},{2,3},{3,0},{4,5},{5,6},{6,7},{7,4},{8,9},{9,10},{10,1... | collective-permute-start | bytes 1572872 | tf_op jit(solution)/shard_map/ppermute | solution.py:20
  131.2 8.3 %collective-permute-done.31 = bf16[1024,256]{1,0:T(8,128)(2,1)S(1)} collective-permute-done((bf16[1024,256]{1,0:T(8,128)(2,1)S(1)}, bf16[1024,256]{1,0:T(8,128)(2,1)S(1)}, u32[]{:S(2)}, u32[]{:S(2)}) %collective-permute-start.31) | collective-permute-done | bytes 524320 | tf_op jit(solution)/shard_map/ppermute | solution.py:20
  141.0 2.0 %collective-permute-done.30 = bf16[1024,256]{1,0:T(8,128)(2,1)S(1)} collective-permute-done((bf16[1024,256]{1,0:T(8,128)(2,1)S(1)}, bf16[1024,256]{1,0:T(8,128)(2,1)S(1)}, u32[]{:S(2)}, u32[]{:S(2)}) %collective-permute-start.30) | collective-permute-done | bytes 524320 | tf_op jit(solution)/shard_map/ppermute | solution.py:20
  143.5 1.8 %collective-permute-start.34 = (bf16[512,256]{1,0:T(8,128)(2,1)S(1)}, bf16[512,256]{1,0:T(8,128)(2,1)S(1)}, u32[]{:S(2)}, u32[]{:S(2)}) collective-permute-start(bf16[512,256]{1,0:T(8,128)(2,1)S(1)} %slice.39), channel_id=1, source_target_pairs={{0,12},{4,0},{8,4},{12,8},{1,13},{5,1},{9,5},{13,9},{2,14},{6,2},{... | collective-permute-start | bytes 786440 | tf_op jit(solution)/shard_map/ppermute | solution.py:20
  145.7 3.1 %collective-permute-start.36 = (bf16[512,256]{1,0:T(8,128)(2,1)S(1)}, bf16[512,256]{1,0:T(8,128)(2,1)S(1)}, u32[]{:S(2)}, u32[]{:S(2)}) collective-permute-start(bf16[512,256]{1,0:T(8,128)(2,1)S(1)} %slice.41), channel_id=1, source_target_pairs={{0,3},{1,0},{2,1},{3,2},{4,7},{5,4},{6,5},{7,6},{8,11},{9,8},{10,9... | collective-permute-start | bytes 786440 | tf_op jit(solution)/shard_map/ppermute | solution.py:20
  149.5 1.6 %collective-permute-done.34 = bf16[512,256]{1,0:T(8,128)(2,1)S(1)} collective-permute-done((bf16[512,256]{1,0:T(8,128)(2,1)S(1)}, bf16[512,256]{1,0:T(8,128)(2,1)S(1)}, u32[]{:S(2)}, u32[]{:S(2)}) %collective-permute-start.34) | collective-permute-done | bytes 262176 | tf_op jit(solution)/shard_map/ppermute | solution.py:20
  151.1 1.8 %collective-permute-done.35 = bf16[512,256]{1,0:T(8,128)(2,1)S(1)} collective-permute-done((bf16[512,256]{1,0:T(8,128)(2,1)S(1)}, bf16[512,256]{1,0:T(8,128)(2,1)S(1)}, u32[]{:S(2)}, u32[]{:S(2)}) %collective-permute-start.35) | collective-permute-done | bytes 262176 | tf_op jit(solution)/shard_map/ppermute | solution.py:20
  (99 shorter events, 45.8 us)
Async XLA Ops:
  2.0 14.1 %all-to-all-start = ((bf16[4,256,256]{2,1,0:T(8,128)(2,1)}), bf16[4,256,256]{2,1,0:T(8,128)(2,1)S(1)}, u32[]{:S(2)}, u32[]{:S(2)}) async-start(bf16[4,256,256]{2,1,0:T(8,128)(2,1)} %bitcast), calls=%async_computation | async-start | bytes 1048576 | tf_op jit(solution)/shard_map/all_to_all | solution.py:31
  7.5 8.5 %collective-permute-start.1 = (bf16[256,256]{1,0:T(8,128)(2,1)S(1)}, bf16[256,256]{1,0:T(8,128)(2,1)S(1)}, u32[]{:S(2)}, u32[]{:S(2)}) collective-permute-start(bf16[256,256]{1,0:T(8,128)(2,1)S(1)} %get-tuple-element.77), channel_id=1, source_target_pairs={{0,12},{4,0},{8,4},{12,8},{1,13},{5,1},{9,5},{13,9},{2,14},{6,2},{... | collective-permute-start | bytes 393224 | tf_op jit(solution)/shard_map/ppermute | solution.py:20
  8.3 7.7 %collective-permute-start.2 = (bf16[256,256]{1,0:T(8,128)(2,1)S(1)}, bf16[256,256]{1,0:T(8,128)(2,1)S(1)}, u32[]{:S(2)}, u32[]{:S(2)}) collective-permute-start(bf16[256,256]{1,0:T(8,128)(2,1)S(1)} %get-tuple-element.77), channel_id=1, source_target_pairs={{0,8},{4,12},{8,0},{12,4},{1,9},{5,13},{9,1},{13,5},{2,10},{6,14},... | collective-permute-start | bytes 393224 | tf_op jit(solution)/shard_map/ppermute | solution.py:20
  17.7 13.5 %collective-permute-start.5 = (bf16[1024,256]{1,0:T(8,128)(2,1)S(1)}, bf16[1024,256]{1,0:T(8,128)(2,1)}, u32[]{:S(2)}, u32[]{:S(2)}) collective-permute-start(bf16[1024,256]{1,0:T(8,128)(2,1)S(1)} %pad_maximum_fusion.1), channel_id=1, source_target_pairs={{0,1},{1,2},{2,3},{3,0},{4,5},{5,6},{6,7},{7,4},{8,9},{9,10},{10,1... | collective-permute-start | bytes 1572872 | tf_op jit(solution)/shard_map/ppermute | solution.py:20
  19.6 11.8 %collective-permute-start.6 = (bf16[1024,256]{1,0:T(8,128)(2,1)S(1)}, bf16[1024,256]{1,0:T(8,128)(2,1)}, u32[]{:S(2)}, u32[]{:S(2)}) collective-permute-start(bf16[1024,256]{1,0:T(8,128)(2,1)S(1)} %pad_maximum_fusion.1), channel_id=1, source_target_pairs={{0,3},{1,0},{2,1},{3,2},{4,7},{5,4},{6,5},{7,6},{8,11},{9,8},{10,9... | collective-permute-start | bytes 1572872 | tf_op jit(solution)/shard_map/ppermute | solution.py:20
  21.0 11.7 %collective-permute-start.3 = (bf16[1024,256]{1,0:T(8,128)(2,1)S(1)}, bf16[1024,256]{1,0:T(8,128)(2,1)}, u32[]{:S(2)}, u32[]{:S(2)}) collective-permute-start(bf16[1024,256]{1,0:T(8,128)(2,1)S(1)} %bitcast.36), channel_id=1, source_target_pairs={{0,4},{4,8},{8,12},{12,0},{1,5},{5,9},{9,13},{13,1},{2,6},{6,10},{... | collective-permute-start | bytes 1572872 | tf_op jit(solution)/shard_map/ppermute | solution.py:20
  22.1 12.6 %collective-permute-start.4 = (bf16[1024,256]{1,0:T(8,128)(2,1)S(1)}, bf16[1024,256]{1,0:T(8,128)(2,1)}, u32[]{:S(2)}, u32[]{:S(2)}) collective-permute-start(bf16[1024,256]{1,0:T(8,128)(2,1)S(1)} %bitcast.37), channel_id=1, source_target_pairs={{0,12},{4,0},{8,4},{12,8},{1,13},{5,1},{9,5},{13,9},{2,14},{6,2},{... | collective-permute-start | bytes 1572872 | tf_op jit(solution)/shard_map/ppermute | solution.py:20
  34.7 10.6 %collective-permute-start.7 = (bf16[1024,256]{1,0:T(8,128)(2,1)}, bf16[1024,256]{1,0:T(8,128)(2,1)S(1)}, u32[]{:S(2)}, u32[]{:S(2)}) collective-permute-start(bf16[1024,256]{1,0:T(8,128)(2,1)} %collective-permute-done.3), channel_id=1, source_target_pairs={{0,4},{4,8},{8,12},{12,0},{1,5},{5,9},{9,13},{13,1},{2,6},{6,10},{... | collective-permute-start | bytes 1572872 | tf_op jit(solution)/shard_map/ppermute | solution.py:20
  35.0 11.8 %collective-permute-start.8 = (bf16[1024,256]{1,0:T(8,128)(2,1)}, bf16[1024,256]{1,0:T(8,128)(2,1)S(1)}, u32[]{:S(2)}, u32[]{:S(2)}) collective-permute-start(bf16[1024,256]{1,0:T(8,128)(2,1)} %collective-permute-done.5), channel_id=1, source_target_pairs={{0,1},{1,2},{2,3},{3,0},{4,5},{5,6},{6,7},{7,4},{8,9},{9,10},{10,1... | collective-permute-start | bytes 1572872 | tf_op jit(solution)/shard_map/ppermute | solution.py:20
  49.4 14.2 %collective-permute-start.9 = (bf16[2,512,128]{2,1,0:T(8,128)(2,1)S(1)}, bf16[2,512,128]{2,1,0:T(8,128)(2,1)S(1)}, u32[]{:S(2)}, u32[]{:S(2)}) collective-permute-start(bf16[2,512,128]{2,1,0:T(8,128)(2,1)S(1)} %get-tuple-element.49.refs_3_.refs_5_), channel_id=1, source_target_pairs={{0,32},{32,64},{64,96},{96,128},{128,160},{160,192},{192,224},{224... | collective-permute-start | bytes 786440 | tf_op jit(solution)/shard_map/ppermute | solution.py:20
  52.5 12.1 %collective-permute-start.13 = (bf16[2,512,128]{2,1,0:T(8,128)(2,1)S(1)}, bf16[2,512,128]{2,1,0:T(8,128)(2,1)S(1)}, u32[]{:S(2)}, u32[]{:S(2)}) collective-permute-start(bf16[2,512,128]{2,1,0:T(8,128)(2,1)S(1)} %collective-permute-done.12.refs_8_.refs_13_), channel_id=1, source_target_pairs={{0,224},{32,0},{64,32},{96,64},{128,96},{160,128},{192,160},{224,1... | collective-permute-start | bytes 786440 | tf_op jit(solution)/shard_map/ppermute | solution.py:20
  58.0 16.0 %collective-permute-start.17 = (bf16[2,512,128]{2,1,0:T(8,128)(2,1)S(1)}, bf16[2,512,128]{2,1,0:T(8,128)(2,1)}, u32[]{:S(2)}, u32[]{:S(2)}) collective-permute-start(bf16[2,512,128]{2,1,0:T(8,128)(2,1)S(1)} %get-tuple-element.49.refs_3_.refs_5_), channel_id=1, source_target_pairs={{0,224},{32,0},{64,32},{96,64},{128,96},{160,128},{192,160},{224,1... | collective-permute-start | bytes 786440 | tf_op jit(solution)/shard_map/ppermute | solution.py:20
  59.0 15.1 %collective-permute-start.19 = (bf16[2,512,128]{2,1,0:T(8,128)(2,1)S(1)}, bf16[2,512,128]{2,1,0:T(8,128)(2,1)}, u32[]{:S(2)}, u32[]{:S(2)}) collective-permute-start(bf16[2,512,128]{2,1,0:T(8,128)(2,1)S(1)} %collective-permute-done.12.refs_8_.refs_13_), channel_id=1, source_target_pairs={{0,32},{32,64},{64,96},{96,128},{128,160},{160,192},{192,224},{224... | collective-permute-start | bytes 786440 | tf_op jit(solution)/shard_map/ppermute | solution.py:20
  63.6 12.4 %collective-permute-start.10 = (bf16[2,512,128]{2,1,0:T(8,128)(2,1)S(1)}, bf16[2,512,128]{2,1,0:T(8,128)(2,1)}, u32[]{:S(2)}, u32[]{:S(2)}) collective-permute-start(bf16[2,512,128]{2,1,0:T(8,128)(2,1)S(1)} %collective-permute-done.9.refs_4_.refs_6_), channel_id=1, source_target_pairs={{0,32},{32,64},{64,96},{96,128},{128,160},{160,192},{192,224},{224... | collective-permute-start | bytes 786440 | tf_op jit(solution)/shard_map/ppermute | solution.py:20
  64.7 11.5 %collective-permute-start.14 = (bf16[2,512,128]{2,1,0:T(8,128)(2,1)S(1)}, bf16[2,512,128]{2,1,0:T(8,128)(2,1)}, u32[]{:S(2)}, u32[]{:S(2)}) collective-permute-start(bf16[2,512,128]{2,1,0:T(8,128)(2,1)S(1)} %collective-permute-done.13.refs_10_.refs_15_), channel_id=1, source_target_pairs={{0,224},{32,0},{64,32},{96,64},{128,96},{160,128},{192,160},{224,1... | collective-permute-start | bytes 786440 | tf_op jit(solution)/shard_map/ppermute | solution.py:20
  68.4 40.5 %all-to-all-start.1 = ((bf16[16,256,256]{2,1,0:T(8,128)(2,1)}), bf16[16,256,256]{2,1,0:T(8,128)(2,1)S(1)}, u32[]{:S(2)}, u32[]{:S(2)}) async-start(bf16[16,256,256]{2,1,0:T(8,128)(2,1)} %copy-done.2), calls=%async_computation.1 | async-start | bytes 4194304 | tf_op jit(solution)/shard_map/all_to_all | solution.py:360
  74.0 9.5 %collective-permute-start.18 = (bf16[2,512,128]{2,1,0:T(8,128)(2,1)}, bf16[2,512,128]{2,1,0:T(8,128)(2,1)S(1)}, u32[]{:S(2)}, u32[]{:S(2)}) collective-permute-start(bf16[2,512,128]{2,1,0:T(8,128)(2,1)} %collective-permute-done.17.refs_5_.refs_7_), channel_id=1, source_target_pairs={{0,224},{32,0},{64,32},{96,64},{128,96},{160,128},{192,160},{224,1... | collective-permute-start | bytes 786440 | tf_op jit(solution)/shard_map/ppermute | solution.py:20
  74.1 10.8 %collective-permute-start.20 = (bf16[2,512,128]{2,1,0:T(8,128)(2,1)}, bf16[2,512,128]{2,1,0:T(8,128)(2,1)S(1)}, u32[]{:S(2)}, u32[]{:S(2)}) collective-permute-start(bf16[2,512,128]{2,1,0:T(8,128)(2,1)} %collective-permute-done.19.refs_9_.refs_14_), channel_id=1, source_target_pairs={{0,32},{32,64},{64,96},{96,128},{128,160},{160,192},{192,224},{224... | collective-permute-start | bytes 786440 | tf_op jit(solution)/shard_map/ppermute | solution.py:20
  76.1 14.3 %collective-permute-start.11 = (bf16[2,512,128]{2,1,0:T(8,128)(2,1)}, bf16[2,512,128]{2,1,0:T(8,128)(2,1)S(1)}, u32[]{:S(2)}, u32[]{:S(2)}) collective-permute-start(bf16[2,512,128]{2,1,0:T(8,128)(2,1)} %collective-permute-done.10.refs_6_.refs_8_), channel_id=1, source_target_pairs={{0,32},{32,64},{64,96},{96,128},{128,160},{160,192},{192,224},{224... | collective-permute-start | bytes 786440 | tf_op jit(solution)/shard_map/ppermute | solution.py:20
  76.2 14.2 %collective-permute-start.15 = (bf16[2,512,128]{2,1,0:T(8,128)(2,1)}, bf16[2,512,128]{2,1,0:T(8,128)(2,1)S(1)}, u32[]{:S(2)}, u32[]{:S(2)}) collective-permute-start(bf16[2,512,128]{2,1,0:T(8,128)(2,1)} %collective-permute-done.14.refs_12_.refs_17_), channel_id=1, source_target_pairs={{0,224},{32,0},{64,32},{96,64},{128,96},{160,128},{192,160},{224,1... | collective-permute-start | bytes 786440 | tf_op jit(solution)/shard_map/ppermute | solution.py:20
  83.4 11.2 %collective-permute-start.21 = (bf16[2,512,128]{2,1,0:T(8,128)(2,1)S(1)}, bf16[2,512,128]{2,1,0:T(8,128)(2,1)S(1)}, u32[]{:S(2)}, u32[]{:S(2)}) collective-permute-start(bf16[2,512,128]{2,1,0:T(8,128)(2,1)S(1)} %collective-permute-done.18.refs_7_.refs_9_), channel_id=1, source_target_pairs={{0,224},{32,0},{64,32},{96,64},{128,96},{160,128},{192,160},{224,1... | collective-permute-start | bytes 786440 | tf_op jit(solution)/shard_map/ppermute | solution.py:20
  84.9 11.1 %collective-permute-start.23 = (bf16[2,512,128]{2,1,0:T(8,128)(2,1)S(1)}, bf16[2,512,128]{2,1,0:T(8,128)(2,1)S(1)}, u32[]{:S(2)}, u32[]{:S(2)}) collective-permute-start(bf16[2,512,128]{2,1,0:T(8,128)(2,1)S(1)} %collective-permute-done.20.refs_11_.refs_16_), channel_id=1, source_target_pairs={{0,32},{32,64},{64,96},{96,128},{128,160},{160,192},{192,224},{224... | collective-permute-start | bytes 786440 | tf_op jit(solution)/shard_map/ppermute | solution.py:20
  90.4 10.2 %collective-permute-start.22 = (bf16[2,512,128]{2,1,0:T(8,128)(2,1)S(1)}, bf16[2,512,128]{2,1,0:T(8,128)(2,1)S(1)}, u32[]{:S(2)}, u32[]{:S(2)}) collective-permute-start(bf16[2,512,128]{2,1,0:T(8,128)(2,1)S(1)} %collective-permute-done.11.refs_3_.refs_10_), channel_id=1, source_target_pairs={{0,32},{32,64},{64,96},{96,128},{128,160},{160,192},{192,224},{224... | collective-permute-start | bytes 786440 | tf_op jit(solution)/shard_map/ppermute | solution.py:20
  91.1 9.5 %collective-permute-start.24 = (bf16[2,512,128]{2,1,0:T(8,128)(2,1)S(1)}, bf16[2,512,128]{2,1,0:T(8,128)(2,1)S(1)}, u32[]{:S(2)}, u32[]{:S(2)}) collective-permute-start(bf16[2,512,128]{2,1,0:T(8,128)(2,1)S(1)} %collective-permute-done.15.refs_6_.refs_19_), channel_id=1, source_target_pairs={{0,224},{32,0},{64,32},{96,64},{128,96},{160,128},{192,160},{224,1... | collective-permute-start | bytes 786440 | tf_op jit(solution)/shard_map/ppermute | solution.py:20
  111.4 14.0 %all-to-all-start.2 = ((bf16[4,256,256]{2,1,0:T(8,128)(2,1)}), bf16[4,256,256]{2,1,0:T(8,128)(2,1)S(1)}, u32[]{:S(2)}, u32[]{:S(2)}) async-start(bf16[4,256,256]{2,1,0:T(8,128)(2,1)} %bitcast.15), calls=%async_computation.2 | async-start | bytes 1048576 | tf_op jit(solution)/shard_map/all_to_all | solution.py:31
  116.2 9.0 %collective-permute-start.27 = (bf16[256,256]{1,0:T(8,128)(2,1)S(1)}, bf16[256,256]{1,0:T(8,128)(2,1)S(1)}, u32[]{:S(2)}, u32[]{:S(2)}) collective-permute-start(bf16[256,256]{1,0:T(8,128)(2,1)S(1)} %get-tuple-element.75), channel_id=1, source_target_pairs={{0,12},{4,0},{8,4},{12,8},{1,13},{5,1},{9,5},{13,9},{2,14},{6,2},{... | collective-permute-start | bytes 393224 | tf_op jit(solution)/shard_map/ppermute | solution.py:20
  125.4 14.1 %collective-permute-start.31 = (bf16[1024,256]{1,0:T(8,128)(2,1)S(1)}, bf16[1024,256]{1,0:T(8,128)(2,1)S(1)}, u32[]{:S(2)}, u32[]{:S(2)}) collective-permute-start(bf16[1024,256]{1,0:T(8,128)(2,1)S(1)} %pad_maximum_fusion.3), channel_id=1, source_target_pairs={{0,1},{1,2},{2,3},{3,0},{4,5},{5,6},{6,7},{7,4},{8,9},{9,10},{10,1... | collective-permute-start | bytes 1572872 | tf_op jit(solution)/shard_map/ppermute | solution.py:20
  127.2 12.3 %collective-permute-start.32 = (bf16[1024,256]{1,0:T(8,128)(2,1)S(1)}, bf16[1024,256]{1,0:T(8,128)(2,1)S(1)}, u32[]{:S(2)}, u32[]{:S(2)}) collective-permute-start(bf16[1024,256]{1,0:T(8,128)(2,1)S(1)} %pad_maximum_fusion.3), channel_id=1, source_target_pairs={{0,3},{1,0},{2,1},{3,2},{4,7},{5,4},{6,5},{7,6},{8,11},{9,8},{10,9... | collective-permute-start | bytes 1572872 | tf_op jit(solution)/shard_map/ppermute | solution.py:20
  128.8 12.3 %collective-permute-start.29 = (bf16[1024,256]{1,0:T(8,128)(2,1)S(1)}, bf16[1024,256]{1,0:T(8,128)(2,1)S(1)}, u32[]{:S(2)}, u32[]{:S(2)}) collective-permute-start(bf16[1024,256]{1,0:T(8,128)(2,1)S(1)} %bitcast.38), channel_id=1, source_target_pairs={{0,4},{4,8},{8,12},{12,0},{1,5},{5,9},{9,13},{13,1},{2,6},{6,10},{... | collective-permute-start | bytes 1572872 | tf_op jit(solution)/shard_map/ppermute | solution.py:20
  129.7 13.3 %collective-permute-start.30 = (bf16[1024,256]{1,0:T(8,128)(2,1)S(1)}, bf16[1024,256]{1,0:T(8,128)(2,1)S(1)}, u32[]{:S(2)}, u32[]{:S(2)}) collective-permute-start(bf16[1024,256]{1,0:T(8,128)(2,1)S(1)} %bitcast.39), channel_id=1, source_target_pairs={{0,12},{4,0},{8,4},{12,8},{1,13},{5,1},{9,5},{13,9},{2,14},{6,2},{... | collective-permute-start | bytes 1572872 | tf_op jit(solution)/shard_map/ppermute | solution.py:20
  143.5 7.7 %collective-permute-start.34 = (bf16[512,256]{1,0:T(8,128)(2,1)S(1)}, bf16[512,256]{1,0:T(8,128)(2,1)S(1)}, u32[]{:S(2)}, u32[]{:S(2)}) collective-permute-start(bf16[512,256]{1,0:T(8,128)(2,1)S(1)} %slice.39), channel_id=1, source_target_pairs={{0,12},{4,0},{8,4},{12,8},{1,13},{5,1},{9,5},{13,9},{2,14},{6,2},{... | collective-permute-start | bytes 786440 | tf_op jit(solution)/shard_map/ppermute | solution.py:20
  145.3 7.7 %collective-permute-start.35 = (bf16[512,256]{1,0:T(8,128)(2,1)S(1)}, bf16[512,256]{1,0:T(8,128)(2,1)S(1)}, u32[]{:S(2)}, u32[]{:S(2)}) collective-permute-start(bf16[512,256]{1,0:T(8,128)(2,1)S(1)} %slice.40), channel_id=1, source_target_pairs={{0,1},{1,2},{2,3},{3,0},{4,5},{5,6},{6,7},{7,4},{8,9},{9,10},{10,1... | collective-permute-start | bytes 786440 | tf_op jit(solution)/shard_map/ppermute | solution.py:20
  (18 other events, 115.1 us)

commit v9 on v8

--- a/solution.py
+++ b/solution.py
@@ -37,13 +37,15 @@
         return v.reshape(-1, n, 256)
 
     sums = partial_matmul((0,), [[blocks(v)] for v in near], w, None, name)
-    far, sums, extra = lax.optimization_barrier((far, sums, extra))
+    lows, highs = zip(*far)
+    lows, sums, extra = lax.optimization_barrier((lows, sums, extra))
     last = []
-    for (low, high), second in zip(far, "yx"):
+    for low, high, second in zip(lows, highs, "yx"):
         if halves:
             last.append((shift(low[: 2 * n], second, 1), shift(high[2 * n :], second, -1)))
         else:
             last.append((shift(low, second, 1),))
+    far = list(zip(lows, highs))
     sums = partial_matmul((1, 2), [[blocks(v) for v in f] for f in far], w, sums, name)
     out = partial_matmul((3,), [[blocks(v) for v in f] for f in last], w, sums, name, finish, out_shape, more)
     return out, extra

time: 156 us -> 154 us (0.987)
  waiting for transfers between devices: 55 us -> 50.2 us
  starting transfers between devices: 62.8 us -> 65.8 us
    ppermute x34, waiting for transfers between devices: 54.1 us -> 48.5 us  [shift(): return lax.ppermute(a, axis, [(i, (i + step) % n) for i in range(n)])]
    ppermute x34, starting transfers between devices: 48.7 us -> 51.6 us  [shift(): return lax.ppermute(a, axis, [(i, (i + step) % n) for i in range(n)])]
  transfers between devices with their start and end apart: 40 -> 40, of which waited for: 25 -> 20; matrix products, arithmetic and copies ran while one was open for 1% -> 0% of each run, Pallas kernels for 12% -> 12%
where the time goes in v9:
time: 154 us; the launch traced here: 153 us
  starting transfers between devices  65.8 us (43%)
  waiting for transfers between devices  50.2 us (33%)
  Pallas kernels  22.9 us (15%)
  local copies, waits for them, and re-layouts  11.1 us (7%)
  other arithmetic  2.75 us (2%)
    ppermute x34, starting transfers between devices, shift(): return lax.ppermute(a, axis, [(i, (i + step) % n) for i in range(n)])  51.6 us
    ppermute x34, waiting for transfers between devices, shift(): return lax.ppermute(a, axis, [(i, (i + step) % n) for i in range(n)])  48.5 us
    pallas_call x6, Pallas kernels, partial_matmul(): pl.pallas_call(lambda *refs: partial_kernel(steps, counts, n, groups, has...  13.1 us
    unnamed x22, local copies, waits for them, and re-layouts  9.53 us
    all_to_all x2, starting transfers between devices, plane_matmul(): lax.all_to_all(jnp.concatenate([a[:n]] * NXY, axis=0), 'x', 0, 0, tiled=T...  8.53 us
    pallas_call x1, Pallas kernels, attend(): pl.pallas_call(attend_kernel, out_shape=(jax.ShapeDtypeStruct((512, DH),...  7 us
    all_to_all x1, starting transfers between devices, body(): w_cols = lax.all_to_all(ordered, ('y', 'x'), 0, 0, tiled=True)  5.64 us
  transfers between devices with their start and end apart: 40, of which 20 were waited for; matrix products, arithmetic and copies ran while one was open for 0% of the time, Pallas kernels for 12%

profile of v9, /device:TPU:24, one launch (start us, length us, event | category | flops | bytes accessed | tf_op | source)
XLA Modules:
  0.0 153.1 jit_solution(1270075855745275874)
XLA Ops:
  2.0 4.3 %all-to-all-start = ((bf16[4,256,256]{2,1,0:T(8,128)(2,1)}), bf16[4,256,256]{2,1,0:T(8,128)(2,1)S(1)}, u32[]{:S(2)}, u32[]{:S(2)}) async-start(bf16[4,256,256]{2,1,0:T(8,128)(2,1)} %bitcast), calls=%async_computation | async-start | bytes 1048576 | tf_op jit(solution)/shard_map/all_to_all | solution.py:31
  9.5 2.8 %collective-permute-done = bf16[256,256]{1,0:T(8,128)(2,1)S(1)} collective-permute-done((bf16[256,256]{1,0:T(8,128)(2,1)S(1)}, bf16[256,256]{1,0:T(8,128)(2,1)S(1)}, u32[]{:S(2)}, u32[]{:S(2)}) %collective-permute-start) | collective-permute-done | bytes 131104 | tf_op jit(solution)/shard_map/ppermute | solution.py:20
  12.4 3.7 %collective-permute-done.1 = bf16[256,256]{1,0:T(8,128)(2,1)S(1)} collective-permute-done((bf16[256,256]{1,0:T(8,128)(2,1)S(1)}, bf16[256,256]{1,0:T(8,128)(2,1)S(1)}, u32[]{:S(2)}, u32[]{:S(2)}) %collective-permute-start.1) | collective-permute-done | bytes 131104 | tf_op jit(solution)/shard_map/ppermute | solution.py:20
  17.0 1.9 %collective-permute-start.4 = (bf16[1024,256]{1,0:T(8,128)(2,1)S(1)}, bf16[1024,256]{1,0:T(8,128)(2,1)}, u32[]{:S(2)}, u32[]{:S(2)}) collective-permute-start(bf16[1024,256]{1,0:T(8,128)(2,1)S(1)} %pad_maximum_fusion.1), channel_id=1, source_target_pairs={{0,1},{1,2},{2,3},{3,0},{4,5},{5,6},{6,7},{7,4},{8,9},{9,10},{10,1... | collective-permute-start | bytes 1572872 | tf_op jit(solution)/shard_map/ppermute | solution.py:20
  24.6 2.8 %copy-done = bf16[4096,3,256]{2,0,1:T(8,128)(2,1)S(1)} copy-done((bf16[4096,3,256]{2,0,1:T(8,128)(2,1)S(1)}, bf16[4096,3,256]{2,0,1:T(8,128)(2,1)}, u32[]{:S(2)}) %copy-start) | copy-done | bytes 6291480
  27.4 1.9 %project0.1.refs_5_ = f32[3,512,256]{2,1,0:T(8,128)S(1)} custom-call(bf16[4,256,256]{2,1,0:T(8,128)(2,1)S(1)} %all-to-all-done, bf16[4,256,256]{2,1,0:T(8,128)(2,1)S(1)} %bitcast.40, bf16[3,4096,256]{2,1,0:T(8,128)(2,1)S(1)} %bitcast.30), custom_call_target="tpu_custom_call" | custom-call | tf_op jit(solution)/shard_map/project0/pallas_call | solution.py:116
  30.9 2.3 %collective-permute-start.5 = (bf16[1024,256]{1,0:T(8,128)(2,1)}, bf16[1024,256]{1,0:T(8,128)(2,1)}, u32[]{:S(2)}, u32[]{:S(2)}) collective-permute-start(bf16[1024,256]{1,0:T(8,128)(2,1)} %collective-permute-done.3), channel_id=1, source_target_pairs={{0,4},{4,8},{8,12},{12,0},{1,5},{5,9},{9,13},{13,1},{2,6},{6,10},{... | collective-permute-start | bytes 1572872 | tf_op jit(solution)/shard_map/ppermute | solution.py:20
  36.5 2.8 %copy-done.1 = bf16[4096,3,256]{2,0,1:T(8,128)(2,1)S(1)} copy-done((bf16[4096,3,256]{2,0,1:T(8,128)(2,1)S(1)}, bf16[4096,3,256]{2,0,1:T(8,128)(2,1)}, u32[]{:S(2)}) %copy-start.1) | copy-done | bytes 6291480
  40.3 5.1 %project1.1.refs_3_ = f32[3,512,256]{2,1,0:T(8,128)S(1)} custom-call(bf16[4,256,256]{2,1,0:T(8,128)(2,1)} %bitcast.8.refs_0_, bf16[4,256,256]{2,1,0:T(8,128)(2,1)} %bitcast.9.refs_1_, bf16[4,256,256]{2,1,0:T(8,128)(2,1)} %bitcast.10.refs_2_, bf16[4,256,256]{2,1,0:T(8,128)(2,1)S(1)} %bitcast.46, bf16[3,4096,256]{2,1,0:T(8,128)(2,1)S(1)} %bitcast.31, ...), custom_call_target="tpu_custom_call" | custom-call | tf_op jit(solution)/shard_map/project1/pallas_call | solution.py:116
  45.4 3.8 %project3.1 = (bf16[512,128]{1,0:T(8,128)(2,1)S(1)}, bf16[2,512,128]{2,1,0:T(8,128)(2,1)S(1)}, bf16[528,128]{1,0:T(8,128)(2,1)}, bf16[2,512,128]{2,1,0:T(8,128)(2,1)S(1)}) custom-call(bf16[4,256,256]{2,1,0:T(8,128)(2,1)} %bitcast.6.refs_0_, bf16[4,256,256]{2,1,0:T(8,128)(2,1)} %bitcast.7.refs_1_, bf16[3,4096,256]{2,1,0:T(8,128)(2,1)S(1)} %bitcast.32, ...), custom_call_target="tpu_custom_call" | custom-call | tf_op jit(solution)/shard_map/project3/pallas_call | solution.py:116
  49.2 2.7 %collective-permute-start.9 = (bf16[2,512,128]{2,1,0:T(8,128)(2,1)S(1)}, bf16[2,512,128]{2,1,0:T(8,128)(2,1)S(1)}, u32[]{:S(2)}, u32[]{:S(2)}) collective-permute-start(bf16[2,512,128]{2,1,0:T(8,128)(2,1)S(1)} %get-tuple-element.43.refs_3_.refs_5_), channel_id=1, source_target_pairs={{0,32},{32,64},{64,96},{96,128},{128,160},{160,192},{192,224},{224... | collective-permute-start | bytes 786440 | tf_op jit(solution)/shard_map/ppermute | solution.py:20
  52.0 5.5 %collective-permute-start.13 = (bf16[2,512,128]{2,1,0:T(8,128)(2,1)S(1)}, bf16[2,512,128]{2,1,0:T(8,128)(2,1)S(1)}, u32[]{:S(2)}, u32[]{:S(2)}) collective-permute-start(bf16[2,512,128]{2,1,0:T(8,128)(2,1)S(1)} %collective-permute-done.12.refs_8_.refs_13_), channel_id=1, source_target_pairs={{0,224},{32,0},{64,32},{96,64},{128,96},{160,128},{192,160},{224,1... | collective-permute-start | bytes 786440 | tf_op jit(solution)/shard_map/ppermute | solution.py:20
  59.5 3.6 %collective-permute-done.9.refs_4_.refs_6_ = bf16[2,512,128]{2,1,0:T(8,128)(2,1)S(1)} collective-permute-done((bf16[2,512,128]{2,1,0:T(8,128)(2,1)S(1)}, bf16[2,512,128]{2,1,0:T(8,128)(2,1)S(1)}, u32[]{:S(2)}, u32[]{:S(2)}) %collective-permute-start.9) | collective-permute-done | bytes 262176 | tf_op jit(solution)/shard_map/ppermute | solution.py:20
  64.1 3.7 %collective-permute-start.14 = (bf16[2,512,128]{2,1,0:T(8,128)(2,1)S(1)}, bf16[2,512,128]{2,1,0:T(8,128)(2,1)}, u32[]{:S(2)}, u32[]{:S(2)}) collective-permute-start(bf16[2,512,128]{2,1,0:T(8,128)(2,1)S(1)} %collective-permute-done.13.refs_10_.refs_15_), channel_id=1, source_target_pairs={{0,224},{32,0},{64,32},{96,64},{128,96},{160,128},{192,160},{224,1... | collective-permute-start | bytes 786440 | tf_op jit(solution)/shard_map/ppermute | solution.py:20
  67.8 5.6 %all-to-all-start.1 = ((bf16[16,256,256]{2,1,0:T(8,128)(2,1)}), bf16[16,256,256]{2,1,0:T(8,128)(2,1)S(1)}, u32[]{:S(2)}, u32[]{:S(2)}) async-start(bf16[16,256,256]{2,1,0:T(8,128)(2,1)} %copy-done.2), calls=%async_computation.1 | async-start | bytes 4194304 | tf_op jit(solution)/shard_map/all_to_all | solution.py:362
  73.6 2.0 %collective-permute-start.20 = (bf16[2,512,128]{2,1,0:T(8,128)(2,1)}, bf16[2,512,128]{2,1,0:T(8,128)(2,1)S(1)}, u32[]{:S(2)}, u32[]{:S(2)}) collective-permute-start(bf16[2,512,128]{2,1,0:T(8,128)(2,1)} %collective-permute-done.19.refs_9_.refs_14_), channel_id=1, source_target_pairs={{0,32},{32,64},{64,96},{96,128},{128,160},{160,192},{192,224},{224... | collective-permute-start | bytes 786440 | tf_op jit(solution)/shard_map/ppermute | solution.py:20
  75.7 3.2 %collective-permute-start.15 = (bf16[2,512,128]{2,1,0:T(8,128)(2,1)}, bf16[2,512,128]{2,1,0:T(8,128)(2,1)S(1)}, u32[]{:S(2)}, u32[]{:S(2)}) collective-permute-start(bf16[2,512,128]{2,1,0:T(8,128)(2,1)} %collective-permute-done.14.refs_12_.refs_17_), channel_id=1, source_target_pairs={{0,224},{32,0},{64,32},{96,64},{128,96},{160,128},{192,160},{224,1... | collective-permute-start | bytes 786440 | tf_op jit(solution)/shard_map/ppermute | solution.py:20
  78.9 4.0 %collective-permute-done.18.refs_7_.refs_9_ = bf16[2,512,128]{2,1,0:T(8,128)(2,1)S(1)} collective-permute-done((bf16[2,512,128]{2,1,0:T(8,128)(2,1)}, bf16[2,512,128]{2,1,0:T(8,128)(2,1)S(1)}, u32[]{:S(2)}, u32[]{:S(2)}) %collective-permute-start.18) | collective-permute-done | bytes 262176 | tf_op jit(solution)/shard_map/ppermute | solution.py:20
  86.4 3.5 %collective-permute-done.11.refs_3_.refs_10_ = bf16[2,512,128]{2,1,0:T(8,128)(2,1)S(1)} collective-permute-done((bf16[2,512,128]{2,1,0:T(8,128)(2,1)}, bf16[2,512,128]{2,1,0:T(8,128)(2,1)S(1)}, u32[]{:S(2)}, u32[]{:S(2)}) %collective-permute-start.11) | collective-permute-done | bytes 262176 | tf_op jit(solution)/shard_map/ppermute | solution.py:20
  90.6 2.5 %collective-permute-start.24 = (bf16[2,512,128]{2,1,0:T(8,128)(2,1)S(1)}, bf16[2,512,128]{2,1,0:T(8,128)(2,1)S(1)}, u32[]{:S(2)}, u32[]{:S(2)}) collective-permute-start(bf16[2,512,128]{2,1,0:T(8,128)(2,1)S(1)} %collective-permute-done.15.refs_6_.refs_19_), channel_id=1, source_target_pairs={{0,224},{32,0},{64,32},{96,64},{128,96},{160,128},{192,160},{224,1... | collective-permute-start | bytes 786440 | tf_op jit(solution)/shard_map/ppermute | solution.py:20
  96.3 3.7 %collective-permute-done.22.refs_12_ = bf16[2,512,128]{2,1,0:T(8,128)(2,1)S(1)} collective-permute-done((bf16[2,512,128]{2,1,0:T(8,128)(2,1)S(1)}, bf16[2,512,128]{2,1,0:T(8,128)(2,1)S(1)}, u32[]{:S(2)}, u32[]{:S(2)}) %collective-permute-start.22) | collective-permute-done | bytes 262176 | tf_op jit(solution)/shard_map/ppermute | solution.py:20
  100.1 7.0 %attend.1 = (bf16[512,128]{1,0:T(8,128)(2,1)S(1)}, bf16[512,128]{1,0:T(8,128)(2,1)S(1)}) custom-call(s32[96]{0:T(128)S(1)} %pad_add_fusion.refs_0_, s32[2]{0:T(128)S(1)} %copy-done.6, s32[2]{0:T(128)S(1)} %copy-done.8, bf16[512,128]{1,0:T(8,128)(2,1)S(1)} %get-tuple-element.45.refs_1_.refs_3_, bf16[528,128]{1,0:T(8,128)(2,1)S(1)} %collective-permute-done.16.refs_2_.refs_4_, ...), custom_call_target="tpu_custom_call" | custom-call | flops 14000000000 | bytes 28000000 | tf_op jit(solution)/shard_map/attend/pallas_call | solution.py:329
  110.2 4.2 %all-to-all-start.2 = ((bf16[4,256,256]{2,1,0:T(8,128)(2,1)}), bf16[4,256,256]{2,1,0:T(8,128)(2,1)S(1)}, u32[]{:S(2)}, u32[]{:S(2)}) async-start(bf16[4,256,256]{2,1,0:T(8,128)(2,1)} %bitcast.15), calls=%async_computation.2 | async-start | bytes 1048576 | tf_op jit(solution)/shard_map/all_to_all | solution.py:31
  117.9 2.5 %collective-permute-done.26 = bf16[256,256]{1,0:T(8,128)(2,1)S(1)} collective-permute-done((bf16[256,256]{1,0:T(8,128)(2,1)S(1)}, bf16[256,256]{1,0:T(8,128)(2,1)S(1)}, u32[]{:S(2)}, u32[]{:S(2)}) %collective-permute-start.26) | collective-permute-done | bytes 131104 | tf_op jit(solution)/shard_map/ppermute | solution.py:20
  120.5 3.6 %collective-permute-done.27 = bf16[256,256]{1,0:T(8,128)(2,1)S(1)} collective-permute-done((bf16[256,256]{1,0:T(8,128)(2,1)S(1)}, bf16[256,256]{1,0:T(8,128)(2,1)S(1)}, u32[]{:S(2)}, u32[]{:S(2)}) %collective-permute-start.27) | collective-permute-done | bytes 131104 | tf_op jit(solution)/shard_map/ppermute | solution.py:20
  124.3 1.8 %collective-permute-start.30 = (bf16[1024,256]{1,0:T(8,128)(2,1)S(1)}, bf16[1024,256]{1,0:T(8,128)(2,1)S(1)}, u32[]{:S(2)}, u32[]{:S(2)}) collective-permute-start(bf16[1024,256]{1,0:T(8,128)(2,1)S(1)} %pad_maximum_fusion.3), channel_id=1, source_target_pairs={{0,1},{1,2},{2,3},{3,0},{4,5},{5,6},{6,7},{7,4},{8,9},{9,10},{10,1... | collective-permute-start | bytes 1572872 | tf_op jit(solution)/shard_map/ppermute | solution.py:20
  130.1 8.3 %collective-permute-done.30 = bf16[1024,256]{1,0:T(8,128)(2,1)S(1)} collective-permute-done((bf16[1024,256]{1,0:T(8,128)(2,1)S(1)}, bf16[1024,256]{1,0:T(8,128)(2,1)S(1)}, u32[]{:S(2)}, u32[]{:S(2)}) %collective-permute-start.30) | collective-permute-done | bytes 524320 | tf_op jit(solution)/shard_map/ppermute | solution.py:20
  138.4 2.3 %collective-permute-start.31 = (bf16[512,256]{1,0:T(8,128)(2,1)S(1)}, bf16[512,256]{1,0:T(8,128)(2,1)S(1)}, u32[]{:S(2)}, u32[]{:S(2)}) collective-permute-start(bf16[512,256]{1,0:T(8,128)(2,1)S(1)} %slice.38), channel_id=1, source_target_pairs={{0,4},{4,8},{8,12},{12,0},{1,5},{5,9},{9,13},{13,1},{2,6},{6,10},{... | collective-permute-start | bytes 786440 | tf_op jit(solution)/shard_map/ppermute | solution.py:20
  140.8 1.5 %collective-permute-start.34 = (bf16[512,256]{1,0:T(8,128)(2,1)S(1)}, bf16[512,256]{1,0:T(8,128)(2,1)S(1)}, u32[]{:S(2)}, u32[]{:S(2)}) collective-permute-start(bf16[512,256]{1,0:T(8,128)(2,1)S(1)} %slice.40), channel_id=1, source_target_pairs={{0,1},{1,2},{2,3},{3,0},{4,5},{5,6},{6,7},{7,4},{8,9},{9,10},{10,1... | collective-permute-start | bytes 786440 | tf_op jit(solution)/shard_map/ppermute | solution.py:20
  142.4 1.9 %collective-permute-start.36 = (bf16[512,256]{1,0:T(8,128)(2,1)S(1)}, bf16[512,256]{1,0:T(8,128)(2,1)S(1)}, u32[]{:S(2)}, u32[]{:S(2)}) collective-permute-start(bf16[512,256]{1,0:T(8,128)(2,1)S(1)} %slice.46), channel_id=1, source_target_pairs={{0,3},{1,0},{2,1},{3,2},{4,7},{5,4},{6,5},{7,6},{8,11},{9,8},{10,9... | collective-permute-start | bytes 786440 | tf_op jit(solution)/shard_map/ppermute | solution.py:20
  145.1 3.4 %collective-permute-done.34 = bf16[512,256]{1,0:T(8,128)(2,1)S(1)} collective-permute-done((bf16[512,256]{1,0:T(8,128)(2,1)S(1)}, bf16[512,256]{1,0:T(8,128)(2,1)S(1)}, u32[]{:S(2)}, u32[]{:S(2)}) %collective-permute-start.34) | collective-permute-done | bytes 262176 | tf_op jit(solution)/shard_map/ppermute | solution.py:20
  148.8 3.1 %collective-permute-done.33 = bf16[512,256]{1,0:T(8,128)(2,1)S(1)} collective-permute-done((bf16[512,256]{1,0:T(8,128)(2,1)S(1)}, bf16[512,256]{1,0:T(8,128)(2,1)S(1)}, u32[]{:S(2)}, u32[]{:S(2)}) %collective-permute-start.33) | collective-permute-done | bytes 262176 | tf_op jit(solution)/shard_map/ppermute | solution.py:20
  (99 shorter events, 41.8 us)
Async XLA Ops:
  2.0 14.1 %all-to-all-start = ((bf16[4,256,256]{2,1,0:T(8,128)(2,1)}), bf16[4,256,256]{2,1,0:T(8,128)(2,1)S(1)}, u32[]{:S(2)}, u32[]{:S(2)}) async-start(bf16[4,256,256]{2,1,0:T(8,128)(2,1)} %bitcast), calls=%async_computation | async-start | bytes 1048576 | tf_op jit(solution)/shard_map/all_to_all | solution.py:31
  7.5 8.5 %collective-permute-start.1 = (bf16[256,256]{1,0:T(8,128)(2,1)S(1)}, bf16[256,256]{1,0:T(8,128)(2,1)S(1)}, u32[]{:S(2)}, u32[]{:S(2)}) collective-permute-start(bf16[256,256]{1,0:T(8,128)(2,1)S(1)} %get-tuple-element.69), channel_id=1, source_target_pairs={{0,12},{4,0},{8,4},{12,8},{1,13},{5,1},{9,5},{13,9},{2,14},{6,2},{... | collective-permute-start | bytes 393224 | tf_op jit(solution)/shard_map/ppermute | solution.py:20
  8.3 7.7 %collective-permute-start.2 = (bf16[256,256]{1,0:T(8,128)(2,1)S(1)}, bf16[256,256]{1,0:T(8,128)(2,1)}, u32[]{:S(2)}, u32[]{:S(2)}) collective-permute-start(bf16[256,256]{1,0:T(8,128)(2,1)S(1)} %get-tuple-element.69), channel_id=1, source_target_pairs={{0,8},{4,12},{8,0},{12,4},{1,9},{5,13},{9,1},{13,5},{2,10},{6,14},... | collective-permute-start | bytes 393224 | tf_op jit(solution)/shard_map/ppermute | solution.py:20
  17.0 13.7 %collective-permute-start.4 = (bf16[1024,256]{1,0:T(8,128)(2,1)S(1)}, bf16[1024,256]{1,0:T(8,128)(2,1)}, u32[]{:S(2)}, u32[]{:S(2)}) collective-permute-start(bf16[1024,256]{1,0:T(8,128)(2,1)S(1)} %pad_maximum_fusion.1), channel_id=1, source_target_pairs={{0,1},{1,2},{2,3},{3,0},{4,5},{5,6},{6,7},{7,4},{8,9},{9,10},{10,1... | collective-permute-start | bytes 1572872 | tf_op jit(solution)/shard_map/ppermute | solution.py:20
  18.9 11.9 %collective-permute-start.3 = (bf16[1024,256]{1,0:T(8,128)(2,1)S(1)}, bf16[1024,256]{1,0:T(8,128)(2,1)}, u32[]{:S(2)}, u32[]{:S(2)}) collective-permute-start(bf16[1024,256]{1,0:T(8,128)(2,1)S(1)} %bitcast.36), channel_id=1, source_target_pairs={{0,4},{4,8},{8,12},{12,0},{1,5},{5,9},{9,13},{13,1},{2,6},{6,10},{... | collective-permute-start | bytes 1572872 | tf_op jit(solution)/shard_map/ppermute | solution.py:20
  22.5 12.4 %collective-permute-start.8 = (bf16[1024,256]{1,0:T(8,128)(2,1)S(1)}, bf16[1024,256]{1,0:T(8,128)(2,1)S(1)}, u32[]{:S(2)}, u32[]{:S(2)}) collective-permute-start(bf16[1024,256]{1,0:T(8,128)(2,1)S(1)} %pad_maximum_fusion.1), channel_id=1, source_target_pairs={{0,3},{1,0},{2,1},{3,2},{4,7},{5,4},{6,5},{7,6},{8,11},{9,8},{10,9... | collective-permute-start | bytes 1572872 | tf_op jit(solution)/shard_map/ppermute | solution.py:20
  23.9 12.6 %collective-permute-start.7 = (bf16[1024,256]{1,0:T(8,128)(2,1)S(1)}, bf16[1024,256]{1,0:T(8,128)(2,1)}, u32[]{:S(2)}, u32[]{:S(2)}) collective-permute-start(bf16[1024,256]{1,0:T(8,128)(2,1)S(1)} %bitcast.37), channel_id=1, source_target_pairs={{0,12},{4,0},{8,4},{12,8},{1,13},{5,1},{9,5},{13,9},{2,14},{6,2},{... | collective-permute-start | bytes 1572872 | tf_op jit(solution)/shard_map/ppermute | solution.py:20
  30.9 14.6 %collective-permute-start.5 = (bf16[1024,256]{1,0:T(8,128)(2,1)}, bf16[1024,256]{1,0:T(8,128)(2,1)}, u32[]{:S(2)}, u32[]{:S(2)}) collective-permute-start(bf16[1024,256]{1,0:T(8,128)(2,1)} %collective-permute-done.3), channel_id=1, source_target_pairs={{0,4},{4,8},{8,12},{12,0},{1,5},{5,9},{9,13},{13,1},{2,6},{6,10},{... | collective-permute-start | bytes 1572872 | tf_op jit(solution)/shard_map/ppermute | solution.py:20
  33.2 12.3 %collective-permute-start.6 = (bf16[1024,256]{1,0:T(8,128)(2,1)}, bf16[1024,256]{1,0:T(8,128)(2,1)}, u32[]{:S(2)}, u32[]{:S(2)}) collective-permute-start(bf16[1024,256]{1,0:T(8,128)(2,1)} %collective-permute-done.4), channel_id=1, source_target_pairs={{0,1},{1,2},{2,3},{3,0},{4,5},{5,6},{6,7},{7,4},{8,9},{9,10},{10,1... | collective-permute-start | bytes 1572872 | tf_op jit(solution)/shard_map/ppermute | solution.py:20
  49.2 13.8 %collective-permute-start.9 = (bf16[2,512,128]{2,1,0:T(8,128)(2,1)S(1)}, bf16[2,512,128]{2,1,0:T(8,128)(2,1)S(1)}, u32[]{:S(2)}, u32[]{:S(2)}) collective-permute-start(bf16[2,512,128]{2,1,0:T(8,128)(2,1)S(1)} %get-tuple-element.43.refs_3_.refs_5_), channel_id=1, source_target_pairs={{0,32},{32,64},{64,96},{96,128},{128,160},{160,192},{192,224},{224... | collective-permute-start | bytes 786440 | tf_op jit(solution)/shard_map/ppermute | solution.py:20
  52.0 12.1 %collective-permute-start.13 = (bf16[2,512,128]{2,1,0:T(8,128)(2,1)S(1)}, bf16[2,512,128]{2,1,0:T(8,128)(2,1)S(1)}, u32[]{:S(2)}, u32[]{:S(2)}) collective-permute-start(bf16[2,512,128]{2,1,0:T(8,128)(2,1)S(1)} %collective-permute-done.12.refs_8_.refs_13_), channel_id=1, source_target_pairs={{0,224},{32,0},{64,32},{96,64},{128,96},{160,128},{192,160},{224,1... | collective-permute-start | bytes 786440 | tf_op jit(solution)/shard_map/ppermute | solution.py:20
  57.4 16.0 %collective-permute-start.17 = (bf16[2,512,128]{2,1,0:T(8,128)(2,1)S(1)}, bf16[2,512,128]{2,1,0:T(8,128)(2,1)}, u32[]{:S(2)}, u32[]{:S(2)}) collective-permute-start(bf16[2,512,128]{2,1,0:T(8,128)(2,1)S(1)} %get-tuple-element.43.refs_3_.refs_5_), channel_id=1, source_target_pairs={{0,224},{32,0},{64,32},{96,64},{128,96},{160,128},{192,160},{224,1... | collective-permute-start | bytes 786440 | tf_op jit(solution)/shard_map/ppermute | solution.py:20
  58.4 15.1 %collective-permute-start.19 = (bf16[2,512,128]{2,1,0:T(8,128)(2,1)S(1)}, bf16[2,512,128]{2,1,0:T(8,128)(2,1)}, u32[]{:S(2)}, u32[]{:S(2)}) collective-permute-start(bf16[2,512,128]{2,1,0:T(8,128)(2,1)S(1)} %collective-permute-done.12.refs_8_.refs_13_), channel_id=1, source_target_pairs={{0,32},{32,64},{64,96},{96,128},{128,160},{160,192},{192,224},{224... | collective-permute-start | bytes 786440 | tf_op jit(solution)/shard_map/ppermute | solution.py:20
  63.1 12.5 %collective-permute-start.10 = (bf16[2,512,128]{2,1,0:T(8,128)(2,1)S(1)}, bf16[2,512,128]{2,1,0:T(8,128)(2,1)}, u32[]{:S(2)}, u32[]{:S(2)}) collective-permute-start(bf16[2,512,128]{2,1,0:T(8,128)(2,1)S(1)} %collective-permute-done.9.refs_4_.refs_6_), channel_id=1, source_target_pairs={{0,32},{32,64},{64,96},{96,128},{128,160},{160,192},{192,224},{224... | collective-permute-start | bytes 786440 | tf_op jit(solution)/shard_map/ppermute | solution.py:20
  64.1 11.6 %collective-permute-start.14 = (bf16[2,512,128]{2,1,0:T(8,128)(2,1)S(1)}, bf16[2,512,128]{2,1,0:T(8,128)(2,1)}, u32[]{:S(2)}, u32[]{:S(2)}) collective-permute-start(bf16[2,512,128]{2,1,0:T(8,128)(2,1)S(1)} %collective-permute-done.13.refs_10_.refs_15_), channel_id=1, source_target_pairs={{0,224},{32,0},{64,32},{96,64},{128,96},{160,128},{192,160},{224,1... | collective-permute-start | bytes 786440 | tf_op jit(solution)/shard_map/ppermute | solution.py:20
  67.8 40.0 %all-to-all-start.1 = ((bf16[16,256,256]{2,1,0:T(8,128)(2,1)}), bf16[16,256,256]{2,1,0:T(8,128)(2,1)S(1)}, u32[]{:S(2)}, u32[]{:S(2)}) async-start(bf16[16,256,256]{2,1,0:T(8,128)(2,1)} %copy-done.2), calls=%async_computation.1 | async-start | bytes 4194304 | tf_op jit(solution)/shard_map/all_to_all | solution.py:362
  73.5 9.5 %collective-permute-start.18 = (bf16[2,512,128]{2,1,0:T(8,128)(2,1)}, bf16[2,512,128]{2,1,0:T(8,128)(2,1)S(1)}, u32[]{:S(2)}, u32[]{:S(2)}) collective-permute-start(bf16[2,512,128]{2,1,0:T(8,128)(2,1)} %collective-permute-done.17.refs_5_.refs_7_), channel_id=1, source_target_pairs={{0,224},{32,0},{64,32},{96,64},{128,96},{160,128},{192,160},{224,1... | collective-permute-start | bytes 786440 | tf_op jit(solution)/shard_map/ppermute | solution.py:20
  73.6 10.7 %collective-permute-start.20 = (bf16[2,512,128]{2,1,0:T(8,128)(2,1)}, bf16[2,512,128]{2,1,0:T(8,128)(2,1)S(1)}, u32[]{:S(2)}, u32[]{:S(2)}) collective-permute-start(bf16[2,512,128]{2,1,0:T(8,128)(2,1)} %collective-permute-done.19.refs_9_.refs_14_), channel_id=1, source_target_pairs={{0,32},{32,64},{64,96},{96,128},{128,160},{160,192},{192,224},{224... | collective-permute-start | bytes 786440 | tf_op jit(solution)/shard_map/ppermute | solution.py:20
  75.6 14.3 %collective-permute-start.11 = (bf16[2,512,128]{2,1,0:T(8,128)(2,1)}, bf16[2,512,128]{2,1,0:T(8,128)(2,1)S(1)}, u32[]{:S(2)}, u32[]{:S(2)}) collective-permute-start(bf16[2,512,128]{2,1,0:T(8,128)(2,1)} %collective-permute-done.10.refs_6_.refs_8_), channel_id=1, source_target_pairs={{0,32},{32,64},{64,96},{96,128},{128,160},{160,192},{192,224},{224... | collective-permute-start | bytes 786440 | tf_op jit(solution)/shard_map/ppermute | solution.py:20
  75.7 14.2 %collective-permute-start.15 = (bf16[2,512,128]{2,1,0:T(8,128)(2,1)}, bf16[2,512,128]{2,1,0:T(8,128)(2,1)S(1)}, u32[]{:S(2)}, u32[]{:S(2)}) collective-permute-start(bf16[2,512,128]{2,1,0:T(8,128)(2,1)} %collective-permute-done.14.refs_12_.refs_17_), channel_id=1, source_target_pairs={{0,224},{32,0},{64,32},{96,64},{128,96},{160,128},{192,160},{224,1... | collective-permute-start | bytes 786440 | tf_op jit(solution)/shard_map/ppermute | solution.py:20
  82.9 11.2 %collective-permute-start.21 = (bf16[2,512,128]{2,1,0:T(8,128)(2,1)S(1)}, bf16[2,512,128]{2,1,0:T(8,128)(2,1)S(1)}, u32[]{:S(2)}, u32[]{:S(2)}) collective-permute-start(bf16[2,512,128]{2,1,0:T(8,128)(2,1)S(1)} %collective-permute-done.18.refs_7_.refs_9_), channel_id=1, source_target_pairs={{0,224},{32,0},{64,32},{96,64},{128,96},{160,128},{192,160},{224,1... | collective-permute-start | bytes 786440 | tf_op jit(solution)/shard_map/ppermute | solution.py:20
  84.2 11.2 %collective-permute-start.23 = (bf16[2,512,128]{2,1,0:T(8,128)(2,1)S(1)}, bf16[2,512,128]{2,1,0:T(8,128)(2,1)S(1)}, u32[]{:S(2)}, u32[]{:S(2)}) collective-permute-start(bf16[2,512,128]{2,1,0:T(8,128)(2,1)S(1)} %collective-permute-done.20.refs_11_.refs_16_), channel_id=1, source_target_pairs={{0,32},{32,64},{64,96},{96,128},{128,160},{160,192},{192,224},{224... | collective-permute-start | bytes 786440 | tf_op jit(solution)/shard_map/ppermute | solution.py:20
  89.9 10.2 %collective-permute-start.22 = (bf16[2,512,128]{2,1,0:T(8,128)(2,1)S(1)}, bf16[2,512,128]{2,1,0:T(8,128)(2,1)S(1)}, u32[]{:S(2)}, u32[]{:S(2)}) collective-permute-start(bf16[2,512,128]{2,1,0:T(8,128)(2,1)S(1)} %collective-permute-done.11.refs_3_.refs_10_), channel_id=1, source_target_pairs={{0,32},{32,64},{64,96},{96,128},{128,160},{160,192},{192,224},{224... | collective-permute-start | bytes 786440 | tf_op jit(solution)/shard_map/ppermute | solution.py:20
  90.6 9.5 %collective-permute-start.24 = (bf16[2,512,128]{2,1,0:T(8,128)(2,1)S(1)}, bf16[2,512,128]{2,1,0:T(8,128)(2,1)S(1)}, u32[]{:S(2)}, u32[]{:S(2)}) collective-permute-start(bf16[2,512,128]{2,1,0:T(8,128)(2,1)S(1)} %collective-permute-done.15.refs_6_.refs_19_), channel_id=1, source_target_pairs={{0,224},{32,0},{64,32},{96,64},{128,96},{160,128},{192,160},{224,1... | collective-permute-start | bytes 786440 | tf_op jit(solution)/shard_map/ppermute | solution.py:20
  110.2 14.0 %all-to-all-start.2 = ((bf16[4,256,256]{2,1,0:T(8,128)(2,1)}), bf16[4,256,256]{2,1,0:T(8,128)(2,1)S(1)}, u32[]{:S(2)}, u32[]{:S(2)}) async-start(bf16[4,256,256]{2,1,0:T(8,128)(2,1)} %bitcast.15), calls=%async_computation.2 | async-start | bytes 1048576 | tf_op jit(solution)/shard_map/all_to_all | solution.py:31
  115.0 9.0 %collective-permute-start.27 = (bf16[256,256]{1,0:T(8,128)(2,1)S(1)}, bf16[256,256]{1,0:T(8,128)(2,1)S(1)}, u32[]{:S(2)}, u32[]{:S(2)}) collective-permute-start(bf16[256,256]{1,0:T(8,128)(2,1)S(1)} %get-tuple-element.67), channel_id=1, source_target_pairs={{0,12},{4,0},{8,4},{12,8},{1,13},{5,1},{9,5},{13,9},{2,14},{6,2},{... | collective-permute-start | bytes 393224 | tf_op jit(solution)/shard_map/ppermute | solution.py:20
  124.3 14.1 %collective-permute-start.30 = (bf16[1024,256]{1,0:T(8,128)(2,1)S(1)}, bf16[1024,256]{1,0:T(8,128)(2,1)S(1)}, u32[]{:S(2)}, u32[]{:S(2)}) collective-permute-start(bf16[1024,256]{1,0:T(8,128)(2,1)S(1)} %pad_maximum_fusion.3), channel_id=1, source_target_pairs={{0,1},{1,2},{2,3},{3,0},{4,5},{5,6},{6,7},{7,4},{8,9},{9,10},{10,1... | collective-permute-start | bytes 1572872 | tf_op jit(solution)/shard_map/ppermute | solution.py:20
  126.1 12.3 %collective-permute-start.29 = (bf16[1024,256]{1,0:T(8,128)(2,1)S(1)}, bf16[1024,256]{1,0:T(8,128)(2,1)S(1)}, u32[]{:S(2)}, u32[]{:S(2)}) collective-permute-start(bf16[1024,256]{1,0:T(8,128)(2,1)S(1)} %bitcast.38), channel_id=1, source_target_pairs={{0,4},{4,8},{8,12},{12,0},{1,5},{5,9},{9,13},{13,1},{2,6},{6,10},{... | collective-permute-start | bytes 1572872 | tf_op jit(solution)/shard_map/ppermute | solution.py:20
  127.1 15.3 %collective-permute-start.35 = (bf16[1024,256]{1,0:T(8,128)(2,1)S(1)}, bf16[1024,256]{1,0:T(8,128)(2,1)S(1)}, u32[]{:S(2)}, u32[]{:S(2)}) collective-permute-start(bf16[1024,256]{1,0:T(8,128)(2,1)S(1)} %pad_maximum_fusion.3), channel_id=1, source_target_pairs={{0,3},{1,0},{2,1},{3,2},{4,7},{5,4},{6,5},{7,6},{8,11},{9,8},{10,9... | collective-permute-start | bytes 1572872 | tf_op jit(solution)/shard_map/ppermute | solution.py:20
  128.6 15.7 %collective-permute-start.32 = (bf16[1024,256]{1,0:T(8,128)(2,1)S(1)}, bf16[1024,256]{1,0:T(8,128)(2,1)S(1)}, u32[]{:S(2)}, u32[]{:S(2)}) collective-permute-start(bf16[1024,256]{1,0:T(8,128)(2,1)S(1)} %bitcast.39), channel_id=1, source_target_pairs={{0,12},{4,0},{8,4},{12,8},{1,13},{5,1},{9,5},{13,9},{2,14},{6,2},{... | collective-permute-start | bytes 1572872 | tf_op jit(solution)/shard_map/ppermute | solution.py:20
  140.8 7.7 %collective-permute-start.34 = (bf16[512,256]{1,0:T(8,128)(2,1)S(1)}, bf16[512,256]{1,0:T(8,128)(2,1)S(1)}, u32[]{:S(2)}, u32[]{:S(2)}) collective-permute-start(bf16[512,256]{1,0:T(8,128)(2,1)S(1)} %slice.40), channel_id=1, source_target_pairs={{0,1},{1,2},{2,3},{3,0},{4,5},{5,6},{6,7},{7,4},{8,9},{9,10},{10,1... | collective-permute-start | bytes 786440 | tf_op jit(solution)/shard_map/ppermute | solution.py:20
  144.2 7.7 %collective-permute-start.33 = (bf16[512,256]{1,0:T(8,128)(2,1)S(1)}, bf16[512,256]{1,0:T(8,128)(2,1)S(1)}, u32[]{:S(2)}, u32[]{:S(2)}) collective-permute-start(bf16[512,256]{1,0:T(8,128)(2,1)S(1)} %slice.45), channel_id=1, source_target_pairs={{0,12},{4,0},{8,4},{12,8},{1,13},{5,1},{9,5},{13,9},{2,14},{6,2},{... | collective-permute-start | bytes 786440 | tf_op jit(solution)/shard_map/ppermute | solution.py:20
  (18 other events, 109.9 us)

commit v10 on v9

--- a/solution.py
+++ b/solution.py
@@ -28,7 +28,7 @@
     n = a.shape[0] // 2
     w = in_vmem(w)
     others = around4(a[n:], "y")
-    by_x = lax.all_to_all(jnp.concatenate([a[:n]] * NXY, axis=0), "x", 0, 0, tiled=True)
+    by_x = lax.all_to_all(jnp.broadcast_to(a[:n], (NXY, n, 256)).reshape(NXY * n, 256), "x", 0, 0, tiled=True)
     by_x, others = lax.optimization_barrier((by_x, others))
     near = [by_x, jnp.concatenate([a[n:], *others], axis=0)]
     far = [(shift(stack, second, 1), shift(stack, second, -1)) for stack, second in zip(near, "yx")]

time: 154 us -> 154 us (level)
  local copies, waits for them, and re-layouts: 11.1 us -> 12.8 us
  other arithmetic: 2.75 us -> 1.06 us
    concatenate x2 -> x0, other arithmetic: 1.69 us -> none  [plane_matmul(): jnp.concatenate([a[:n]] * NXY, axis=0)]
    broadcast_in_dim x0 -> x2, local copies, waits for them, and re-layouts: none -> 1.69 us  [plane_matmul(): jnp.broadcast_to(a[:n], (NXY, n, 256)).reshape(NXY * n, 256)]
where the time goes in v10:
time: 154 us; the launch traced here: 153 us
  starting transfers between devices  65.8 us (43%)
  waiting for transfers between devices  50.2 us (33%)
  Pallas kernels  22.9 us (15%)
  local copies, waits for them, and re-layouts  12.8 us (8%)
    ppermute x34, starting transfers between devices, shift(): return lax.ppermute(a, axis, [(i, (i + step) % n) for i in range(n)])  51.6 us
    ppermute x34, waiting for transfers between devices, shift(): return lax.ppermute(a, axis, [(i, (i + step) % n) for i in range(n)])  48.5 us
    pallas_call x6, Pallas kernels, partial_matmul(): pl.pallas_call(lambda *refs: partial_kernel(steps, counts, n, groups, has...  13.1 us
    unnamed x22, local copies, waits for them, and re-layouts  9.53 us
    all_to_all x2, starting transfers between devices, plane_matmul(): lax.all_to_all(jnp.broadcast_to(a[:n], (NXY, n, 256)).reshape(NXY * n, 25...  8.53 us
    pallas_call x1, Pallas kernels, attend(): pl.pallas_call(attend_kernel, out_shape=(jax.ShapeDtypeStruct((512, DH),...  7 us
    all_to_all x1, starting transfers between devices, body(): w_cols = lax.all_to_all(ordered, ('y', 'x'), 0, 0, tiled=True)  5.64 us
  transfers between devices with their start and end apart: 40, of which 20 were waited for; matrix products, arithmetic and copies ran while one was open for 0% of the time, Pallas kernels for 12%

profile of v10, /device:TPU:24, one launch (start us, length us, event | category | flops | bytes accessed | tf_op | source)
XLA Modules:
  0.0 153.1 jit_solution(17619201540103756901)
XLA Ops:
  2.0 4.3 %all-to-all-start = ((bf16[4,256,256]{2,1,0:T(8,128)(2,1)}), bf16[4,256,256]{2,1,0:T(8,128)(2,1)S(1)}, u32[]{:S(2)}, u32[]{:S(2)}) async-start(bf16[4,256,256]{2,1,0:T(8,128)(2,1)} %broadcast_in_dim.10), calls=%async_computation | async-start | bytes 1048576 | tf_op jit(solution)/shard_map/all_to_all | solution.py:31
  9.5 2.8 %collective-permute-done = bf16[256,256]{1,0:T(8,128)(2,1)S(1)} collective-permute-done((bf16[256,256]{1,0:T(8,128)(2,1)S(1)}, bf16[256,256]{1,0:T(8,128)(2,1)S(1)}, u32[]{:S(2)}, u32[]{:S(2)}) %collective-permute-start) | collective-permute-done | bytes 131104 | tf_op jit(solution)/shard_map/ppermute | solution.py:20
  12.4 3.7 %collective-permute-done.1 = bf16[256,256]{1,0:T(8,128)(2,1)S(1)} collective-permute-done((bf16[256,256]{1,0:T(8,128)(2,1)S(1)}, bf16[256,256]{1,0:T(8,128)(2,1)S(1)}, u32[]{:S(2)}, u32[]{:S(2)}) %collective-permute-start.1) | collective-permute-done | bytes 131104 | tf_op jit(solution)/shard_map/ppermute | solution.py:20
  17.0 1.9 %collective-permute-start.4 = (bf16[1024,256]{1,0:T(8,128)(2,1)S(1)}, bf16[1024,256]{1,0:T(8,128)(2,1)}, u32[]{:S(2)}, u32[]{:S(2)}) collective-permute-start(bf16[1024,256]{1,0:T(8,128)(2,1)S(1)} %pad_maximum_fusion), channel_id=1, source_target_pairs={{0,1},{1,2},{2,3},{3,0},{4,5},{5,6},{6,7},{7,4},{8,9},{9,10},{10,1... | collective-permute-start | bytes 1572872 | tf_op jit(solution)/shard_map/ppermute | solution.py:20
  24.6 2.8 %copy-done = bf16[4096,3,256]{2,0,1:T(8,128)(2,1)S(1)} copy-done((bf16[4096,3,256]{2,0,1:T(8,128)(2,1)S(1)}, bf16[4096,3,256]{2,0,1:T(8,128)(2,1)}, u32[]{:S(2)}) %copy-start) | copy-done | bytes 6291480
  27.4 1.9 %project0.1.refs_5_ = f32[3,512,256]{2,1,0:T(8,128)S(1)} custom-call(bf16[4,256,256]{2,1,0:T(8,128)(2,1)S(1)} %all-to-all-done, bf16[4,256,256]{2,1,0:T(8,128)(2,1)S(1)} %bitcast.38, bf16[3,4096,256]{2,1,0:T(8,128)(2,1)S(1)} %bitcast.28), custom_call_target="tpu_custom_call" | custom-call | tf_op jit(solution)/shard_map/project0/pallas_call | solution.py:116
  30.9 2.3 %collective-permute-start.5 = (bf16[1024,256]{1,0:T(8,128)(2,1)}, bf16[1024,256]{1,0:T(8,128)(2,1)}, u32[]{:S(2)}, u32[]{:S(2)}) collective-permute-start(bf16[1024,256]{1,0:T(8,128)(2,1)} %collective-permute-done.3), channel_id=1, source_target_pairs={{0,4},{4,8},{8,12},{12,0},{1,5},{5,9},{9,13},{13,1},{2,6},{6,10},{... | collective-permute-start | bytes 1572872 | tf_op jit(solution)/shard_map/ppermute | solution.py:20
  36.5 2.8 %copy-done.1 = bf16[4096,3,256]{2,0,1:T(8,128)(2,1)S(1)} copy-done((bf16[4096,3,256]{2,0,1:T(8,128)(2,1)S(1)}, bf16[4096,3,256]{2,0,1:T(8,128)(2,1)}, u32[]{:S(2)}) %copy-start.1) | copy-done | bytes 6291480
  40.3 5.1 %project1.1.refs_3_ = f32[3,512,256]{2,1,0:T(8,128)S(1)} custom-call(bf16[4,256,256]{2,1,0:T(8,128)(2,1)} %bitcast.7.refs_0_, bf16[4,256,256]{2,1,0:T(8,128)(2,1)} %bitcast.8.refs_1_, bf16[4,256,256]{2,1,0:T(8,128)(2,1)} %bitcast.9.refs_2_, bf16[4,256,256]{2,1,0:T(8,128)(2,1)S(1)} %bitcast.44, bf16[3,4096,256]{2,1,0:T(8,128)(2,1)S(1)} %bitcast.29, ...), custom_call_target="tpu_custom_call" | custom-call | tf_op jit(solution)/shard_map/project1/pallas_call | solution.py:116
  45.4 3.8 %project3.1 = (bf16[512,128]{1,0:T(8,128)(2,1)S(1)}, bf16[2,512,128]{2,1,0:T(8,128)(2,1)S(1)}, bf16[528,128]{1,0:T(8,128)(2,1)}, bf16[2,512,128]{2,1,0:T(8,128)(2,1)S(1)}) custom-call(bf16[4,256,256]{2,1,0:T(8,128)(2,1)} %bitcast.5.refs_0_, bf16[4,256,256]{2,1,0:T(8,128)(2,1)} %bitcast.6.refs_1_, bf16[3,4096,256]{2,1,0:T(8,128)(2,1)S(1)} %bitcast.30, ...), custom_call_target="tpu_custom_call" | custom-call | tf_op jit(solution)/shard_map/project3/pallas_call | solution.py:116
  49.2 2.7 %collective-permute-start.9 = (bf16[2,512,128]{2,1,0:T(8,128)(2,1)S(1)}, bf16[2,512,128]{2,1,0:T(8,128)(2,1)S(1)}, u32[]{:S(2)}, u32[]{:S(2)}) collective-permute-start(bf16[2,512,128]{2,1,0:T(8,128)(2,1)S(1)} %get-tuple-element.43.refs_3_.refs_5_), channel_id=1, source_target_pairs={{0,32},{32,64},{64,96},{96,128},{128,160},{160,192},{192,224},{224... | collective-permute-start | bytes 786440 | tf_op jit(solution)/shard_map/ppermute | solution.py:20
  52.0 5.5 %collective-permute-start.13 = (bf16[2,512,128]{2,1,0:T(8,128)(2,1)S(1)}, bf16[2,512,128]{2,1,0:T(8,128)(2,1)S(1)}, u32[]{:S(2)}, u32[]{:S(2)}) collective-permute-start(bf16[2,512,128]{2,1,0:T(8,128)(2,1)S(1)} %collective-permute-done.12.refs_8_.refs_13_), channel_id=1, source_target_pairs={{0,224},{32,0},{64,32},{96,64},{128,96},{160,128},{192,160},{224,1... | collective-permute-start | bytes 786440 | tf_op jit(solution)/shard_map/ppermute | solution.py:20
  59.5 3.6 %collective-permute-done.9.refs_4_.refs_6_ = bf16[2,512,128]{2,1,0:T(8,128)(2,1)S(1)} collective-permute-done((bf16[2,512,128]{2,1,0:T(8,128)(2,1)S(1)}, bf16[2,512,128]{2,1,0:T(8,128)(2,1)S(1)}, u32[]{:S(2)}, u32[]{:S(2)}) %collective-permute-start.9) | collective-permute-done | bytes 262176 | tf_op jit(solution)/shard_map/ppermute | solution.py:20
  64.1 3.7 %collective-permute-start.14 = (bf16[2,512,128]{2,1,0:T(8,128)(2,1)S(1)}, bf16[2,512,128]{2,1,0:T(8,128)(2,1)}, u32[]{:S(2)}, u32[]{:S(2)}) collective-permute-start(bf16[2,512,128]{2,1,0:T(8,128)(2,1)S(1)} %collective-permute-done.13.refs_10_.refs_15_), channel_id=1, source_target_pairs={{0,224},{32,0},{64,32},{96,64},{128,96},{160,128},{192,160},{224,1... | collective-permute-start | bytes 786440 | tf_op jit(solution)/shard_map/ppermute | solution.py:20
  67.8 5.6 %all-to-all-start.1 = ((bf16[16,256,256]{2,1,0:T(8,128)(2,1)}), bf16[16,256,256]{2,1,0:T(8,128)(2,1)S(1)}, u32[]{:S(2)}, u32[]{:S(2)}) async-start(bf16[16,256,256]{2,1,0:T(8,128)(2,1)} %copy-done.2), calls=%async_computation.1 | async-start | bytes 4194304 | tf_op jit(solution)/shard_map/all_to_all | solution.py:362
  73.6 2.0 %collective-permute-start.20 = (bf16[2,512,128]{2,1,0:T(8,128)(2,1)}, bf16[2,512,128]{2,1,0:T(8,128)(2,1)S(1)}, u32[]{:S(2)}, u32[]{:S(2)}) collective-permute-start(bf16[2,512,128]{2,1,0:T(8,128)(2,1)} %collective-permute-done.19.refs_9_.refs_14_), channel_id=1, source_target_pairs={{0,32},{32,64},{64,96},{96,128},{128,160},{160,192},{192,224},{224... | collective-permute-start | bytes 786440 | tf_op jit(solution)/shard_map/ppermute | solution.py:20
  75.7 3.2 %collective-permute-start.15 = (bf16[2,512,128]{2,1,0:T(8,128)(2,1)}, bf16[2,512,128]{2,1,0:T(8,128)(2,1)S(1)}, u32[]{:S(2)}, u32[]{:S(2)}) collective-permute-start(bf16[2,512,128]{2,1,0:T(8,128)(2,1)} %collective-permute-done.14.refs_12_.refs_17_), channel_id=1, source_target_pairs={{0,224},{32,0},{64,32},{96,64},{128,96},{160,128},{192,160},{224,1... | collective-permute-start | bytes 786440 | tf_op jit(solution)/shard_map/ppermute | solution.py:20
  78.9 4.0 %collective-permute-done.18.refs_7_.refs_9_ = bf16[2,512,128]{2,1,0:T(8,128)(2,1)S(1)} collective-permute-done((bf16[2,512,128]{2,1,0:T(8,128)(2,1)}, bf16[2,512,128]{2,1,0:T(8,128)(2,1)S(1)}, u32[]{:S(2)}, u32[]{:S(2)}) %collective-permute-start.18) | collective-permute-done | bytes 262176 | tf_op jit(solution)/shard_map/ppermute | solution.py:20
  86.4 3.5 %collective-permute-done.11.refs_3_.refs_10_ = bf16[2,512,128]{2,1,0:T(8,128)(2,1)S(1)} collective-permute-done((bf16[2,512,128]{2,1,0:T(8,128)(2,1)}, bf16[2,512,128]{2,1,0:T(8,128)(2,1)S(1)}, u32[]{:S(2)}, u32[]{:S(2)}) %collective-permute-start.11) | collective-permute-done | bytes 262176 | tf_op jit(solution)/shard_map/ppermute | solution.py:20
  90.6 2.5 %collective-permute-start.24 = (bf16[2,512,128]{2,1,0:T(8,128)(2,1)S(1)}, bf16[2,512,128]{2,1,0:T(8,128)(2,1)S(1)}, u32[]{:S(2)}, u32[]{:S(2)}) collective-permute-start(bf16[2,512,128]{2,1,0:T(8,128)(2,1)S(1)} %collective-permute-done.15.refs_6_.refs_19_), channel_id=1, source_target_pairs={{0,224},{32,0},{64,32},{96,64},{128,96},{160,128},{192,160},{224,1... | collective-permute-start | bytes 786440 | tf_op jit(solution)/shard_map/ppermute | solution.py:20
  96.3 3.7 %collective-permute-done.22.refs_12_ = bf16[2,512,128]{2,1,0:T(8,128)(2,1)S(1)} collective-permute-done((bf16[2,512,128]{2,1,0:T(8,128)(2,1)S(1)}, bf16[2,512,128]{2,1,0:T(8,128)(2,1)S(1)}, u32[]{:S(2)}, u32[]{:S(2)}) %collective-permute-start.22) | collective-permute-done | bytes 262176 | tf_op jit(solution)/shard_map/ppermute | solution.py:20
  100.1 7.0 %attend.1 = (bf16[512,128]{1,0:T(8,128)(2,1)S(1)}, bf16[512,128]{1,0:T(8,128)(2,1)S(1)}) custom-call(s32[96]{0:T(128)S(1)} %pad_add_fusion.refs_0_, s32[2]{0:T(128)S(1)} %copy-done.6, s32[2]{0:T(128)S(1)} %copy-done.8, bf16[512,128]{1,0:T(8,128)(2,1)S(1)} %get-tuple-element.45.refs_1_.refs_3_, bf16[528,128]{1,0:T(8,128)(2,1)S(1)} %collective-permute-done.16.refs_2_.refs_4_, ...), custom_call_target="tpu_custom_call" | custom-call | flops 14000000000 | bytes 28000000 | tf_op jit(solution)/shard_map/attend/pallas_call | solution.py:329
  110.2 4.2 %all-to-all-start.2 = ((bf16[4,256,256]{2,1,0:T(8,128)(2,1)}), bf16[4,256,256]{2,1,0:T(8,128)(2,1)S(1)}, u32[]{:S(2)}, u32[]{:S(2)}) async-start(bf16[4,256,256]{2,1,0:T(8,128)(2,1)} %broadcast_in_dim.11), calls=%async_computation.2 | async-start | bytes 1048576 | tf_op jit(solution)/shard_map/all_to_all | solution.py:31
  117.9 2.5 %collective-permute-done.26 = bf16[256,256]{1,0:T(8,128)(2,1)S(1)} collective-permute-done((bf16[256,256]{1,0:T(8,128)(2,1)S(1)}, bf16[256,256]{1,0:T(8,128)(2,1)S(1)}, u32[]{:S(2)}, u32[]{:S(2)}) %collective-permute-start.26) | collective-permute-done | bytes 131104 | tf_op jit(solution)/shard_map/ppermute | solution.py:20
  120.5 3.6 %collective-permute-done.27 = bf16[256,256]{1,0:T(8,128)(2,1)S(1)} collective-permute-done((bf16[256,256]{1,0:T(8,128)(2,1)S(1)}, bf16[256,256]{1,0:T(8,128)(2,1)S(1)}, u32[]{:S(2)}, u32[]{:S(2)}) %collective-permute-start.27) | collective-permute-done | bytes 131104 | tf_op jit(solution)/shard_map/ppermute | solution.py:20
  124.3 1.8 %collective-permute-start.30 = (bf16[1024,256]{1,0:T(8,128)(2,1)S(1)}, bf16[1024,256]{1,0:T(8,128)(2,1)S(1)}, u32[]{:S(2)}, u32[]{:S(2)}) collective-permute-start(bf16[1024,256]{1,0:T(8,128)(2,1)S(1)} %pad_maximum_fusion.1), channel_id=1, source_target_pairs={{0,1},{1,2},{2,3},{3,0},{4,5},{5,6},{6,7},{7,4},{8,9},{9,10},{10,1... | collective-permute-start | bytes 1572872 | tf_op jit(solution)/shard_map/ppermute | solution.py:20
  130.1 8.3 %collective-permute-done.30 = bf16[1024,256]{1,0:T(8,128)(2,1)S(1)} collective-permute-done((bf16[1024,256]{1,0:T(8,128)(2,1)S(1)}, bf16[1024,256]{1,0:T(8,128)(2,1)S(1)}, u32[]{:S(2)}, u32[]{:S(2)}) %collective-permute-start.30) | collective-permute-done | bytes 524320 | tf_op jit(solution)/shard_map/ppermute | solution.py:20
  138.4 2.3 %collective-permute-start.31 = (bf16[512,256]{1,0:T(8,128)(2,1)S(1)}, bf16[512,256]{1,0:T(8,128)(2,1)S(1)}, u32[]{:S(2)}, u32[]{:S(2)}) collective-permute-start(bf16[512,256]{1,0:T(8,128)(2,1)S(1)} %slice.38), channel_id=1, source_target_pairs={{0,4},{4,8},{8,12},{12,0},{1,5},{5,9},{9,13},{13,1},{2,6},{6,10},{... | collective-permute-start | bytes 786440 | tf_op jit(solution)/shard_map/ppermute | solution.py:20
  140.8 1.5 %collective-permute-start.34 = (bf16[512,256]{1,0:T(8,128)(2,1)S(1)}, bf16[512,256]{1,0:T(8,128)(2,1)S(1)}, u32[]{:S(2)}, u32[]{:S(2)}) collective-permute-start(bf16[512,256]{1,0:T(8,128)(2,1)S(1)} %slice.40), channel_id=1, source_target_pairs={{0,1},{1,2},{2,3},{3,0},{4,5},{5,6},{6,7},{7,4},{8,9},{9,10},{10,1... | collective-permute-start | bytes 786440 | tf_op jit(solution)/shard_map/ppermute | solution.py:20
  142.4 1.9 %collective-permute-start.36 = (bf16[512,256]{1,0:T(8,128)(2,1)S(1)}, bf16[512,256]{1,0:T(8,128)(2,1)S(1)}, u32[]{:S(2)}, u32[]{:S(2)}) collective-permute-start(bf16[512,256]{1,0:T(8,128)(2,1)S(1)} %slice.46), channel_id=1, source_target_pairs={{0,3},{1,0},{2,1},{3,2},{4,7},{5,4},{6,5},{7,6},{8,11},{9,8},{10,9... | collective-permute-start | bytes 786440 | tf_op jit(solution)/shard_map/ppermute | solution.py:20
  145.1 3.4 %collective-permute-done.34 = bf16[512,256]{1,0:T(8,128)(2,1)S(1)} collective-permute-done((bf16[512,256]{1,0:T(8,128)(2,1)S(1)}, bf16[512,256]{1,0:T(8,128)(2,1)S(1)}, u32[]{:S(2)}, u32[]{:S(2)}) %collective-permute-start.34) | collective-permute-done | bytes 262176 | tf_op jit(solution)/shard_map/ppermute | solution.py:20
  148.8 3.1 %collective-permute-done.33 = bf16[512,256]{1,0:T(8,128)(2,1)S(1)} collective-permute-done((bf16[512,256]{1,0:T(8,128)(2,1)S(1)}, bf16[512,256]{1,0:T(8,128)(2,1)S(1)}, u32[]{:S(2)}, u32[]{:S(2)}) %collective-permute-start.33) | collective-permute-done | bytes 262176 | tf_op jit(solution)/shard_map/ppermute | solution.py:20
  (99 shorter events, 41.8 us)
Async XLA Ops:
  2.0 14.1 %all-to-all-start = ((bf16[4,256,256]{2,1,0:T(8,128)(2,1)}), bf16[4,256,256]{2,1,0:T(8,128)(2,1)S(1)}, u32[]{:S(2)}, u32[]{:S(2)}) async-start(bf16[4,256,256]{2,1,0:T(8,128)(2,1)} %broadcast_in_dim.10), calls=%async_computation | async-start | bytes 1048576 | tf_op jit(solution)/shard_map/all_to_all | solution.py:31
  7.5 8.5 %collective-permute-start.1 = (bf16[256,256]{1,0:T(8,128)(2,1)S(1)}, bf16[256,256]{1,0:T(8,128)(2,1)S(1)}, u32[]{:S(2)}, u32[]{:S(2)}) collective-permute-start(bf16[256,256]{1,0:T(8,128)(2,1)S(1)} %get-tuple-element.69), channel_id=1, source_target_pairs={{0,12},{4,0},{8,4},{12,8},{1,13},{5,1},{9,5},{13,9},{2,14},{6,2},{... | collective-permute-start | bytes 393224 | tf_op jit(solution)/shard_map/ppermute | solution.py:20
  8.3 7.7 %collective-permute-start.2 = (bf16[256,256]{1,0:T(8,128)(2,1)S(1)}, bf16[256,256]{1,0:T(8,128)(2,1)}, u32[]{:S(2)}, u32[]{:S(2)}) collective-permute-start(bf16[256,256]{1,0:T(8,128)(2,1)S(1)} %get-tuple-element.69), channel_id=1, source_target_pairs={{0,8},{4,12},{8,0},{12,4},{1,9},{5,13},{9,1},{13,5},{2,10},{6,14},... | collective-permute-start | bytes 393224 | tf_op jit(solution)/shard_map/ppermute | solution.py:20
  17.0 13.7 %collective-permute-start.4 = (bf16[1024,256]{1,0:T(8,128)(2,1)S(1)}, bf16[1024,256]{1,0:T(8,128)(2,1)}, u32[]{:S(2)}, u32[]{:S(2)}) collective-permute-start(bf16[1024,256]{1,0:T(8,128)(2,1)S(1)} %pad_maximum_fusion), channel_id=1, source_target_pairs={{0,1},{1,2},{2,3},{3,0},{4,5},{5,6},{6,7},{7,4},{8,9},{9,10},{10,1... | collective-permute-start | bytes 1572872 | tf_op jit(solution)/shard_map/ppermute | solution.py:20
  18.9 11.9 %collective-permute-start.3 = (bf16[1024,256]{1,0:T(8,128)(2,1)S(1)}, bf16[1024,256]{1,0:T(8,128)(2,1)}, u32[]{:S(2)}, u32[]{:S(2)}) collective-permute-start(bf16[1024,256]{1,0:T(8,128)(2,1)S(1)} %bitcast.34), channel_id=1, source_target_pairs={{0,4},{4,8},{8,12},{12,0},{1,5},{5,9},{9,13},{13,1},{2,6},{6,10},{... | collective-permute-start | bytes 1572872 | tf_op jit(solution)/shard_map/ppermute | solution.py:20
  22.5 12.4 %collective-permute-start.8 = (bf16[1024,256]{1,0:T(8,128)(2,1)S(1)}, bf16[1024,256]{1,0:T(8,128)(2,1)S(1)}, u32[]{:S(2)}, u32[]{:S(2)}) collective-permute-start(bf16[1024,256]{1,0:T(8,128)(2,1)S(1)} %pad_maximum_fusion), channel_id=1, source_target_pairs={{0,3},{1,0},{2,1},{3,2},{4,7},{5,4},{6,5},{7,6},{8,11},{9,8},{10,9... | collective-permute-start | bytes 1572872 | tf_op jit(solution)/shard_map/ppermute | solution.py:20
  23.9 12.6 %collective-permute-start.7 = (bf16[1024,256]{1,0:T(8,128)(2,1)S(1)}, bf16[1024,256]{1,0:T(8,128)(2,1)}, u32[]{:S(2)}, u32[]{:S(2)}) collective-permute-start(bf16[1024,256]{1,0:T(8,128)(2,1)S(1)} %bitcast.35), channel_id=1, source_target_pairs={{0,12},{4,0},{8,4},{12,8},{1,13},{5,1},{9,5},{13,9},{2,14},{6,2},{... | collective-permute-start | bytes 1572872 | tf_op jit(solution)/shard_map/ppermute | solution.py:20
  30.9 14.6 %collective-permute-start.5 = (bf16[1024,256]{1,0:T(8,128)(2,1)}, bf16[1024,256]{1,0:T(8,128)(2,1)}, u32[]{:S(2)}, u32[]{:S(2)}) collective-permute-start(bf16[1024,256]{1,0:T(8,128)(2,1)} %collective-permute-done.3), channel_id=1, source_target_pairs={{0,4},{4,8},{8,12},{12,0},{1,5},{5,9},{9,13},{13,1},{2,6},{6,10},{... | collective-permute-start | bytes 1572872 | tf_op jit(solution)/shard_map/ppermute | solution.py:20
  33.2 12.3 %collective-permute-start.6 = (bf16[1024,256]{1,0:T(8,128)(2,1)}, bf16[1024,256]{1,0:T(8,128)(2,1)}, u32[]{:S(2)}, u32[]{:S(2)}) collective-permute-start(bf16[1024,256]{1,0:T(8,128)(2,1)} %collective-permute-done.4), channel_id=1, source_target_pairs={{0,1},{1,2},{2,3},{3,0},{4,5},{5,6},{6,7},{7,4},{8,9},{9,10},{10,1... | collective-permute-start | bytes 1572872 | tf_op jit(solution)/shard_map/ppermute | solution.py:20
  49.2 13.8 %collective-permute-start.9 = (bf16[2,512,128]{2,1,0:T(8,128)(2,1)S(1)}, bf16[2,512,128]{2,1,0:T(8,128)(2,1)S(1)}, u32[]{:S(2)}, u32[]{:S(2)}) collective-permute-start(bf16[2,512,128]{2,1,0:T(8,128)(2,1)S(1)} %get-tuple-element.43.refs_3_.refs_5_), channel_id=1, source_target_pairs={{0,32},{32,64},{64,96},{96,128},{128,160},{160,192},{192,224},{224... | collective-permute-start | bytes 786440 | tf_op jit(solution)/shard_map/ppermute | solution.py:20
  52.0 12.1 %collective-permute-start.13 = (bf16[2,512,128]{2,1,0:T(8,128)(2,1)S(1)}, bf16[2,512,128]{2,1,0:T(8,128)(2,1)S(1)}, u32[]{:S(2)}, u32[]{:S(2)}) collective-permute-start(bf16[2,512,128]{2,1,0:T(8,128)(2,1)S(1)} %collective-permute-done.12.refs_8_.refs_13_), channel_id=1, source_target_pairs={{0,224},{32,0},{64,32},{96,64},{128,96},{160,128},{192,160},{224,1... | collective-permute-start | bytes 786440 | tf_op jit(solution)/shard_map/ppermute | solution.py:20
  57.4 16.0 %collective-permute-start.17 = (bf16[2,512,128]{2,1,0:T(8,128)(2,1)S(1)}, bf16[2,512,128]{2,1,0:T(8,128)(2,1)}, u32[]{:S(2)}, u32[]{:S(2)}) collective-permute-start(bf16[2,512,128]{2,1,0:T(8,128)(2,1)S(1)} %get-tuple-element.43.refs_3_.refs_5_), channel_id=1, source_target_pairs={{0,224},{32,0},{64,32},{96,64},{128,96},{160,128},{192,160},{224,1... | collective-permute-start | bytes 786440 | tf_op jit(solution)/shard_map/ppermute | solution.py:20
  58.4 15.1 %collective-permute-start.19 = (bf16[2,512,128]{2,1,0:T(8,128)(2,1)S(1)}, bf16[2,512,128]{2,1,0:T(8,128)(2,1)}, u32[]{:S(2)}, u32[]{:S(2)}) collective-permute-start(bf16[2,512,128]{2,1,0:T(8,128)(2,1)S(1)} %collective-permute-done.12.refs_8_.refs_13_), channel_id=1, source_target_pairs={{0,32},{32,64},{64,96},{96,128},{128,160},{160,192},{192,224},{224... | collective-permute-start | bytes 786440 | tf_op jit(solution)/shard_map/ppermute | solution.py:20
  63.1 12.5 %collective-permute-start.10 = (bf16[2,512,128]{2,1,0:T(8,128)(2,1)S(1)}, bf16[2,512,128]{2,1,0:T(8,128)(2,1)}, u32[]{:S(2)}, u32[]{:S(2)}) collective-permute-start(bf16[2,512,128]{2,1,0:T(8,128)(2,1)S(1)} %collective-permute-done.9.refs_4_.refs_6_), channel_id=1, source_target_pairs={{0,32},{32,64},{64,96},{96,128},{128,160},{160,192},{192,224},{224... | collective-permute-start | bytes 786440 | tf_op jit(solution)/shard_map/ppermute | solution.py:20
  64.1 11.6 %collective-permute-start.14 = (bf16[2,512,128]{2,1,0:T(8,128)(2,1)S(1)}, bf16[2,512,128]{2,1,0:T(8,128)(2,1)}, u32[]{:S(2)}, u32[]{:S(2)}) collective-permute-start(bf16[2,512,128]{2,1,0:T(8,128)(2,1)S(1)} %collective-permute-done.13.refs_10_.refs_15_), channel_id=1, source_target_pairs={{0,224},{32,0},{64,32},{96,64},{128,96},{160,128},{192,160},{224,1... | collective-permute-start | bytes 786440 | tf_op jit(solution)/shard_map/ppermute | solution.py:20
  67.8 40.0 %all-to-all-start.1 = ((bf16[16,256,256]{2,1,0:T(8,128)(2,1)}), bf16[16,256,256]{2,1,0:T(8,128)(2,1)S(1)}, u32[]{:S(2)}, u32[]{:S(2)}) async-start(bf16[16,256,256]{2,1,0:T(8,128)(2,1)} %copy-done.2), calls=%async_computation.1 | async-start | bytes 4194304 | tf_op jit(solution)/shard_map/all_to_all | solution.py:362
  73.5 9.5 %collective-permute-start.18 = (bf16[2,512,128]{2,1,0:T(8,128)(2,1)}, bf16[2,512,128]{2,1,0:T(8,128)(2,1)S(1)}, u32[]{:S(2)}, u32[]{:S(2)}) collective-permute-start(bf16[2,512,128]{2,1,0:T(8,128)(2,1)} %collective-permute-done.17.refs_5_.refs_7_), channel_id=1, source_target_pairs={{0,224},{32,0},{64,32},{96,64},{128,96},{160,128},{192,160},{224,1... | collective-permute-start | bytes 786440 | tf_op jit(solution)/shard_map/ppermute | solution.py:20
  73.6 10.7 %collective-permute-start.20 = (bf16[2,512,128]{2,1,0:T(8,128)(2,1)}, bf16[2,512,128]{2,1,0:T(8,128)(2,1)S(1)}, u32[]{:S(2)}, u32[]{:S(2)}) collective-permute-start(bf16[2,512,128]{2,1,0:T(8,128)(2,1)} %collective-permute-done.19.refs_9_.refs_14_), channel_id=1, source_target_pairs={{0,32},{32,64},{64,96},{96,128},{128,160},{160,192},{192,224},{224... | collective-permute-start | bytes 786440 | tf_op jit(solution)/shard_map/ppermute | solution.py:20
  75.6 14.3 %collective-permute-start.11 = (bf16[2,512,128]{2,1,0:T(8,128)(2,1)}, bf16[2,512,128]{2,1,0:T(8,128)(2,1)S(1)}, u32[]{:S(2)}, u32[]{:S(2)}) collective-permute-start(bf16[2,512,128]{2,1,0:T(8,128)(2,1)} %collective-permute-done.10.refs_6_.refs_8_), channel_id=1, source_target_pairs={{0,32},{32,64},{64,96},{96,128},{128,160},{160,192},{192,224},{224... | collective-permute-start | bytes 786440 | tf_op jit(solution)/shard_map/ppermute | solution.py:20
  75.7 14.2 %collective-permute-start.15 = (bf16[2,512,128]{2,1,0:T(8,128)(2,1)}, bf16[2,512,128]{2,1,0:T(8,128)(2,1)S(1)}, u32[]{:S(2)}, u32[]{:S(2)}) collective-permute-start(bf16[2,512,128]{2,1,0:T(8,128)(2,1)} %collective-permute-done.14.refs_12_.refs_17_), channel_id=1, source_target_pairs={{0,224},{32,0},{64,32},{96,64},{128,96},{160,128},{192,160},{224,1... | collective-permute-start | bytes 786440 | tf_op jit(solution)/shard_map/ppermute | solution.py:20
  82.9 11.2 %collective-permute-start.21 = (bf16[2,512,128]{2,1,0:T(8,128)(2,1)S(1)}, bf16[2,512,128]{2,1,0:T(8,128)(2,1)S(1)}, u32[]{:S(2)}, u32[]{:S(2)}) collective-permute-start(bf16[2,512,128]{2,1,0:T(8,128)(2,1)S(1)} %collective-permute-done.18.refs_7_.refs_9_), channel_id=1, source_target_pairs={{0,224},{32,0},{64,32},{96,64},{128,96},{160,128},{192,160},{224,1... | collective-permute-start | bytes 786440 | tf_op jit(solution)/shard_map/ppermute | solution.py:20
  84.2 11.2 %collective-permute-start.23 = (bf16[2,512,128]{2,1,0:T(8,128)(2,1)S(1)}, bf16[2,512,128]{2,1,0:T(8,128)(2,1)S(1)}, u32[]{:S(2)}, u32[]{:S(2)}) collective-permute-start(bf16[2,512,128]{2,1,0:T(8,128)(2,1)S(1)} %collective-permute-done.20.refs_11_.refs_16_), channel_id=1, source_target_pairs={{0,32},{32,64},{64,96},{96,128},{128,160},{160,192},{192,224},{224... | collective-permute-start | bytes 786440 | tf_op jit(solution)/shard_map/ppermute | solution.py:20
  89.9 10.2 %collective-permute-start.22 = (bf16[2,512,128]{2,1,0:T(8,128)(2,1)S(1)}, bf16[2,512,128]{2,1,0:T(8,128)(2,1)S(1)}, u32[]{:S(2)}, u32[]{:S(2)}) collective-permute-start(bf16[2,512,128]{2,1,0:T(8,128)(2,1)S(1)} %collective-permute-done.11.refs_3_.refs_10_), channel_id=1, source_target_pairs={{0,32},{32,64},{64,96},{96,128},{128,160},{160,192},{192,224},{224... | collective-permute-start | bytes 786440 | tf_op jit(solution)/shard_map/ppermute | solution.py:20
  90.6 9.5 %collective-permute-start.24 = (bf16[2,512,128]{2,1,0:T(8,128)(2,1)S(1)}, bf16[2,512,128]{2,1,0:T(8,128)(2,1)S(1)}, u32[]{:S(2)}, u32[]{:S(2)}) collective-permute-start(bf16[2,512,128]{2,1,0:T(8,128)(2,1)S(1)} %collective-permute-done.15.refs_6_.refs_19_), channel_id=1, source_target_pairs={{0,224},{32,0},{64,32},{96,64},{128,96},{160,128},{192,160},{224,1... | collective-permute-start | bytes 786440 | tf_op jit(solution)/shard_map/ppermute | solution.py:20
  110.2 14.0 %all-to-all-start.2 = ((bf16[4,256,256]{2,1,0:T(8,128)(2,1)}), bf16[4,256,256]{2,1,0:T(8,128)(2,1)S(1)}, u32[]{:S(2)}, u32[]{:S(2)}) async-start(bf16[4,256,256]{2,1,0:T(8,128)(2,1)} %broadcast_in_dim.11), calls=%async_computation.2 | async-start | bytes 1048576 | tf_op jit(solution)/shard_map/all_to_all | solution.py:31
  115.0 9.0 %collective-permute-start.27 = (bf16[256,256]{1,0:T(8,128)(2,1)S(1)}, bf16[256,256]{1,0:T(8,128)(2,1)S(1)}, u32[]{:S(2)}, u32[]{:S(2)}) collective-permute-start(bf16[256,256]{1,0:T(8,128)(2,1)S(1)} %get-tuple-element.67), channel_id=1, source_target_pairs={{0,12},{4,0},{8,4},{12,8},{1,13},{5,1},{9,5},{13,9},{2,14},{6,2},{... | collective-permute-start | bytes 393224 | tf_op jit(solution)/shard_map/ppermute | solution.py:20
  124.3 14.1 %collective-permute-start.30 = (bf16[1024,256]{1,0:T(8,128)(2,1)S(1)}, bf16[1024,256]{1,0:T(8,128)(2,1)S(1)}, u32[]{:S(2)}, u32[]{:S(2)}) collective-permute-start(bf16[1024,256]{1,0:T(8,128)(2,1)S(1)} %pad_maximum_fusion.1), channel_id=1, source_target_pairs={{0,1},{1,2},{2,3},{3,0},{4,5},{5,6},{6,7},{7,4},{8,9},{9,10},{10,1... | collective-permute-start | bytes 1572872 | tf_op jit(solution)/shard_map/ppermute | solution.py:20
  126.1 12.3 %collective-permute-start.29 = (bf16[1024,256]{1,0:T(8,128)(2,1)S(1)}, bf16[1024,256]{1,0:T(8,128)(2,1)S(1)}, u32[]{:S(2)}, u32[]{:S(2)}) collective-permute-start(bf16[1024,256]{1,0:T(8,128)(2,1)S(1)} %bitcast.36), channel_id=1, source_target_pairs={{0,4},{4,8},{8,12},{12,0},{1,5},{5,9},{9,13},{13,1},{2,6},{6,10},{... | collective-permute-start | bytes 1572872 | tf_op jit(solution)/shard_map/ppermute | solution.py:20
  127.1 15.3 %collective-permute-start.35 = (bf16[1024,256]{1,0:T(8,128)(2,1)S(1)}, bf16[1024,256]{1,0:T(8,128)(2,1)S(1)}, u32[]{:S(2)}, u32[]{:S(2)}) collective-permute-start(bf16[1024,256]{1,0:T(8,128)(2,1)S(1)} %pad_maximum_fusion.1), channel_id=1, source_target_pairs={{0,3},{1,0},{2,1},{3,2},{4,7},{5,4},{6,5},{7,6},{8,11},{9,8},{10,9... | collective-permute-start | bytes 1572872 | tf_op jit(solution)/shard_map/ppermute | solution.py:20
  128.6 15.7 %collective-permute-start.32 = (bf16[1024,256]{1,0:T(8,128)(2,1)S(1)}, bf16[1024,256]{1,0:T(8,128)(2,1)S(1)}, u32[]{:S(2)}, u32[]{:S(2)}) collective-permute-start(bf16[1024,256]{1,0:T(8,128)(2,1)S(1)} %bitcast.37), channel_id=1, source_target_pairs={{0,12},{4,0},{8,4},{12,8},{1,13},{5,1},{9,5},{13,9},{2,14},{6,2},{... | collective-permute-start | bytes 1572872 | tf_op jit(solution)/shard_map/ppermute | solution.py:20
  140.8 7.7 %collective-permute-start.34 = (bf16[512,256]{1,0:T(8,128)(2,1)S(1)}, bf16[512,256]{1,0:T(8,128)(2,1)S(1)}, u32[]{:S(2)}, u32[]{:S(2)}) collective-permute-start(bf16[512,256]{1,0:T(8,128)(2,1)S(1)} %slice.40), channel_id=1, source_target_pairs={{0,1},{1,2},{2,3},{3,0},{4,5},{5,6},{6,7},{7,4},{8,9},{9,10},{10,1... | collective-permute-start | bytes 786440 | tf_op jit(solution)/shard_map/ppermute | solution.py:20
  144.2 7.7 %collective-permute-start.33 = (bf16[512,256]{1,0:T(8,128)(2,1)S(1)}, bf16[512,256]{1,0:T(8,128)(2,1)S(1)}, u32[]{:S(2)}, u32[]{:S(2)}) collective-permute-start(bf16[512,256]{1,0:T(8,128)(2,1)S(1)} %slice.45), channel_id=1, source_target_pairs={{0,12},{4,0},{8,4},{12,8},{1,13},{5,1},{9,5},{13,9},{2,14},{6,2},{... | collective-permute-start | bytes 786440 | tf_op jit(solution)/shard_map/ppermute | solution.py:20
  (18 other events, 109.9 us)

commit v11 on v10

--- a/solution.py
+++ b/solution.py
@@ -358,9 +358,9 @@
     )
     own = z_ring(own)
     other = swap(send_kv)
-    ordered, _ = lax.optimization_barrier((ordered, other))
+    other = z_ring(other)
+    ordered, _ = lax.optimization_barrier((ordered, own[3:5]))
     w_cols = lax.all_to_all(ordered, ("y", "x"), 0, 0, tiled=True)
-    other = z_ring(other)
     theirs = swap(send_q)
     ids, _ = lax.optimization_barrier((theirs[512:], own[1:3]))
     rand = jnp.concatenate([rand, ids[0, :48].astype(jnp.int32)])

time: 154 us -> 161 us (1.045)
  starting transfers between devices: 65.8 us -> 69.7 us
  waiting for transfers between devices: 50.2 us -> 53.7 us
    ppermute x34, starting transfers between devices: 51.6 us -> 55.6 us  [shift(): return lax.ppermute(a, axis, [(i, (i + step) % n) for i in range(n)])]
    ppermute x34, waiting for transfers between devices: 48.5 us -> 51.9 us  [shift(): return lax.ppermute(a, axis, [(i, (i + step) % n) for i in range(n)])]
  transfers between devices with their start and end apart: 40 -> 40, of which waited for: 20 -> 20; matrix products, arithmetic and copies ran while one was open for 0% -> 0% of each run, Pallas kernels for 12% -> 11%
where the time goes in v11:
time: 161 us
  starting transfers between devices  69.7 us (43%)
  waiting for transfers between devices  53.7 us (33%)
  Pallas kernels  23.1 us (14%)
  local copies, waits for them, and re-layouts  12.8 us (8%)
    ppermute x34, starting transfers between devices, shift(): return lax.ppermute(a, axis, [(i, (i + step) % n) for i in range(n)])  55.6 us
    ppermute x34, waiting for transfers between devices, shift(): return lax.ppermute(a, axis, [(i, (i + step) % n) for i in range(n)])  51.9 us
    pallas_call x6, Pallas kernels, partial_matmul(): pl.pallas_call(lambda *refs: partial_kernel(steps, counts, n, groups, has...  13.1 us
    unnamed x22, local copies, waits for them, and re-layouts  9.53 us
    all_to_all x2, starting transfers between devices, plane_matmul(): lax.all_to_all(jnp.broadcast_to(a[:n], (NXY, n, 256)).reshape(NXY * n, 25...  8.53 us
    pallas_call x1, Pallas kernels, attend(): pl.pallas_call(attend_kernel, out_shape=(jax.ShapeDtypeStruct((512, DH),...  7.08 us
    all_to_all x1, starting transfers between devices, body(): w_cols = lax.all_to_all(ordered, ('y', 'x'), 0, 0, tiled=True)  5.64 us
  transfers between devices with their start and end apart: 40, of which 20 were waited for; matrix products, arithmetic and copies ran while one was open for 0% of the time, Pallas kernels for 11%

profile of v11, /device:TPU:24, one launch (start us, length us, event | category | flops | bytes accessed | tf_op | source)
XLA Modules:
  0.0 160.6 jit_solution(1091181442616280746)
XLA Ops:
  2.0 4.3 %all-to-all-start = ((bf16[4,256,256]{2,1,0:T(8,128)(2,1)}), bf16[4,256,256]{2,1,0:T(8,128)(2,1)S(1)}, u32[]{:S(2)}, u32[]{:S(2)}) async-start(bf16[4,256,256]{2,1,0:T(8,128)(2,1)} %broadcast_in_dim.10), calls=%async_computation | async-start | bytes 1048576 | tf_op jit(solution)/shard_map/all_to_all | solution.py:31
  9.5 2.8 %collective-permute-done = bf16[256,256]{1,0:T(8,128)(2,1)S(1)} collective-permute-done((bf16[256,256]{1,0:T(8,128)(2,1)S(1)}, bf16[256,256]{1,0:T(8,128)(2,1)S(1)}, u32[]{:S(2)}, u32[]{:S(2)}) %collective-permute-start) | collective-permute-done | bytes 131104 | tf_op jit(solution)/shard_map/ppermute | solution.py:20
  12.4 3.7 %collective-permute-done.1 = bf16[256,256]{1,0:T(8,128)(2,1)S(1)} collective-permute-done((bf16[256,256]{1,0:T(8,128)(2,1)S(1)}, bf16[256,256]{1,0:T(8,128)(2,1)S(1)}, u32[]{:S(2)}, u32[]{:S(2)}) %collective-permute-start.1) | collective-permute-done | bytes 131104 | tf_op jit(solution)/shard_map/ppermute | solution.py:20
  17.0 1.9 %collective-permute-start.4 = (bf16[1024,256]{1,0:T(8,128)(2,1)S(1)}, bf16[1024,256]{1,0:T(8,128)(2,1)}, u32[]{:S(2)}, u32[]{:S(2)}) collective-permute-start(bf16[1024,256]{1,0:T(8,128)(2,1)S(1)} %pad_maximum_fusion), channel_id=1, source_target_pairs={{0,1},{1,2},{2,3},{3,0},{4,5},{5,6},{6,7},{7,4},{8,9},{9,10},{10,1... | collective-permute-start | bytes 1572872 | tf_op jit(solution)/shard_map/ppermute | solution.py:20
  24.6 2.8 %copy-done = bf16[4096,3,256]{2,0,1:T(8,128)(2,1)S(1)} copy-done((bf16[4096,3,256]{2,0,1:T(8,128)(2,1)S(1)}, bf16[4096,3,256]{2,0,1:T(8,128)(2,1)}, u32[]{:S(2)}) %copy-start) | copy-done | bytes 6291480
  27.4 1.9 %project0.1.refs_5_ = f32[3,512,256]{2,1,0:T(8,128)S(1)} custom-call(bf16[4,256,256]{2,1,0:T(8,128)(2,1)S(1)} %all-to-all-done, bf16[4,256,256]{2,1,0:T(8,128)(2,1)S(1)} %bitcast.38, bf16[3,4096,256]{2,1,0:T(8,128)(2,1)S(1)} %bitcast.28), custom_call_target="tpu_custom_call" | custom-call | tf_op jit(solution)/shard_map/project0/pallas_call | solution.py:116
  30.9 2.3 %collective-permute-start.5 = (bf16[1024,256]{1,0:T(8,128)(2,1)}, bf16[1024,256]{1,0:T(8,128)(2,1)}, u32[]{:S(2)}, u32[]{:S(2)}) collective-permute-start(bf16[1024,256]{1,0:T(8,128)(2,1)} %collective-permute-done.3), channel_id=1, source_target_pairs={{0,4},{4,8},{8,12},{12,0},{1,5},{5,9},{9,13},{13,1},{2,6},{6,10},{... | collective-permute-start | bytes 1572872 | tf_op jit(solution)/shard_map/ppermute | solution.py:20
  36.5 2.8 %copy-done.1 = bf16[4096,3,256]{2,0,1:T(8,128)(2,1)S(1)} copy-done((bf16[4096,3,256]{2,0,1:T(8,128)(2,1)S(1)}, bf16[4096,3,256]{2,0,1:T(8,128)(2,1)}, u32[]{:S(2)}) %copy-start.1) | copy-done | bytes 6291480
  40.3 5.1 %project1.1.refs_3_ = f32[3,512,256]{2,1,0:T(8,128)S(1)} custom-call(bf16[4,256,256]{2,1,0:T(8,128)(2,1)} %bitcast.7.refs_0_, bf16[4,256,256]{2,1,0:T(8,128)(2,1)} %bitcast.8.refs_1_, bf16[4,256,256]{2,1,0:T(8,128)(2,1)} %bitcast.9.refs_2_, bf16[4,256,256]{2,1,0:T(8,128)(2,1)S(1)} %bitcast.44, bf16[3,4096,256]{2,1,0:T(8,128)(2,1)S(1)} %bitcast.29, ...), custom_call_target="tpu_custom_call" | custom-call | tf_op jit(solution)/shard_map/project1/pallas_call | solution.py:116
  45.4 3.8 %project3.1 = (bf16[512,128]{1,0:T(8,128)(2,1)S(1)}, bf16[2,512,128]{2,1,0:T(8,128)(2,1)S(1)}, bf16[528,128]{1,0:T(8,128)(2,1)}, bf16[2,512,128]{2,1,0:T(8,128)(2,1)S(1)}) custom-call(bf16[4,256,256]{2,1,0:T(8,128)(2,1)} %bitcast.5.refs_0_, bf16[4,256,256]{2,1,0:T(8,128)(2,1)} %bitcast.6.refs_1_, bf16[3,4096,256]{2,1,0:T(8,128)(2,1)S(1)} %bitcast.30, ...), custom_call_target="tpu_custom_call" | custom-call | tf_op jit(solution)/shard_map/project3/pallas_call | solution.py:116
  49.2 2.7 %collective-permute-start.9 = (bf16[2,512,128]{2,1,0:T(8,128)(2,1)S(1)}, bf16[2,512,128]{2,1,0:T(8,128)(2,1)S(1)}, u32[]{:S(2)}, u32[]{:S(2)}) collective-permute-start(bf16[2,512,128]{2,1,0:T(8,128)(2,1)S(1)} %get-tuple-element.43.refs_3_.refs_5_), channel_id=1, source_target_pairs={{0,32},{32,64},{64,96},{96,128},{128,160},{160,192},{192,224},{224... | collective-permute-start | bytes 786440 | tf_op jit(solution)/shard_map/ppermute | solution.py:20
  52.0 3.9 %collective-permute-start.17 = (bf16[2,512,128]{2,1,0:T(8,128)(2,1)S(1)}, bf16[2,512,128]{2,1,0:T(8,128)(2,1)S(1)}, u32[]{:S(2)}, u32[]{:S(2)}) collective-permute-start(bf16[2,512,128]{2,1,0:T(8,128)(2,1)S(1)} %get-tuple-element.43.refs_3_.refs_5_), channel_id=1, source_target_pairs={{0,224},{32,0},{64,32},{96,64},{128,96},{160,128},{192,160},{224,1... | collective-permute-start | bytes 786440 | tf_op jit(solution)/shard_map/ppermute | solution.py:20
  55.9 2.0 %collective-permute-start.13 = (bf16[2,512,128]{2,1,0:T(8,128)(2,1)S(1)}, bf16[2,512,128]{2,1,0:T(8,128)(2,1)}, u32[]{:S(2)}, u32[]{:S(2)}) collective-permute-start(bf16[2,512,128]{2,1,0:T(8,128)(2,1)S(1)} %collective-permute-done.12.refs_8_.refs_13_), channel_id=1, source_target_pairs={{0,224},{32,0},{64,32},{96,64},{128,96},{160,128},{192,160},{224,1... | collective-permute-start | bytes 786440 | tf_op jit(solution)/shard_map/ppermute | solution.py:20
  57.9 4.9 %collective-permute-done.9.refs_4_.refs_6_ = bf16[2,512,128]{2,1,0:T(8,128)(2,1)S(1)} collective-permute-done((bf16[2,512,128]{2,1,0:T(8,128)(2,1)S(1)}, bf16[2,512,128]{2,1,0:T(8,128)(2,1)S(1)}, u32[]{:S(2)}, u32[]{:S(2)}) %collective-permute-start.9) | collective-permute-done | bytes 262176 | tf_op jit(solution)/shard_map/ppermute | solution.py:20
  62.9 3.3 %collective-permute-start.18 = (bf16[2,512,128]{2,1,0:T(8,128)(2,1)S(1)}, bf16[2,512,128]{2,1,0:T(8,128)(2,1)}, u32[]{:S(2)}, u32[]{:S(2)}) collective-permute-start(bf16[2,512,128]{2,1,0:T(8,128)(2,1)S(1)} %collective-permute-done.17.refs_5_.refs_7_), channel_id=1, source_target_pairs={{0,224},{32,0},{64,32},{96,64},{128,96},{160,128},{192,160},{224,1... | collective-permute-start | bytes 786440 | tf_op jit(solution)/shard_map/ppermute | solution.py:20
  66.2 1.9 %collective-permute-done.13.refs_10_.refs_15_ = bf16[2,512,128]{2,1,0:T(8,128)(2,1)} collective-permute-done((bf16[2,512,128]{2,1,0:T(8,128)(2,1)S(1)}, bf16[2,512,128]{2,1,0:T(8,128)(2,1)}, u32[]{:S(2)}, u32[]{:S(2)}) %collective-permute-start.13) | collective-permute-done | bytes 262176 | tf_op jit(solution)/shard_map/ppermute | solution.py:20
  68.1 3.8 %collective-permute-start.14 = (bf16[2,512,128]{2,1,0:T(8,128)(2,1)}, bf16[2,512,128]{2,1,0:T(8,128)(2,1)}, u32[]{:S(2)}, u32[]{:S(2)}) collective-permute-start(bf16[2,512,128]{2,1,0:T(8,128)(2,1)} %collective-permute-done.13.refs_10_.refs_15_), channel_id=1, source_target_pairs={{0,224},{32,0},{64,32},{96,64},{128,96},{160,128},{192,160},{224,1... | collective-permute-start | bytes 786440 | tf_op jit(solution)/shard_map/ppermute | solution.py:20
  73.8 5.6 %all-to-all-start.1 = ((bf16[16,256,256]{2,1,0:T(8,128)(2,1)}), bf16[16,256,256]{2,1,0:T(8,128)(2,1)S(1)}, u32[]{:S(2)}, u32[]{:S(2)}) async-start(bf16[16,256,256]{2,1,0:T(8,128)(2,1)} %copy-done.2), calls=%async_computation.1 | async-start | bytes 4194304 | tf_op jit(solution)/shard_map/all_to_all | solution.py:363
  80.1 3.0 %collective-permute-start.20 = (bf16[2,512,128]{2,1,0:T(8,128)(2,1)}, bf16[2,512,128]{2,1,0:T(8,128)(2,1)S(1)}, u32[]{:S(2)}, u32[]{:S(2)}) collective-permute-start(bf16[2,512,128]{2,1,0:T(8,128)(2,1)} %collective-permute-done.19.refs_9_.refs_14_), channel_id=1, source_target_pairs={{0,32},{32,64},{64,96},{96,128},{128,160},{160,192},{192,224},{224... | collective-permute-start | bytes 786440 | tf_op jit(solution)/shard_map/ppermute | solution.py:20
  83.6 1.9 %collective-permute-start.21 = (bf16[2,512,128]{2,1,0:T(8,128)(2,1)}, bf16[2,512,128]{2,1,0:T(8,128)(2,1)S(1)}, u32[]{:S(2)}, u32[]{:S(2)}) collective-permute-start(bf16[2,512,128]{2,1,0:T(8,128)(2,1)} %collective-permute-done.18.refs_7_.refs_9_), channel_id=1, source_target_pairs={{0,224},{32,0},{64,32},{96,64},{128,96},{160,128},{192,160},{224,1... | collective-permute-start | bytes 786440 | tf_op jit(solution)/shard_map/ppermute | solution.py:20
  85.5 8.9 %collective-permute-done.20.refs_11_.refs_16_ = bf16[2,512,128]{2,1,0:T(8,128)(2,1)S(1)} collective-permute-done((bf16[2,512,128]{2,1,0:T(8,128)(2,1)}, bf16[2,512,128]{2,1,0:T(8,128)(2,1)S(1)}, u32[]{:S(2)}, u32[]{:S(2)}) %collective-permute-start.20) | collective-permute-done | bytes 262176 | tf_op jit(solution)/shard_map/ppermute | solution.py:20
  95.8 2.0 %collective-permute-start.22 = (bf16[2,512,128]{2,1,0:T(8,128)(2,1)S(1)}, bf16[2,512,128]{2,1,0:T(8,128)(2,1)S(1)}, u32[]{:S(2)}, u32[]{:S(2)}) collective-permute-start(bf16[2,512,128]{2,1,0:T(8,128)(2,1)S(1)} %collective-permute-done.11.refs_3_.refs_10_), channel_id=1, source_target_pairs={{0,32},{32,64},{64,96},{96,128},{128,160},{160,192},{192,224},{224... | collective-permute-start | bytes 786440 | tf_op jit(solution)/shard_map/ppermute | solution.py:20
  97.8 4.7 %collective-permute-start.24 = (bf16[2,512,128]{2,1,0:T(8,128)(2,1)S(1)}, bf16[2,512,128]{2,1,0:T(8,128)(2,1)S(1)}, u32[]{:S(2)}, u32[]{:S(2)}) collective-permute-start(bf16[2,512,128]{2,1,0:T(8,128)(2,1)S(1)} %collective-permute-done.15.refs_6_.refs_19_), channel_id=1, source_target_pairs={{0,224},{32,0},{64,32},{96,64},{128,96},{160,128},{192,160},{224,1... | collective-permute-start | bytes 786440 | tf_op jit(solution)/shard_map/ppermute | solution.py:20
  103.6 4.0 %collective-permute-done.22.refs_12_ = bf16[2,512,128]{2,1,0:T(8,128)(2,1)S(1)} collective-permute-done((bf16[2,512,128]{2,1,0:T(8,128)(2,1)S(1)}, bf16[2,512,128]{2,1,0:T(8,128)(2,1)S(1)}, u32[]{:S(2)}, u32[]{:S(2)}) %collective-permute-start.22) | collective-permute-done | bytes 262176 | tf_op jit(solution)/shard_map/ppermute | solution.py:20
  107.6 7.1 %attend.1 = (bf16[512,128]{1,0:T(8,128)(2,1)S(1)}, bf16[512,128]{1,0:T(8,128)(2,1)S(1)}) custom-call(s32[96]{0:T(128)S(1)} %pad_add_fusion.refs_0_, s32[2]{0:T(128)S(1)} %copy-done.6, s32[2]{0:T(128)S(1)} %copy-done.8, bf16[512,128]{1,0:T(8,128)(2,1)S(1)} %get-tuple-element.45.refs_1_.refs_3_, bf16[528,128]{1,0:T(8,128)(2,1)S(1)} %collective-permute-done.16.refs_2_.refs_4_, ...), custom_call_target="tpu_custom_call" | custom-call | flops 14000000000 | bytes 28000000 | tf_op jit(solution)/shard_map/attend/pallas_call | solution.py:329
  117.8 4.2 %all-to-all-start.2 = ((bf16[4,256,256]{2,1,0:T(8,128)(2,1)}), bf16[4,256,256]{2,1,0:T(8,128)(2,1)S(1)}, u32[]{:S(2)}, u32[]{:S(2)}) async-start(bf16[4,256,256]{2,1,0:T(8,128)(2,1)} %broadcast_in_dim.11), calls=%async_computation.2 | async-start | bytes 1048576 | tf_op jit(solution)/shard_map/all_to_all | solution.py:31
  125.5 2.5 %collective-permute-done.26 = bf16[256,256]{1,0:T(8,128)(2,1)S(1)} collective-permute-done((bf16[256,256]{1,0:T(8,128)(2,1)S(1)}, bf16[256,256]{1,0:T(8,128)(2,1)S(1)}, u32[]{:S(2)}, u32[]{:S(2)}) %collective-permute-start.26) | collective-permute-done | bytes 131104 | tf_op jit(solution)/shard_map/ppermute | solution.py:20
  128.0 3.5 %collective-permute-done.27 = bf16[256,256]{1,0:T(8,128)(2,1)S(1)} collective-permute-done((bf16[256,256]{1,0:T(8,128)(2,1)S(1)}, bf16[256,256]{1,0:T(8,128)(2,1)S(1)}, u32[]{:S(2)}, u32[]{:S(2)}) %collective-permute-start.27) | collective-permute-done | bytes 131104 | tf_op jit(solution)/shard_map/ppermute | solution.py:20
  137.6 8.3 %collective-permute-done.30 = bf16[1024,256]{1,0:T(8,128)(2,1)S(1)} collective-permute-done((bf16[1024,256]{1,0:T(8,128)(2,1)S(1)}, bf16[1024,256]{1,0:T(8,128)(2,1)S(1)}, u32[]{:S(2)}, u32[]{:S(2)}) %collective-permute-start.30) | collective-permute-done | bytes 524320 | tf_op jit(solution)/shard_map/ppermute | solution.py:20
  146.0 2.3 %collective-permute-start.31 = (bf16[512,256]{1,0:T(8,128)(2,1)S(1)}, bf16[512,256]{1,0:T(8,128)(2,1)S(1)}, u32[]{:S(2)}, u32[]{:S(2)}) collective-permute-start(bf16[512,256]{1,0:T(8,128)(2,1)S(1)} %slice.38), channel_id=1, source_target_pairs={{0,4},{4,8},{8,12},{12,0},{1,5},{5,9},{9,13},{13,1},{2,6},{6,10},{... | collective-permute-start | bytes 786440 | tf_op jit(solution)/shard_map/ppermute | solution.py:20
  152.6 3.4 %collective-permute-done.34 = bf16[512,256]{1,0:T(8,128)(2,1)S(1)} collective-permute-done((bf16[512,256]{1,0:T(8,128)(2,1)S(1)}, bf16[512,256]{1,0:T(8,128)(2,1)S(1)}, u32[]{:S(2)}, u32[]{:S(2)}) %collective-permute-start.34) | collective-permute-done | bytes 262176 | tf_op jit(solution)/shard_map/ppermute | solution.py:20
  156.4 3.1 %collective-permute-done.33 = bf16[512,256]{1,0:T(8,128)(2,1)S(1)} collective-permute-done((bf16[512,256]{1,0:T(8,128)(2,1)S(1)}, bf16[512,256]{1,0:T(8,128)(2,1)S(1)}, u32[]{:S(2)}, u32[]{:S(2)}) %collective-permute-start.33) | collective-permute-done | bytes 262176 | tf_op jit(solution)/shard_map/ppermute | solution.py:20
  (99 shorter events, 41.7 us)
Async XLA Ops:
  2.0 14.1 %all-to-all-start = ((bf16[4,256,256]{2,1,0:T(8,128)(2,1)}), bf16[4,256,256]{2,1,0:T(8,128)(2,1)S(1)}, u32[]{:S(2)}, u32[]{:S(2)}) async-start(bf16[4,256,256]{2,1,0:T(8,128)(2,1)} %broadcast_in_dim.10), calls=%async_computation | async-start | bytes 1048576 | tf_op jit(solution)/shard_map/all_to_all | solution.py:31
  7.5 8.5 %collective-permute-start.1 = (bf16[256,256]{1,0:T(8,128)(2,1)S(1)}, bf16[256,256]{1,0:T(8,128)(2,1)S(1)}, u32[]{:S(2)}, u32[]{:S(2)}) collective-permute-start(bf16[256,256]{1,0:T(8,128)(2,1)S(1)} %get-tuple-element.69), channel_id=1, source_target_pairs={{0,12},{4,0},{8,4},{12,8},{1,13},{5,1},{9,5},{13,9},{2,14},{6,2},{... | collective-permute-start | bytes 393224 | tf_op jit(solution)/shard_map/ppermute | solution.py:20
  8.3 7.7 %collective-permute-start.2 = (bf16[256,256]{1,0:T(8,128)(2,1)S(1)}, bf16[256,256]{1,0:T(8,128)(2,1)}, u32[]{:S(2)}, u32[]{:S(2)}) collective-permute-start(bf16[256,256]{1,0:T(8,128)(2,1)S(1)} %get-tuple-element.69), channel_id=1, source_target_pairs={{0,8},{4,12},{8,0},{12,4},{1,9},{5,13},{9,1},{13,5},{2,10},{6,14},... | collective-permute-start | bytes 393224 | tf_op jit(solution)/shard_map/ppermute | solution.py:20
  17.0 13.7 %collective-permute-start.4 = (bf16[1024,256]{1,0:T(8,128)(2,1)S(1)}, bf16[1024,256]{1,0:T(8,128)(2,1)}, u32[]{:S(2)}, u32[]{:S(2)}) collective-permute-start(bf16[1024,256]{1,0:T(8,128)(2,1)S(1)} %pad_maximum_fusion), channel_id=1, source_target_pairs={{0,1},{1,2},{2,3},{3,0},{4,5},{5,6},{6,7},{7,4},{8,9},{9,10},{10,1... | collective-permute-start | bytes 1572872 | tf_op jit(solution)/shard_map/ppermute | solution.py:20
  18.9 11.9 %collective-permute-start.3 = (bf16[1024,256]{1,0:T(8,128)(2,1)S(1)}, bf16[1024,256]{1,0:T(8,128)(2,1)}, u32[]{:S(2)}, u32[]{:S(2)}) collective-permute-start(bf16[1024,256]{1,0:T(8,128)(2,1)S(1)} %bitcast.34), channel_id=1, source_target_pairs={{0,4},{4,8},{8,12},{12,0},{1,5},{5,9},{9,13},{13,1},{2,6},{6,10},{... | collective-permute-start | bytes 1572872 | tf_op jit(solution)/shard_map/ppermute | solution.py:20
  22.5 12.4 %collective-permute-start.8 = (bf16[1024,256]{1,0:T(8,128)(2,1)S(1)}, bf16[1024,256]{1,0:T(8,128)(2,1)S(1)}, u32[]{:S(2)}, u32[]{:S(2)}) collective-permute-start(bf16[1024,256]{1,0:T(8,128)(2,1)S(1)} %pad_maximum_fusion), channel_id=1, source_target_pairs={{0,3},{1,0},{2,1},{3,2},{4,7},{5,4},{6,5},{7,6},{8,11},{9,8},{10,9... | collective-permute-start | bytes 1572872 | tf_op jit(solution)/shard_map/ppermute | solution.py:20
  23.9 12.6 %collective-permute-start.7 = (bf16[1024,256]{1,0:T(8,128)(2,1)S(1)}, bf16[1024,256]{1,0:T(8,128)(2,1)}, u32[]{:S(2)}, u32[]{:S(2)}) collective-permute-start(bf16[1024,256]{1,0:T(8,128)(2,1)S(1)} %bitcast.35), channel_id=1, source_target_pairs={{0,12},{4,0},{8,4},{12,8},{1,13},{5,1},{9,5},{13,9},{2,14},{6,2},{... | collective-permute-start | bytes 1572872 | tf_op jit(solution)/shard_map/ppermute | solution.py:20
  30.9 14.6 %collective-permute-start.5 = (bf16[1024,256]{1,0:T(8,128)(2,1)}, bf16[1024,256]{1,0:T(8,128)(2,1)}, u32[]{:S(2)}, u32[]{:S(2)}) collective-permute-start(bf16[1024,256]{1,0:T(8,128)(2,1)} %collective-permute-done.3), channel_id=1, source_target_pairs={{0,4},{4,8},{8,12},{12,0},{1,5},{5,9},{9,13},{13,1},{2,6},{6,10},{... | collective-permute-start | bytes 1572872 | tf_op jit(solution)/shard_map/ppermute | solution.py:20
  33.2 12.3 %collective-permute-start.6 = (bf16[1024,256]{1,0:T(8,128)(2,1)}, bf16[1024,256]{1,0:T(8,128)(2,1)}, u32[]{:S(2)}, u32[]{:S(2)}) collective-permute-start(bf16[1024,256]{1,0:T(8,128)(2,1)} %collective-permute-done.4), channel_id=1, source_target_pairs={{0,1},{1,2},{2,3},{3,0},{4,5},{5,6},{6,7},{7,4},{8,9},{9,10},{10,1... | collective-permute-start | bytes 1572872 | tf_op jit(solution)/shard_map/ppermute | solution.py:20
  49.2 13.6 %collective-permute-start.9 = (bf16[2,512,128]{2,1,0:T(8,128)(2,1)S(1)}, bf16[2,512,128]{2,1,0:T(8,128)(2,1)S(1)}, u32[]{:S(2)}, u32[]{:S(2)}) collective-permute-start(bf16[2,512,128]{2,1,0:T(8,128)(2,1)S(1)} %get-tuple-element.43.refs_3_.refs_5_), channel_id=1, source_target_pairs={{0,32},{32,64},{64,96},{96,128},{128,160},{160,192},{192,224},{224... | collective-permute-start | bytes 786440 | tf_op jit(solution)/shard_map/ppermute | solution.py:20
  52.0 10.9 %collective-permute-start.17 = (bf16[2,512,128]{2,1,0:T(8,128)(2,1)S(1)}, bf16[2,512,128]{2,1,0:T(8,128)(2,1)S(1)}, u32[]{:S(2)}, u32[]{:S(2)}) collective-permute-start(bf16[2,512,128]{2,1,0:T(8,128)(2,1)S(1)} %get-tuple-element.43.refs_3_.refs_5_), channel_id=1, source_target_pairs={{0,224},{32,0},{64,32},{96,64},{128,96},{160,128},{192,160},{224,1... | collective-permute-start | bytes 786440 | tf_op jit(solution)/shard_map/ppermute | solution.py:20
  55.9 12.2 %collective-permute-start.13 = (bf16[2,512,128]{2,1,0:T(8,128)(2,1)S(1)}, bf16[2,512,128]{2,1,0:T(8,128)(2,1)}, u32[]{:S(2)}, u32[]{:S(2)}) collective-permute-start(bf16[2,512,128]{2,1,0:T(8,128)(2,1)S(1)} %collective-permute-done.12.refs_8_.refs_13_), channel_id=1, source_target_pairs={{0,224},{32,0},{64,32},{96,64},{128,96},{160,128},{192,160},{224,1... | collective-permute-start | bytes 786440 | tf_op jit(solution)/shard_map/ppermute | solution.py:20
  62.9 10.5 %collective-permute-start.10 = (bf16[2,512,128]{2,1,0:T(8,128)(2,1)S(1)}, bf16[2,512,128]{2,1,0:T(8,128)(2,1)}, u32[]{:S(2)}, u32[]{:S(2)}) collective-permute-start(bf16[2,512,128]{2,1,0:T(8,128)(2,1)S(1)} %collective-permute-done.9.refs_4_.refs_6_), channel_id=1, source_target_pairs={{0,32},{32,64},{64,96},{96,128},{128,160},{160,192},{192,224},{224... | collective-permute-start | bytes 786440 | tf_op jit(solution)/shard_map/ppermute | solution.py:20
  62.9 10.9 %collective-permute-start.18 = (bf16[2,512,128]{2,1,0:T(8,128)(2,1)S(1)}, bf16[2,512,128]{2,1,0:T(8,128)(2,1)}, u32[]{:S(2)}, u32[]{:S(2)}) collective-permute-start(bf16[2,512,128]{2,1,0:T(8,128)(2,1)S(1)} %collective-permute-done.17.refs_5_.refs_7_), channel_id=1, source_target_pairs={{0,224},{32,0},{64,32},{96,64},{128,96},{160,128},{192,160},{224,1... | collective-permute-start | bytes 786440 | tf_op jit(solution)/shard_map/ppermute | solution.py:20
  66.2 13.9 %collective-permute-start.19 = (bf16[2,512,128]{2,1,0:T(8,128)(2,1)S(1)}, bf16[2,512,128]{2,1,0:T(8,128)(2,1)}, u32[]{:S(2)}, u32[]{:S(2)}) collective-permute-start(bf16[2,512,128]{2,1,0:T(8,128)(2,1)S(1)} %collective-permute-done.12.refs_8_.refs_13_), channel_id=1, source_target_pairs={{0,32},{32,64},{64,96},{96,128},{128,160},{160,192},{192,224},{224... | collective-permute-start | bytes 786440 | tf_op jit(solution)/shard_map/ppermute | solution.py:20
  68.1 15.0 %collective-permute-start.14 = (bf16[2,512,128]{2,1,0:T(8,128)(2,1)}, bf16[2,512,128]{2,1,0:T(8,128)(2,1)}, u32[]{:S(2)}, u32[]{:S(2)}) collective-permute-start(bf16[2,512,128]{2,1,0:T(8,128)(2,1)} %collective-permute-done.13.refs_10_.refs_15_), channel_id=1, source_target_pairs={{0,224},{32,0},{64,32},{96,64},{128,96},{160,128},{192,160},{224,1... | collective-permute-start | bytes 786440 | tf_op jit(solution)/shard_map/ppermute | solution.py:20
  73.8 41.6 %all-to-all-start.1 = ((bf16[16,256,256]{2,1,0:T(8,128)(2,1)}), bf16[16,256,256]{2,1,0:T(8,128)(2,1)S(1)}, u32[]{:S(2)}, u32[]{:S(2)}) async-start(bf16[16,256,256]{2,1,0:T(8,128)(2,1)} %copy-done.2), calls=%async_computation.1 | async-start | bytes 4194304 | tf_op jit(solution)/shard_map/all_to_all | solution.py:363
  79.4 16.4 %collective-permute-start.11 = (bf16[2,512,128]{2,1,0:T(8,128)(2,1)}, bf16[2,512,128]{2,1,0:T(8,128)(2,1)S(1)}, u32[]{:S(2)}, u32[]{:S(2)}) collective-permute-start(bf16[2,512,128]{2,1,0:T(8,128)(2,1)} %collective-permute-done.10.refs_6_.refs_8_), channel_id=1, source_target_pairs={{0,32},{32,64},{64,96},{96,128},{128,160},{160,192},{192,224},{224... | collective-permute-start | bytes 786440 | tf_op jit(solution)/shard_map/ppermute | solution.py:20
  80.1 14.3 %collective-permute-start.20 = (bf16[2,512,128]{2,1,0:T(8,128)(2,1)}, bf16[2,512,128]{2,1,0:T(8,128)(2,1)S(1)}, u32[]{:S(2)}, u32[]{:S(2)}) collective-permute-start(bf16[2,512,128]{2,1,0:T(8,128)(2,1)} %collective-permute-done.19.refs_9_.refs_14_), channel_id=1, source_target_pairs={{0,32},{32,64},{64,96},{96,128},{128,160},{160,192},{192,224},{224... | collective-permute-start | bytes 786440 | tf_op jit(solution)/shard_map/ppermute | solution.py:20
  83.1 12.7 %collective-permute-start.15 = (bf16[2,512,128]{2,1,0:T(8,128)(2,1)}, bf16[2,512,128]{2,1,0:T(8,128)(2,1)S(1)}, u32[]{:S(2)}, u32[]{:S(2)}) collective-permute-start(bf16[2,512,128]{2,1,0:T(8,128)(2,1)} %collective-permute-done.14.refs_12_.refs_17_), channel_id=1, source_target_pairs={{0,224},{32,0},{64,32},{96,64},{128,96},{160,128},{192,160},{224,1... | collective-permute-start | bytes 786440 | tf_op jit(solution)/shard_map/ppermute | solution.py:20
  83.6 18.9 %collective-permute-start.21 = (bf16[2,512,128]{2,1,0:T(8,128)(2,1)}, bf16[2,512,128]{2,1,0:T(8,128)(2,1)S(1)}, u32[]{:S(2)}, u32[]{:S(2)}) collective-permute-start(bf16[2,512,128]{2,1,0:T(8,128)(2,1)} %collective-permute-done.18.refs_7_.refs_9_), channel_id=1, source_target_pairs={{0,224},{32,0},{64,32},{96,64},{128,96},{160,128},{192,160},{224,1... | collective-permute-start | bytes 786440 | tf_op jit(solution)/shard_map/ppermute | solution.py:20
  94.4 8.4 %collective-permute-start.23 = (bf16[2,512,128]{2,1,0:T(8,128)(2,1)S(1)}, bf16[2,512,128]{2,1,0:T(8,128)(2,1)S(1)}, u32[]{:S(2)}, u32[]{:S(2)}) collective-permute-start(bf16[2,512,128]{2,1,0:T(8,128)(2,1)S(1)} %collective-permute-done.20.refs_11_.refs_16_), channel_id=1, source_target_pairs={{0,32},{32,64},{64,96},{96,128},{128,160},{160,192},{192,224},{224... | collective-permute-start | bytes 786440 | tf_op jit(solution)/shard_map/ppermute | solution.py:20
  95.8 11.7 %collective-permute-start.22 = (bf16[2,512,128]{2,1,0:T(8,128)(2,1)S(1)}, bf16[2,512,128]{2,1,0:T(8,128)(2,1)S(1)}, u32[]{:S(2)}, u32[]{:S(2)}) collective-permute-start(bf16[2,512,128]{2,1,0:T(8,128)(2,1)S(1)} %collective-permute-done.11.refs_3_.refs_10_), channel_id=1, source_target_pairs={{0,32},{32,64},{64,96},{96,128},{128,160},{160,192},{192,224},{224... | collective-permute-start | bytes 786440 | tf_op jit(solution)/shard_map/ppermute | solution.py:20
  97.8 9.8 %collective-permute-start.24 = (bf16[2,512,128]{2,1,0:T(8,128)(2,1)S(1)}, bf16[2,512,128]{2,1,0:T(8,128)(2,1)S(1)}, u32[]{:S(2)}, u32[]{:S(2)}) collective-permute-start(bf16[2,512,128]{2,1,0:T(8,128)(2,1)S(1)} %collective-permute-done.15.refs_6_.refs_19_), channel_id=1, source_target_pairs={{0,224},{32,0},{64,32},{96,64},{128,96},{160,128},{192,160},{224,1... | collective-permute-start | bytes 786440 | tf_op jit(solution)/shard_map/ppermute | solution.py:20
  117.8 14.0 %all-to-all-start.2 = ((bf16[4,256,256]{2,1,0:T(8,128)(2,1)}), bf16[4,256,256]{2,1,0:T(8,128)(2,1)S(1)}, u32[]{:S(2)}, u32[]{:S(2)}) async-start(bf16[4,256,256]{2,1,0:T(8,128)(2,1)} %broadcast_in_dim.11), calls=%async_computation.2 | async-start | bytes 1048576 | tf_op jit(solution)/shard_map/all_to_all | solution.py:31
  122.6 9.0 %collective-permute-start.27 = (bf16[256,256]{1,0:T(8,128)(2,1)S(1)}, bf16[256,256]{1,0:T(8,128)(2,1)S(1)}, u32[]{:S(2)}, u32[]{:S(2)}) collective-permute-start(bf16[256,256]{1,0:T(8,128)(2,1)S(1)} %get-tuple-element.67), channel_id=1, source_target_pairs={{0,12},{4,0},{8,4},{12,8},{1,13},{5,1},{9,5},{13,9},{2,14},{6,2},{... | collective-permute-start | bytes 393224 | tf_op jit(solution)/shard_map/ppermute | solution.py:20
  131.9 14.1 %collective-permute-start.30 = (bf16[1024,256]{1,0:T(8,128)(2,1)S(1)}, bf16[1024,256]{1,0:T(8,128)(2,1)S(1)}, u32[]{:S(2)}, u32[]{:S(2)}) collective-permute-start(bf16[1024,256]{1,0:T(8,128)(2,1)S(1)} %pad_maximum_fusion.1), channel_id=1, source_target_pairs={{0,1},{1,2},{2,3},{3,0},{4,5},{5,6},{6,7},{7,4},{8,9},{9,10},{10,1... | collective-permute-start | bytes 1572872 | tf_op jit(solution)/shard_map/ppermute | solution.py:20
  133.6 12.3 %collective-permute-start.29 = (bf16[1024,256]{1,0:T(8,128)(2,1)S(1)}, bf16[1024,256]{1,0:T(8,128)(2,1)S(1)}, u32[]{:S(2)}, u32[]{:S(2)}) collective-permute-start(bf16[1024,256]{1,0:T(8,128)(2,1)S(1)} %bitcast.36), channel_id=1, source_target_pairs={{0,4},{4,8},{8,12},{12,0},{1,5},{5,9},{9,13},{13,1},{2,6},{6,10},{... | collective-permute-start | bytes 1572872 | tf_op jit(solution)/shard_map/ppermute | solution.py:20
  134.6 15.3 %collective-permute-start.35 = (bf16[1024,256]{1,0:T(8,128)(2,1)S(1)}, bf16[1024,256]{1,0:T(8,128)(2,1)S(1)}, u32[]{:S(2)}, u32[]{:S(2)}) collective-permute-start(bf16[1024,256]{1,0:T(8,128)(2,1)S(1)} %pad_maximum_fusion.1), channel_id=1, source_target_pairs={{0,3},{1,0},{2,1},{3,2},{4,7},{5,4},{6,5},{7,6},{8,11},{9,8},{10,9... | collective-permute-start | bytes 1572872 | tf_op jit(solution)/shard_map/ppermute | solution.py:20
  136.1 15.7 %collective-permute-start.32 = (bf16[1024,256]{1,0:T(8,128)(2,1)S(1)}, bf16[1024,256]{1,0:T(8,128)(2,1)S(1)}, u32[]{:S(2)}, u32[]{:S(2)}) collective-permute-start(bf16[1024,256]{1,0:T(8,128)(2,1)S(1)} %bitcast.37), channel_id=1, source_target_pairs={{0,12},{4,0},{8,4},{12,8},{1,13},{5,1},{9,5},{13,9},{2,14},{6,2},{... | collective-permute-start | bytes 1572872 | tf_op jit(solution)/shard_map/ppermute | solution.py:20
  148.4 7.7 %collective-permute-start.34 = (bf16[512,256]{1,0:T(8,128)(2,1)S(1)}, bf16[512,256]{1,0:T(8,128)(2,1)S(1)}, u32[]{:S(2)}, u32[]{:S(2)}) collective-permute-start(bf16[512,256]{1,0:T(8,128)(2,1)S(1)} %slice.40), channel_id=1, source_target_pairs={{0,1},{1,2},{2,3},{3,0},{4,5},{5,6},{6,7},{7,4},{8,9},{9,10},{10,1... | collective-permute-start | bytes 786440 | tf_op jit(solution)/shard_map/ppermute | solution.py:20
  151.8 7.7 %collective-permute-start.33 = (bf16[512,256]{1,0:T(8,128)(2,1)S(1)}, bf16[512,256]{1,0:T(8,128)(2,1)S(1)}, u32[]{:S(2)}, u32[]{:S(2)}) collective-permute-start(bf16[512,256]{1,0:T(8,128)(2,1)S(1)} %slice.45), channel_id=1, source_target_pairs={{0,12},{4,0},{8,4},{12,8},{1,13},{5,1},{9,5},{13,9},{2,14},{6,2},{... | collective-permute-start | bytes 786440 | tf_op jit(solution)/shard_map/ppermute | solution.py:20
  (18 other events, 117.2 us)

commit v12 on v11

--- a/solution.py
+++ b/solution.py
@@ -359,7 +359,7 @@
     own = z_ring(own)
     other = swap(send_kv)
     other = z_ring(other)
-    ordered, _ = lax.optimization_barrier((ordered, own[3:5]))
+    ordered, _ = lax.optimization_barrier((ordered, other[1:3]))
     w_cols = lax.all_to_all(ordered, ("y", "x"), 0, 0, tiled=True)
     theirs = swap(send_q)
     ids, _ = lax.optimization_barrier((theirs[512:], own[1:3]))

time: 161 us -> 155 us (0.963)
  waiting for transfers between devices: 53.7 us -> 49.3 us
    ppermute x34, waiting for transfers between devices: 51.9 us -> 47.5 us  [shift(): return lax.ppermute(a, axis, [(i, (i + step) % n) for i in range(n)])]
    ppermute x34, starting transfers between devices: 55.6 us -> 53.9 us  [shift(): return lax.ppermute(a, axis, [(i, (i + step) % n) for i in range(n)])]
  transfers between devices with their start and end apart: 40 -> 40, of which waited for: 20 -> 20; matrix products, arithmetic and copies ran while one was open for 0% -> 0% of each run, Pallas kernels for 11% -> 12%
where the time goes in v12:
time: 155 us; the launch traced here: 154 us
  starting transfers between devices  68.1 us (44%)
  waiting for transfers between devices  49.3 us (32%)
  Pallas kernels  22.9 us (15%)
  local copies, waits for them, and re-layouts  12.8 us (8%)
    ppermute x34, starting transfers between devices, shift(): return lax.ppermute(a, axis, [(i, (i + step) % n) for i in range(n)])  53.9 us
    ppermute x34, waiting for transfers between devices, shift(): return lax.ppermute(a, axis, [(i, (i + step) % n) for i in range(n)])  47.5 us
    pallas_call x6, Pallas kernels, partial_matmul(): pl.pallas_call(lambda *refs: partial_kernel(steps, counts, n, groups, has...  13.1 us
    unnamed x22, local copies, waits for them, and re-layouts  9.53 us
    all_to_all x2, starting transfers between devices, plane_matmul(): lax.all_to_all(jnp.broadcast_to(a[:n], (NXY, n, 256)).reshape(NXY * n, 25...  8.53 us
    pallas_call x1, Pallas kernels, attend(): pl.pallas_call(attend_kernel, out_shape=(jax.ShapeDtypeStruct((512, DH),...  7 us
    all_to_all x1, starting transfers between devices, body(): w_cols = lax.all_to_all(ordered, ('y', 'x'), 0, 0, tiled=True)  5.64 us
  transfers between devices with their start and end apart: 40, of which 20 were waited for; matrix products, arithmetic and copies ran while one was open for 0% of the time, Pallas kernels for 12%

profile of v12, /device:TPU:24, one launch (start us, length us, event | category | flops | bytes accessed | tf_op | source)
XLA Modules:
  0.0 154.4 jit_solution(18399339141181104009)
XLA Ops:
  2.0 4.3 %all-to-all-start = ((bf16[4,256,256]{2,1,0:T(8,128)(2,1)}), bf16[4,256,256]{2,1,0:T(8,128)(2,1)S(1)}, u32[]{:S(2)}, u32[]{:S(2)}) async-start(bf16[4,256,256]{2,1,0:T(8,128)(2,1)} %broadcast_in_dim.10), calls=%async_computation | async-start | bytes 1048576 | tf_op jit(solution)/shard_map/all_to_all | solution.py:31
  9.5 2.8 %collective-permute-done = bf16[256,256]{1,0:T(8,128)(2,1)S(1)} collective-permute-done((bf16[256,256]{1,0:T(8,128)(2,1)S(1)}, bf16[256,256]{1,0:T(8,128)(2,1)S(1)}, u32[]{:S(2)}, u32[]{:S(2)}) %collective-permute-start) | collective-permute-done | bytes 131104 | tf_op jit(solution)/shard_map/ppermute | solution.py:20
  12.4 3.7 %collective-permute-done.1 = bf16[256,256]{1,0:T(8,128)(2,1)S(1)} collective-permute-done((bf16[256,256]{1,0:T(8,128)(2,1)S(1)}, bf16[256,256]{1,0:T(8,128)(2,1)S(1)}, u32[]{:S(2)}, u32[]{:S(2)}) %collective-permute-start.1) | collective-permute-done | bytes 131104 | tf_op jit(solution)/shard_map/ppermute | solution.py:20
  17.0 1.9 %collective-permute-start.4 = (bf16[1024,256]{1,0:T(8,128)(2,1)S(1)}, bf16[1024,256]{1,0:T(8,128)(2,1)}, u32[]{:S(2)}, u32[]{:S(2)}) collective-permute-start(bf16[1024,256]{1,0:T(8,128)(2,1)S(1)} %pad_maximum_fusion), channel_id=1, source_target_pairs={{0,1},{1,2},{2,3},{3,0},{4,5},{5,6},{6,7},{7,4},{8,9},{9,10},{10,1... | collective-permute-start | bytes 1572872 | tf_op jit(solution)/shard_map/ppermute | solution.py:20
  24.6 2.8 %copy-done = bf16[4096,3,256]{2,0,1:T(8,128)(2,1)S(1)} copy-done((bf16[4096,3,256]{2,0,1:T(8,128)(2,1)S(1)}, bf16[4096,3,256]{2,0,1:T(8,128)(2,1)}, u32[]{:S(2)}) %copy-start) | copy-done | bytes 6291480
  27.4 1.9 %project0.1.refs_5_ = f32[3,512,256]{2,1,0:T(8,128)S(1)} custom-call(bf16[4,256,256]{2,1,0:T(8,128)(2,1)S(1)} %all-to-all-done, bf16[4,256,256]{2,1,0:T(8,128)(2,1)S(1)} %bitcast.38, bf16[3,4096,256]{2,1,0:T(8,128)(2,1)S(1)} %bitcast.28), custom_call_target="tpu_custom_call" | custom-call | tf_op jit(solution)/shard_map/project0/pallas_call | solution.py:116
  30.9 2.3 %collective-permute-start.5 = (bf16[1024,256]{1,0:T(8,128)(2,1)}, bf16[1024,256]{1,0:T(8,128)(2,1)}, u32[]{:S(2)}, u32[]{:S(2)}) collective-permute-start(bf16[1024,256]{1,0:T(8,128)(2,1)} %collective-permute-done.3), channel_id=1, source_target_pairs={{0,4},{4,8},{8,12},{12,0},{1,5},{5,9},{9,13},{13,1},{2,6},{6,10},{... | collective-permute-start | bytes 1572872 | tf_op jit(solution)/shard_map/ppermute | solution.py:20
  36.5 2.8 %copy-done.1 = bf16[4096,3,256]{2,0,1:T(8,128)(2,1)S(1)} copy-done((bf16[4096,3,256]{2,0,1:T(8,128)(2,1)S(1)}, bf16[4096,3,256]{2,0,1:T(8,128)(2,1)}, u32[]{:S(2)}) %copy-start.1) | copy-done | bytes 6291480
  40.3 5.1 %project1.1.refs_3_ = f32[3,512,256]{2,1,0:T(8,128)S(1)} custom-call(bf16[4,256,256]{2,1,0:T(8,128)(2,1)} %bitcast.7.refs_0_, bf16[4,256,256]{2,1,0:T(8,128)(2,1)} %bitcast.8.refs_1_, bf16[4,256,256]{2,1,0:T(8,128)(2,1)} %bitcast.9.refs_2_, bf16[4,256,256]{2,1,0:T(8,128)(2,1)S(1)} %bitcast.44, bf16[3,4096,256]{2,1,0:T(8,128)(2,1)S(1)} %bitcast.29, ...), custom_call_target="tpu_custom_call" | custom-call | tf_op jit(solution)/shard_map/project1/pallas_call | solution.py:116
  45.4 3.8 %project3.1 = (bf16[512,128]{1,0:T(8,128)(2,1)S(1)}, bf16[2,512,128]{2,1,0:T(8,128)(2,1)S(1)}, bf16[528,128]{1,0:T(8,128)(2,1)}, bf16[2,512,128]{2,1,0:T(8,128)(2,1)S(1)}) custom-call(bf16[4,256,256]{2,1,0:T(8,128)(2,1)} %bitcast.5.refs_0_, bf16[4,256,256]{2,1,0:T(8,128)(2,1)} %bitcast.6.refs_1_, bf16[3,4096,256]{2,1,0:T(8,128)(2,1)S(1)} %bitcast.30, ...), custom_call_target="tpu_custom_call" | custom-call | tf_op jit(solution)/shard_map/project3/pallas_call | solution.py:116
  49.2 2.7 %collective-permute-start.9 = (bf16[2,512,128]{2,1,0:T(8,128)(2,1)S(1)}, bf16[2,512,128]{2,1,0:T(8,128)(2,1)S(1)}, u32[]{:S(2)}, u32[]{:S(2)}) collective-permute-start(bf16[2,512,128]{2,1,0:T(8,128)(2,1)S(1)} %get-tuple-element.43.refs_3_.refs_5_), channel_id=1, source_target_pairs={{0,32},{32,64},{64,96},{96,128},{128,160},{160,192},{192,224},{224... | collective-permute-start | bytes 786440 | tf_op jit(solution)/shard_map/ppermute | solution.py:20
  52.0 5.5 %collective-permute-start.13 = (bf16[2,512,128]{2,1,0:T(8,128)(2,1)S(1)}, bf16[2,512,128]{2,1,0:T(8,128)(2,1)S(1)}, u32[]{:S(2)}, u32[]{:S(2)}) collective-permute-start(bf16[2,512,128]{2,1,0:T(8,128)(2,1)S(1)} %collective-permute-done.12.refs_8_.refs_13_), channel_id=1, source_target_pairs={{0,224},{32,0},{64,32},{96,64},{128,96},{160,128},{192,160},{224,1... | collective-permute-start | bytes 786440 | tf_op jit(solution)/shard_map/ppermute | solution.py:20
  57.4 3.2 %collective-permute-start.17 = (bf16[2,512,128]{2,1,0:T(8,128)(2,1)S(1)}, bf16[2,512,128]{2,1,0:T(8,128)(2,1)}, u32[]{:S(2)}, u32[]{:S(2)}) collective-permute-start(bf16[2,512,128]{2,1,0:T(8,128)(2,1)S(1)} %get-tuple-element.43.refs_3_.refs_5_), channel_id=1, source_target_pairs={{0,224},{32,0},{64,32},{96,64},{128,96},{160,128},{192,160},{224,1... | collective-permute-start | bytes 786440 | tf_op jit(solution)/shard_map/ppermute | solution.py:20
  60.7 2.4 %collective-permute-done.9.refs_4_.refs_6_ = bf16[2,512,128]{2,1,0:T(8,128)(2,1)S(1)} collective-permute-done((bf16[2,512,128]{2,1,0:T(8,128)(2,1)S(1)}, bf16[2,512,128]{2,1,0:T(8,128)(2,1)S(1)}, u32[]{:S(2)}, u32[]{:S(2)}) %collective-permute-start.9) | collective-permute-done | bytes 262176 | tf_op jit(solution)/shard_map/ppermute | solution.py:20
  64.1 3.7 %collective-permute-start.14 = (bf16[2,512,128]{2,1,0:T(8,128)(2,1)S(1)}, bf16[2,512,128]{2,1,0:T(8,128)(2,1)}, u32[]{:S(2)}, u32[]{:S(2)}) collective-permute-start(bf16[2,512,128]{2,1,0:T(8,128)(2,1)S(1)} %collective-permute-done.13.refs_10_.refs_15_), channel_id=1, source_target_pairs={{0,224},{32,0},{64,32},{96,64},{128,96},{160,128},{192,160},{224,1... | collective-permute-start | bytes 786440 | tf_op jit(solution)/shard_map/ppermute | solution.py:20
  68.8 5.6 %all-to-all-start.1 = ((bf16[16,256,256]{2,1,0:T(8,128)(2,1)}), bf16[16,256,256]{2,1,0:T(8,128)(2,1)S(1)}, u32[]{:S(2)}, u32[]{:S(2)}) async-start(bf16[16,256,256]{2,1,0:T(8,128)(2,1)} %copy-done.2), calls=%async_computation.1 | async-start | bytes 4194304 | tf_op jit(solution)/shard_map/all_to_all | solution.py:363
  74.4 2.0 %collective-permute-start.18 = (bf16[2,512,128]{2,1,0:T(8,128)(2,1)}, bf16[2,512,128]{2,1,0:T(8,128)(2,1)S(1)}, u32[]{:S(2)}, u32[]{:S(2)}) collective-permute-start(bf16[2,512,128]{2,1,0:T(8,128)(2,1)} %collective-permute-done.17.refs_5_.refs_7_), channel_id=1, source_target_pairs={{0,224},{32,0},{64,32},{96,64},{128,96},{160,128},{192,160},{224,1... | collective-permute-start | bytes 786440 | tf_op jit(solution)/shard_map/ppermute | solution.py:20
  76.6 3.2 %collective-permute-start.15 = (bf16[2,512,128]{2,1,0:T(8,128)(2,1)}, bf16[2,512,128]{2,1,0:T(8,128)(2,1)S(1)}, u32[]{:S(2)}, u32[]{:S(2)}) collective-permute-start(bf16[2,512,128]{2,1,0:T(8,128)(2,1)} %collective-permute-done.14.refs_12_.refs_17_), channel_id=1, source_target_pairs={{0,224},{32,0},{64,32},{96,64},{128,96},{160,128},{192,160},{224,1... | collective-permute-start | bytes 786440 | tf_op jit(solution)/shard_map/ppermute | solution.py:20
  79.9 4.1 %collective-permute-done.18.refs_7_.refs_9_ = bf16[2,512,128]{2,1,0:T(8,128)(2,1)S(1)} collective-permute-done((bf16[2,512,128]{2,1,0:T(8,128)(2,1)}, bf16[2,512,128]{2,1,0:T(8,128)(2,1)S(1)}, u32[]{:S(2)}, u32[]{:S(2)}) %collective-permute-start.18) | collective-permute-done | bytes 262176 | tf_op jit(solution)/shard_map/ppermute | solution.py:20
  84.0 3.2 %collective-permute-start.21 = (bf16[2,512,128]{2,1,0:T(8,128)(2,1)S(1)}, bf16[2,512,128]{2,1,0:T(8,128)(2,1)S(1)}, u32[]{:S(2)}, u32[]{:S(2)}) collective-permute-start(bf16[2,512,128]{2,1,0:T(8,128)(2,1)S(1)} %collective-permute-done.18.refs_7_.refs_9_), channel_id=1, source_target_pairs={{0,224},{32,0},{64,32},{96,64},{128,96},{160,128},{192,160},{224,1... | collective-permute-start | bytes 786440 | tf_op jit(solution)/shard_map/ppermute | solution.py:20
  88.5 4.2 %collective-permute-done.11.refs_3_.refs_10_ = bf16[2,512,128]{2,1,0:T(8,128)(2,1)S(1)} collective-permute-done((bf16[2,512,128]{2,1,0:T(8,128)(2,1)}, bf16[2,512,128]{2,1,0:T(8,128)(2,1)S(1)}, u32[]{:S(2)}, u32[]{:S(2)}) %collective-permute-start.11) | collective-permute-done | bytes 262176 | tf_op jit(solution)/shard_map/ppermute | solution.py:20
  92.8 3.2 %collective-permute-start.24 = (bf16[2,512,128]{2,1,0:T(8,128)(2,1)S(1)}, bf16[2,512,128]{2,1,0:T(8,128)(2,1)S(1)}, u32[]{:S(2)}, u32[]{:S(2)}) collective-permute-start(bf16[2,512,128]{2,1,0:T(8,128)(2,1)S(1)} %collective-permute-done.15.refs_6_.refs_19_), channel_id=1, source_target_pairs={{0,224},{32,0},{64,32},{96,64},{128,96},{160,128},{192,160},{224,1... | collective-permute-start | bytes 786440 | tf_op jit(solution)/shard_map/ppermute | solution.py:20
  96.0 2.4 %collective-permute-done.23.refs_5_.refs_18_ = bf16[2,512,128]{2,1,0:T(8,128)(2,1)S(1)} collective-permute-done((bf16[2,512,128]{2,1,0:T(8,128)(2,1)S(1)}, bf16[2,512,128]{2,1,0:T(8,128)(2,1)S(1)}, u32[]{:S(2)}, u32[]{:S(2)}) %collective-permute-start.23) | collective-permute-done | bytes 262176 | tf_op jit(solution)/shard_map/ppermute | solution.py:20
  99.2 2.2 %collective-permute-done.22.refs_12_ = bf16[2,512,128]{2,1,0:T(8,128)(2,1)S(1)} collective-permute-done((bf16[2,512,128]{2,1,0:T(8,128)(2,1)S(1)}, bf16[2,512,128]{2,1,0:T(8,128)(2,1)S(1)}, u32[]{:S(2)}, u32[]{:S(2)}) %collective-permute-start.22) | collective-permute-done | bytes 262176 | tf_op jit(solution)/shard_map/ppermute | solution.py:20
  101.5 7.0 %attend.1 = (bf16[512,128]{1,0:T(8,128)(2,1)S(1)}, bf16[512,128]{1,0:T(8,128)(2,1)S(1)}) custom-call(s32[96]{0:T(128)S(1)} %pad_add_fusion.refs_0_, s32[2]{0:T(128)S(1)} %copy-done.6, s32[2]{0:T(128)S(1)} %copy-done.8, bf16[512,128]{1,0:T(8,128)(2,1)S(1)} %get-tuple-element.45.refs_1_.refs_3_, bf16[528,128]{1,0:T(8,128)(2,1)S(1)} %collective-permute-done.16.refs_2_.refs_4_, ...), custom_call_target="tpu_custom_call" | custom-call | flops 14000000000 | bytes 28000000 | tf_op jit(solution)/shard_map/attend/pallas_call | solution.py:329
  111.6 4.2 %all-to-all-start.2 = ((bf16[4,256,256]{2,1,0:T(8,128)(2,1)}), bf16[4,256,256]{2,1,0:T(8,128)(2,1)S(1)}, u32[]{:S(2)}, u32[]{:S(2)}) async-start(bf16[4,256,256]{2,1,0:T(8,128)(2,1)} %broadcast_in_dim.11), calls=%async_computation.2 | async-start | bytes 1048576 | tf_op jit(solution)/shard_map/all_to_all | solution.py:31
  119.3 2.5 %collective-permute-done.26 = bf16[256,256]{1,0:T(8,128)(2,1)S(1)} collective-permute-done((bf16[256,256]{1,0:T(8,128)(2,1)S(1)}, bf16[256,256]{1,0:T(8,128)(2,1)S(1)}, u32[]{:S(2)}, u32[]{:S(2)}) %collective-permute-start.26) | collective-permute-done | bytes 131104 | tf_op jit(solution)/shard_map/ppermute | solution.py:20
  121.9 3.5 %collective-permute-done.27 = bf16[256,256]{1,0:T(8,128)(2,1)S(1)} collective-permute-done((bf16[256,256]{1,0:T(8,128)(2,1)S(1)}, bf16[256,256]{1,0:T(8,128)(2,1)S(1)}, u32[]{:S(2)}, u32[]{:S(2)}) %collective-permute-start.27) | collective-permute-done | bytes 131104 | tf_op jit(solution)/shard_map/ppermute | solution.py:20
  131.5 8.3 %collective-permute-done.30 = bf16[1024,256]{1,0:T(8,128)(2,1)S(1)} collective-permute-done((bf16[1024,256]{1,0:T(8,128)(2,1)S(1)}, bf16[1024,256]{1,0:T(8,128)(2,1)S(1)}, u32[]{:S(2)}, u32[]{:S(2)}) %collective-permute-start.30) | collective-permute-done | bytes 524320 | tf_op jit(solution)/shard_map/ppermute | solution.py:20
  139.8 2.3 %collective-permute-start.31 = (bf16[512,256]{1,0:T(8,128)(2,1)S(1)}, bf16[512,256]{1,0:T(8,128)(2,1)S(1)}, u32[]{:S(2)}, u32[]{:S(2)}) collective-permute-start(bf16[512,256]{1,0:T(8,128)(2,1)S(1)} %slice.38), channel_id=1, source_target_pairs={{0,4},{4,8},{8,12},{12,0},{1,5},{5,9},{9,13},{13,1},{2,6},{6,10},{... | collective-permute-start | bytes 786440 | tf_op jit(solution)/shard_map/ppermute | solution.py:20
  146.5 3.4 %collective-permute-done.34 = bf16[512,256]{1,0:T(8,128)(2,1)S(1)} collective-permute-done((bf16[512,256]{1,0:T(8,128)(2,1)S(1)}, bf16[512,256]{1,0:T(8,128)(2,1)S(1)}, u32[]{:S(2)}, u32[]{:S(2)}) %collective-permute-start.34) | collective-permute-done | bytes 262176 | tf_op jit(solution)/shard_map/ppermute | solution.py:20
  150.2 3.1 %collective-permute-done.33 = bf16[512,256]{1,0:T(8,128)(2,1)S(1)} collective-permute-done((bf16[512,256]{1,0:T(8,128)(2,1)S(1)}, bf16[512,256]{1,0:T(8,128)(2,1)S(1)}, u32[]{:S(2)}, u32[]{:S(2)}) %collective-permute-start.33) | collective-permute-done | bytes 262176 | tf_op jit(solution)/shard_map/ppermute | solution.py:20
  (99 shorter events, 40.6 us)
Async XLA Ops:
  2.0 14.1 %all-to-all-start = ((bf16[4,256,256]{2,1,0:T(8,128)(2,1)}), bf16[4,256,256]{2,1,0:T(8,128)(2,1)S(1)}, u32[]{:S(2)}, u32[]{:S(2)}) async-start(bf16[4,256,256]{2,1,0:T(8,128)(2,1)} %broadcast_in_dim.10), calls=%async_computation | async-start | bytes 1048576 | tf_op jit(solution)/shard_map/all_to_all | solution.py:31
  7.5 8.5 %collective-permute-start.1 = (bf16[256,256]{1,0:T(8,128)(2,1)S(1)}, bf16[256,256]{1,0:T(8,128)(2,1)S(1)}, u32[]{:S(2)}, u32[]{:S(2)}) collective-permute-start(bf16[256,256]{1,0:T(8,128)(2,1)S(1)} %get-tuple-element.69), channel_id=1, source_target_pairs={{0,12},{4,0},{8,4},{12,8},{1,13},{5,1},{9,5},{13,9},{2,14},{6,2},{... | collective-permute-start | bytes 393224 | tf_op jit(solution)/shard_map/ppermute | solution.py:20
  8.3 7.7 %collective-permute-start.2 = (bf16[256,256]{1,0:T(8,128)(2,1)S(1)}, bf16[256,256]{1,0:T(8,128)(2,1)}, u32[]{:S(2)}, u32[]{:S(2)}) collective-permute-start(bf16[256,256]{1,0:T(8,128)(2,1)S(1)} %get-tuple-element.69), channel_id=1, source_target_pairs={{0,8},{4,12},{8,0},{12,4},{1,9},{5,13},{9,1},{13,5},{2,10},{6,14},... | collective-permute-start | bytes 393224 | tf_op jit(solution)/shard_map/ppermute | solution.py:20
  17.0 13.7 %collective-permute-start.4 = (bf16[1024,256]{1,0:T(8,128)(2,1)S(1)}, bf16[1024,256]{1,0:T(8,128)(2,1)}, u32[]{:S(2)}, u32[]{:S(2)}) collective-permute-start(bf16[1024,256]{1,0:T(8,128)(2,1)S(1)} %pad_maximum_fusion), channel_id=1, source_target_pairs={{0,1},{1,2},{2,3},{3,0},{4,5},{5,6},{6,7},{7,4},{8,9},{9,10},{10,1... | collective-permute-start | bytes 1572872 | tf_op jit(solution)/shard_map/ppermute | solution.py:20
  18.9 11.9 %collective-permute-start.3 = (bf16[1024,256]{1,0:T(8,128)(2,1)S(1)}, bf16[1024,256]{1,0:T(8,128)(2,1)}, u32[]{:S(2)}, u32[]{:S(2)}) collective-permute-start(bf16[1024,256]{1,0:T(8,128)(2,1)S(1)} %bitcast.34), channel_id=1, source_target_pairs={{0,4},{4,8},{8,12},{12,0},{1,5},{5,9},{9,13},{13,1},{2,6},{6,10},{... | collective-permute-start | bytes 1572872 | tf_op jit(solution)/shard_map/ppermute | solution.py:20
  22.5 12.4 %collective-permute-start.8 = (bf16[1024,256]{1,0:T(8,128)(2,1)S(1)}, bf16[1024,256]{1,0:T(8,128)(2,1)S(1)}, u32[]{:S(2)}, u32[]{:S(2)}) collective-permute-start(bf16[1024,256]{1,0:T(8,128)(2,1)S(1)} %pad_maximum_fusion), channel_id=1, source_target_pairs={{0,3},{1,0},{2,1},{3,2},{4,7},{5,4},{6,5},{7,6},{8,11},{9,8},{10,9... | collective-permute-start | bytes 1572872 | tf_op jit(solution)/shard_map/ppermute | solution.py:20
  23.9 12.6 %collective-permute-start.7 = (bf16[1024,256]{1,0:T(8,128)(2,1)S(1)}, bf16[1024,256]{1,0:T(8,128)(2,1)}, u32[]{:S(2)}, u32[]{:S(2)}) collective-permute-start(bf16[1024,256]{1,0:T(8,128)(2,1)S(1)} %bitcast.35), channel_id=1, source_target_pairs={{0,12},{4,0},{8,4},{12,8},{1,13},{5,1},{9,5},{13,9},{2,14},{6,2},{... | collective-permute-start | bytes 1572872 | tf_op jit(solution)/shard_map/ppermute | solution.py:20
  30.9 14.6 %collective-permute-start.5 = (bf16[1024,256]{1,0:T(8,128)(2,1)}, bf16[1024,256]{1,0:T(8,128)(2,1)}, u32[]{:S(2)}, u32[]{:S(2)}) collective-permute-start(bf16[1024,256]{1,0:T(8,128)(2,1)} %collective-permute-done.3), channel_id=1, source_target_pairs={{0,4},{4,8},{8,12},{12,0},{1,5},{5,9},{9,13},{13,1},{2,6},{6,10},{... | collective-permute-start | bytes 1572872 | tf_op jit(solution)/shard_map/ppermute | solution.py:20
  33.2 12.3 %collective-permute-start.6 = (bf16[1024,256]{1,0:T(8,128)(2,1)}, bf16[1024,256]{1,0:T(8,128)(2,1)}, u32[]{:S(2)}, u32[]{:S(2)}) collective-permute-start(bf16[1024,256]{1,0:T(8,128)(2,1)} %collective-permute-done.4), channel_id=1, source_target_pairs={{0,1},{1,2},{2,3},{3,0},{4,5},{5,6},{6,7},{7,4},{8,9},{9,10},{10,1... | collective-permute-start | bytes 1572872 | tf_op jit(solution)/shard_map/ppermute | solution.py:20
  49.2 13.8 %collective-permute-start.9 = (bf16[2,512,128]{2,1,0:T(8,128)(2,1)S(1)}, bf16[2,512,128]{2,1,0:T(8,128)(2,1)S(1)}, u32[]{:S(2)}, u32[]{:S(2)}) collective-permute-start(bf16[2,512,128]{2,1,0:T(8,128)(2,1)S(1)} %get-tuple-element.43.refs_3_.refs_5_), channel_id=1, source_target_pairs={{0,32},{32,64},{64,96},{96,128},{128,160},{160,192},{192,224},{224... | collective-permute-start | bytes 786440 | tf_op jit(solution)/shard_map/ppermute | solution.py:20
  52.0 12.1 %collective-permute-start.13 = (bf16[2,512,128]{2,1,0:T(8,128)(2,1)S(1)}, bf16[2,512,128]{2,1,0:T(8,128)(2,1)S(1)}, u32[]{:S(2)}, u32[]{:S(2)}) collective-permute-start(bf16[2,512,128]{2,1,0:T(8,128)(2,1)S(1)} %collective-permute-done.12.refs_8_.refs_13_), channel_id=1, source_target_pairs={{0,224},{32,0},{64,32},{96,64},{128,96},{160,128},{192,160},{224,1... | collective-permute-start | bytes 786440 | tf_op jit(solution)/shard_map/ppermute | solution.py:20
  57.4 11.3 %collective-permute-start.19 = (bf16[2,512,128]{2,1,0:T(8,128)(2,1)S(1)}, bf16[2,512,128]{2,1,0:T(8,128)(2,1)}, u32[]{:S(2)}, u32[]{:S(2)}) collective-permute-start(bf16[2,512,128]{2,1,0:T(8,128)(2,1)S(1)} %collective-permute-done.12.refs_8_.refs_13_), channel_id=1, source_target_pairs={{0,32},{32,64},{64,96},{96,128},{128,160},{160,192},{192,224},{224... | collective-permute-start | bytes 786440 | tf_op jit(solution)/shard_map/ppermute | solution.py:20
  57.4 17.0 %collective-permute-start.17 = (bf16[2,512,128]{2,1,0:T(8,128)(2,1)S(1)}, bf16[2,512,128]{2,1,0:T(8,128)(2,1)}, u32[]{:S(2)}, u32[]{:S(2)}) collective-permute-start(bf16[2,512,128]{2,1,0:T(8,128)(2,1)S(1)} %get-tuple-element.43.refs_3_.refs_5_), channel_id=1, source_target_pairs={{0,224},{32,0},{64,32},{96,64},{128,96},{160,128},{192,160},{224,1... | collective-permute-start | bytes 786440 | tf_op jit(solution)/shard_map/ppermute | solution.py:20
  63.1 13.5 %collective-permute-start.10 = (bf16[2,512,128]{2,1,0:T(8,128)(2,1)S(1)}, bf16[2,512,128]{2,1,0:T(8,128)(2,1)}, u32[]{:S(2)}, u32[]{:S(2)}) collective-permute-start(bf16[2,512,128]{2,1,0:T(8,128)(2,1)S(1)} %collective-permute-done.9.refs_4_.refs_6_), channel_id=1, source_target_pairs={{0,32},{32,64},{64,96},{96,128},{128,160},{160,192},{192,224},{224... | collective-permute-start | bytes 786440 | tf_op jit(solution)/shard_map/ppermute | solution.py:20
  64.1 12.5 %collective-permute-start.14 = (bf16[2,512,128]{2,1,0:T(8,128)(2,1)S(1)}, bf16[2,512,128]{2,1,0:T(8,128)(2,1)}, u32[]{:S(2)}, u32[]{:S(2)}) collective-permute-start(bf16[2,512,128]{2,1,0:T(8,128)(2,1)S(1)} %collective-permute-done.13.refs_10_.refs_15_), channel_id=1, source_target_pairs={{0,224},{32,0},{64,32},{96,64},{128,96},{160,128},{192,160},{224,1... | collective-permute-start | bytes 786440 | tf_op jit(solution)/shard_map/ppermute | solution.py:20
  68.8 40.4 %all-to-all-start.1 = ((bf16[16,256,256]{2,1,0:T(8,128)(2,1)}), bf16[16,256,256]{2,1,0:T(8,128)(2,1)S(1)}, u32[]{:S(2)}, u32[]{:S(2)}) async-start(bf16[16,256,256]{2,1,0:T(8,128)(2,1)} %copy-done.2), calls=%async_computation.1 | async-start | bytes 4194304 | tf_op jit(solution)/shard_map/all_to_all | solution.py:363
  74.4 9.5 %collective-permute-start.18 = (bf16[2,512,128]{2,1,0:T(8,128)(2,1)}, bf16[2,512,128]{2,1,0:T(8,128)(2,1)S(1)}, u32[]{:S(2)}, u32[]{:S(2)}) collective-permute-start(bf16[2,512,128]{2,1,0:T(8,128)(2,1)} %collective-permute-done.17.refs_5_.refs_7_), channel_id=1, source_target_pairs={{0,224},{32,0},{64,32},{96,64},{128,96},{160,128},{192,160},{224,1... | collective-permute-start | bytes 786440 | tf_op jit(solution)/shard_map/ppermute | solution.py:20
  76.5 10.7 %collective-permute-start.20 = (bf16[2,512,128]{2,1,0:T(8,128)(2,1)}, bf16[2,512,128]{2,1,0:T(8,128)(2,1)S(1)}, u32[]{:S(2)}, u32[]{:S(2)}) collective-permute-start(bf16[2,512,128]{2,1,0:T(8,128)(2,1)} %collective-permute-done.19.refs_9_.refs_14_), channel_id=1, source_target_pairs={{0,32},{32,64},{64,96},{96,128},{128,160},{160,192},{192,224},{224... | collective-permute-start | bytes 786440 | tf_op jit(solution)/shard_map/ppermute | solution.py:20
  76.6 16.2 %collective-permute-start.11 = (bf16[2,512,128]{2,1,0:T(8,128)(2,1)}, bf16[2,512,128]{2,1,0:T(8,128)(2,1)S(1)}, u32[]{:S(2)}, u32[]{:S(2)}) collective-permute-start(bf16[2,512,128]{2,1,0:T(8,128)(2,1)} %collective-permute-done.10.refs_6_.refs_8_), channel_id=1, source_target_pairs={{0,32},{32,64},{64,96},{96,128},{128,160},{160,192},{192,224},{224... | collective-permute-start | bytes 786440 | tf_op jit(solution)/shard_map/ppermute | solution.py:20
  76.6 16.2 %collective-permute-start.15 = (bf16[2,512,128]{2,1,0:T(8,128)(2,1)}, bf16[2,512,128]{2,1,0:T(8,128)(2,1)S(1)}, u32[]{:S(2)}, u32[]{:S(2)}) collective-permute-start(bf16[2,512,128]{2,1,0:T(8,128)(2,1)} %collective-permute-done.14.refs_12_.refs_17_), channel_id=1, source_target_pairs={{0,224},{32,0},{64,32},{96,64},{128,96},{160,128},{192,160},{224,1... | collective-permute-start | bytes 786440 | tf_op jit(solution)/shard_map/ppermute | solution.py:20
  84.0 12.0 %collective-permute-start.21 = (bf16[2,512,128]{2,1,0:T(8,128)(2,1)S(1)}, bf16[2,512,128]{2,1,0:T(8,128)(2,1)S(1)}, u32[]{:S(2)}, u32[]{:S(2)}) collective-permute-start(bf16[2,512,128]{2,1,0:T(8,128)(2,1)S(1)} %collective-permute-done.18.refs_7_.refs_9_), channel_id=1, source_target_pairs={{0,224},{32,0},{64,32},{96,64},{128,96},{160,128},{192,160},{224,1... | collective-permute-start | bytes 786440 | tf_op jit(solution)/shard_map/ppermute | solution.py:20
  87.1 11.2 %collective-permute-start.23 = (bf16[2,512,128]{2,1,0:T(8,128)(2,1)S(1)}, bf16[2,512,128]{2,1,0:T(8,128)(2,1)S(1)}, u32[]{:S(2)}, u32[]{:S(2)}) collective-permute-start(bf16[2,512,128]{2,1,0:T(8,128)(2,1)S(1)} %collective-permute-done.20.refs_11_.refs_16_), channel_id=1, source_target_pairs={{0,32},{32,64},{64,96},{96,128},{128,160},{160,192},{192,224},{224... | collective-permute-start | bytes 786440 | tf_op jit(solution)/shard_map/ppermute | solution.py:20
  92.8 8.7 %collective-permute-start.22 = (bf16[2,512,128]{2,1,0:T(8,128)(2,1)S(1)}, bf16[2,512,128]{2,1,0:T(8,128)(2,1)S(1)}, u32[]{:S(2)}, u32[]{:S(2)}) collective-permute-start(bf16[2,512,128]{2,1,0:T(8,128)(2,1)S(1)} %collective-permute-done.11.refs_3_.refs_10_), channel_id=1, source_target_pairs={{0,32},{32,64},{64,96},{96,128},{128,160},{160,192},{192,224},{224... | collective-permute-start | bytes 786440 | tf_op jit(solution)/shard_map/ppermute | solution.py:20
  92.8 8.7 %collective-permute-start.24 = (bf16[2,512,128]{2,1,0:T(8,128)(2,1)S(1)}, bf16[2,512,128]{2,1,0:T(8,128)(2,1)S(1)}, u32[]{:S(2)}, u32[]{:S(2)}) collective-permute-start(bf16[2,512,128]{2,1,0:T(8,128)(2,1)S(1)} %collective-permute-done.15.refs_6_.refs_19_), channel_id=1, source_target_pairs={{0,224},{32,0},{64,32},{96,64},{128,96},{160,128},{192,160},{224,1... | collective-permute-start | bytes 786440 | tf_op jit(solution)/shard_map/ppermute | solution.py:20
  111.6 14.0 %all-to-all-start.2 = ((bf16[4,256,256]{2,1,0:T(8,128)(2,1)}), bf16[4,256,256]{2,1,0:T(8,128)(2,1)S(1)}, u32[]{:S(2)}, u32[]{:S(2)}) async-start(bf16[4,256,256]{2,1,0:T(8,128)(2,1)} %broadcast_in_dim.11), calls=%async_computation.2 | async-start | bytes 1048576 | tf_op jit(solution)/shard_map/all_to_all | solution.py:31
  116.4 9.0 %collective-permute-start.27 = (bf16[256,256]{1,0:T(8,128)(2,1)S(1)}, bf16[256,256]{1,0:T(8,128)(2,1)S(1)}, u32[]{:S(2)}, u32[]{:S(2)}) collective-permute-start(bf16[256,256]{1,0:T(8,128)(2,1)S(1)} %get-tuple-element.67), channel_id=1, source_target_pairs={{0,12},{4,0},{8,4},{12,8},{1,13},{5,1},{9,5},{13,9},{2,14},{6,2},{... | collective-permute-start | bytes 393224 | tf_op jit(solution)/shard_map/ppermute | solution.py:20
  125.7 14.1 %collective-permute-start.30 = (bf16[1024,256]{1,0:T(8,128)(2,1)S(1)}, bf16[1024,256]{1,0:T(8,128)(2,1)S(1)}, u32[]{:S(2)}, u32[]{:S(2)}) collective-permute-start(bf16[1024,256]{1,0:T(8,128)(2,1)S(1)} %pad_maximum_fusion.1), channel_id=1, source_target_pairs={{0,1},{1,2},{2,3},{3,0},{4,5},{5,6},{6,7},{7,4},{8,9},{9,10},{10,1... | collective-permute-start | bytes 1572872 | tf_op jit(solution)/shard_map/ppermute | solution.py:20
  127.4 12.3 %collective-permute-start.29 = (bf16[1024,256]{1,0:T(8,128)(2,1)S(1)}, bf16[1024,256]{1,0:T(8,128)(2,1)S(1)}, u32[]{:S(2)}, u32[]{:S(2)}) collective-permute-start(bf16[1024,256]{1,0:T(8,128)(2,1)S(1)} %bitcast.36), channel_id=1, source_target_pairs={{0,4},{4,8},{8,12},{12,0},{1,5},{5,9},{9,13},{13,1},{2,6},{6,10},{... | collective-permute-start | bytes 1572872 | tf_op jit(solution)/shard_map/ppermute | solution.py:20
  128.5 15.3 %collective-permute-start.35 = (bf16[1024,256]{1,0:T(8,128)(2,1)S(1)}, bf16[1024,256]{1,0:T(8,128)(2,1)S(1)}, u32[]{:S(2)}, u32[]{:S(2)}) collective-permute-start(bf16[1024,256]{1,0:T(8,128)(2,1)S(1)} %pad_maximum_fusion.1), channel_id=1, source_target_pairs={{0,3},{1,0},{2,1},{3,2},{4,7},{5,4},{6,5},{7,6},{8,11},{9,8},{10,9... | collective-permute-start | bytes 1572872 | tf_op jit(solution)/shard_map/ppermute | solution.py:20
  130.0 15.7 %collective-permute-start.32 = (bf16[1024,256]{1,0:T(8,128)(2,1)S(1)}, bf16[1024,256]{1,0:T(8,128)(2,1)S(1)}, u32[]{:S(2)}, u32[]{:S(2)}) collective-permute-start(bf16[1024,256]{1,0:T(8,128)(2,1)S(1)} %bitcast.37), channel_id=1, source_target_pairs={{0,12},{4,0},{8,4},{12,8},{1,13},{5,1},{9,5},{13,9},{2,14},{6,2},{... | collective-permute-start | bytes 1572872 | tf_op jit(solution)/shard_map/ppermute | solution.py:20
  142.2 7.7 %collective-permute-start.34 = (bf16[512,256]{1,0:T(8,128)(2,1)S(1)}, bf16[512,256]{1,0:T(8,128)(2,1)S(1)}, u32[]{:S(2)}, u32[]{:S(2)}) collective-permute-start(bf16[512,256]{1,0:T(8,128)(2,1)S(1)} %slice.40), channel_id=1, source_target_pairs={{0,1},{1,2},{2,3},{3,0},{4,5},{5,6},{6,7},{7,4},{8,9},{9,10},{10,1... | collective-permute-start | bytes 786440 | tf_op jit(solution)/shard_map/ppermute | solution.py:20
  145.6 7.7 %collective-permute-start.33 = (bf16[512,256]{1,0:T(8,128)(2,1)S(1)}, bf16[512,256]{1,0:T(8,128)(2,1)S(1)}, u32[]{:S(2)}, u32[]{:S(2)}) collective-permute-start(bf16[512,256]{1,0:T(8,128)(2,1)S(1)} %slice.45), channel_id=1, source_target_pairs={{0,12},{4,0},{8,4},{12,8},{1,13},{5,1},{9,5},{13,9},{2,14},{6,2},{... | collective-permute-start | bytes 786440 | tf_op jit(solution)/shard_map/ppermute | solution.py:20
  (18 other events, 111.3 us)
